TPU v7x, 512 devices: a whole 4x4x16 slice. The times are simulated.
512 devices in a mesh: dp: 64 (over y, x, z_lo), mp: 8 (over z_hi, core).
Axes of the slice: x: 4, y: 4, z: 16 (z_hi: 4, z_lo: 4; z = z_hi * 4 + z_lo), core: 2. Of those that a mesh axis runs over, the one named last changes fastest.
Arguments:
- normed: bfloat16 [4096, 6144], P('mp', 'dp'), may hold values from -6 to 6
- hidden_cot: bfloat16 [4096, 12288], P('mp', 'dp'), may hold values from -6 to 6
- up_rows: bfloat16 [12288, 6144], P('dp'), may hold values from -0.078125 to 0.078125
Outputs:
- hidden: bfloat16 [4096, 12288], P('mp', 'dp')
- input_grad: bfloat16 [4096, 6144], P('mp', 'dp')
- up_grad: bfloat16 [12288, 6144], P('dp')
All inputs are finite; a program needn't handle non-finite values.
Results may differ from a plain program's by a relative error of at most 0.013.
Values may be sent and summed in bfloat16 or wider, within the bound.
No kernel may reach another device: no remote copies, remote signals or barrier semaphores. Data moves between devices by JAX's collectives and lax.ppermute only.
A program may use at most 64 MiB of HBM per device.

v0:
```python
import jax
import jax.numpy as jnp
from jax import lax
from jax.sharding import PartitionSpec as P

inv_sqrt_two = 0.7071067811865476
inv_sqrt_two_pi = 0.3989422804014327


def gelu_parts(preact):
    normal_cdf = 0.5 * (1.0 + lax.erf(preact * inv_sqrt_two))
    gelu_out = preact * normal_cdf
    gelu_slope = normal_cdf + preact * jnp.exp(-0.5 * preact * preact) * inv_sqrt_two_pi
    return (gelu_out, gelu_slope)


def contract_last(left, right):
    return lax.dot_general(
        left, right, (((1,), (1,)), ((), ())), preferred_element_type=jnp.float32
    )


def contract_first(left, right):
    return lax.dot_general(
        left, right, (((0,), (0,)), ((), ())), preferred_element_type=jnp.float32
    )


def local(normed, hidden_cot, up_rows):
    full_in = lax.all_gather(normed, "dp", axis=1, tiled=True)
    column_rows = lax.all_to_all(up_rows, "dp", split_axis=1, concat_axis=0, tiled=True)
    replicas = lax.axis_size("mp")
    preact = contract_last(full_in, up_rows)
    gelu_out, gelu_slope = gelu_parts(preact)
    hidden = gelu_out.astype(jnp.bfloat16)
    hidden_grad = (hidden_cot.astype(jnp.float32) * gelu_slope).astype(jnp.bfloat16)
    up_term = contract_first(hidden_grad, full_in)
    up_total = lax.psum(up_term.astype(jnp.bfloat16), "mp").astype(jnp.float32)
    up_grad = (up_total / replicas).astype(jnp.bfloat16)
    input_total = jnp.dot(
        lax.all_gather(hidden_grad, "dp", axis=1, tiled=True),
        column_rows,
        preferred_element_type=jnp.float32,
    )
    input_grad = input_total.astype(jnp.bfloat16)
    return (hidden, input_grad, up_grad)


def solution(mesh):
    return jax.shard_map(
        local,
        mesh=mesh,
        in_specs=(P("mp", "dp"), P("mp", "dp"), P("dp", None)),
        out_specs=(P("mp", "dp"), P("mp", "dp"), P("dp", None)),
        check_vma=False,
    )
```

profile of v0, /device:TPU:128, one launch (start us, length us, event | category | flops | bytes accessed | tf_op | source)
XLA Modules:
  0.0 975.7 jit_solution(11073580016380807391)
XLA Ops:
  7.2 0.0 all-gather.3.cloned.1.call-start
  7.2 0.7 all-gather.3.cloned.1.call-update
  7.9 0.0 all-reduce.2.cloned.1.call-start
  7.9 379.4 %all-gather.3.cloned.1.call-done = bf16[512,6144]{0,1:T(8,128)(2,1)} async-done(((bf16[512,96]{0,1:T(8,128)(2,1)}), bf16[512,6144]{0,1:T(8,128)(2,1)}) %all-gather.3.cloned.1.call-update) | async-done | bytes 6291472 | tf_op jit(solution)/shard_map/all_gather | solution.py:30
  387.4 5.7 fusion.5
  393.1 0.0 copy-start
  393.1 6.4 convolution_convert_fusion
  399.5 0.0 copy-done
  399.5 0.0 all-reduce.2.cloned.1.call-update
  399.5 0.0 all-gather.5.cloned.1.call-start
  399.6 0.7 all-gather.5.cloned.1.call-update
  400.3 3.0 copy.7
  403.3 95.6 %all_to_all.19 = bf16[192,64,96]{0,2,1:T(8,128)(2,1)S(1)} all-to-all(bf16[192,64,96]{0,2,1:T(8,128)(2,1)S(1)} %bitcast.11), channel_id=1, replica_groups=mesh['dp'=64,'mp'=8] {'dp'}, dimensions={1} | all-to-all | bytes 4718592 | tf_op jit(solution)/shard_map/all_to_all | solution.py:31
  498.8 3.4 copy.8
  502.3 5.1 all_to_all.17
  507.4 50.8 %all-reduce.2.cloned.1.call-done = bf16[192,6144]{1,0:T(8,128)(2,1)} async-done(((bf16[192,6144]{1,0:T(8,128)(2,1)}), bf16[192,6144]{1,0:T(8,128)(2,1)}) %all-reduce.2.cloned.1.call-update) | async-done | bytes 2359312 | tf_op jit(solution)/shard_map/psum | solution.py:38
  558.2 3.5 multiply_convert_fusion
  561.7 400.1 %all-gather.5.cloned.1.call-done = bf16[512,12288]{0,1:T(8,128)(2,1)} async-done(((bf16[512,192]{0,1:T(8,128)(2,1)}), bf16[512,12288]{0,1:T(8,128)(2,1)}) %all-gather.5.cloned.1.call-update) | async-done | bytes 12582928 | tf_op jit(solution)/shard_map/all_gather | solution.py:41
  961.8 7.3 convolution_convert_fusion.1
Async XLA Ops:
  7.2 380.2 %all-gather.3.cloned.1.call-start = ((), (), s32[]{:S(2)}) async-start(), calls=%async_computation.1 | async-start | bytes 6389760 | tf_op jit(solution)/shard_map/all_gather | solution.py:30
  7.9 550.3 %all-reduce.2.cloned.1.call-start = ((), (), s32[]{:S(2)}) async-start(), calls=%async_computation.3 | async-start | bytes 4718592 | tf_op jit(solution)/shard_map/psum | solution.py:38
  393.1 6.4 copy-start
  399.5 562.3 %all-gather.5.cloned.1.call-start = ((), (), s32[]{:S(2)}) async-start(), calls=%async_computation.2 | async-start | bytes 12779520 | tf_op jit(solution)/shard_map/all_gather | solution.py:41
Sparse Core Ops, SparseCore 0:
  10.0 377.2 all-gather.2
  399.6 158.5 all-reduce.1
  560.3 401.4 all-gather.4
where the time goes:
time: 976 us
  waiting for transfers between devices  832 us (85%)
  blocking collectives  95.6 us (10%)
  matrix products  19.5 us (2%)
  between operations  13.8 us (1%)
  local copies, waits for them, and re-layouts  11.6 us (1%)
    all_gather x1, waiting for transfers between devices, local(): lax.all_gather(hidden_grad, 'dp', axis=1, tiled=True)  400 us
    all_gather x1, waiting for transfers between devices, local(): full_in = lax.all_gather(normed, 'dp', axis=1, tiled=True)  379 us
    all_to_all x1, blocking collectives, local(): lax.all_to_all(up_rows, 'dp', split_axis=1, concat_axis=0, tiled=True)  95.6 us
    psum x1, waiting for transfers between devices, local(): up_total = lax.psum(up_term.astype(jnp.bfloat16), 'mp').astype(jnp.float32)  50.8 us
  transfers between devices with their start and end apart: 3, of which 3 were waited for; matrix products, arithmetic and copies ran while one was open for 1% of the time, Pallas kernels for 0%

commit v1 on v0

v1 whole, which is shorter than its diff:
```python
import jax
import jax.numpy as jnp
from jax import lax
from jax.experimental import pallas as pl
from jax.experimental.pallas import tpu as pltpu
from jax.sharding import Mesh
from jax.sharding import PartitionSpec as P


inv_sqrt_two = 0.7071067811865476
inv_sqrt_two_pi = 0.3989422804014327


RING = 4
F32 = jnp.float32
BF16 = jnp.bfloat16


def gelu_parts(preact):
    normal_cdf = 0.5 * (1.0 + lax.erf(preact * inv_sqrt_two))
    gelu_out = preact * normal_cdf
    gelu_slope = normal_cdf + preact * jnp.exp(-0.5 * preact * preact) * inv_sqrt_two_pi
    return (gelu_out, gelu_slope)


def shift(value, axis, by):
    size = lax.axis_size(axis)
    return lax.ppermute(value, axis, [(i, (i + by) % size) for i in range(size)])


def dot(left, right, dims):
    return lax.dot_general(left, right, (dims, ((), ())), preferred_element_type=F32)


def column_of(pos_ref, outer, inner, width):
    core = pos_ref[2]
    dy = outer + core * (inner - outer)
    dx = inner + core * (outer - inner)
    y = lax.rem(pos_ref[0] + dy, RING)
    x = lax.rem(pos_ref[1] + dx, RING)
    return pl.multiple_of((y * RING + x) * width, 128)


def order_kernel(pos_ref, up_ref, out_ref):
    width = up_ref.shape[1] // (RING * RING)
    for outer in range(RING):
        for inner in range(RING):
            out_ref[:, pl.ds((outer * RING + inner) * width, width)] = up_ref[
                :, pl.ds(column_of(pos_ref, outer, inner, width), width)
            ]


def forward_kernel(pos_ref, *refs):
    pieces = refs[0:RING]
    cot_ref, up_ref, hidden_ref, grad_ref, keep_ref, send_ref = refs[RING:]
    depth = pieces[0].shape[0]
    width = depth // RING
    rows = keep_ref.shape[0]
    total = dot(up_ref[:, pl.ds(0, depth)], pieces[0][...], ((1,), (0,)))
    for d in range(1, RING):
        total += dot(up_ref[:, pl.ds(d * depth, depth)], pieces[d][...], ((1,), (0,)))
    gelu_out, gelu_slope = gelu_parts(total)
    hidden_ref[...] = gelu_out.astype(BF16)
    grad_ref[...] = (cot_ref[...].astype(F32) * gelu_slope).astype(BF16)
    core, zh = pos_ref[2], pos_ref[3]
    for half, out_ref in ((1 - core, send_ref), (core, keep_ref)):
        grads = grad_ref[pl.ds(pl.multiple_of(half * rows, 16), rows), :]
        for d in range(RING):
            term = dot(grads, pieces[d][...], ((1,), (1,))).astype(BF16)
            for inner in range(RING):
                column = column_of(pos_ref, d, inner, width) + (RING - zh) * depth
                column = pl.multiple_of(lax.rem(column, RING * depth), 128)
                out_ref[:, pl.ds(column, width)] = term[:, inner * width : (inner + 1) * width]


def input_grad_kernel(grad_ref, up_ref, *outs):
    grads = grad_ref[...]
    depth = outs[0].shape[0]
    for d in range(RING):
        term = dot(up_ref[:, pl.ds(d * depth, depth)], grads, ((0,), (0,)))
        outs[d][...] = term.astype(BF16)


def place_kernel(pos_ref, own_ref, own_last_ref, other_ref, other_last_ref, out_ref):
    core, zh = pos_ref[2], pos_ref[3]
    rows, depth = own_last_ref.shape
    for half, most, last in ((core, own_ref, own_last_ref), (1 - core, other_ref, other_last_ref)):
        where = pl.ds(pl.multiple_of(half * rows, 16), rows)
        for d, (ref, at) in enumerate(((most, 0), (most, 1), (last, 0), (most, 2))):
            column = pl.multiple_of(lax.rem(zh + d, RING) * depth, 128)
            out_ref[where, pl.ds(column, depth)] = ref[:, at * depth : (at + 1) * depth]


def vmem(count):
    return [pl.BlockSpec(memory_space=pltpu.VMEM)] * count


def turn(value, late, by):
    def target(y, x, c):
        if (c == 0) != late:
            return (y, (x + by) % RING, c)
        return ((y + by) % RING, x, c)

    def flat(y, x, c):
        return (y * RING + x) * 2 + c

    spots = [(y, x, c) for y in range(RING) for x in range(RING) for c in range(2)]
    return lax.ppermute(value, ("y", "x", "c"), [(flat(*s), flat(*target(*s))) for s in spots])


def gather(value, late):
    return [value] + [turn(value, late, -d) for d in range(1, RING)]


def add_up(values):
    total = values[0].astype(F32)
    for value in values[1:]:
        total = total + value.astype(F32)
    return total


def scatter_sum(values, late):
    return add_up([values[0]] + [turn(values[d], late, d) for d in range(1, RING)])


def work(normed, hidden_cot, up_rows):
    y, x, zl, zh, core = (lax.axis_index(a) for a in ("y", "x", "zl", "zh", "c"))
    pos = jnp.stack([y, x, core, zh]).astype(jnp.int32)
    hid, width = up_rows.shape
    tokens = normed.shape[0]
    scalars = pl.BlockSpec(memory_space=pltpu.SMEM)

    ordered = pl.pallas_call(
        order_kernel,
        in_specs=[scalars] + vmem(1),
        out_specs=vmem(1)[0],
        out_shape=jax.ShapeDtypeStruct((hid, width), BF16),
        name="order",
        cost_estimate=pl.CostEstimate(flops=0, bytes_accessed=4 * hid * width, transcendentals=0),
    )(pos, up_rows)

    block = lax.all_gather(normed.T, "zl", axis=0, tiled=True)
    pieces = gather(jnp.concatenate(gather(block, False), axis=0), True)

    hidden, hidden_grad, keep, send = pl.pallas_call(
        forward_kernel,
        in_specs=[scalars] + vmem(RING + 2),
        out_specs=vmem(4),
        out_shape=[jax.ShapeDtypeStruct((hid, tokens), BF16)] * 2
        + [jax.ShapeDtypeStruct((hid // 2, width), BF16)] * 2,
        name="forward",
        cost_estimate=pl.CostEstimate(
            flops=4 * hid * tokens * width, bytes_accessed=14_000_000, transcendentals=hid * tokens * 2
        ),
    )(pos, *pieces, hidden_cot.T, ordered)

    depth = width // RING
    rows = hid // 2
    arrived = shift(send, "c", 1)
    quarters = [
        (keep[:, d * depth : (d + 1) * depth].astype(F32) + arrived[:, d * depth : (d + 1) * depth].astype(F32)).astype(BF16)
        for d in range(RING)
    ]
    upper = shift(quarters[2][: rows // 2], "zh", 1)
    lower = shift(quarters[2][rows // 2 :], "zh", -1)
    ahead = jnp.concatenate([add_up([quarters[1][: rows // 2], upper]).astype(BF16), quarters[1][rows // 2 :]], axis=0)
    behind = jnp.concatenate([quarters[3][: rows // 2], add_up([quarters[3][rows // 2 :], lower]).astype(BF16)], axis=0)
    arrived = [shift(ahead, "zh", 1), shift(behind, "zh", -1)]
    mine = (add_up([quarters[0]] + arrived) / (2 * RING)).astype(BF16)
    before = shift(mine, "zh", 1)
    after = shift(mine, "zh", -1)
    across = [shift(before[: rows // 2], "zh", 1), shift(after[rows // 2 :], "zh", -1)]
    most = jnp.concatenate([mine, after, before], axis=1)
    last = jnp.concatenate(across, axis=0)
    other_most = shift(most, "c", 1)
    other_last = shift(last, "c", 1)
    up_grad = pl.pallas_call(
        place_kernel,
        in_specs=[scalars] + vmem(4),
        out_specs=vmem(1)[0],
        out_shape=jax.ShapeDtypeStruct((hid, width), BF16),
        name="place",
        cost_estimate=pl.CostEstimate(flops=0, bytes_accessed=4 * hid * width, transcendentals=0),
    )(pos, most, last, other_most, other_last)

    parts = pl.pallas_call(
        input_grad_kernel,
        in_specs=vmem(2),
        out_specs=vmem(RING),
        out_shape=[jax.ShapeDtypeStruct((width // RING, tokens), BF16)] * RING,
        name="partial",
        cost_estimate=pl.CostEstimate(
            flops=2 * hid * tokens * width, bytes_accessed=9_000_000, transcendentals=0
        ),
    )(hidden_grad, ordered)
    stage = scatter_sum(parts, True).astype(BF16)
    depth = stage.shape[0] // RING
    stage = scatter_sum([stage[d * depth : (d + 1) * depth] for d in range(RING)], False).astype(BF16)
    depth = stage.shape[0] // RING
    shares = [lax.dynamic_slice_in_dim(stage, ((zl + d) % RING) * depth, depth, axis=0) for d in range(RING)]
    input_grad = add_up(shares[:1] + [shift(shares[d], "zl", d) for d in range(1, RING)]).astype(BF16)
    return (hidden.T, input_grad.T, up_grad)


def solution(mesh):
    inner = Mesh(mesh.devices.reshape(RING, RING, RING, RING, 2), ("y", "x", "zl", "zh", "c"))
    tokens, features = ("zh", "c"), ("y", "x", "zl")
    return jax.shard_map(
        work,
        mesh=inner,
        in_specs=(P(tokens, features), P(tokens, features), P(features, None)),
        out_specs=(P(tokens, features), P(tokens, features), P(features, None)),
        check_vma=False,
    )
```

time: 976 us -> 244 us (0.25)
  the two profiles are of different devices: /device:TPU:128 before, /device:TPU:8 now
where the time goes in v1:
time: 244 us; the launch traced here: 243 us
  starting transfers between devices  114 us (47%)
  waiting for transfers between devices  79.2 us (32%)
  Pallas kernels  21.6 us (9%)
  blocking collectives  16 us (7%)
  other arithmetic  8.3 us (3%)
  local copies, waits for them, and re-layouts  2.62 us (1%)
    ppermute x14, starting transfers between devices, shift(): lax.ppermute(value, axis, [(i, (i + by) % size) for i in range(size)])  74.7 us
    ppermute x14, waiting for transfers between devices, shift(): lax.ppermute(value, axis, [(i, (i + by) % size) for i in range(size)])  40.7 us
    ppermute x12, starting transfers between devices, turn(): lax.ppermute(value, ('y', 'x', 'c'), [(flat(*s), flat(*target(*s))) for s...  39.2 us
    ppermute x12, waiting for transfers between devices, turn(): lax.ppermute(value, ('y', 'x', 'c'), [(flat(*s), flat(*target(*s))) for s...  38.5 us
    all_gather x1, blocking collectives, work(): block = lax.all_gather(normed.T, 'zl', axis=0, tiled=True)  16 us
    pallas_call x1, Pallas kernels, work(): pl.pallas_call(forward_kernel, in_specs=[scalars] + vmem(RING + 2), out_s...  10 us
    pallas_call x1, Pallas kernels, work(): pl.pallas_call(input_grad_kernel, in_specs=vmem(2), out_specs=vmem(RING),...  5.04 us
  transfers between devices with their start and end apart: 26, of which 12 were waited for; matrix products, arithmetic and copies ran while one was open for 3% of the time, Pallas kernels for 3%

profile of v1, /device:TPU:8, one launch (start us, length us, event | category | flops | bytes accessed | tf_op | source)
XLA Modules:
  0.0 242.9 jit_solution(6174878791552405339)
XLA Ops:
  0.6 16.0 %all_gather.3 = bf16[384,512]{1,0:T(8,128)(2,1)S(1)} all-gather(bf16[96,512]{1,0:T(8,128)(2,1)} %bitcast.9), channel_id=1, replica_groups=mesh['y'=4,'x'=4,'zl'=4,'zh'=4,'c'=2] {'zl'}, dimensions={0}, use_global_device_ids=true | all-gather | bytes 491520 | tf_op jit(solution)/shard_map/all_gather | solution.py:142
  16.6 4.7 %collective-permute-start = (bf16[384,512]{1,0:T(8,128)(2,1)S(1)}, bf16[384,512]{1,0:T(8,128)(2,1)S(1)}, u32[]{:S(2)}, u32[]{:S(2)}) collective-permute-start(bf16[384,512]{1,0:T(8,128)(2,1)S(1)} %all_gather.3), channel_id=1, source_target_pairs={{0,96},{1,385},{32,0},{33,417},{64,32},{65,449},{96,64},{97,481},{... | collective-permute-start | bytes 1179656 | tf_op jit(solution)/shard_map/ppermute | solution.py:108
  21.3 2.7 %collective-permute-start.1 = (bf16[384,512]{1,0:T(8,128)(2,1)S(1)}, bf16[384,512]{1,0:T(8,128)(2,1)S(1)}, u32[]{:S(2)}, u32[]{:S(2)}) collective-permute-start(bf16[384,512]{1,0:T(8,128)(2,1)S(1)} %all_gather.3), channel_id=1, source_target_pairs={{0,64},{1,257},{32,96},{33,289},{64,0},{65,321},{96,32},{97,353},{... | collective-permute-start | bytes 1179656 | tf_op jit(solution)/shard_map/ppermute | solution.py:108
  24.0 2.8 %collective-permute-start.2 = (bf16[384,512]{1,0:T(8,128)(2,1)S(1)}, bf16[384,512]{1,0:T(8,128)(2,1)S(1)}, u32[]{:S(2)}, u32[]{:S(2)}) collective-permute-start(bf16[384,512]{1,0:T(8,128)(2,1)S(1)} %all_gather.3), channel_id=1, source_target_pairs={{0,32},{1,129},{32,64},{33,161},{64,96},{65,193},{96,0},{97,225},{... | collective-permute-start | bytes 1179656 | tf_op jit(solution)/shard_map/ppermute | solution.py:108
  26.9 4.0 %collective-permute-done = bf16[384,512]{1,0:T(8,128)(2,1)S(1)} collective-permute-done((bf16[384,512]{1,0:T(8,128)(2,1)S(1)}, bf16[384,512]{1,0:T(8,128)(2,1)S(1)}, u32[]{:S(2)}, u32[]{:S(2)}) %collective-permute-start) | collective-permute-done | bytes 393248 | tf_op jit(solution)/shard_map/ppermute | solution.py:108
  32.6 4.1 %collective-permute-done.2 = bf16[384,512]{1,0:T(8,128)(2,1)S(1)} collective-permute-done((bf16[384,512]{1,0:T(8,128)(2,1)S(1)}, bf16[384,512]{1,0:T(8,128)(2,1)S(1)}, u32[]{:S(2)}, u32[]{:S(2)}) %collective-permute-start.2) | collective-permute-done | bytes 393248 | tf_op jit(solution)/shard_map/ppermute | solution.py:108
  36.7 4.3 %collective-permute-start.3 = (bf16[1536,512]{1,0:T(8,128)(2,1)S(1)}, bf16[1536,512]{1,0:T(8,128)(2,1)S(1)}, u32[]{:S(2)}, u32[]{:S(2)}) collective-permute-start(bf16[1536,512]{1,0:T(8,128)(2,1)S(1)} %constant_dynamic-update-slice_fusion.refs_0_), channel_id=1, source_target_pairs={{0,384},{1,97},{32,416},{33,1},{64,448},{65,33},{96,480},{97,65},{... | collective-permute-start | bytes 4718600 | tf_op jit(solution)/shard_map/ppermute | solution.py:108
  41.0 2.5 %collective-permute-start.4 = (bf16[1536,512]{1,0:T(8,128)(2,1)S(1)}, bf16[1536,512]{1,0:T(8,128)(2,1)}, u32[]{:S(2)}, u32[]{:S(2)}) collective-permute-start(bf16[1536,512]{1,0:T(8,128)(2,1)S(1)} %constant_dynamic-update-slice_fusion.refs_0_), channel_id=1, source_target_pairs={{0,256},{1,65},{32,288},{33,97},{64,320},{65,1},{96,352},{97,33},{... | collective-permute-start | bytes 4718600 | tf_op jit(solution)/shard_map/ppermute | solution.py:108
  43.6 3.8 %collective-permute-start.5 = (bf16[1536,512]{1,0:T(8,128)(2,1)S(1)}, bf16[1536,512]{1,0:T(8,128)(2,1)}, u32[]{:S(2)}, u32[]{:S(2)}) collective-permute-start(bf16[1536,512]{1,0:T(8,128)(2,1)S(1)} %constant_dynamic-update-slice_fusion.refs_0_), channel_id=1, source_target_pairs={{0,128},{1,33},{32,160},{33,65},{64,192},{65,97},{96,224},{97,1},{... | collective-permute-start | bytes 4718600 | tf_op jit(solution)/shard_map/ppermute | solution.py:108
  48.0 3.3 %order.1.refs_5_.up_ref = bf16[192,6144]{1,0:T(8,128)(2,1)} custom-call(s32[4]{0:T(128)} %pad_add_fusion.pos_ref, bf16[192,6144]{1,0:T(8,128)(2,1)} %up_ref.1), custom_call_target="tpu_custom_call" | custom-call | bytes 4718592 | tf_op jit(solution)/shard_map/order/pallas_call | solution.py:133
  51.3 7.7 %collective-permute-done.3.refs_1_ = bf16[1536,512]{1,0:T(8,128)(2,1)S(1)} collective-permute-done((bf16[1536,512]{1,0:T(8,128)(2,1)S(1)}, bf16[1536,512]{1,0:T(8,128)(2,1)S(1)}, u32[]{:S(2)}, u32[]{:S(2)}) %collective-permute-start.3) | collective-permute-done | bytes 1572896 | tf_op jit(solution)/shard_map/ppermute | solution.py:108
  59.0 18.0 %collective-permute-done.4.refs_2_ = bf16[1536,512]{1,0:T(8,128)(2,1)} collective-permute-done((bf16[1536,512]{1,0:T(8,128)(2,1)S(1)}, bf16[1536,512]{1,0:T(8,128)(2,1)}, u32[]{:S(2)}, u32[]{:S(2)}) %collective-permute-start.4) | collective-permute-done | bytes 1572896 | tf_op jit(solution)/shard_map/ppermute | solution.py:108
  77.0 3.0 %collective-permute-done.5.refs_3_ = bf16[1536,512]{1,0:T(8,128)(2,1)} collective-permute-done((bf16[1536,512]{1,0:T(8,128)(2,1)S(1)}, bf16[1536,512]{1,0:T(8,128)(2,1)}, u32[]{:S(2)}, u32[]{:S(2)}) %collective-permute-start.5) | collective-permute-done | bytes 1572896 | tf_op jit(solution)/shard_map/ppermute | solution.py:108
  80.0 10.0 %forward.1 = (bf16[192,512]{1,0:T(8,128)(2,1)}, bf16[192,512]{1,0:T(8,128)(2,1)}, bf16[96,6144]{1,0:T(8,128)(2,1)}, bf16[96,6144]{1,0:T(8,128)(2,1)}) custom-call(s32[4]{0:T(128)} %pad_add_fusion.pos_ref, bf16[1536,512]{1,0:T(8,128)(2,1)} %copy-done.6, bf16[1536,512]{1,0:T(8,128)(2,1)} %copy-done.7, bf16[1536,512]{1,0:T(8,128)(2,1)} %collective-permute-done.4.refs_2_, ...), custom_call_target="tpu_custom_call" | custom-call | flops 2415919104 | bytes 14000000 | tf_op jit(solution)/shard_map/forward/pallas_call | solution.py:145
  92.0 3.0 %collective-permute-done.15 = bf16[96,6144]{1,0:T(8,128)(2,1)S(1)} collective-permute-done((bf16[96,6144]{1,0:T(8,128)(2,1)}, bf16[96,6144]{1,0:T(8,128)(2,1)S(1)}, u32[]{:S(2)}, u32[]{:S(2)}) %collective-permute-start.15) | collective-permute-done | bytes 1179680 | tf_op jit(solution)/shard_map/ppermute | solution.py:28
  97.5 9.1 %collective-permute-start.16 = (bf16[48,1536]{1,0:T(8,128)(2,1)S(1)}, bf16[48,1536]{1,0:T(8,128)(2,1)S(1)}, u32[]{:S(2)}, u32[]{:S(2)}) collective-permute-start(bf16[48,1536]{1,0:T(8,128)(2,1)S(1)} %get-tuple-element.28), channel_id=1, source_target_pairs={{0,2},{2,4},{4,6},{6,0},{1,3},{3,5},{5,7},{7,1},{8,10},{10,12},{12... | collective-permute-start | bytes 442376 | tf_op jit(solution)/shard_map/ppermute | solution.py:28
  106.6 5.0 %partial.1 = (bf16[1536,512]{1,0:T(8,128)(2,1)}, bf16[1536,512]{1,0:T(8,128)(2,1)}, bf16[1536,512]{1,0:T(8,128)(2,1)}, bf16[1536,512]{1,0:T(8,128)(2,1)}) custom-call(bf16[192,512]{1,0:T(8,128)(2,1)} %get-tuple-element.12.grad_ref, bf16[192,6144]{1,0:T(8,128)(2,1)} %order.1.refs_5_.up_ref), custom_call_target="tpu_custom_call" | custom-call | flops 1207959552 | bytes 9000000 | tf_op jit(solution)/shard_map/partial/pallas_call | solution.py:186
  111.6 3.3 %collective-permute-start.6 = (bf16[1536,512]{1,0:T(8,128)(2,1)}, bf16[1536,512]{1,0:T(8,128)(2,1)S(1)}, u32[]{:S(2)}, u32[]{:S(2)}) collective-permute-start(bf16[1536,512]{1,0:T(8,128)(2,1)} %get-tuple-element.14), channel_id=1, source_target_pairs={{0,128},{1,33},{32,160},{33,65},{64,192},{65,97},{96,224},{97,1},{... | collective-permute-start | bytes 4718600 | tf_op jit(solution)/shard_map/ppermute | solution.py:108
  115.0 5.4 %collective-permute-start.7 = (bf16[1536,512]{1,0:T(8,128)(2,1)}, bf16[1536,512]{1,0:T(8,128)(2,1)}, u32[]{:S(2)}, u32[]{:S(2)}) collective-permute-start(bf16[1536,512]{1,0:T(8,128)(2,1)} %get-tuple-element.15), channel_id=1, source_target_pairs={{0,256},{1,65},{32,288},{33,97},{64,320},{65,1},{96,352},{97,33},{... | collective-permute-start | bytes 4718600 | tf_op jit(solution)/shard_map/ppermute | solution.py:108
  122.3 4.1 %collective-permute-start.18 = (bf16[48,1536]{1,0:T(8,128)(2,1)}, bf16[48,1536]{1,0:T(8,128)(2,1)S(1)}, u32[]{:S(2)}, u32[]{:S(2)}) collective-permute-start(bf16[48,1536]{1,0:T(8,128)(2,1)} %get-tuple-element.29), channel_id=1, source_target_pairs={{0,6},{2,0},{4,2},{6,4},{1,7},{3,1},{5,3},{7,5},{8,14},{10,8},{12,... | collective-permute-start | bytes 442376 | tf_op jit(solution)/shard_map/ppermute | solution.py:28
  127.2 5.7 %collective-permute-start.17 = (bf16[96,1536]{1,0:T(8,128)(2,1)}, bf16[96,1536]{1,0:T(8,128)(2,1)}, u32[]{:S(2)}, u32[]{:S(2)}) collective-permute-start(bf16[96,1536]{1,0:T(8,128)(2,1)} %pad_maximum_fusion.1), channel_id=1, source_target_pairs={{0,2},{2,4},{4,6},{6,0},{1,3},{3,5},{5,7},{7,1},{8,10},{10,12},{12... | collective-permute-start | bytes 884744 | tf_op jit(solution)/shard_map/ppermute | solution.py:28
  132.9 11.5 %collective-permute-done.18 = bf16[48,1536]{1,0:T(8,128)(2,1)S(1)} collective-permute-done((bf16[48,1536]{1,0:T(8,128)(2,1)}, bf16[48,1536]{1,0:T(8,128)(2,1)S(1)}, u32[]{:S(2)}, u32[]{:S(2)}) %collective-permute-start.18) | collective-permute-done | bytes 147488 | tf_op jit(solution)/shard_map/ppermute | solution.py:28
  146.4 22.0 %collective-permute-done.19 = bf16[96,1536]{1,0:T(8,128)(2,1)} collective-permute-done((bf16[96,1536]{1,0:T(8,128)(2,1)S(1)}, bf16[96,1536]{1,0:T(8,128)(2,1)}, u32[]{:S(2)}, u32[]{:S(2)}) %collective-permute-start.19) | collective-permute-done | bytes 294944 | tf_op jit(solution)/shard_map/ppermute | solution.py:28
  169.8 11.1 %collective-permute-start.21 = (bf16[96,1536]{1,0:T(8,128)(2,1)S(1)}, bf16[96,1536]{1,0:T(8,128)(2,1)S(1)}, u32[]{:S(2)}, u32[]{:S(2)}) collective-permute-start(bf16[96,1536]{1,0:T(8,128)(2,1)S(1)} %multiply_convert_fusion), channel_id=1, source_target_pairs={{0,2},{2,4},{4,6},{6,0},{1,3},{3,5},{5,7},{7,1},{8,10},{10,12},{12... | collective-permute-start | bytes 884744 | tf_op jit(solution)/shard_map/ppermute | solution.py:28
  180.9 17.1 %collective-permute-start.20 = (bf16[96,1536]{1,0:T(8,128)(2,1)S(1)}, bf16[96,1536]{1,0:T(8,128)(2,1)S(1)}, u32[]{:S(2)}, u32[]{:S(2)}) collective-permute-start(bf16[96,1536]{1,0:T(8,128)(2,1)S(1)} %multiply_convert_fusion), channel_id=1, source_target_pairs={{0,6},{2,0},{4,2},{6,4},{1,7},{3,1},{5,3},{7,5},{8,14},{10,8},{12,... | collective-permute-start | bytes 884744 | tf_op jit(solution)/shard_map/ppermute | solution.py:28
  198.1 2.7 %add_convert_fusion = bf16[1536,512]{1,0:T(8,128)(2,1)S(1)} fusion(bf16[1536,512]{1,0:T(8,128)(2,1)} %collective-permute-done.8, bf16[1536,512]{1,0:T(8,128)(2,1)} %collective-permute-done.7, bf16[1536,512]{1,0:T(8,128)(2,1)S(1)} %collective-permute-done.6, bf16[1536,512]{1,0:T(8,128)(2,1)S(1)} %copy-done.1), kind=kLoop, calls=%fused_computation | loop fusion | flops 6291456 | bytes 7864320 | tf_op jit(solution)/shard_map/convert_element_type | solution.py:196
  204.8 3.9 %collective-permute-start.9 = (bf16[384,512]{1,0:T(8,128)(2,1)S(1)}, bf16[384,512]{1,0:T(8,128)(2,1)S(1)}, u32[]{:S(2)}, u32[]{:S(2)}) collective-permute-start(bf16[384,512]{1,0:T(8,128)(2,1)S(1)} %get-tuple-element.22), channel_id=1, source_target_pairs={{0,32},{1,129},{32,64},{33,161},{64,96},{65,193},{96,0},{97,225},{... | collective-permute-start | bytes 1179656 | tf_op jit(solution)/shard_map/ppermute | solution.py:108
  208.7 8.5 %collective-permute-start.22 = (bf16[48,1536]{1,0:T(8,128)(2,1)S(1)}, bf16[48,1536]{1,0:T(8,128)(2,1)S(1)}, u32[]{:S(2)}, u32[]{:S(2)}) collective-permute-start(bf16[48,1536]{1,0:T(8,128)(2,1)S(1)} %slice.94), channel_id=1, source_target_pairs={{0,2},{2,4},{4,6},{6,0},{1,3},{3,5},{5,7},{7,1},{8,10},{10,12},{12... | collective-permute-start | bytes 442376 | tf_op jit(solution)/shard_map/ppermute | solution.py:28
  223.4 5.4 %collective-permute-start.13 = (bf16[96,512]{1,0:T(8,128)(2,1)S(1)}, bf16[96,512]{1,0:T(8,128)(2,1)S(1)}, u32[]{:S(2)}, u32[]{:S(2)}) collective-permute-start(bf16[96,512]{1,0:T(8,128)(2,1)S(1)} %get-tuple-element.27), channel_id=1, source_target_pairs={{0,16},{8,24},{16,0},{24,8},{1,17},{9,25},{17,1},{25,9},{2,18},{10... | collective-permute-start | bytes 294920 | tf_op jit(solution)/shard_map/ppermute | solution.py:28
  228.8 2.3 collective-permute-start.14
  233.2 2.7 %collective-permute-done.13 = bf16[96,512]{1,0:T(8,128)(2,1)S(1)} collective-permute-done((bf16[96,512]{1,0:T(8,128)(2,1)S(1)}, bf16[96,512]{1,0:T(8,128)(2,1)S(1)}, u32[]{:S(2)}, u32[]{:S(2)}) %collective-permute-start.13) | collective-permute-done | bytes 98336 | tf_op jit(solution)/shard_map/ppermute | solution.py:28
  239.7 3.2 %place.1 = bf16[192,6144]{1,0:T(8,128)(2,1)} custom-call(s32[4]{0:T(128)} %pad_add_fusion.pos_ref, bf16[96,4608]{1,0:T(8,128)(2,1)} %copy-done, bf16[96,1536]{1,0:T(8,128)(2,1)} %copy-done.4, bf16[96,4608]{1,0:T(8,128)(2,1)} %copy-done.3, bf16[96,1536]{1,0:T(8,128)(2,1)} %copy-done.5), custom_call_target="tpu_custom_call" | custom-call | bytes 4718592 | tf_op jit(solution)/shard_map/place/pallas_call | solution.py:177
  (65 shorter events, 28.8 us)
Async XLA Ops:
  16.6 14.2 %collective-permute-start = (bf16[384,512]{1,0:T(8,128)(2,1)S(1)}, bf16[384,512]{1,0:T(8,128)(2,1)S(1)}, u32[]{:S(2)}, u32[]{:S(2)}) collective-permute-start(bf16[384,512]{1,0:T(8,128)(2,1)S(1)} %all_gather.3), channel_id=1, source_target_pairs={{0,96},{1,385},{32,0},{33,417},{64,32},{65,449},{96,64},{97,481},{... | collective-permute-start | bytes 1179656 | tf_op jit(solution)/shard_map/ppermute | solution.py:108
  21.3 11.3 %collective-permute-start.1 = (bf16[384,512]{1,0:T(8,128)(2,1)S(1)}, bf16[384,512]{1,0:T(8,128)(2,1)S(1)}, u32[]{:S(2)}, u32[]{:S(2)}) collective-permute-start(bf16[384,512]{1,0:T(8,128)(2,1)S(1)} %all_gather.3), channel_id=1, source_target_pairs={{0,64},{1,257},{32,96},{33,289},{64,0},{65,321},{96,32},{97,353},{... | collective-permute-start | bytes 1179656 | tf_op jit(solution)/shard_map/ppermute | solution.py:108
  24.0 12.7 %collective-permute-start.2 = (bf16[384,512]{1,0:T(8,128)(2,1)S(1)}, bf16[384,512]{1,0:T(8,128)(2,1)S(1)}, u32[]{:S(2)}, u32[]{:S(2)}) collective-permute-start(bf16[384,512]{1,0:T(8,128)(2,1)S(1)} %all_gather.3), channel_id=1, source_target_pairs={{0,32},{1,129},{32,64},{33,161},{64,96},{65,193},{96,0},{97,225},{... | collective-permute-start | bytes 1179656 | tf_op jit(solution)/shard_map/ppermute | solution.py:108
  36.7 14.6 %copy-start.6 = (bf16[1536,512]{1,0:T(8,128)(2,1)}, bf16[1536,512]{1,0:T(8,128)(2,1)S(1)}, u32[]{:S(2)}) copy-start(bf16[1536,512]{1,0:T(8,128)(2,1)S(1)} %constant_dynamic-update-slice_fusion.refs_0_) | copy-start | bytes 4718596
  36.7 22.3 %collective-permute-start.3 = (bf16[1536,512]{1,0:T(8,128)(2,1)S(1)}, bf16[1536,512]{1,0:T(8,128)(2,1)S(1)}, u32[]{:S(2)}, u32[]{:S(2)}) collective-permute-start(bf16[1536,512]{1,0:T(8,128)(2,1)S(1)} %constant_dynamic-update-slice_fusion.refs_0_), channel_id=1, source_target_pairs={{0,384},{1,97},{32,416},{33,1},{64,448},{65,33},{96,480},{97,65},{... | collective-permute-start | bytes 4718600 | tf_op jit(solution)/shard_map/ppermute | solution.py:108
  41.0 36.0 %collective-permute-start.4 = (bf16[1536,512]{1,0:T(8,128)(2,1)S(1)}, bf16[1536,512]{1,0:T(8,128)(2,1)}, u32[]{:S(2)}, u32[]{:S(2)}) collective-permute-start(bf16[1536,512]{1,0:T(8,128)(2,1)S(1)} %constant_dynamic-update-slice_fusion.refs_0_), channel_id=1, source_target_pairs={{0,256},{1,65},{32,288},{33,97},{64,320},{65,1},{96,352},{97,33},{... | collective-permute-start | bytes 4718600 | tf_op jit(solution)/shard_map/ppermute | solution.py:108
  43.6 36.4 %collective-permute-start.5 = (bf16[1536,512]{1,0:T(8,128)(2,1)S(1)}, bf16[1536,512]{1,0:T(8,128)(2,1)}, u32[]{:S(2)}, u32[]{:S(2)}) collective-permute-start(bf16[1536,512]{1,0:T(8,128)(2,1)S(1)} %constant_dynamic-update-slice_fusion.refs_0_), channel_id=1, source_target_pairs={{0,128},{1,33},{32,160},{33,65},{64,192},{65,97},{96,224},{97,1},{... | collective-permute-start | bytes 4718600 | tf_op jit(solution)/shard_map/ppermute | solution.py:108
  59.0 21.0 %copy-start.7 = (bf16[1536,512]{1,0:T(8,128)(2,1)}, bf16[1536,512]{1,0:T(8,128)(2,1)S(1)}, u32[]{:S(2)}) copy-start(bf16[1536,512]{1,0:T(8,128)(2,1)S(1)} %collective-permute-done.3.refs_1_) | copy-start | bytes 4718596
  90.1 4.9 %collective-permute-start.15 = (bf16[96,6144]{1,0:T(8,128)(2,1)}, bf16[96,6144]{1,0:T(8,128)(2,1)S(1)}, u32[]{:S(2)}, u32[]{:S(2)}) collective-permute-start(bf16[96,6144]{1,0:T(8,128)(2,1)} %get-tuple-element.18), channel_id=1, source_target_pairs={{0,1},{1,0},{2,3},{3,2},{4,5},{5,4},{6,7},{7,6},{8,9},{9,8},{10,11... | collective-permute-start | bytes 3538952 | tf_op jit(solution)/shard_map/ppermute | solution.py:28
  95.0 2.5 %copy-start.2 = (bf16[96,6144]{1,0:T(8,128)(2,1)}, bf16[96,6144]{1,0:T(8,128)(2,1)S(1)}, u32[]{:S(2)}) copy-start(bf16[96,6144]{1,0:T(8,128)(2,1)S(1)} %collective-permute-done.15) | copy-start | bytes 3538948
  97.5 28.9 %collective-permute-start.16 = (bf16[48,1536]{1,0:T(8,128)(2,1)S(1)}, bf16[48,1536]{1,0:T(8,128)(2,1)S(1)}, u32[]{:S(2)}, u32[]{:S(2)}) collective-permute-start(bf16[48,1536]{1,0:T(8,128)(2,1)S(1)} %get-tuple-element.28), channel_id=1, source_target_pairs={{0,2},{2,4},{4,6},{6,0},{1,3},{3,5},{5,7},{7,1},{8,10},{10,12},{12... | collective-permute-start | bytes 442376 | tf_op jit(solution)/shard_map/ppermute | solution.py:28
  111.6 86.4 %collective-permute-start.6 = (bf16[1536,512]{1,0:T(8,128)(2,1)}, bf16[1536,512]{1,0:T(8,128)(2,1)S(1)}, u32[]{:S(2)}, u32[]{:S(2)}) collective-permute-start(bf16[1536,512]{1,0:T(8,128)(2,1)} %get-tuple-element.14), channel_id=1, source_target_pairs={{0,128},{1,33},{32,160},{33,65},{64,192},{65,97},{96,224},{97,1},{... | collective-permute-start | bytes 4718600 | tf_op jit(solution)/shard_map/ppermute | solution.py:108
  115.0 83.1 %collective-permute-start.7 = (bf16[1536,512]{1,0:T(8,128)(2,1)}, bf16[1536,512]{1,0:T(8,128)(2,1)}, u32[]{:S(2)}, u32[]{:S(2)}) collective-permute-start(bf16[1536,512]{1,0:T(8,128)(2,1)} %get-tuple-element.15), channel_id=1, source_target_pairs={{0,256},{1,65},{32,288},{33,97},{64,320},{65,1},{96,352},{97,33},{... | collective-permute-start | bytes 4718600 | tf_op jit(solution)/shard_map/ppermute | solution.py:108
  120.4 77.7 %collective-permute-start.8 = (bf16[1536,512]{1,0:T(8,128)(2,1)}, bf16[1536,512]{1,0:T(8,128)(2,1)}, u32[]{:S(2)}, u32[]{:S(2)}) collective-permute-start(bf16[1536,512]{1,0:T(8,128)(2,1)} %get-tuple-element.16), channel_id=1, source_target_pairs={{0,384},{1,97},{32,416},{33,1},{64,448},{65,33},{96,480},{97,65},{... | collective-permute-start | bytes 4718600 | tf_op jit(solution)/shard_map/ppermute | solution.py:108
  122.3 22.0 %collective-permute-start.18 = (bf16[48,1536]{1,0:T(8,128)(2,1)}, bf16[48,1536]{1,0:T(8,128)(2,1)S(1)}, u32[]{:S(2)}, u32[]{:S(2)}) collective-permute-start(bf16[48,1536]{1,0:T(8,128)(2,1)} %get-tuple-element.29), channel_id=1, source_target_pairs={{0,6},{2,0},{4,2},{6,4},{1,7},{3,1},{5,3},{7,5},{8,14},{10,8},{12,... | collective-permute-start | bytes 442376 | tf_op jit(solution)/shard_map/ppermute | solution.py:28
  126.5 71.6 %copy-start.1 = (bf16[1536,512]{1,0:T(8,128)(2,1)S(1)}, bf16[1536,512]{1,0:T(8,128)(2,1)}, u32[]{:S(2)}) copy-start(bf16[1536,512]{1,0:T(8,128)(2,1)} %get-tuple-element.13) | copy-start | bytes 4718596
  127.2 19.2 %collective-permute-start.17 = (bf16[96,1536]{1,0:T(8,128)(2,1)}, bf16[96,1536]{1,0:T(8,128)(2,1)}, u32[]{:S(2)}, u32[]{:S(2)}) collective-permute-start(bf16[96,1536]{1,0:T(8,128)(2,1)} %pad_maximum_fusion.1), channel_id=1, source_target_pairs={{0,2},{2,4},{4,6},{6,0},{1,3},{3,5},{5,7},{7,1},{8,10},{10,12},{12... | collective-permute-start | bytes 884744 | tf_op jit(solution)/shard_map/ppermute | solution.py:28
  144.4 23.9 %collective-permute-start.19 = (bf16[96,1536]{1,0:T(8,128)(2,1)S(1)}, bf16[96,1536]{1,0:T(8,128)(2,1)}, u32[]{:S(2)}, u32[]{:S(2)}) collective-permute-start(bf16[96,1536]{1,0:T(8,128)(2,1)S(1)} %pad_maximum_fusion.2), channel_id=1, source_target_pairs={{0,6},{2,0},{4,2},{6,4},{1,7},{3,1},{5,3},{7,5},{8,14},{10,8},{12,... | collective-permute-start | bytes 884744 | tf_op jit(solution)/shard_map/ppermute | solution.py:28
  169.8 38.9 %collective-permute-start.21 = (bf16[96,1536]{1,0:T(8,128)(2,1)S(1)}, bf16[96,1536]{1,0:T(8,128)(2,1)S(1)}, u32[]{:S(2)}, u32[]{:S(2)}) collective-permute-start(bf16[96,1536]{1,0:T(8,128)(2,1)S(1)} %multiply_convert_fusion), channel_id=1, source_target_pairs={{0,2},{2,4},{4,6},{6,0},{1,3},{3,5},{5,7},{7,1},{8,10},{10,12},{12... | collective-permute-start | bytes 884744 | tf_op jit(solution)/shard_map/ppermute | solution.py:28
  180.9 36.3 %collective-permute-start.20 = (bf16[96,1536]{1,0:T(8,128)(2,1)S(1)}, bf16[96,1536]{1,0:T(8,128)(2,1)S(1)}, u32[]{:S(2)}, u32[]{:S(2)}) collective-permute-start(bf16[96,1536]{1,0:T(8,128)(2,1)S(1)} %multiply_convert_fusion), channel_id=1, source_target_pairs={{0,6},{2,0},{4,2},{6,4},{1,7},{3,1},{5,3},{7,5},{8,14},{10,8},{12,... | collective-permute-start | bytes 884744 | tf_op jit(solution)/shard_map/ppermute | solution.py:28
  200.9 18.4 %collective-permute-start.10 = (bf16[384,512]{1,0:T(8,128)(2,1)S(1)}, bf16[384,512]{1,0:T(8,128)(2,1)S(1)}, u32[]{:S(2)}, u32[]{:S(2)}) collective-permute-start(bf16[384,512]{1,0:T(8,128)(2,1)S(1)} %get-tuple-element.24), channel_id=1, source_target_pairs={{0,64},{1,257},{32,96},{33,289},{64,0},{65,321},{96,32},{97,353},{... | collective-permute-start | bytes 1179656 | tf_op jit(solution)/shard_map/ppermute | solution.py:108
  202.8 18.4 %collective-permute-start.11 = (bf16[384,512]{1,0:T(8,128)(2,1)S(1)}, bf16[384,512]{1,0:T(8,128)(2,1)S(1)}, u32[]{:S(2)}, u32[]{:S(2)}) collective-permute-start(bf16[384,512]{1,0:T(8,128)(2,1)S(1)} %get-tuple-element.23), channel_id=1, source_target_pairs={{0,96},{1,385},{32,0},{33,417},{64,32},{65,449},{96,64},{97,481},{... | collective-permute-start | bytes 1179656 | tf_op jit(solution)/shard_map/ppermute | solution.py:108
  204.8 16.5 %collective-permute-start.9 = (bf16[384,512]{1,0:T(8,128)(2,1)S(1)}, bf16[384,512]{1,0:T(8,128)(2,1)S(1)}, u32[]{:S(2)}, u32[]{:S(2)}) collective-permute-start(bf16[384,512]{1,0:T(8,128)(2,1)S(1)} %get-tuple-element.22), channel_id=1, source_target_pairs={{0,32},{1,129},{32,64},{33,161},{64,96},{65,193},{96,0},{97,225},{... | collective-permute-start | bytes 1179656 | tf_op jit(solution)/shard_map/ppermute | solution.py:108
  208.7 20.1 %collective-permute-start.22 = (bf16[48,1536]{1,0:T(8,128)(2,1)S(1)}, bf16[48,1536]{1,0:T(8,128)(2,1)S(1)}, u32[]{:S(2)}, u32[]{:S(2)}) collective-permute-start(bf16[48,1536]{1,0:T(8,128)(2,1)S(1)} %slice.94), channel_id=1, source_target_pairs={{0,2},{2,4},{4,6},{6,0},{1,3},{3,5},{5,7},{7,1},{8,10},{10,12},{12... | collective-permute-start | bytes 442376 | tf_op jit(solution)/shard_map/ppermute | solution.py:28
  217.3 13.9 %collective-permute-start.23 = (bf16[48,1536]{1,0:T(8,128)(2,1)S(1)}, bf16[48,1536]{1,0:T(8,128)(2,1)S(1)}, u32[]{:S(2)}, u32[]{:S(2)}) collective-permute-start(bf16[48,1536]{1,0:T(8,128)(2,1)S(1)} %slice.95), channel_id=1, source_target_pairs={{0,6},{2,0},{4,2},{6,4},{1,7},{3,1},{5,3},{7,5},{8,14},{10,8},{12,... | collective-permute-start | bytes 442376 | tf_op jit(solution)/shard_map/ppermute | solution.py:28
  219.3 11.9 %copy-start = (bf16[96,4608]{1,0:T(8,128)(2,1)}, bf16[96,4608]{1,0:T(8,128)(2,1)S(1)}, u32[]{:S(2)}) copy-start(bf16[96,4608]{1,0:T(8,128)(2,1)S(1)} %pad_maximum_fusion.own_ref) | copy-start | bytes 2654212
  219.3 18.8 %collective-permute-start.24 = (bf16[96,4608]{1,0:T(8,128)(2,1)S(1)}, bf16[96,4608]{1,0:T(8,128)(2,1)S(1)}, u32[]{:S(2)}, u32[]{:S(2)}) collective-permute-start(bf16[96,4608]{1,0:T(8,128)(2,1)S(1)} %pad_maximum_fusion.own_ref), channel_id=1, source_target_pairs={{0,1},{1,0},{2,3},{3,2},{4,5},{5,4},{6,7},{7,6},{8,9},{9,8},{10,11... | collective-permute-start | bytes 2654216 | tf_op jit(solution)/shard_map/ppermute | solution.py:28
  221.5 11.7 %collective-permute-start.12 = (bf16[96,512]{1,0:T(8,128)(2,1)S(1)}, bf16[96,512]{1,0:T(8,128)(2,1)S(1)}, u32[]{:S(2)}, u32[]{:S(2)}) collective-permute-start(bf16[96,512]{1,0:T(8,128)(2,1)S(1)} %get-tuple-element.25), channel_id=1, source_target_pairs={{0,8},{8,16},{16,24},{24,0},{1,9},{9,17},{17,25},{25,1},{2,10},{10... | collective-permute-start | bytes 294920 | tf_op jit(solution)/shard_map/ppermute | solution.py:28
  223.4 12.4 %collective-permute-start.13 = (bf16[96,512]{1,0:T(8,128)(2,1)S(1)}, bf16[96,512]{1,0:T(8,128)(2,1)S(1)}, u32[]{:S(2)}, u32[]{:S(2)}) collective-permute-start(bf16[96,512]{1,0:T(8,128)(2,1)S(1)} %get-tuple-element.27), channel_id=1, source_target_pairs={{0,16},{8,24},{16,0},{24,8},{1,17},{9,25},{17,1},{25,9},{2,18},{10... | collective-permute-start | bytes 294920 | tf_op jit(solution)/shard_map/ppermute | solution.py:28
  228.8 8.5 %collective-permute-start.14 = (bf16[96,512]{1,0:T(8,128)(2,1)S(1)}, bf16[96,512]{1,0:T(8,128)(2,1)S(1)}, u32[]{:S(2)}, u32[]{:S(2)}) collective-permute-start(bf16[96,512]{1,0:T(8,128)(2,1)S(1)} %get-tuple-element.26), channel_id=1, source_target_pairs={{0,24},{8,0},{16,8},{24,16},{1,25},{9,1},{17,9},{25,17},{2,26},{10... | collective-permute-start | bytes 294920 | tf_op jit(solution)/shard_map/ppermute | solution.py:28
  231.2 6.8 %copy-start.4 = (bf16[96,1536]{1,0:T(8,128)(2,1)}, bf16[96,1536]{1,0:T(8,128)(2,1)S(1)}, u32[]{:S(2)}) copy-start(bf16[96,1536]{1,0:T(8,128)(2,1)S(1)} %constant_dynamic-update-slice_fusion.4.own_last_ref) | copy-start | bytes 884740
  231.3 6.8 %collective-permute-start.25 = (bf16[96,1536]{1,0:T(8,128)(2,1)S(1)}, bf16[96,1536]{1,0:T(8,128)(2,1)S(1)}, u32[]{:S(2)}, u32[]{:S(2)}) collective-permute-start(bf16[96,1536]{1,0:T(8,128)(2,1)S(1)} %constant_dynamic-update-slice_fusion.4.own_last_ref), channel_id=1, source_target_pairs={{0,1},{1,0},{2,3},{3,2},{4,5},{5,4},{6,7},{7,6},{8,9},{9,8},{10,11... | collective-permute-start | bytes 884744 | tf_op jit(solution)/shard_map/ppermute | solution.py:28
  (2 other events, 1.7 us)

commit v2 on v1

--- a/solution.py
+++ b/solution.py
@@ -50,27 +50,40 @@
             ]
 
 
+def early_kernel(up_ref, *refs):
+    total_ref = refs[-1]
+    depth = refs[0].shape[0]
+    total = None
+    for place, ref in zip((0, 1, 2, 3, 6, 7), refs[:-1]):
+        term = dot(up_ref[:, pl.ds(place * depth, depth)], ref[...], ((1,), (0,)))
+        total = term if total is None else total + term
+    total_ref[...] = total
+
+
 def forward_kernel(pos_ref, *refs):
-    pieces = refs[0:RING]
-    cot_ref, up_ref, hidden_ref, grad_ref, keep_ref, send_ref = refs[RING:]
+    pieces = refs[0 : 2 * RING]
+    early_ref, cot_ref, up_ref, hidden_ref, grad_ref, keep_ref, send_ref, packed_ref = refs[2 * RING :]
     depth = pieces[0].shape[0]
-    width = depth // RING
+    width = depth // 2
     rows = keep_ref.shape[0]
-    total = dot(up_ref[:, pl.ds(0, depth)], pieces[0][...], ((1,), (0,)))
-    for d in range(1, RING):
-        total += dot(up_ref[:, pl.ds(d * depth, depth)], pieces[d][...], ((1,), (0,)))
+    total = early_ref[...]
+    for place in (4, 5):
+        total += dot(up_ref[:, pl.ds(place * depth, depth)], pieces[place][...], ((1,), (0,)))
     gelu_out, gelu_slope = gelu_parts(total)
     hidden_ref[...] = gelu_out.astype(BF16)
     grad_ref[...] = (cot_ref[...].astype(F32) * gelu_slope).astype(BF16)
     core, zh = pos_ref[2], pos_ref[3]
-    for half, out_ref in ((1 - core, send_ref), (core, keep_ref)):
-        grads = grad_ref[pl.ds(pl.multiple_of(half * rows, 16), rows), :]
-        for d in range(RING):
-            term = dot(grads, pieces[d][...], ((1,), (1,))).astype(BF16)
-            for inner in range(RING):
-                column = column_of(pos_ref, d, inner, width) + (RING - zh) * depth
-                column = pl.multiple_of(lax.rem(column, RING * depth), 128)
-                out_ref[:, pl.ds(column, width)] = term[:, inner * width : (inner + 1) * width]
+    for at, half in enumerate((1 - core, core)):
+        packed_ref[pl.ds(at * rows, rows), :] = grad_ref[pl.ds(pl.multiple_of(half * rows, 16), rows), :]
+    grads = packed_ref[...]
+    for place, piece in enumerate(pieces):
+        term = dot(grads, piece[...], ((1,), (1,))).astype(BF16)
+        for part in range(2):
+            block = 2 * place + part
+            column = column_of(pos_ref, block // RING, block % RING, width) + (RING - zh) * 2 * depth
+            column = pl.multiple_of(lax.rem(column, 2 * RING * depth), 128)
+            send_ref[:, pl.ds(column, width)] = term[:rows, part * width : (part + 1) * width]
+            keep_ref[:, pl.ds(column, width)] = term[rows:, part * width : (part + 1) * width]
 
 
 def input_grad_kernel(grad_ref, up_ref, *outs):
@@ -81,12 +94,13 @@
         outs[d][...] = term.astype(BF16)
 
 
-def place_kernel(pos_ref, own_ref, own_last_ref, other_ref, other_last_ref, out_ref):
+def place_kernel(pos_ref, *refs):
     core, zh = pos_ref[2], pos_ref[3]
-    rows, depth = own_last_ref.shape
-    for half, most, last in ((core, own_ref, own_last_ref), (1 - core, other_ref, other_last_ref)):
+    out_ref = refs[-1]
+    rows, depth = refs[0].shape
+    for half, (mine, near, far) in ((core, refs[0:3]), (1 - core, refs[3:6])):
         where = pl.ds(pl.multiple_of(half * rows, 16), rows)
-        for d, (ref, at) in enumerate(((most, 0), (most, 1), (last, 0), (most, 2))):
+        for d, ref, at in ((0, mine, 0), (1, near, 0), (3, near, 1), (2, far, 0)):
             column = pl.multiple_of(lax.rem(zh + d, RING) * depth, 128)
             out_ref[where, pl.ds(column, depth)] = ref[:, at * depth : (at + 1) * depth]
 
@@ -140,48 +154,56 @@
     )(pos, up_rows)
 
     block = lax.all_gather(normed.T, "zl", axis=0, tiled=True)
-    pieces = gather(jnp.concatenate(gather(block, False), axis=0), True)
+    quarters = gather(block, False)
+    upper, lower = jnp.concatenate(quarters[:2], axis=0), jnp.concatenate(quarters[2:], axis=0)
+    upper1, lower3 = turn(upper, True, -1), turn(lower, True, 1)
+    lower1, upper3 = turn(lower, True, -1), turn(upper, True, 1)
+    upper2, lower2 = turn(upper1, True, -1), turn(lower3, True, 1)
+    pieces = [upper, lower, upper1, lower1, upper2, lower2, upper3, lower3]
+    early = pl.pallas_call(
+        early_kernel,
+        in_specs=vmem(7),
+        out_specs=vmem(1)[0],
+        out_shape=jax.ShapeDtypeStruct((hid, tokens), F32),
+        name="early",
+        cost_estimate=pl.CostEstimate(flops=3 * hid * tokens * width // 2, bytes_accessed=7_000_000, transcendentals=0),
+    )(ordered, *pieces[:4], *pieces[6:])
 
     hidden, hidden_grad, keep, send = pl.pallas_call(
         forward_kernel,
-        in_specs=[scalars] + vmem(RING + 2),
+        in_specs=[scalars] + vmem(2 * RING + 3),
         out_specs=vmem(4),
         out_shape=[jax.ShapeDtypeStruct((hid, tokens), BF16)] * 2
         + [jax.ShapeDtypeStruct((hid // 2, width), BF16)] * 2,
+        scratch_shapes=[pltpu.VMEM((hid, tokens), BF16)],
         name="forward",
         cost_estimate=pl.CostEstimate(
-            flops=4 * hid * tokens * width, bytes_accessed=14_000_000, transcendentals=hid * tokens * 2
+            flops=3 * hid * tokens * width, bytes_accessed=14_000_000, transcendentals=hid * tokens * 2
         ),
-    )(pos, *pieces, hidden_cot.T, ordered)
+    )(pos, *pieces, early, hidden_cot.T, ordered)
 
     depth = width // RING
-    rows = hid // 2
     arrived = shift(send, "c", 1)
     quarters = [
-        (keep[:, d * depth : (d + 1) * depth].astype(F32) + arrived[:, d * depth : (d + 1) * depth].astype(F32)).astype(BF16)
+        add_up([keep[:, d * depth : (d + 1) * depth], arrived[:, d * depth : (d + 1) * depth]]).astype(BF16)
         for d in range(RING)
     ]
-    upper = shift(quarters[2][: rows // 2], "zh", 1)
-    lower = shift(quarters[2][rows // 2 :], "zh", -1)
-    ahead = jnp.concatenate([add_up([quarters[1][: rows // 2], upper]).astype(BF16), quarters[1][rows // 2 :]], axis=0)
-    behind = jnp.concatenate([quarters[3][: rows // 2], add_up([quarters[3][rows // 2 :], lower]).astype(BF16)], axis=0)
-    arrived = [shift(ahead, "zh", 1), shift(behind, "zh", -1)]
+    arrived = [shift(quarters[2], "zh", 2)]
+    arrived += [shift(quarters[1], "zh", 1), shift(quarters[3], "zh", -1)]
     mine = (add_up([quarters[0]] + arrived) / (2 * RING)).astype(BF16)
-    before = shift(mine, "zh", 1)
-    after = shift(mine, "zh", -1)
-    across = [shift(before[: rows // 2], "zh", 1), shift(after[rows // 2 :], "zh", -1)]
-    most = jnp.concatenate([mine, after, before], axis=1)
-    last = jnp.concatenate(across, axis=0)
-    other_most = shift(most, "c", 1)
-    other_last = shift(last, "c", 1)
+    far = shift(mine, "zh", 2)
+    near = jnp.concatenate([shift(mine, "zh", -1), shift(mine, "zh", 1)], axis=1)
+    other_mine = shift(mine, "c", 1)
+    other_near = shift(near, "c", 1)
+    other_far = shift(far, "c", 1)
     up_grad = pl.pallas_call(
         place_kernel,
-        in_specs=[scalars] + vmem(4),
+        in_specs=[scalars] + vmem(6),
         out_specs=vmem(1)[0],
         out_shape=jax.ShapeDtypeStruct((hid, width), BF16),
         name="place",
         cost_estimate=pl.CostEstimate(flops=0, bytes_accessed=4 * hid * width, transcendentals=0),
-    )(pos, most, last, other_most, other_last)
+    )(pos, mine, near, far, other_mine, other_near, other_far)
 
     parts = pl.pallas_call(
         input_grad_kernel,

time: 244 us -> 257 us (1.053)
  the two profiles are of different devices: /device:TPU:8 before, /device:TPU:15 now
where the time goes in v2:
time: 257 us; the launch traced here: 256 us
  starting transfers between devices  160 us (62%)
  waiting for transfers between devices  46.4 us (18%)
  Pallas kernels  24.5 us (10%)
  blocking collectives  14.3 us (6%)
  other arithmetic  7.99 us (3%)
    ppermute x13, starting transfers between devices, shift(): lax.ppermute(value, axis, [(i, (i + by) % size) for i in range(size)])  118 us
    ppermute x15, starting transfers between devices, turn(): lax.ppermute(value, ('y', 'x', 'c'), [(flat(*s), flat(*target(*s))) for s...  41.7 us
    ppermute x13, waiting for transfers between devices, shift(): lax.ppermute(value, axis, [(i, (i + by) % size) for i in range(size)])  33.9 us
    all_gather x1, blocking collectives, work(): block = lax.all_gather(normed.T, 'zl', axis=0, tiled=True)  14.3 us
    ppermute x15, waiting for transfers between devices, turn(): lax.ppermute(value, ('y', 'x', 'c'), [(flat(*s), flat(*target(*s))) for s...  12.4 us
    pallas_call x1, Pallas kernels, work(): pl.pallas_call(forward_kernel, in_specs=[scalars] + vmem(2 * RING + 3), o...  7.91 us
    pallas_call x1, Pallas kernels, work(): pl.pallas_call(input_grad_kernel, in_specs=vmem(2), out_specs=vmem(RING),...  5.15 us
  transfers between devices with their start and end apart: 28, of which 12 were waited for; matrix products, arithmetic and copies ran while one was open for 3% of the time, Pallas kernels for 5%

profile of v2, /device:TPU:15, one launch (start us, length us, event | category | flops | bytes accessed | tf_op | source)
XLA Modules:
  0.0 256.4 jit_solution(1507787197952239445)
XLA Ops:
  0.6 14.3 %all_gather.3 = bf16[384,512]{1,0:T(8,128)(2,1)S(1)} all-gather(bf16[96,512]{1,0:T(8,128)(2,1)} %bitcast.10), channel_id=1, replica_groups=mesh['y'=4,'x'=4,'zl'=4,'zh'=4,'c'=2] {'zl'}, dimensions={0}, use_global_device_ids=true | all-gather | bytes 491520 | tf_op jit(solution)/shard_map/all_gather | solution.py:156
  14.9 3.9 %collective-permute-start.1 = (bf16[384,512]{1,0:T(8,128)(2,1)S(1)}, bf16[384,512]{1,0:T(8,128)(2,1)S(1)}, u32[]{:S(2)}, u32[]{:S(2)}) collective-permute-start(bf16[384,512]{1,0:T(8,128)(2,1)S(1)} %all_gather.3), channel_id=1, source_target_pairs={{0,64},{1,257},{32,96},{33,289},{64,0},{65,321},{96,32},{97,353},{... | collective-permute-start | bytes 1179656 | tf_op jit(solution)/shard_map/ppermute | solution.py:122
  20.8 3.4 %collective-permute-start = (bf16[384,512]{1,0:T(8,128)(2,1)S(1)}, bf16[384,512]{1,0:T(8,128)(2,1)S(1)}, u32[]{:S(2)}, u32[]{:S(2)}) collective-permute-start(bf16[384,512]{1,0:T(8,128)(2,1)S(1)} %all_gather.3), channel_id=1, source_target_pairs={{0,96},{1,385},{32,0},{33,417},{64,32},{65,449},{96,64},{97,481},{... | collective-permute-start | bytes 1179656 | tf_op jit(solution)/shard_map/ppermute | solution.py:122
  25.2 4.3 %collective-permute-done.2 = bf16[384,512]{1,0:T(8,128)(2,1)S(1)} collective-permute-done((bf16[384,512]{1,0:T(8,128)(2,1)S(1)}, bf16[384,512]{1,0:T(8,128)(2,1)S(1)}, u32[]{:S(2)}, u32[]{:S(2)}) %collective-permute-start.2) | collective-permute-done | bytes 393248 | tf_op jit(solution)/shard_map/ppermute | solution.py:122
  31.8 3.2 %collective-permute-start.3 = (bf16[768,512]{1,0:T(8,128)(2,1)S(1)}, bf16[768,512]{1,0:T(8,128)(2,1)S(1)}, u32[]{:S(2)}, u32[]{:S(2)}) collective-permute-start(bf16[768,512]{1,0:T(8,128)(2,1)S(1)} %constant_dynamic-update-slice_fusion.refs_0_), channel_id=1, source_target_pairs={{0,384},{1,97},{32,416},{33,1},{64,448},{65,33},{96,480},{97,65},{... | collective-permute-start | bytes 2359304 | tf_op jit(solution)/shard_map/ppermute | solution.py:122
  35.0 2.5 collective-permute-start.4
  37.4 4.0 %collective-permute-start.8 = (bf16[768,512]{1,0:T(8,128)(2,1)S(1)}, bf16[768,512]{1,0:T(8,128)(2,1)}, u32[]{:S(2)}, u32[]{:S(2)}) collective-permute-start(bf16[768,512]{1,0:T(8,128)(2,1)S(1)} %constant_dynamic-update-slice_fusion.refs_0_), channel_id=1, source_target_pairs={{0,128},{1,33},{32,160},{33,65},{64,192},{65,97},{96,224},{97,1},{... | collective-permute-start | bytes 2359304 | tf_op jit(solution)/shard_map/ppermute | solution.py:122
  42.7 3.0 %collective-permute-start.7 = (bf16[768,512]{1,0:T(8,128)(2,1)S(1)}, bf16[768,512]{1,0:T(8,128)(2,1)}, u32[]{:S(2)}, u32[]{:S(2)}) collective-permute-start(bf16[768,512]{1,0:T(8,128)(2,1)S(1)} %collective-permute-done.6.refs_5_.refs_7_), channel_id=1, source_target_pairs={{0,128},{1,33},{32,160},{33,65},{64,192},{65,97},{96,224},{97,1},{... | collective-permute-start | bytes 2359304 | tf_op jit(solution)/shard_map/ppermute | solution.py:122
  48.7 3.4 %order.1.up_ref.refs_10_ = bf16[192,6144]{1,0:T(8,128)(2,1)} custom-call(s32[4]{0:T(128)} %pad_add_fusion.pos_ref, bf16[192,6144]{1,0:T(8,128)(2,1)} %up_ref.1), custom_call_target="tpu_custom_call" | custom-call | bytes 4718592 | tf_op jit(solution)/shard_map/order/pallas_call | solution.py:147
  54.3 4.9 %early.1.refs_8_ = f32[192,512]{1,0:T(8,128)} custom-call(bf16[192,6144]{1,0:T(8,128)(2,1)} %order.1.up_ref.refs_10_, bf16[768,512]{1,0:T(8,128)(2,1)} %copy-done, bf16[768,512]{1,0:T(8,128)(2,1)} %copy-done.1, bf16[768,512]{1,0:T(8,128)(2,1)} %copy-done.3, bf16[768,512]{1,0:T(8,128)(2,1)} %collective-permute-done.4.refs_3_, ...), custom_call_target="tpu_custom_call" | custom-call | flops 905969664 | bytes 7000000 | tf_op jit(solution)/shard_map/early/pallas_call | solution.py:163
  59.6 3.1 %collective-permute-done.5.refs_4_ = bf16[768,512]{1,0:T(8,128)(2,1)} collective-permute-done((bf16[768,512]{1,0:T(8,128)(2,1)S(1)}, bf16[768,512]{1,0:T(8,128)(2,1)}, u32[]{:S(2)}, u32[]{:S(2)}) %collective-permute-start.5) | collective-permute-done | bytes 786464 | tf_op jit(solution)/shard_map/ppermute | solution.py:122
  62.7 7.9 %forward.1 = (bf16[192,512]{1,0:T(8,128)(2,1)}, bf16[192,512]{1,0:T(8,128)(2,1)}, bf16[96,6144]{1,0:T(8,128)(2,1)}, bf16[96,6144]{1,0:T(8,128)(2,1)}) custom-call(s32[4]{0:T(128)} %pad_add_fusion.pos_ref, bf16[768,512]{1,0:T(8,128)(2,1)} %copy-done, bf16[768,512]{1,0:T(8,128)(2,1)} %copy-done.1, bf16[768,512]{1,0:T(8,128)(2,1)} %copy-done.3, ...), custom_call_target="tpu_custom_call" | custom-call | flops 1811939328 | bytes 14000000 | tf_op jit(solution)/shard_map/forward/pallas_call | solution.py:172
  70.6 7.1 %collective-permute-start.18 = (bf16[96,6144]{1,0:T(8,128)(2,1)}, bf16[96,6144]{1,0:T(8,128)(2,1)}, u32[]{:S(2)}, u32[]{:S(2)}) collective-permute-start(bf16[96,6144]{1,0:T(8,128)(2,1)} %get-tuple-element.18), channel_id=1, source_target_pairs={{0,1},{1,0},{2,3},{3,2},{4,5},{5,4},{6,7},{7,6},{8,9},{9,8},{10,11... | collective-permute-start | bytes 3538952 | tf_op jit(solution)/shard_map/ppermute | solution.py:28
  77.8 5.2 %partial.1 = (bf16[1536,512]{1,0:T(8,128)(2,1)}, bf16[1536,512]{1,0:T(8,128)(2,1)}, bf16[1536,512]{1,0:T(8,128)(2,1)}, bf16[1536,512]{1,0:T(8,128)(2,1)}) custom-call(bf16[192,512]{1,0:T(8,128)(2,1)} %get-tuple-element.12.grad_ref, bf16[192,6144]{1,0:T(8,128)(2,1)} %order.1.up_ref.refs_10_), custom_call_target="tpu_custom_call" | custom-call | flops 1207959552 | bytes 9000000 | tf_op jit(solution)/shard_map/partial/pallas_call | solution.py:208
  82.9 2.3 collective-permute-start.10
  85.2 5.1 %collective-permute-start.11 = (bf16[1536,512]{1,0:T(8,128)(2,1)}, bf16[1536,512]{1,0:T(8,128)(2,1)}, u32[]{:S(2)}, u32[]{:S(2)}) collective-permute-start(bf16[1536,512]{1,0:T(8,128)(2,1)} %get-tuple-element.16), channel_id=1, source_target_pairs={{0,384},{1,97},{32,416},{33,1},{64,448},{65,33},{96,480},{97,65},{... | collective-permute-start | bytes 4718600 | tf_op jit(solution)/shard_map/ppermute | solution.py:122
  94.4 14.4 %collective-permute-start.19 = (bf16[96,1536]{1,0:T(8,128)(2,1)S(1)}, bf16[96,1536]{1,0:T(8,128)(2,1)}, u32[]{:S(2)}, u32[]{:S(2)}) collective-permute-start(bf16[96,1536]{1,0:T(8,128)(2,1)S(1)} %get-tuple-element.19), channel_id=1, source_target_pairs={{0,4},{2,6},{4,0},{6,2},{1,5},{3,7},{5,1},{7,3},{8,12},{10,14},{12... | collective-permute-start | bytes 884744 | tf_op jit(solution)/shard_map/ppermute | solution.py:28
  108.9 4.0 %collective-permute-start.20 = (bf16[96,1536]{1,0:T(8,128)(2,1)}, bf16[96,1536]{1,0:T(8,128)(2,1)S(1)}, u32[]{:S(2)}, u32[]{:S(2)}) collective-permute-start(bf16[96,1536]{1,0:T(8,128)(2,1)} %get-tuple-element.21), channel_id=1, source_target_pairs={{0,2},{2,4},{4,6},{6,0},{1,3},{3,5},{5,7},{7,1},{8,10},{10,12},{12... | collective-permute-start | bytes 884744 | tf_op jit(solution)/shard_map/ppermute | solution.py:28
  112.9 7.5 %collective-permute-done.19 = bf16[96,1536]{1,0:T(8,128)(2,1)} collective-permute-done((bf16[96,1536]{1,0:T(8,128)(2,1)S(1)}, bf16[96,1536]{1,0:T(8,128)(2,1)}, u32[]{:S(2)}, u32[]{:S(2)}) %collective-permute-start.19) | collective-permute-done | bytes 294944 | tf_op jit(solution)/shard_map/ppermute | solution.py:28
  120.4 23.6 %collective-permute-start.21 = (bf16[96,1536]{1,0:T(8,128)(2,1)}, bf16[96,1536]{1,0:T(8,128)(2,1)}, u32[]{:S(2)}, u32[]{:S(2)}) collective-permute-start(bf16[96,1536]{1,0:T(8,128)(2,1)} %get-tuple-element.20), channel_id=1, source_target_pairs={{0,6},{2,0},{4,2},{6,4},{1,7},{3,1},{5,3},{7,5},{8,14},{10,8},{12,... | collective-permute-start | bytes 884744 | tf_op jit(solution)/shard_map/ppermute | solution.py:28
  144.8 14.3 %collective-permute-done.21 = bf16[96,1536]{1,0:T(8,128)(2,1)} collective-permute-done((bf16[96,1536]{1,0:T(8,128)(2,1)}, bf16[96,1536]{1,0:T(8,128)(2,1)}, u32[]{:S(2)}, u32[]{:S(2)}) %collective-permute-start.21) | collective-permute-done | bytes 294944 | tf_op jit(solution)/shard_map/ppermute | solution.py:28
  160.6 21.3 %collective-permute-start.22 = (bf16[96,1536]{1,0:T(8,128)(2,1)S(1)}, bf16[96,1536]{1,0:T(8,128)(2,1)S(1)}, u32[]{:S(2)}, u32[]{:S(2)}) collective-permute-start(bf16[96,1536]{1,0:T(8,128)(2,1)S(1)} %multiply_convert_fusion.refs_0_), channel_id=1, source_target_pairs={{0,6},{2,0},{4,2},{6,4},{1,7},{3,1},{5,3},{7,5},{8,14},{10,8},{12,... | collective-permute-start | bytes 884744 | tf_op jit(solution)/shard_map/ppermute | solution.py:28
  183.9 7.0 %collective-permute-start.24 = (bf16[96,1536]{1,0:T(8,128)(2,1)S(1)}, bf16[96,1536]{1,0:T(8,128)(2,1)}, u32[]{:S(2)}, u32[]{:S(2)}) collective-permute-start(bf16[96,1536]{1,0:T(8,128)(2,1)S(1)} %multiply_convert_fusion.refs_0_), channel_id=1, source_target_pairs={{0,4},{2,6},{4,0},{6,2},{1,5},{3,7},{5,1},{7,3},{8,12},{10,14},{12... | collective-permute-start | bytes 884744 | tf_op jit(solution)/shard_map/ppermute | solution.py:28
  190.9 2.7 %add_convert_fusion = bf16[1536,512]{1,0:T(8,128)(2,1)S(1)} fusion(bf16[1536,512]{1,0:T(8,128)(2,1)} %collective-permute-done.11, bf16[1536,512]{1,0:T(8,128)(2,1)S(1)} %collective-permute-done.10, bf16[1536,512]{1,0:T(8,128)(2,1)} %collective-permute-done.9, bf16[1536,512]{1,0:T(8,128)(2,1)S(1)} %copy-done.4), kind=kLoop, calls=%fused_computation | loop fusion | flops 6291456 | bytes 7864320 | tf_op jit(solution)/shard_map/convert_element_type | solution.py:218
  198.7 2.3 collective-permute-start.14
  201.0 10.0 %collective-permute-done.23 = bf16[96,1536]{1,0:T(8,128)(2,1)S(1)} collective-permute-done((bf16[96,1536]{1,0:T(8,128)(2,1)S(1)}, bf16[96,1536]{1,0:T(8,128)(2,1)S(1)}, u32[]{:S(2)}, u32[]{:S(2)}) %collective-permute-start.23) | collective-permute-done | bytes 294944 | tf_op jit(solution)/shard_map/ppermute | solution.py:28
  211.0 4.1 %collective-permute-start.26 = (bf16[96,3072]{1,0:T(8,128)(2,1)S(1)}, bf16[96,3072]{1,0:T(8,128)(2,1)S(1)}, u32[]{:S(2)}, u32[]{:S(2)}) collective-permute-start(bf16[96,3072]{1,0:T(8,128)(2,1)S(1)} %constant_dynamic-update-slice_fusion.4.refs_1_), channel_id=1, source_target_pairs={{0,1},{1,0},{2,3},{3,2},{4,5},{5,4},{6,7},{7,6},{8,9},{9,8},{10,11... | collective-permute-start | bytes 1769480 | tf_op jit(solution)/shard_map/ppermute | solution.py:28
  215.4 9.5 %collective-permute-start.15 = (bf16[96,512]{1,0:T(8,128)(2,1)S(1)}, bf16[96,512]{1,0:T(8,128)(2,1)S(1)}, u32[]{:S(2)}, u32[]{:S(2)}) collective-permute-start(bf16[96,512]{1,0:T(8,128)(2,1)S(1)} %get-tuple-element.25), channel_id=1, source_target_pairs={{0,8},{8,16},{16,24},{24,0},{1,9},{9,17},{17,25},{25,1},{2,10},{10... | collective-permute-start | bytes 294920 | tf_op jit(solution)/shard_map/ppermute | solution.py:28
  224.9 9.1 %collective-permute-start.16 = (bf16[96,512]{1,0:T(8,128)(2,1)S(1)}, bf16[96,512]{1,0:T(8,128)(2,1)S(1)}, u32[]{:S(2)}, u32[]{:S(2)}) collective-permute-start(bf16[96,512]{1,0:T(8,128)(2,1)S(1)} %get-tuple-element.27), channel_id=1, source_target_pairs={{0,16},{8,24},{16,0},{24,8},{1,17},{9,25},{17,1},{25,9},{2,18},{10... | collective-permute-start | bytes 294920 | tf_op jit(solution)/shard_map/ppermute | solution.py:28
  234.0 4.3 %collective-permute-start.17 = (bf16[96,512]{1,0:T(8,128)(2,1)S(1)}, bf16[96,512]{1,0:T(8,128)(2,1)S(1)}, u32[]{:S(2)}, u32[]{:S(2)}) collective-permute-start(bf16[96,512]{1,0:T(8,128)(2,1)S(1)} %get-tuple-element.26), channel_id=1, source_target_pairs={{0,24},{8,0},{16,8},{24,16},{1,25},{9,1},{17,9},{25,17},{2,26},{10... | collective-permute-start | bytes 294920 | tf_op jit(solution)/shard_map/ppermute | solution.py:28
  238.3 9.7 %collective-permute-start.25 = (bf16[96,1536]{1,0:T(8,128)(2,1)S(1)}, bf16[96,1536]{1,0:T(8,128)(2,1)S(1)}, u32[]{:S(2)}, u32[]{:S(2)}) collective-permute-start(bf16[96,1536]{1,0:T(8,128)(2,1)S(1)} %multiply_convert_fusion.refs_0_), channel_id=1, source_target_pairs={{0,1},{1,0},{2,3},{3,2},{4,5},{5,4},{6,7},{7,6},{8,9},{9,8},{10,11... | collective-permute-start | bytes 884744 | tf_op jit(solution)/shard_map/ppermute | solution.py:28
  253.2 3.2 %place.1 = bf16[192,6144]{1,0:T(8,128)(2,1)} custom-call(s32[4]{0:T(128)} %pad_add_fusion.pos_ref, bf16[96,1536]{1,0:T(8,128)(2,1)} %copy-done.6, bf16[96,3072]{1,0:T(8,128)(2,1)} %copy-done.5, bf16[96,1536]{1,0:T(8,128)(2,1)} %collective-permute-done.24.refs_2_, bf16[96,1536]{1,0:T(8,128)(2,1)} %copy-done.9, bf16[96,3072]{1,0:T(8,128)(2,1)} %copy-done.8, ...), custom_call_target="tpu_custom_call" | custom-call | bytes 4718592 | tf_op jit(solution)/shard_map/place/pallas_call | solution.py:199
  (68 shorter events, 30.8 us)
Async XLA Ops:
  14.9 10.3 %collective-permute-start.1 = (bf16[384,512]{1,0:T(8,128)(2,1)S(1)}, bf16[384,512]{1,0:T(8,128)(2,1)S(1)}, u32[]{:S(2)}, u32[]{:S(2)}) collective-permute-start(bf16[384,512]{1,0:T(8,128)(2,1)S(1)} %all_gather.3), channel_id=1, source_target_pairs={{0,64},{1,257},{32,96},{33,289},{64,0},{65,321},{96,32},{97,353},{... | collective-permute-start | bytes 1179656 | tf_op jit(solution)/shard_map/ppermute | solution.py:122
  18.8 10.8 %collective-permute-start.2 = (bf16[384,512]{1,0:T(8,128)(2,1)S(1)}, bf16[384,512]{1,0:T(8,128)(2,1)S(1)}, u32[]{:S(2)}, u32[]{:S(2)}) collective-permute-start(bf16[384,512]{1,0:T(8,128)(2,1)S(1)} %all_gather.3), channel_id=1, source_target_pairs={{0,32},{1,129},{32,64},{33,161},{64,96},{65,193},{96,0},{97,225},{... | collective-permute-start | bytes 1179656 | tf_op jit(solution)/shard_map/ppermute | solution.py:122
  20.8 11.0 %collective-permute-start = (bf16[384,512]{1,0:T(8,128)(2,1)S(1)}, bf16[384,512]{1,0:T(8,128)(2,1)S(1)}, u32[]{:S(2)}, u32[]{:S(2)}) collective-permute-start(bf16[384,512]{1,0:T(8,128)(2,1)S(1)} %all_gather.3), channel_id=1, source_target_pairs={{0,96},{1,385},{32,0},{33,417},{64,32},{65,449},{96,64},{97,481},{... | collective-permute-start | bytes 1179656 | tf_op jit(solution)/shard_map/ppermute | solution.py:122
  29.6 22.4 %copy-start.1 = (bf16[768,512]{1,0:T(8,128)(2,1)}, bf16[768,512]{1,0:T(8,128)(2,1)S(1)}, u32[]{:S(2)}) copy-start(bf16[768,512]{1,0:T(8,128)(2,1)S(1)} %constant_dynamic-update-slice_fusion.2.refs_1_) | copy-start | bytes 2359300
  29.6 13.0 %collective-permute-start.6 = (bf16[768,512]{1,0:T(8,128)(2,1)S(1)}, bf16[768,512]{1,0:T(8,128)(2,1)S(1)}, u32[]{:S(2)}, u32[]{:S(2)}) collective-permute-start(bf16[768,512]{1,0:T(8,128)(2,1)S(1)} %constant_dynamic-update-slice_fusion.2.refs_1_), channel_id=1, source_target_pairs={{0,128},{1,33},{32,160},{33,65},{64,192},{65,97},{96,224},{97,1},{... | collective-permute-start | bytes 2359304 | tf_op jit(solution)/shard_map/ppermute | solution.py:122
  31.8 13.9 %collective-permute-start.3 = (bf16[768,512]{1,0:T(8,128)(2,1)S(1)}, bf16[768,512]{1,0:T(8,128)(2,1)S(1)}, u32[]{:S(2)}, u32[]{:S(2)}) collective-permute-start(bf16[768,512]{1,0:T(8,128)(2,1)S(1)} %constant_dynamic-update-slice_fusion.refs_0_), channel_id=1, source_target_pairs={{0,384},{1,97},{32,416},{33,1},{64,448},{65,33},{96,480},{97,65},{... | collective-permute-start | bytes 2359304 | tf_op jit(solution)/shard_map/ppermute | solution.py:122
  35.0 19.3 %collective-permute-start.4 = (bf16[768,512]{1,0:T(8,128)(2,1)S(1)}, bf16[768,512]{1,0:T(8,128)(2,1)}, u32[]{:S(2)}, u32[]{:S(2)}) collective-permute-start(bf16[768,512]{1,0:T(8,128)(2,1)S(1)} %constant_dynamic-update-slice_fusion.2.refs_1_), channel_id=1, source_target_pairs={{0,384},{1,97},{32,416},{33,1},{64,448},{65,33},{96,480},{97,65},{... | collective-permute-start | bytes 2359304 | tf_op jit(solution)/shard_map/ppermute | solution.py:122
  37.4 16.8 %collective-permute-start.8 = (bf16[768,512]{1,0:T(8,128)(2,1)S(1)}, bf16[768,512]{1,0:T(8,128)(2,1)}, u32[]{:S(2)}, u32[]{:S(2)}) collective-permute-start(bf16[768,512]{1,0:T(8,128)(2,1)S(1)} %constant_dynamic-update-slice_fusion.refs_0_), channel_id=1, source_target_pairs={{0,128},{1,33},{32,160},{33,65},{64,192},{65,97},{96,224},{97,1},{... | collective-permute-start | bytes 2359304 | tf_op jit(solution)/shard_map/ppermute | solution.py:122
  42.7 17.0 %collective-permute-start.7 = (bf16[768,512]{1,0:T(8,128)(2,1)S(1)}, bf16[768,512]{1,0:T(8,128)(2,1)}, u32[]{:S(2)}, u32[]{:S(2)}) collective-permute-start(bf16[768,512]{1,0:T(8,128)(2,1)S(1)} %collective-permute-done.6.refs_5_.refs_7_), channel_id=1, source_target_pairs={{0,128},{1,33},{32,160},{33,65},{64,192},{65,97},{96,224},{97,1},{... | collective-permute-start | bytes 2359304 | tf_op jit(solution)/shard_map/ppermute | solution.py:122
  45.7 17.0 %collective-permute-start.5 = (bf16[768,512]{1,0:T(8,128)(2,1)S(1)}, bf16[768,512]{1,0:T(8,128)(2,1)}, u32[]{:S(2)}, u32[]{:S(2)}) collective-permute-start(bf16[768,512]{1,0:T(8,128)(2,1)S(1)} %collective-permute-done.3.refs_2_), channel_id=1, source_target_pairs={{0,384},{1,97},{32,416},{33,1},{64,448},{65,33},{96,480},{97,65},{... | collective-permute-start | bytes 2359304 | tf_op jit(solution)/shard_map/ppermute | solution.py:122
  70.6 21.6 %collective-permute-start.18 = (bf16[96,6144]{1,0:T(8,128)(2,1)}, bf16[96,6144]{1,0:T(8,128)(2,1)}, u32[]{:S(2)}, u32[]{:S(2)}) collective-permute-start(bf16[96,6144]{1,0:T(8,128)(2,1)} %get-tuple-element.18), channel_id=1, source_target_pairs={{0,1},{1,0},{2,3},{3,2},{4,5},{5,4},{6,7},{7,6},{8,9},{9,8},{10,11... | collective-permute-start | bytes 3538952 | tf_op jit(solution)/shard_map/ppermute | solution.py:28
  82.9 101.0 %collective-permute-start.10 = (bf16[1536,512]{1,0:T(8,128)(2,1)}, bf16[1536,512]{1,0:T(8,128)(2,1)S(1)}, u32[]{:S(2)}, u32[]{:S(2)}) collective-permute-start(bf16[1536,512]{1,0:T(8,128)(2,1)} %get-tuple-element.15), channel_id=1, source_target_pairs={{0,256},{1,65},{32,288},{33,97},{64,320},{65,1},{96,352},{97,33},{... | collective-permute-start | bytes 4718600 | tf_op jit(solution)/shard_map/ppermute | solution.py:122
  85.2 105.7 %collective-permute-start.11 = (bf16[1536,512]{1,0:T(8,128)(2,1)}, bf16[1536,512]{1,0:T(8,128)(2,1)}, u32[]{:S(2)}, u32[]{:S(2)}) collective-permute-start(bf16[1536,512]{1,0:T(8,128)(2,1)} %get-tuple-element.16), channel_id=1, source_target_pairs={{0,384},{1,97},{32,416},{33,1},{64,448},{65,33},{96,480},{97,65},{... | collective-permute-start | bytes 4718600 | tf_op jit(solution)/shard_map/ppermute | solution.py:122
  90.3 100.6 %collective-permute-start.9 = (bf16[1536,512]{1,0:T(8,128)(2,1)}, bf16[1536,512]{1,0:T(8,128)(2,1)}, u32[]{:S(2)}, u32[]{:S(2)}) collective-permute-start(bf16[1536,512]{1,0:T(8,128)(2,1)} %get-tuple-element.14), channel_id=1, source_target_pairs={{0,128},{1,33},{32,160},{33,65},{64,192},{65,97},{96,224},{97,1},{... | collective-permute-start | bytes 4718600 | tf_op jit(solution)/shard_map/ppermute | solution.py:122
  94.4 96.5 %copy-start.4 = (bf16[1536,512]{1,0:T(8,128)(2,1)S(1)}, bf16[1536,512]{1,0:T(8,128)(2,1)}, u32[]{:S(2)}) copy-start(bf16[1536,512]{1,0:T(8,128)(2,1)} %get-tuple-element.13) | copy-start | bytes 4718596
  94.4 26.0 %collective-permute-start.19 = (bf16[96,1536]{1,0:T(8,128)(2,1)S(1)}, bf16[96,1536]{1,0:T(8,128)(2,1)}, u32[]{:S(2)}, u32[]{:S(2)}) collective-permute-start(bf16[96,1536]{1,0:T(8,128)(2,1)S(1)} %get-tuple-element.19), channel_id=1, source_target_pairs={{0,4},{2,6},{4,0},{6,2},{1,5},{3,7},{5,1},{7,3},{8,12},{10,14},{12... | collective-permute-start | bytes 884744 | tf_op jit(solution)/shard_map/ppermute | solution.py:28
  108.9 35.2 %collective-permute-start.20 = (bf16[96,1536]{1,0:T(8,128)(2,1)}, bf16[96,1536]{1,0:T(8,128)(2,1)S(1)}, u32[]{:S(2)}, u32[]{:S(2)}) collective-permute-start(bf16[96,1536]{1,0:T(8,128)(2,1)} %get-tuple-element.21), channel_id=1, source_target_pairs={{0,2},{2,4},{4,6},{6,0},{1,3},{3,5},{5,7},{7,1},{8,10},{10,12},{12... | collective-permute-start | bytes 884744 | tf_op jit(solution)/shard_map/ppermute | solution.py:28
  120.4 38.7 %collective-permute-start.21 = (bf16[96,1536]{1,0:T(8,128)(2,1)}, bf16[96,1536]{1,0:T(8,128)(2,1)}, u32[]{:S(2)}, u32[]{:S(2)}) collective-permute-start(bf16[96,1536]{1,0:T(8,128)(2,1)} %get-tuple-element.20), channel_id=1, source_target_pairs={{0,6},{2,0},{4,2},{6,4},{1,7},{3,1},{5,3},{7,5},{8,14},{10,8},{12,... | collective-permute-start | bytes 884744 | tf_op jit(solution)/shard_map/ppermute | solution.py:28
  160.6 77.7 %copy-start.6 = (bf16[96,1536]{1,0:T(8,128)(2,1)}, bf16[96,1536]{1,0:T(8,128)(2,1)S(1)}, u32[]{:S(2)}) copy-start(bf16[96,1536]{1,0:T(8,128)(2,1)S(1)} %multiply_convert_fusion.refs_0_) | copy-start | bytes 884740
  160.6 38.1 %collective-permute-start.22 = (bf16[96,1536]{1,0:T(8,128)(2,1)S(1)}, bf16[96,1536]{1,0:T(8,128)(2,1)S(1)}, u32[]{:S(2)}, u32[]{:S(2)}) collective-permute-start(bf16[96,1536]{1,0:T(8,128)(2,1)S(1)} %multiply_convert_fusion.refs_0_), channel_id=1, source_target_pairs={{0,6},{2,0},{4,2},{6,4},{1,7},{3,1},{5,3},{7,5},{8,14},{10,8},{12,... | collective-permute-start | bytes 884744 | tf_op jit(solution)/shard_map/ppermute | solution.py:28
  181.9 29.0 %collective-permute-start.23 = (bf16[96,1536]{1,0:T(8,128)(2,1)S(1)}, bf16[96,1536]{1,0:T(8,128)(2,1)S(1)}, u32[]{:S(2)}, u32[]{:S(2)}) collective-permute-start(bf16[96,1536]{1,0:T(8,128)(2,1)S(1)} %multiply_convert_fusion.refs_0_), channel_id=1, source_target_pairs={{0,2},{2,4},{4,6},{6,0},{1,3},{3,5},{5,7},{7,1},{8,10},{10,12},{12... | collective-permute-start | bytes 884744 | tf_op jit(solution)/shard_map/ppermute | solution.py:28
  183.9 54.4 %collective-permute-start.24 = (bf16[96,1536]{1,0:T(8,128)(2,1)S(1)}, bf16[96,1536]{1,0:T(8,128)(2,1)}, u32[]{:S(2)}, u32[]{:S(2)}) collective-permute-start(bf16[96,1536]{1,0:T(8,128)(2,1)S(1)} %multiply_convert_fusion.refs_0_), channel_id=1, source_target_pairs={{0,4},{2,6},{4,0},{6,2},{1,5},{3,7},{5,1},{7,3},{8,12},{10,14},{12... | collective-permute-start | bytes 884744 | tf_op jit(solution)/shard_map/ppermute | solution.py:28
  193.7 21.4 %collective-permute-start.12 = (bf16[384,512]{1,0:T(8,128)(2,1)S(1)}, bf16[384,512]{1,0:T(8,128)(2,1)S(1)}, u32[]{:S(2)}, u32[]{:S(2)}) collective-permute-start(bf16[384,512]{1,0:T(8,128)(2,1)S(1)} %get-tuple-element.22), channel_id=1, source_target_pairs={{0,32},{1,129},{32,64},{33,161},{64,96},{65,193},{96,0},{97,225},{... | collective-permute-start | bytes 1179656 | tf_op jit(solution)/shard_map/ppermute | solution.py:122
  195.7 19.5 %collective-permute-start.13 = (bf16[384,512]{1,0:T(8,128)(2,1)S(1)}, bf16[384,512]{1,0:T(8,128)(2,1)S(1)}, u32[]{:S(2)}, u32[]{:S(2)}) collective-permute-start(bf16[384,512]{1,0:T(8,128)(2,1)S(1)} %get-tuple-element.24), channel_id=1, source_target_pairs={{0,64},{1,257},{32,96},{33,289},{64,0},{65,321},{96,32},{97,353},{... | collective-permute-start | bytes 1179656 | tf_op jit(solution)/shard_map/ppermute | solution.py:122
  198.7 16.4 %collective-permute-start.14 = (bf16[384,512]{1,0:T(8,128)(2,1)S(1)}, bf16[384,512]{1,0:T(8,128)(2,1)S(1)}, u32[]{:S(2)}, u32[]{:S(2)}) collective-permute-start(bf16[384,512]{1,0:T(8,128)(2,1)S(1)} %get-tuple-element.23), channel_id=1, source_target_pairs={{0,96},{1,385},{32,0},{33,417},{64,32},{65,449},{96,64},{97,481},{... | collective-permute-start | bytes 1179656 | tf_op jit(solution)/shard_map/ppermute | solution.py:122
  211.0 40.7 %copy-start.5 = (bf16[96,3072]{1,0:T(8,128)(2,1)}, bf16[96,3072]{1,0:T(8,128)(2,1)S(1)}, u32[]{:S(2)}) copy-start(bf16[96,3072]{1,0:T(8,128)(2,1)S(1)} %constant_dynamic-update-slice_fusion.4.refs_1_) | copy-start | bytes 1769476
  211.0 40.7 %collective-permute-start.26 = (bf16[96,3072]{1,0:T(8,128)(2,1)S(1)}, bf16[96,3072]{1,0:T(8,128)(2,1)S(1)}, u32[]{:S(2)}, u32[]{:S(2)}) collective-permute-start(bf16[96,3072]{1,0:T(8,128)(2,1)S(1)} %constant_dynamic-update-slice_fusion.4.refs_1_), channel_id=1, source_target_pairs={{0,1},{1,0},{2,3},{3,2},{4,5},{5,4},{6,7},{7,6},{8,9},{9,8},{10,11... | collective-permute-start | bytes 1769480 | tf_op jit(solution)/shard_map/ppermute | solution.py:28
  215.4 32.6 %collective-permute-start.15 = (bf16[96,512]{1,0:T(8,128)(2,1)S(1)}, bf16[96,512]{1,0:T(8,128)(2,1)S(1)}, u32[]{:S(2)}, u32[]{:S(2)}) collective-permute-start(bf16[96,512]{1,0:T(8,128)(2,1)S(1)} %get-tuple-element.25), channel_id=1, source_target_pairs={{0,8},{8,16},{16,24},{24,0},{1,9},{9,17},{17,25},{25,1},{2,10},{10... | collective-permute-start | bytes 294920 | tf_op jit(solution)/shard_map/ppermute | solution.py:28
  224.9 25.1 %collective-permute-start.16 = (bf16[96,512]{1,0:T(8,128)(2,1)S(1)}, bf16[96,512]{1,0:T(8,128)(2,1)S(1)}, u32[]{:S(2)}, u32[]{:S(2)}) collective-permute-start(bf16[96,512]{1,0:T(8,128)(2,1)S(1)} %get-tuple-element.27), channel_id=1, source_target_pairs={{0,16},{8,24},{16,0},{24,8},{1,17},{9,25},{17,1},{25,9},{2,18},{10... | collective-permute-start | bytes 294920 | tf_op jit(solution)/shard_map/ppermute | solution.py:28
  234.0 15.9 %collective-permute-start.17 = (bf16[96,512]{1,0:T(8,128)(2,1)S(1)}, bf16[96,512]{1,0:T(8,128)(2,1)S(1)}, u32[]{:S(2)}, u32[]{:S(2)}) collective-permute-start(bf16[96,512]{1,0:T(8,128)(2,1)S(1)} %get-tuple-element.26), channel_id=1, source_target_pairs={{0,24},{8,0},{16,8},{24,16},{1,25},{9,1},{17,9},{25,17},{2,26},{10... | collective-permute-start | bytes 294920 | tf_op jit(solution)/shard_map/ppermute | solution.py:28
  238.3 12.4 %collective-permute-start.25 = (bf16[96,1536]{1,0:T(8,128)(2,1)S(1)}, bf16[96,1536]{1,0:T(8,128)(2,1)S(1)}, u32[]{:S(2)}, u32[]{:S(2)}) collective-permute-start(bf16[96,1536]{1,0:T(8,128)(2,1)S(1)} %multiply_convert_fusion.refs_0_), channel_id=1, source_target_pairs={{0,1},{1,0},{2,3},{3,2},{4,5},{5,4},{6,7},{7,6},{8,9},{9,8},{10,11... | collective-permute-start | bytes 884744 | tf_op jit(solution)/shard_map/ppermute | solution.py:28
  248.0 3.7 %collective-permute-start.27 = (bf16[96,1536]{1,0:T(8,128)(2,1)}, bf16[96,1536]{1,0:T(8,128)(2,1)S(1)}, u32[]{:S(2)}, u32[]{:S(2)}) collective-permute-start(bf16[96,1536]{1,0:T(8,128)(2,1)} %collective-permute-done.24.refs_2_), channel_id=1, source_target_pairs={{0,1},{1,0},{2,3},{3,2},{4,5},{5,4},{6,7},{7,6},{8,9},{9,8},{10,11... | collective-permute-start | bytes 884744 | tf_op jit(solution)/shard_map/ppermute | solution.py:28
  (8 other events, 53.7 us)

commit v3 on v2

--- a/solution.py
+++ b/solution.py
@@ -188,11 +188,23 @@
         add_up([keep[:, d * depth : (d + 1) * depth], arrived[:, d * depth : (d + 1) * depth]]).astype(BF16)
         for d in range(RING)
     ]
-    arrived = [shift(quarters[2], "zh", 2)]
-    arrived += [shift(quarters[1], "zh", 1), shift(quarters[3], "zh", -1)]
-    mine = (add_up([quarters[0]] + arrived) / (2 * RING)).astype(BF16)
-    far = shift(mine, "zh", 2)
-    near = jnp.concatenate([shift(mine, "zh", -1), shift(mine, "zh", 1)], axis=1)
+    mid = quarters[0].shape[0] // 2
+    upper = [quarter[:mid] for quarter in quarters]
+    lower = [quarter[mid:] for quarter in quarters]
+    upper_in, lower_in = shift(upper[2], "zh", 1), shift(lower[2], "zh", -1)
+    lower_from_left, upper_from_right = shift(lower[1], "zh", 1), shift(upper[3], "zh", -1)
+    upper_from_left = shift(add_up([upper[1], upper_in]).astype(BF16), "zh", 1)
+    lower_from_right = shift(add_up([lower[3], lower_in]).astype(BF16), "zh", -1)
+    upper0 = (add_up([upper[0], upper_from_left, upper_from_right]) / (2 * RING)).astype(BF16)
+    lower0 = (add_up([lower[0], lower_from_left, lower_from_right]) / (2 * RING)).astype(BF16)
+    upper1, lower3 = shift(upper0, "zh", -1), shift(lower0, "zh", 1)
+    lower1, upper3 = shift(lower0, "zh", -1), shift(upper0, "zh", 1)
+    upper2, lower2 = shift(upper1, "zh", -1), shift(lower3, "zh", 1)
+    mine = jnp.concatenate([upper0, lower0], axis=0)
+    near = jnp.concatenate(
+        [jnp.concatenate([upper1, upper3], axis=1), jnp.concatenate([lower1, lower3], axis=1)], axis=0
+    )
+    far = jnp.concatenate([upper2, lower2], axis=0)
     other_mine = shift(mine, "c", 1)
     other_near = shift(near, "c", 1)
     other_far = shift(far, "c", 1)
@@ -215,7 +227,9 @@
             flops=2 * hid * tokens * width, bytes_accessed=9_000_000, transcendentals=0
         ),
     )(hidden_grad, ordered)
-    stage = scatter_sum(parts, True).astype(BF16)
+    arrived = [turn(parts[2], True, 2)]
+    arrived += [turn(parts[1], True, 1), turn(parts[3], True, 3)]
+    stage = add_up([parts[0]] + arrived).astype(BF16)
     depth = stage.shape[0] // RING
     stage = scatter_sum([stage[d * depth : (d + 1) * depth] for d in range(RING)], False).astype(BF16)
     depth = stage.shape[0] // RING

time: 257 us -> 252 us (0.981)
  the two profiles are of different devices: /device:TPU:15 before, /device:TPU:27 now
where the time goes in v3:
time: 252 us; the launch traced here: 251 us
  starting transfers between devices  156 us (62%)
  waiting for transfers between devices  41.7 us (17%)
  Pallas kernels  24.4 us (10%)
  blocking collectives  14.3 us (6%)
  other arithmetic  10.2 us (4%)
  local copies, waits for them, and re-layouts  2.62 us (1%)
    ppermute x19, starting transfers between devices, shift(): lax.ppermute(value, axis, [(i, (i + by) % size) for i in range(size)])  115 us
    ppermute x15, starting transfers between devices, turn(): lax.ppermute(value, ('y', 'x', 'c'), [(flat(*s), flat(*target(*s))) for s...  41.6 us
    ppermute x19, waiting for transfers between devices, shift(): lax.ppermute(value, axis, [(i, (i + by) % size) for i in range(size)])  30.6 us
    all_gather x1, blocking collectives, work(): block = lax.all_gather(normed.T, 'zl', axis=0, tiled=True)  14.3 us
    ppermute x15, waiting for transfers between devices, turn(): lax.ppermute(value, ('y', 'x', 'c'), [(flat(*s), flat(*target(*s))) for s...  11.1 us
    pallas_call x1, Pallas kernels, work(): pl.pallas_call(forward_kernel, in_specs=[scalars] + vmem(2 * RING + 3), o...  7.97 us
    pallas_call x1, Pallas kernels, work(): pl.pallas_call(input_grad_kernel, in_specs=vmem(2), out_specs=vmem(RING),...  5.08 us
  transfers between devices with their start and end apart: 34, of which 16 were waited for; matrix products, arithmetic and copies ran while one was open for 3% of the time, Pallas kernels for 5%

profile of v3, /device:TPU:27, one launch (start us, length us, event | category | flops | bytes accessed | tf_op | source)
XLA Modules:
  0.0 250.7 jit_solution(17644265469987197245)
XLA Ops:
  0.6 14.3 %all_gather.3 = bf16[384,512]{1,0:T(8,128)(2,1)S(1)} all-gather(bf16[96,512]{1,0:T(8,128)(2,1)} %bitcast.10), channel_id=1, replica_groups=mesh['y'=4,'x'=4,'zl'=4,'zh'=4,'c'=2] {'zl'}, dimensions={0}, use_global_device_ids=true | all-gather | bytes 491520 | tf_op jit(solution)/shard_map/all_gather | solution.py:156
  17.8 3.8 %collective-permute-start.2 = (bf16[384,512]{1,0:T(8,128)(2,1)S(1)}, bf16[384,512]{1,0:T(8,128)(2,1)S(1)}, u32[]{:S(2)}, u32[]{:S(2)}) collective-permute-start(bf16[384,512]{1,0:T(8,128)(2,1)S(1)} %all_gather.3), channel_id=1, source_target_pairs={{0,32},{1,129},{32,64},{33,161},{64,96},{65,193},{96,0},{97,225},{... | collective-permute-start | bytes 1179656 | tf_op jit(solution)/shard_map/ppermute | solution.py:122
  27.0 3.1 %collective-permute-start.6 = (bf16[768,512]{1,0:T(8,128)(2,1)S(1)}, bf16[768,512]{1,0:T(8,128)(2,1)S(1)}, u32[]{:S(2)}, u32[]{:S(2)}) collective-permute-start(bf16[768,512]{1,0:T(8,128)(2,1)S(1)} %constant_dynamic-update-slice_fusion.2.refs_1_), channel_id=1, source_target_pairs={{0,128},{1,33},{32,160},{33,65},{64,192},{65,97},{96,224},{97,1},{... | collective-permute-start | bytes 2359304 | tf_op jit(solution)/shard_map/ppermute | solution.py:122
  33.8 4.4 %collective-permute-start.4 = (bf16[768,512]{1,0:T(8,128)(2,1)S(1)}, bf16[768,512]{1,0:T(8,128)(2,1)}, u32[]{:S(2)}, u32[]{:S(2)}) collective-permute-start(bf16[768,512]{1,0:T(8,128)(2,1)S(1)} %constant_dynamic-update-slice_fusion.2.refs_1_), channel_id=1, source_target_pairs={{0,384},{1,97},{32,416},{33,1},{64,448},{65,33},{96,480},{97,65},{... | collective-permute-start | bytes 2359304 | tf_op jit(solution)/shard_map/ppermute | solution.py:122
  40.8 3.0 %collective-permute-start.7 = (bf16[768,512]{1,0:T(8,128)(2,1)S(1)}, bf16[768,512]{1,0:T(8,128)(2,1)}, u32[]{:S(2)}, u32[]{:S(2)}) collective-permute-start(bf16[768,512]{1,0:T(8,128)(2,1)S(1)} %collective-permute-done.6.refs_5_.refs_7_), channel_id=1, source_target_pairs={{0,128},{1,33},{32,160},{33,65},{64,192},{65,97},{96,224},{97,1},{... | collective-permute-start | bytes 2359304 | tf_op jit(solution)/shard_map/ppermute | solution.py:122
  47.8 3.4 %order.1.up_ref.refs_10_ = bf16[192,6144]{1,0:T(8,128)(2,1)} custom-call(s32[4]{0:T(128)} %pad_add_fusion.pos_ref, bf16[192,6144]{1,0:T(8,128)(2,1)} %up_ref.1), custom_call_target="tpu_custom_call" | custom-call | bytes 4718592 | tf_op jit(solution)/shard_map/order/pallas_call | solution.py:147
  52.9 4.8 %early.1.refs_8_ = f32[192,512]{1,0:T(8,128)} custom-call(bf16[192,6144]{1,0:T(8,128)(2,1)} %order.1.up_ref.refs_10_, bf16[768,512]{1,0:T(8,128)(2,1)} %copy-done, bf16[768,512]{1,0:T(8,128)(2,1)} %copy-done.1, bf16[768,512]{1,0:T(8,128)(2,1)} %copy-done.3, bf16[768,512]{1,0:T(8,128)(2,1)} %collective-permute-done.4.refs_3_, ...), custom_call_target="tpu_custom_call" | custom-call | flops 905969664 | bytes 7000000 | tf_op jit(solution)/shard_map/early/pallas_call | solution.py:163
  61.3 8.0 %forward.1 = (bf16[192,512]{1,0:T(8,128)(2,1)}, bf16[192,512]{1,0:T(8,128)(2,1)}, bf16[96,6144]{1,0:T(8,128)(2,1)}, bf16[96,6144]{1,0:T(8,128)(2,1)}) custom-call(s32[4]{0:T(128)} %pad_add_fusion.pos_ref, bf16[768,512]{1,0:T(8,128)(2,1)} %copy-done, bf16[768,512]{1,0:T(8,128)(2,1)} %copy-done.1, bf16[768,512]{1,0:T(8,128)(2,1)} %copy-done.3, ...), custom_call_target="tpu_custom_call" | custom-call | flops 1811939328 | bytes 14000000 | tf_op jit(solution)/shard_map/forward/pallas_call | solution.py:172
  69.3 9.2 %collective-permute-start.18 = (bf16[96,6144]{1,0:T(8,128)(2,1)}, bf16[96,6144]{1,0:T(8,128)(2,1)S(1)}, u32[]{:S(2)}, u32[]{:S(2)}) collective-permute-start(bf16[96,6144]{1,0:T(8,128)(2,1)} %get-tuple-element.18), channel_id=1, source_target_pairs={{0,1},{1,0},{2,3},{3,2},{4,5},{5,4},{6,7},{7,6},{8,9},{9,8},{10,11... | collective-permute-start | bytes 3538952 | tf_op jit(solution)/shard_map/ppermute | solution.py:28
  84.2 10.7 %collective-permute-start.23 = (bf16[48,1536]{1,0:T(8,128)(2,1)}, bf16[48,1536]{1,0:T(8,128)(2,1)}, u32[]{:S(2)}, u32[]{:S(2)}) collective-permute-start(bf16[48,1536]{1,0:T(8,128)(2,1)} %get-tuple-element.32), channel_id=1, source_target_pairs={{0,6},{2,0},{4,2},{6,4},{1,7},{3,1},{5,3},{7,5},{8,14},{10,8},{12,... | collective-permute-start | bytes 442376 | tf_op jit(solution)/shard_map/ppermute | solution.py:28
  94.9 5.1 %partial.1 = (bf16[1536,512]{1,0:T(8,128)(2,1)}, bf16[1536,512]{1,0:T(8,128)(2,1)}, bf16[1536,512]{1,0:T(8,128)(2,1)}, bf16[1536,512]{1,0:T(8,128)(2,1)}) custom-call(bf16[192,512]{1,0:T(8,128)(2,1)} %get-tuple-element.12.grad_ref, bf16[192,6144]{1,0:T(8,128)(2,1)} %order.1.up_ref.refs_10_), custom_call_target="tpu_custom_call" | custom-call | flops 1207959552 | bytes 9000000 | tf_op jit(solution)/shard_map/partial/pallas_call | solution.py:220
  100.0 3.0 %collective-permute-start.10 = (bf16[1536,512]{1,0:T(8,128)(2,1)}, bf16[1536,512]{1,0:T(8,128)(2,1)S(1)}, u32[]{:S(2)}, u32[]{:S(2)}) collective-permute-start(bf16[1536,512]{1,0:T(8,128)(2,1)} %get-tuple-element.15), channel_id=1, source_target_pairs={{0,128},{1,33},{32,160},{33,65},{64,192},{65,97},{96,224},{97,1},{... | collective-permute-start | bytes 4718600 | tf_op jit(solution)/shard_map/ppermute | solution.py:122
  110.7 6.9 %collective-permute-start.21 = (bf16[48,1536]{1,0:T(8,128)(2,1)S(1)}, bf16[48,1536]{1,0:T(8,128)(2,1)}, u32[]{:S(2)}, u32[]{:S(2)}) collective-permute-start(bf16[48,1536]{1,0:T(8,128)(2,1)S(1)} %slice.91), channel_id=1, source_target_pairs={{0,6},{2,0},{4,2},{6,4},{1,7},{3,1},{5,3},{7,5},{8,14},{10,8},{12,... | collective-permute-start | bytes 442376 | tf_op jit(solution)/shard_map/ppermute | solution.py:28
  123.2 6.8 %collective-permute-done.21 = bf16[48,1536]{1,0:T(8,128)(2,1)} collective-permute-done((bf16[48,1536]{1,0:T(8,128)(2,1)S(1)}, bf16[48,1536]{1,0:T(8,128)(2,1)}, u32[]{:S(2)}, u32[]{:S(2)}) %collective-permute-start.21) | collective-permute-done | bytes 147488 | tf_op jit(solution)/shard_map/ppermute | solution.py:28
  130.0 6.6 %collective-permute-start.24 = (bf16[48,1536]{1,0:T(8,128)(2,1)}, bf16[48,1536]{1,0:T(8,128)(2,1)S(1)}, u32[]{:S(2)}, u32[]{:S(2)}) collective-permute-start(bf16[48,1536]{1,0:T(8,128)(2,1)} %add_convert_fusion.6), channel_id=1, source_target_pairs={{0,6},{2,0},{4,2},{6,4},{1,7},{3,1},{5,3},{7,5},{8,14},{10,8},{12,... | collective-permute-start | bytes 442376 | tf_op jit(solution)/shard_map/ppermute | solution.py:28
  136.6 3.2 %collective-permute-start.20 = (bf16[48,1536]{1,0:T(8,128)(2,1)}, bf16[48,1536]{1,0:T(8,128)(2,1)S(1)}, u32[]{:S(2)}, u32[]{:S(2)}) collective-permute-start(bf16[48,1536]{1,0:T(8,128)(2,1)} %add_convert_fusion.7), channel_id=1, source_target_pairs={{0,2},{2,4},{4,6},{6,0},{1,3},{3,5},{5,7},{7,1},{8,10},{10,12},{12... | collective-permute-start | bytes 442376 | tf_op jit(solution)/shard_map/ppermute | solution.py:28
  139.9 4.9 %collective-permute-done.24 = bf16[48,1536]{1,0:T(8,128)(2,1)S(1)} collective-permute-done((bf16[48,1536]{1,0:T(8,128)(2,1)}, bf16[48,1536]{1,0:T(8,128)(2,1)S(1)}, u32[]{:S(2)}, u32[]{:S(2)}) %collective-permute-start.24) | collective-permute-done | bytes 147488 | tf_op jit(solution)/shard_map/ppermute | solution.py:28
  148.0 5.2 %collective-permute-start.25 = (bf16[48,1536]{1,0:T(8,128)(2,1)S(1)}, bf16[48,1536]{1,0:T(8,128)(2,1)S(1)}, u32[]{:S(2)}, u32[]{:S(2)}) collective-permute-start(bf16[48,1536]{1,0:T(8,128)(2,1)S(1)} %get-tuple-element.29), channel_id=1, source_target_pairs={{0,6},{2,0},{4,2},{6,4},{1,7},{3,1},{5,3},{7,5},{8,14},{10,8},{12,... | collective-permute-start | bytes 442376 | tf_op jit(solution)/shard_map/ppermute | solution.py:28
  153.2 4.0 %collective-permute-start.28 = (bf16[48,1536]{1,0:T(8,128)(2,1)S(1)}, bf16[48,1536]{1,0:T(8,128)(2,1)S(1)}, u32[]{:S(2)}, u32[]{:S(2)}) collective-permute-start(bf16[48,1536]{1,0:T(8,128)(2,1)S(1)} %get-tuple-element.30), channel_id=1, source_target_pairs={{0,2},{2,4},{4,6},{6,0},{1,3},{3,5},{5,7},{7,1},{8,10},{10,12},{12... | collective-permute-start | bytes 442376 | tf_op jit(solution)/shard_map/ppermute | solution.py:28
  157.3 4.7 %collective-permute-start.26 = (bf16[48,1536]{1,0:T(8,128)(2,1)S(1)}, bf16[48,1536]{1,0:T(8,128)(2,1)S(1)}, u32[]{:S(2)}, u32[]{:S(2)}) collective-permute-start(bf16[48,1536]{1,0:T(8,128)(2,1)S(1)} %get-tuple-element.29), channel_id=1, source_target_pairs={{0,2},{2,4},{4,6},{6,0},{1,3},{3,5},{5,7},{7,1},{8,10},{10,12},{12... | collective-permute-start | bytes 442376 | tf_op jit(solution)/shard_map/ppermute | solution.py:28
  162.0 4.5 %collective-permute-start.27 = (bf16[48,1536]{1,0:T(8,128)(2,1)S(1)}, bf16[48,1536]{1,0:T(8,128)(2,1)S(1)}, u32[]{:S(2)}, u32[]{:S(2)}) collective-permute-start(bf16[48,1536]{1,0:T(8,128)(2,1)S(1)} %get-tuple-element.30), channel_id=1, source_target_pairs={{0,6},{2,0},{4,2},{6,4},{1,7},{3,1},{5,3},{7,5},{8,14},{10,8},{12,... | collective-permute-start | bytes 442376 | tf_op jit(solution)/shard_map/ppermute | solution.py:28
  166.5 16.3 %collective-permute-start.31 = (bf16[96,1536]{1,0:T(8,128)(2,1)S(1)}, bf16[96,1536]{1,0:T(8,128)(2,1)}, u32[]{:S(2)}, u32[]{:S(2)}) collective-permute-start(bf16[96,1536]{1,0:T(8,128)(2,1)S(1)} %pad_maximum_fusion.refs_0_), channel_id=1, source_target_pairs={{0,1},{1,0},{2,3},{3,2},{4,5},{5,4},{6,7},{7,6},{8,9},{9,8},{10,11... | collective-permute-start | bytes 884744 | tf_op jit(solution)/shard_map/ppermute | solution.py:28
  189.7 3.2 %collective-permute-start.14 = (bf16[384,512]{1,0:T(8,128)(2,1)S(1)}, bf16[384,512]{1,0:T(8,128)(2,1)S(1)}, u32[]{:S(2)}, u32[]{:S(2)}) collective-permute-start(bf16[384,512]{1,0:T(8,128)(2,1)S(1)} %get-tuple-element.24), channel_id=1, source_target_pairs={{0,96},{1,385},{32,0},{33,417},{64,32},{65,449},{96,64},{97,481},{... | collective-permute-start | bytes 1179656 | tf_op jit(solution)/shard_map/ppermute | solution.py:122
  193.0 6.7 %collective-permute-start.29 = (bf16[48,1536]{1,0:T(8,128)(2,1)S(1)}, bf16[48,1536]{1,0:T(8,128)(2,1)S(1)}, u32[]{:S(2)}, u32[]{:S(2)}) collective-permute-start(bf16[48,1536]{1,0:T(8,128)(2,1)S(1)} %collective-permute-done.25), channel_id=1, source_target_pairs={{0,6},{2,0},{4,2},{6,4},{1,7},{3,1},{5,3},{7,5},{8,14},{10,8},{12,... | collective-permute-start | bytes 442376 | tf_op jit(solution)/shard_map/ppermute | solution.py:28
  199.7 6.3 %collective-permute-done.29 = bf16[48,1536]{1,0:T(8,128)(2,1)S(1)} collective-permute-done((bf16[48,1536]{1,0:T(8,128)(2,1)S(1)}, bf16[48,1536]{1,0:T(8,128)(2,1)S(1)}, u32[]{:S(2)}, u32[]{:S(2)}) %collective-permute-start.29) | collective-permute-done | bytes 147488 | tf_op jit(solution)/shard_map/ppermute | solution.py:28
  206.1 4.8 %collective-permute-start.32 = (bf16[96,3072]{1,0:T(8,128)(2,1)S(1)}, bf16[96,3072]{1,0:T(8,128)(2,1)S(1)}, u32[]{:S(2)}, u32[]{:S(2)}) collective-permute-start(bf16[96,3072]{1,0:T(8,128)(2,1)S(1)} %maximum_maximum_fusion.refs_1_), channel_id=1, source_target_pairs={{0,1},{1,0},{2,3},{3,2},{4,5},{5,4},{6,7},{7,6},{8,9},{9,8},{10,11... | collective-permute-start | bytes 1769480 | tf_op jit(solution)/shard_map/ppermute | solution.py:28
  210.9 8.7 %collective-permute-start.30 = (bf16[48,1536]{1,0:T(8,128)(2,1)S(1)}, bf16[48,1536]{1,0:T(8,128)(2,1)S(1)}, u32[]{:S(2)}, u32[]{:S(2)}) collective-permute-start(bf16[48,1536]{1,0:T(8,128)(2,1)S(1)} %collective-permute-done.28), channel_id=1, source_target_pairs={{0,2},{2,4},{4,6},{6,0},{1,3},{3,5},{5,7},{7,1},{8,10},{10,12},{12... | collective-permute-start | bytes 442376 | tf_op jit(solution)/shard_map/ppermute | solution.py:28
  221.8 5.7 %collective-permute-start.16 = (bf16[96,512]{1,0:T(8,128)(2,1)S(1)}, bf16[96,512]{1,0:T(8,128)(2,1)S(1)}, u32[]{:S(2)}, u32[]{:S(2)}) collective-permute-start(bf16[96,512]{1,0:T(8,128)(2,1)S(1)} %get-tuple-element.28), channel_id=1, source_target_pairs={{0,16},{8,24},{16,0},{24,8},{1,17},{9,25},{17,1},{25,9},{2,18},{10... | collective-permute-start | bytes 294920 | tf_op jit(solution)/shard_map/ppermute | solution.py:28
  227.5 6.1 %collective-permute-done.30 = bf16[48,1536]{1,0:T(8,128)(2,1)S(1)} collective-permute-done((bf16[48,1536]{1,0:T(8,128)(2,1)S(1)}, bf16[48,1536]{1,0:T(8,128)(2,1)S(1)}, u32[]{:S(2)}, u32[]{:S(2)}) %collective-permute-start.30) | collective-permute-done | bytes 147488 | tf_op jit(solution)/shard_map/ppermute | solution.py:28
  233.6 7.8 %collective-permute-start.17 = (bf16[96,512]{1,0:T(8,128)(2,1)S(1)}, bf16[96,512]{1,0:T(8,128)(2,1)S(1)}, u32[]{:S(2)}, u32[]{:S(2)}) collective-permute-start(bf16[96,512]{1,0:T(8,128)(2,1)S(1)} %get-tuple-element.27), channel_id=1, source_target_pairs={{0,24},{8,0},{16,8},{24,16},{1,25},{9,1},{17,9},{25,17},{2,26},{10... | collective-permute-start | bytes 294920 | tf_op jit(solution)/shard_map/ppermute | solution.py:28
  241.4 3.3 %collective-permute-start.33 = (bf16[96,1536]{1,0:T(8,128)(2,1)S(1)}, bf16[96,1536]{1,0:T(8,128)(2,1)S(1)}, u32[]{:S(2)}, u32[]{:S(2)}) collective-permute-start(bf16[96,1536]{1,0:T(8,128)(2,1)S(1)} %constant_dynamic-update-slice_fusion.4.refs_2_), channel_id=1, source_target_pairs={{0,1},{1,0},{2,3},{3,2},{4,5},{5,4},{6,7},{7,6},{8,9},{9,8},{10,11... | collective-permute-start | bytes 884744 | tf_op jit(solution)/shard_map/ppermute | solution.py:28
  247.5 3.2 %place.1 = bf16[192,6144]{1,0:T(8,128)(2,1)} custom-call(s32[4]{0:T(128)} %pad_add_fusion.pos_ref, bf16[96,1536]{1,0:T(8,128)(2,1)} %copy-done.7, bf16[96,3072]{1,0:T(8,128)(2,1)} %copy-done.4, bf16[96,1536]{1,0:T(8,128)(2,1)} %copy-done.8, bf16[96,1536]{1,0:T(8,128)(2,1)} %collective-permute-done.31.refs_3_, bf16[96,3072]{1,0:T(8,128)(2,1)} %copy-done.9, ...), custom_call_target="tpu_custom_call" | custom-call | bytes 4718592 | tf_op jit(solution)/shard_map/place/pallas_call | solution.py:211
  (85 shorter events, 57.7 us)
Async XLA Ops:
  14.9 10.0 %collective-permute-start.1 = (bf16[384,512]{1,0:T(8,128)(2,1)S(1)}, bf16[384,512]{1,0:T(8,128)(2,1)S(1)}, u32[]{:S(2)}, u32[]{:S(2)}) collective-permute-start(bf16[384,512]{1,0:T(8,128)(2,1)S(1)} %all_gather.3), channel_id=1, source_target_pairs={{0,64},{1,257},{32,96},{33,289},{64,0},{65,321},{96,32},{97,353},{... | collective-permute-start | bytes 1179656 | tf_op jit(solution)/shard_map/ppermute | solution.py:122
  21.6 9.7 %collective-permute-start = (bf16[384,512]{1,0:T(8,128)(2,1)S(1)}, bf16[384,512]{1,0:T(8,128)(2,1)S(1)}, u32[]{:S(2)}, u32[]{:S(2)}) collective-permute-start(bf16[384,512]{1,0:T(8,128)(2,1)S(1)} %all_gather.3), channel_id=1, source_target_pairs={{0,96},{1,385},{32,0},{33,417},{64,32},{65,449},{96,64},{97,481},{... | collective-permute-start | bytes 1179656 | tf_op jit(solution)/shard_map/ppermute | solution.py:122
  27.0 13.8 %collective-permute-start.6 = (bf16[768,512]{1,0:T(8,128)(2,1)S(1)}, bf16[768,512]{1,0:T(8,128)(2,1)S(1)}, u32[]{:S(2)}, u32[]{:S(2)}) collective-permute-start(bf16[768,512]{1,0:T(8,128)(2,1)S(1)} %constant_dynamic-update-slice_fusion.2.refs_1_), channel_id=1, source_target_pairs={{0,128},{1,33},{32,160},{33,65},{64,192},{65,97},{96,224},{97,1},{... | collective-permute-start | bytes 2359304 | tf_op jit(solution)/shard_map/ppermute | solution.py:122
  31.4 13.0 %collective-permute-start.3 = (bf16[768,512]{1,0:T(8,128)(2,1)S(1)}, bf16[768,512]{1,0:T(8,128)(2,1)S(1)}, u32[]{:S(2)}, u32[]{:S(2)}) collective-permute-start(bf16[768,512]{1,0:T(8,128)(2,1)S(1)} %constant_dynamic-update-slice_fusion.refs_0_), channel_id=1, source_target_pairs={{0,384},{1,97},{32,416},{33,1},{64,448},{65,33},{96,480},{97,65},{... | collective-permute-start | bytes 2359304 | tf_op jit(solution)/shard_map/ppermute | solution.py:122
  33.8 19.1 %collective-permute-start.4 = (bf16[768,512]{1,0:T(8,128)(2,1)S(1)}, bf16[768,512]{1,0:T(8,128)(2,1)}, u32[]{:S(2)}, u32[]{:S(2)}) collective-permute-start(bf16[768,512]{1,0:T(8,128)(2,1)S(1)} %constant_dynamic-update-slice_fusion.2.refs_1_), channel_id=1, source_target_pairs={{0,384},{1,97},{32,416},{33,1},{64,448},{65,33},{96,480},{97,65},{... | collective-permute-start | bytes 2359304 | tf_op jit(solution)/shard_map/ppermute | solution.py:122
  38.2 14.7 %collective-permute-start.8 = (bf16[768,512]{1,0:T(8,128)(2,1)S(1)}, bf16[768,512]{1,0:T(8,128)(2,1)}, u32[]{:S(2)}, u32[]{:S(2)}) collective-permute-start(bf16[768,512]{1,0:T(8,128)(2,1)S(1)} %constant_dynamic-update-slice_fusion.refs_0_), channel_id=1, source_target_pairs={{0,128},{1,33},{32,160},{33,65},{64,192},{65,97},{96,224},{97,1},{... | collective-permute-start | bytes 2359304 | tf_op jit(solution)/shard_map/ppermute | solution.py:122
  40.8 19.0 %collective-permute-start.7 = (bf16[768,512]{1,0:T(8,128)(2,1)S(1)}, bf16[768,512]{1,0:T(8,128)(2,1)}, u32[]{:S(2)}, u32[]{:S(2)}) collective-permute-start(bf16[768,512]{1,0:T(8,128)(2,1)S(1)} %collective-permute-done.6.refs_5_.refs_7_), channel_id=1, source_target_pairs={{0,128},{1,33},{32,160},{33,65},{64,192},{65,97},{96,224},{97,1},{... | collective-permute-start | bytes 2359304 | tf_op jit(solution)/shard_map/ppermute | solution.py:122
  44.4 17.0 %collective-permute-start.5 = (bf16[768,512]{1,0:T(8,128)(2,1)S(1)}, bf16[768,512]{1,0:T(8,128)(2,1)}, u32[]{:S(2)}, u32[]{:S(2)}) collective-permute-start(bf16[768,512]{1,0:T(8,128)(2,1)S(1)} %collective-permute-done.3.refs_2_), channel_id=1, source_target_pairs={{0,384},{1,97},{32,416},{33,1},{64,448},{65,33},{96,480},{97,65},{... | collective-permute-start | bytes 2359304 | tf_op jit(solution)/shard_map/ppermute | solution.py:122
  69.3 11.9 %collective-permute-start.18 = (bf16[96,6144]{1,0:T(8,128)(2,1)}, bf16[96,6144]{1,0:T(8,128)(2,1)S(1)}, u32[]{:S(2)}, u32[]{:S(2)}) collective-permute-start(bf16[96,6144]{1,0:T(8,128)(2,1)} %get-tuple-element.18), channel_id=1, source_target_pairs={{0,1},{1,0},{2,3},{3,2},{4,5},{5,4},{6,7},{7,6},{8,9},{9,8},{10,11... | collective-permute-start | bytes 3538952 | tf_op jit(solution)/shard_map/ppermute | solution.py:28
  84.2 26.5 %collective-permute-start.23 = (bf16[48,1536]{1,0:T(8,128)(2,1)}, bf16[48,1536]{1,0:T(8,128)(2,1)}, u32[]{:S(2)}, u32[]{:S(2)}) collective-permute-start(bf16[48,1536]{1,0:T(8,128)(2,1)} %get-tuple-element.32), channel_id=1, source_target_pairs={{0,6},{2,0},{4,2},{6,4},{1,7},{3,1},{5,3},{7,5},{8,14},{10,8},{12,... | collective-permute-start | bytes 442376 | tf_op jit(solution)/shard_map/ppermute | solution.py:28
  100.0 57.3 %collective-permute-start.10 = (bf16[1536,512]{1,0:T(8,128)(2,1)}, bf16[1536,512]{1,0:T(8,128)(2,1)S(1)}, u32[]{:S(2)}, u32[]{:S(2)}) collective-permute-start(bf16[1536,512]{1,0:T(8,128)(2,1)} %get-tuple-element.15), channel_id=1, source_target_pairs={{0,128},{1,33},{32,160},{33,65},{64,192},{65,97},{96,224},{97,1},{... | collective-permute-start | bytes 4718600 | tf_op jit(solution)/shard_map/ppermute | solution.py:122
  103.0 59.0 %collective-permute-start.11 = (bf16[1536,512]{1,0:T(8,128)(2,1)}, bf16[1536,512]{1,0:T(8,128)(2,1)}, u32[]{:S(2)}, u32[]{:S(2)}) collective-permute-start(bf16[1536,512]{1,0:T(8,128)(2,1)} %get-tuple-element.16), channel_id=1, source_target_pairs={{0,384},{1,97},{32,416},{33,1},{64,448},{65,33},{96,480},{97,65},{... | collective-permute-start | bytes 4718600 | tf_op jit(solution)/shard_map/ppermute | solution.py:122
  105.3 61.2 %collective-permute-start.9 = (bf16[1536,512]{1,0:T(8,128)(2,1)}, bf16[1536,512]{1,0:T(8,128)(2,1)}, u32[]{:S(2)}, u32[]{:S(2)}) collective-permute-start(bf16[1536,512]{1,0:T(8,128)(2,1)} %get-tuple-element.14), channel_id=1, source_target_pairs={{0,256},{1,65},{32,288},{33,97},{64,320},{65,1},{96,352},{97,33},{... | collective-permute-start | bytes 4718600 | tf_op jit(solution)/shard_map/ppermute | solution.py:122
  108.2 12.4 %collective-permute-start.19 = (bf16[48,1536]{1,0:T(8,128)(2,1)}, bf16[48,1536]{1,0:T(8,128)(2,1)S(1)}, u32[]{:S(2)}, u32[]{:S(2)}) collective-permute-start(bf16[48,1536]{1,0:T(8,128)(2,1)} %get-tuple-element.31), channel_id=1, source_target_pairs={{0,2},{2,4},{4,6},{6,0},{1,3},{3,5},{5,7},{7,1},{8,10},{10,12},{12... | collective-permute-start | bytes 442376 | tf_op jit(solution)/shard_map/ppermute | solution.py:28
  110.7 19.3 %collective-permute-start.21 = (bf16[48,1536]{1,0:T(8,128)(2,1)S(1)}, bf16[48,1536]{1,0:T(8,128)(2,1)}, u32[]{:S(2)}, u32[]{:S(2)}) collective-permute-start(bf16[48,1536]{1,0:T(8,128)(2,1)S(1)} %slice.91), channel_id=1, source_target_pairs={{0,6},{2,0},{4,2},{6,4},{1,7},{3,1},{5,3},{7,5},{8,14},{10,8},{12,... | collective-permute-start | bytes 442376 | tf_op jit(solution)/shard_map/ppermute | solution.py:28
  120.6 16.0 %collective-permute-start.22 = (bf16[48,1536]{1,0:T(8,128)(2,1)S(1)}, bf16[48,1536]{1,0:T(8,128)(2,1)}, u32[]{:S(2)}, u32[]{:S(2)}) collective-permute-start(bf16[48,1536]{1,0:T(8,128)(2,1)S(1)} %slice.93), channel_id=1, source_target_pairs={{0,2},{2,4},{4,6},{6,0},{1,3},{3,5},{5,7},{7,1},{8,10},{10,12},{12... | collective-permute-start | bytes 442376 | tf_op jit(solution)/shard_map/ppermute | solution.py:28
  130.0 14.8 %collective-permute-start.24 = (bf16[48,1536]{1,0:T(8,128)(2,1)}, bf16[48,1536]{1,0:T(8,128)(2,1)S(1)}, u32[]{:S(2)}, u32[]{:S(2)}) collective-permute-start(bf16[48,1536]{1,0:T(8,128)(2,1)} %add_convert_fusion.6), channel_id=1, source_target_pairs={{0,6},{2,0},{4,2},{6,4},{1,7},{3,1},{5,3},{7,5},{8,14},{10,8},{12,... | collective-permute-start | bytes 442376 | tf_op jit(solution)/shard_map/ppermute | solution.py:28
  136.6 10.1 %collective-permute-start.20 = (bf16[48,1536]{1,0:T(8,128)(2,1)}, bf16[48,1536]{1,0:T(8,128)(2,1)S(1)}, u32[]{:S(2)}, u32[]{:S(2)}) collective-permute-start(bf16[48,1536]{1,0:T(8,128)(2,1)} %add_convert_fusion.7), channel_id=1, source_target_pairs={{0,2},{2,4},{4,6},{6,0},{1,3},{3,5},{5,7},{7,1},{8,10},{10,12},{12... | collective-permute-start | bytes 442376 | tf_op jit(solution)/shard_map/ppermute | solution.py:28
  148.0 37.7 %collective-permute-start.25 = (bf16[48,1536]{1,0:T(8,128)(2,1)S(1)}, bf16[48,1536]{1,0:T(8,128)(2,1)S(1)}, u32[]{:S(2)}, u32[]{:S(2)}) collective-permute-start(bf16[48,1536]{1,0:T(8,128)(2,1)S(1)} %get-tuple-element.29), channel_id=1, source_target_pairs={{0,6},{2,0},{4,2},{6,4},{1,7},{3,1},{5,3},{7,5},{8,14},{10,8},{12,... | collective-permute-start | bytes 442376 | tf_op jit(solution)/shard_map/ppermute | solution.py:28
  153.2 34.4 %collective-permute-start.28 = (bf16[48,1536]{1,0:T(8,128)(2,1)S(1)}, bf16[48,1536]{1,0:T(8,128)(2,1)S(1)}, u32[]{:S(2)}, u32[]{:S(2)}) collective-permute-start(bf16[48,1536]{1,0:T(8,128)(2,1)S(1)} %get-tuple-element.30), channel_id=1, source_target_pairs={{0,2},{2,4},{4,6},{6,0},{1,3},{3,5},{5,7},{7,1},{8,10},{10,12},{12... | collective-permute-start | bytes 442376 | tf_op jit(solution)/shard_map/ppermute | solution.py:28
  157.3 32.5 %collective-permute-start.26 = (bf16[48,1536]{1,0:T(8,128)(2,1)S(1)}, bf16[48,1536]{1,0:T(8,128)(2,1)S(1)}, u32[]{:S(2)}, u32[]{:S(2)}) collective-permute-start(bf16[48,1536]{1,0:T(8,128)(2,1)S(1)} %get-tuple-element.29), channel_id=1, source_target_pairs={{0,2},{2,4},{4,6},{6,0},{1,3},{3,5},{5,7},{7,1},{8,10},{10,12},{12... | collective-permute-start | bytes 442376 | tf_op jit(solution)/shard_map/ppermute | solution.py:28
  162.0 31.0 %collective-permute-start.27 = (bf16[48,1536]{1,0:T(8,128)(2,1)S(1)}, bf16[48,1536]{1,0:T(8,128)(2,1)S(1)}, u32[]{:S(2)}, u32[]{:S(2)}) collective-permute-start(bf16[48,1536]{1,0:T(8,128)(2,1)S(1)} %get-tuple-element.30), channel_id=1, source_target_pairs={{0,6},{2,0},{4,2},{6,4},{1,7},{3,1},{5,3},{7,5},{8,14},{10,8},{12,... | collective-permute-start | bytes 442376 | tf_op jit(solution)/shard_map/ppermute | solution.py:28
  166.5 79.0 %collective-permute-start.31 = (bf16[96,1536]{1,0:T(8,128)(2,1)S(1)}, bf16[96,1536]{1,0:T(8,128)(2,1)}, u32[]{:S(2)}, u32[]{:S(2)}) collective-permute-start(bf16[96,1536]{1,0:T(8,128)(2,1)S(1)} %pad_maximum_fusion.refs_0_), channel_id=1, source_target_pairs={{0,1},{1,0},{2,3},{3,2},{4,5},{5,4},{6,7},{7,6},{8,9},{9,8},{10,11... | collective-permute-start | bytes 884744 | tf_op jit(solution)/shard_map/ppermute | solution.py:28
  185.7 25.2 %collective-permute-start.12 = (bf16[384,512]{1,0:T(8,128)(2,1)S(1)}, bf16[384,512]{1,0:T(8,128)(2,1)S(1)}, u32[]{:S(2)}, u32[]{:S(2)}) collective-permute-start(bf16[384,512]{1,0:T(8,128)(2,1)S(1)} %get-tuple-element.23), channel_id=1, source_target_pairs={{0,32},{1,129},{32,64},{33,161},{64,96},{65,193},{96,0},{97,225},{... | collective-permute-start | bytes 1179656 | tf_op jit(solution)/shard_map/ppermute | solution.py:122
  187.6 32.0 %collective-permute-start.13 = (bf16[384,512]{1,0:T(8,128)(2,1)S(1)}, bf16[384,512]{1,0:T(8,128)(2,1)S(1)}, u32[]{:S(2)}, u32[]{:S(2)}) collective-permute-start(bf16[384,512]{1,0:T(8,128)(2,1)S(1)} %get-tuple-element.25), channel_id=1, source_target_pairs={{0,64},{1,257},{32,96},{33,289},{64,0},{65,321},{96,32},{97,353},{... | collective-permute-start | bytes 1179656 | tf_op jit(solution)/shard_map/ppermute | solution.py:122
  189.7 29.9 %collective-permute-start.14 = (bf16[384,512]{1,0:T(8,128)(2,1)S(1)}, bf16[384,512]{1,0:T(8,128)(2,1)S(1)}, u32[]{:S(2)}, u32[]{:S(2)}) collective-permute-start(bf16[384,512]{1,0:T(8,128)(2,1)S(1)} %get-tuple-element.24), channel_id=1, source_target_pairs={{0,96},{1,385},{32,0},{33,417},{64,32},{65,449},{96,64},{97,481},{... | collective-permute-start | bytes 1179656 | tf_op jit(solution)/shard_map/ppermute | solution.py:122
  193.0 13.1 %collective-permute-start.29 = (bf16[48,1536]{1,0:T(8,128)(2,1)S(1)}, bf16[48,1536]{1,0:T(8,128)(2,1)S(1)}, u32[]{:S(2)}, u32[]{:S(2)}) collective-permute-start(bf16[48,1536]{1,0:T(8,128)(2,1)S(1)} %collective-permute-done.25), channel_id=1, source_target_pairs={{0,6},{2,0},{4,2},{6,4},{1,7},{3,1},{5,3},{7,5},{8,14},{10,8},{12,... | collective-permute-start | bytes 442376 | tf_op jit(solution)/shard_map/ppermute | solution.py:28
  206.1 39.9 %collective-permute-start.32 = (bf16[96,3072]{1,0:T(8,128)(2,1)S(1)}, bf16[96,3072]{1,0:T(8,128)(2,1)S(1)}, u32[]{:S(2)}, u32[]{:S(2)}) collective-permute-start(bf16[96,3072]{1,0:T(8,128)(2,1)S(1)} %maximum_maximum_fusion.refs_1_), channel_id=1, source_target_pairs={{0,1},{1,0},{2,3},{3,2},{4,5},{5,4},{6,7},{7,6},{8,9},{9,8},{10,11... | collective-permute-start | bytes 1769480 | tf_op jit(solution)/shard_map/ppermute | solution.py:28
  210.9 22.7 %collective-permute-start.30 = (bf16[48,1536]{1,0:T(8,128)(2,1)S(1)}, bf16[48,1536]{1,0:T(8,128)(2,1)S(1)}, u32[]{:S(2)}, u32[]{:S(2)}) collective-permute-start(bf16[48,1536]{1,0:T(8,128)(2,1)S(1)} %collective-permute-done.28), channel_id=1, source_target_pairs={{0,2},{2,4},{4,6},{6,0},{1,3},{3,5},{5,7},{7,1},{8,10},{10,12},{12... | collective-permute-start | bytes 442376 | tf_op jit(solution)/shard_map/ppermute | solution.py:28
  219.9 21.6 %collective-permute-start.15 = (bf16[96,512]{1,0:T(8,128)(2,1)S(1)}, bf16[96,512]{1,0:T(8,128)(2,1)S(1)}, u32[]{:S(2)}, u32[]{:S(2)}) collective-permute-start(bf16[96,512]{1,0:T(8,128)(2,1)S(1)} %get-tuple-element.26), channel_id=1, source_target_pairs={{0,8},{8,16},{16,24},{24,0},{1,9},{9,17},{17,25},{25,1},{2,10},{10... | collective-permute-start | bytes 294920 | tf_op jit(solution)/shard_map/ppermute | solution.py:28
  221.8 23.0 %collective-permute-start.16 = (bf16[96,512]{1,0:T(8,128)(2,1)S(1)}, bf16[96,512]{1,0:T(8,128)(2,1)S(1)}, u32[]{:S(2)}, u32[]{:S(2)}) collective-permute-start(bf16[96,512]{1,0:T(8,128)(2,1)S(1)} %get-tuple-element.28), channel_id=1, source_target_pairs={{0,16},{8,24},{16,0},{24,8},{1,17},{9,25},{17,1},{25,9},{2,18},{10... | collective-permute-start | bytes 294920 | tf_op jit(solution)/shard_map/ppermute | solution.py:28
  233.6 11.2 %collective-permute-start.17 = (bf16[96,512]{1,0:T(8,128)(2,1)S(1)}, bf16[96,512]{1,0:T(8,128)(2,1)S(1)}, u32[]{:S(2)}, u32[]{:S(2)}) collective-permute-start(bf16[96,512]{1,0:T(8,128)(2,1)S(1)} %get-tuple-element.27), channel_id=1, source_target_pairs={{0,24},{8,0},{16,8},{24,16},{1,25},{9,1},{17,9},{25,17},{2,26},{10... | collective-permute-start | bytes 294920 | tf_op jit(solution)/shard_map/ppermute | solution.py:28
  (13 other events, 250.4 us)

commit v4 on v2

--- a/solution.py
+++ b/solution.py
@@ -32,12 +32,15 @@
     return lax.dot_general(left, right, (dims, ((), ())), preferred_element_type=F32)
 
 
-def column_of(pos_ref, outer, inner, width):
+def spot_of(pos_ref, outer, inner):
     core = pos_ref[2]
     dy = outer + core * (inner - outer)
     dx = inner + core * (outer - inner)
-    y = lax.rem(pos_ref[0] + dy, RING)
-    x = lax.rem(pos_ref[1] + dx, RING)
+    return lax.rem(pos_ref[0] + dy, RING), lax.rem(pos_ref[1] + dx, RING)
+
+
+def column_of(pos_ref, outer, inner, width):
+    y, x = spot_of(pos_ref, outer, inner)
     return pl.multiple_of((y * RING + x) * width, 128)
 
 
@@ -62,10 +65,10 @@
 
 def forward_kernel(pos_ref, *refs):
     pieces = refs[0 : 2 * RING]
-    early_ref, cot_ref, up_ref, hidden_ref, grad_ref, keep_ref, send_ref, packed_ref = refs[2 * RING :]
+    early_ref, cot_ref, up_ref, hidden_ref, grad_ref, keep_ref, send_ref, packed_ref, term_ref = refs[2 * RING :]
     depth = pieces[0].shape[0]
     width = depth // 2
-    rows = keep_ref.shape[0]
+    rows = keep_ref.shape[1]
     total = early_ref[...]
     for place in (4, 5):
         total += dot(up_ref[:, pl.ds(place * depth, depth)], pieces[place][...], ((1,), (0,)))
@@ -73,17 +76,23 @@
     hidden_ref[...] = gelu_out.astype(BF16)
     grad_ref[...] = (cot_ref[...].astype(F32) * gelu_slope).astype(BF16)
     core, zh = pos_ref[2], pos_ref[3]
-    for at, half in enumerate((1 - core, core)):
+    for at, half in enumerate((core, 1 - core)):
         packed_ref[pl.ds(at * rows, rows), :] = grad_ref[pl.ds(pl.multiple_of(half * rows, 16), rows), :]
     grads = packed_ref[...]
     for place, piece in enumerate(pieces):
         term = dot(grads, piece[...], ((1,), (1,))).astype(BF16)
         for part in range(2):
             block = 2 * place + part
-            column = column_of(pos_ref, block // RING, block % RING, width) + (RING - zh) * 2 * depth
-            column = pl.multiple_of(lax.rem(column, 2 * RING * depth), 128)
-            send_ref[:, pl.ds(column, width)] = term[:rows, part * width : (part + 1) * width]
-            keep_ref[:, pl.ds(column, width)] = term[rows:, part * width : (part + 1) * width]
+            y, x = spot_of(pos_ref, block // RING, block % RING)
+            quarter = lax.rem(y + RING - zh, RING)
+            where = pl.ds(pl.multiple_of(x * width, 128), width)
+            for at in range(2):
+                term_ref[at, quarter, :, where] = term[at * rows : (at + 1) * rows, part * width : (part + 1) * width]
+    near, away = 1 + 2 * core, 3 - 2 * core
+    for at, (half, quarter) in enumerate(((0, 2), (1, near), (0, near), (0, 0), (1, 0))):
+        keep_ref[at] = term_ref[half, quarter]
+    for at, (half, quarter) in enumerate(((1, 2), (0, away), (1, away), (1, 0), (0, 0))):
+        send_ref[at] = term_ref[half, quarter]
 
 
 def input_grad_kernel(grad_ref, up_ref, *outs):
@@ -94,15 +103,23 @@
         outs[d][...] = term.astype(BF16)
 
 
-def place_kernel(pos_ref, *refs):
+def place_kernel(pos_ref, mine_ref, next_ref, far_ref, other_next_ref, other_far_ref, out_ref):
     core, zh = pos_ref[2], pos_ref[3]
-    out_ref = refs[-1]
-    rows, depth = refs[0].shape
-    for half, (mine, near, far) in ((core, refs[0:3]), (1 - core, refs[3:6])):
-        where = pl.ds(pl.multiple_of(half * rows, 16), rows)
-        for d, ref, at in ((0, mine, 0), (1, near, 0), (3, near, 1), (2, far, 0)):
-            column = pl.multiple_of(lax.rem(zh + d, RING) * depth, 128)
-            out_ref[where, pl.ds(column, depth)] = ref[:, at * depth : (at + 1) * depth]
+    rows, depth = far_ref.shape
+    lead = pl.ds(pl.multiple_of(core * rows, 16), rows)
+    follow = pl.ds(pl.multiple_of((1 - core) * rows, 16), rows)
+
+    def at(d):
+        return pl.ds(pl.multiple_of(lax.rem(zh + d, RING) * depth, 128), depth)
+
+    out_ref[lead, at(0)] = mine_ref[0]
+    out_ref[follow, at(0)] = mine_ref[1]
+    out_ref[lead, at(3 - 2 * core)] = next_ref[0]
+    out_ref[follow, at(3 - 2 * core)] = next_ref[1]
+    out_ref[follow, at(1 + 2 * core)] = other_next_ref[0]
+    out_ref[lead, at(1 + 2 * core)] = other_next_ref[1]
+    out_ref[lead, at(2)] = far_ref[...]
+    out_ref[follow, at(2)] = other_far_ref[...]
 
 
 def vmem(count):
@@ -120,6 +137,13 @@
 
     spots = [(y, x, c) for y in range(RING) for x in range(RING) for c in range(2)]
     return lax.ppermute(value, ("y", "x", "c"), [(flat(*s), flat(*target(*s))) for s in spots])
+
+
+def advance(value):
+    pairs = []
+    for zh in range(RING):
+        pairs += [(zh * 2, (zh + 1) % RING * 2), (zh * 2 + 1, (zh - 1) % RING * 2 + 1)]
+    return lax.ppermute(value, ("zh", "c"), pairs)
 
 
 def gather(value, late):
@@ -174,36 +198,43 @@
         in_specs=[scalars] + vmem(2 * RING + 3),
         out_specs=vmem(4),
         out_shape=[jax.ShapeDtypeStruct((hid, tokens), BF16)] * 2
-        + [jax.ShapeDtypeStruct((hid // 2, width), BF16)] * 2,
-        scratch_shapes=[pltpu.VMEM((hid, tokens), BF16)],
+        + [jax.ShapeDtypeStruct((5, hid // 2, width // RING), BF16)] * 2,
+        scratch_shapes=[
+            pltpu.VMEM((hid, tokens), BF16),
+            pltpu.VMEM((2, RING, hid // 2, width // RING), BF16),
+        ],
         name="forward",
         cost_estimate=pl.CostEstimate(
             flops=3 * hid * tokens * width, bytes_accessed=14_000_000, transcendentals=hid * tokens * 2
         ),
     )(pos, *pieces, early, hidden_cot.T, ordered)
 
-    depth = width // RING
     arrived = shift(send, "c", 1)
-    quarters = [
-        add_up([keep[:, d * depth : (d + 1) * depth], arrived[:, d * depth : (d + 1) * depth]]).astype(BF16)
-        for d in range(RING)
-    ]
-    arrived = [shift(quarters[2], "zh", 2)]
-    arrived += [shift(quarters[1], "zh", 1), shift(quarters[3], "zh", -1)]
-    mine = (add_up([quarters[0]] + arrived) / (2 * RING)).astype(BF16)
-    far = shift(mine, "zh", 2)
-    near = jnp.concatenate([shift(mine, "zh", -1), shift(mine, "zh", 1)], axis=1)
-    other_mine = shift(mine, "c", 1)
+    opposite, follow, lead = (add_up([keep[at], arrived[at]]) for at in range(3))
+    passed = advance(opposite.astype(BF16))
+    follow_in = advance(follow.astype(BF16))
+    lead_in = advance((lead + passed.astype(F32)).astype(BF16))
+    other_in = shift(jnp.stack([follow_in, lead_in]), "c", 1)
+
+    def finish(at, here, there):
+        left, right = jnp.where(core == 0, here, there), jnp.where(core == 0, there, here)
+        return (add_up([keep[at], arrived[at], left, right]) / (2 * RING)).astype(BF16)
+
+    mine_lead, mine_follow = finish(3, lead_in, other_in[0]), finish(4, follow_in, other_in[1])
+    next_lead = advance(mine_lead)
+    next_follow = advance(mine_follow)
+    far = advance(next_lead)
+    near = jnp.stack([next_lead, next_follow])
     other_near = shift(near, "c", 1)
     other_far = shift(far, "c", 1)
     up_grad = pl.pallas_call(
         place_kernel,
-        in_specs=[scalars] + vmem(6),
+        in_specs=[scalars] + vmem(5),
         out_specs=vmem(1)[0],
         out_shape=jax.ShapeDtypeStruct((hid, width), BF16),
         name="place",
         cost_estimate=pl.CostEstimate(flops=0, bytes_accessed=4 * hid * width, transcendentals=0),
-    )(pos, mine, near, far, other_mine, other_near, other_far)
+    )(pos, jnp.stack([mine_lead, mine_follow]), near, far, other_near, other_far)
 
     parts = pl.pallas_call(
         input_grad_kernel,

time: 257 us -> 232 us (0.903)
  the two profiles are of different devices: /device:TPU:15 before, /device:TPU:1 now
where the time goes in v4:
time: 232 us; the launch traced here: 231 us
  starting transfers between devices  138 us (59%)
  waiting for transfers between devices  33.2 us (14%)
  Pallas kernels  24.7 us (11%)
  blocking collectives  14.9 us (6%)
  other arithmetic  13.4 us (6%)
  local copies, waits for them, and re-layouts  5.44 us (2%)
    ppermute x15, starting transfers between devices, turn(): lax.ppermute(value, ('y', 'x', 'c'), [(flat(*s), flat(*target(*s))) for s...  52.2 us
    ppermute x7, starting transfers between devices, shift(): lax.ppermute(value, axis, [(i, (i + by) % size) for i in range(size)])  47.9 us
    ppermute x6, starting transfers between devices, advance(): return lax.ppermute(value, ('zh', 'c'), pairs)  38.2 us
    ppermute x6, waiting for transfers between devices, advance(): return lax.ppermute(value, ('zh', 'c'), pairs)  20.9 us
    all_gather x1, blocking collectives, work(): block = lax.all_gather(normed.T, 'zl', axis=0, tiled=True)  14.9 us
    ppermute x15, waiting for transfers between devices, turn(): lax.ppermute(value, ('y', 'x', 'c'), [(flat(*s), flat(*target(*s))) for s...  9.02 us
    pallas_call x1, Pallas kernels, work(): pl.pallas_call(forward_kernel, in_specs=[scalars] + vmem(2 * RING + 3), o...  8.27 us
    pallas_call x1, Pallas kernels, work(): pl.pallas_call(input_grad_kernel, in_specs=vmem(2), out_specs=vmem(RING),...  5.08 us
  transfers between devices with their start and end apart: 28, of which 11 were waited for; matrix products, arithmetic and copies ran while one was open for 7% of the time, Pallas kernels for 6%

profile of v4, /device:TPU:1, one launch (start us, length us, event | category | flops | bytes accessed | tf_op | source)
XLA Modules:
  0.0 231.2 jit_solution(354719464186691672)
XLA Ops:
  0.6 14.9 %all_gather.3 = bf16[384,512]{1,0:T(8,128)(2,1)S(1)} all-gather(bf16[96,512]{1,0:T(8,128)(2,1)} %bitcast.53), channel_id=1, replica_groups=mesh['y'=4,'x'=4,'zl'=4,'zh'=4,'c'=2] {'zl'}, dimensions={0}, use_global_device_ids=true | all-gather | bytes 491520 | tf_op jit(solution)/shard_map/all_gather | solution.py:180
  15.6 5.0 %collective-permute-start.1 = (bf16[384,512]{1,0:T(8,128)(2,1)S(1)}, bf16[384,512]{1,0:T(8,128)(2,1)S(1)}, u32[]{:S(2)}, u32[]{:S(2)}) collective-permute-start(bf16[384,512]{1,0:T(8,128)(2,1)S(1)} %all_gather.3), channel_id=1, source_target_pairs={{0,64},{1,257},{32,96},{33,289},{64,0},{65,321},{96,32},{97,353},{... | collective-permute-start | bytes 1179656 | tf_op jit(solution)/shard_map/ppermute | solution.py:139
  22.9 4.2 %collective-permute-start = (bf16[384,512]{1,0:T(8,128)(2,1)S(1)}, bf16[384,512]{1,0:T(8,128)(2,1)S(1)}, u32[]{:S(2)}, u32[]{:S(2)}) collective-permute-start(bf16[384,512]{1,0:T(8,128)(2,1)S(1)} %all_gather.3), channel_id=1, source_target_pairs={{0,96},{1,385},{32,0},{33,417},{64,32},{65,449},{96,64},{97,481},{... | collective-permute-start | bytes 1179656 | tf_op jit(solution)/shard_map/ppermute | solution.py:139
  27.1 3.4 %collective-permute-done.2 = bf16[384,512]{1,0:T(8,128)(2,1)S(1)} collective-permute-done((bf16[384,512]{1,0:T(8,128)(2,1)S(1)}, bf16[384,512]{1,0:T(8,128)(2,1)S(1)}, u32[]{:S(2)}, u32[]{:S(2)}) %collective-permute-start.2) | collective-permute-done | bytes 393248 | tf_op jit(solution)/shard_map/ppermute | solution.py:139
  30.6 2.8 %collective-permute-start.6 = (bf16[768,512]{1,0:T(8,128)(2,1)S(1)}, bf16[768,512]{1,0:T(8,128)(2,1)S(1)}, u32[]{:S(2)}, u32[]{:S(2)}) collective-permute-start(bf16[768,512]{1,0:T(8,128)(2,1)S(1)} %constant_dynamic-update-slice_fusion.2.refs_1_), channel_id=1, source_target_pairs={{0,128},{1,33},{32,160},{33,65},{64,192},{65,97},{96,224},{97,1},{... | collective-permute-start | bytes 2359304 | tf_op jit(solution)/shard_map/ppermute | solution.py:139
  33.5 3.7 %collective-permute-start.3 = (bf16[768,512]{1,0:T(8,128)(2,1)S(1)}, bf16[768,512]{1,0:T(8,128)(2,1)S(1)}, u32[]{:S(2)}, u32[]{:S(2)}) collective-permute-start(bf16[768,512]{1,0:T(8,128)(2,1)S(1)} %constant_dynamic-update-slice_fusion.refs_0_), channel_id=1, source_target_pairs={{0,384},{1,97},{32,416},{33,1},{64,448},{65,33},{96,480},{97,65},{... | collective-permute-start | bytes 2359304 | tf_op jit(solution)/shard_map/ppermute | solution.py:139
  37.2 2.9 %collective-permute-start.4 = (bf16[768,512]{1,0:T(8,128)(2,1)S(1)}, bf16[768,512]{1,0:T(8,128)(2,1)}, u32[]{:S(2)}, u32[]{:S(2)}) collective-permute-start(bf16[768,512]{1,0:T(8,128)(2,1)S(1)} %constant_dynamic-update-slice_fusion.2.refs_1_), channel_id=1, source_target_pairs={{0,384},{1,97},{32,416},{33,1},{64,448},{65,33},{96,480},{97,65},{... | collective-permute-start | bytes 2359304 | tf_op jit(solution)/shard_map/ppermute | solution.py:139
  40.1 2.4 %collective-permute-start.8 = (bf16[768,512]{1,0:T(8,128)(2,1)S(1)}, bf16[768,512]{1,0:T(8,128)(2,1)}, u32[]{:S(2)}, u32[]{:S(2)}) collective-permute-start(bf16[768,512]{1,0:T(8,128)(2,1)S(1)} %constant_dynamic-update-slice_fusion.refs_0_), channel_id=1, source_target_pairs={{0,128},{1,33},{32,160},{33,65},{64,192},{65,97},{96,224},{97,1},{... | collective-permute-start | bytes 2359304 | tf_op jit(solution)/shard_map/ppermute | solution.py:139
  42.5 3.8 %collective-permute-done.6.refs_5_.refs_7_ = bf16[768,512]{1,0:T(8,128)(2,1)S(1)} collective-permute-done((bf16[768,512]{1,0:T(8,128)(2,1)S(1)}, bf16[768,512]{1,0:T(8,128)(2,1)S(1)}, u32[]{:S(2)}, u32[]{:S(2)}) %collective-permute-start.6) | collective-permute-done | bytes 786464 | tf_op jit(solution)/shard_map/ppermute | solution.py:139
  48.2 4.6 %collective-permute-start.5 = (bf16[768,512]{1,0:T(8,128)(2,1)S(1)}, bf16[768,512]{1,0:T(8,128)(2,1)}, u32[]{:S(2)}, u32[]{:S(2)}) collective-permute-start(bf16[768,512]{1,0:T(8,128)(2,1)S(1)} %collective-permute-done.3.refs_2_), channel_id=1, source_target_pairs={{0,384},{1,97},{32,416},{33,1},{64,448},{65,33},{96,480},{97,65},{... | collective-permute-start | bytes 2359304 | tf_op jit(solution)/shard_map/ppermute | solution.py:139
  53.4 3.4 %order.1.up_ref.refs_10_ = bf16[192,6144]{1,0:T(8,128)(2,1)} custom-call(s32[4]{0:T(128)} %pad_add_fusion.pos_ref, bf16[192,6144]{1,0:T(8,128)(2,1)} %up_ref.1), custom_call_target="tpu_custom_call" | custom-call | bytes 4718592 | tf_op jit(solution)/shard_map/order/pallas_call | solution.py:171
  56.8 4.9 %early.1.refs_8_ = f32[192,512]{1,0:T(8,128)} custom-call(bf16[192,6144]{1,0:T(8,128)(2,1)} %order.1.up_ref.refs_10_, bf16[768,512]{1,0:T(8,128)(2,1)} %copy-done, bf16[768,512]{1,0:T(8,128)(2,1)} %copy-done.1, bf16[768,512]{1,0:T(8,128)(2,1)} %copy-done.3, bf16[768,512]{1,0:T(8,128)(2,1)} %collective-permute-done.4.refs_3_, ...), custom_call_target="tpu_custom_call" | custom-call | flops 905969664 | bytes 7000000 | tf_op jit(solution)/shard_map/early/pallas_call | solution.py:187
  63.5 8.3 %forward.1 = (bf16[192,512]{1,0:T(8,128)(2,1)}, bf16[192,512]{1,0:T(8,128)(2,1)}, bf16[5,96,1536]{2,1,0:T(8,128)(2,1)}, bf16[5,96,1536]{2,1,0:T(8,128)(2,1)}) custom-call(s32[4]{0:T(128)} %pad_add_fusion.pos_ref, bf16[768,512]{1,0:T(8,128)(2,1)} %copy-done, bf16[768,512]{1,0:T(8,128)(2,1)} %copy-done.1, bf16[768,512]{1,0:T(8,128)(2,1)} %copy-done.3, ...), custom_call_target="tpu_custom_call" | custom-call | flops 1811939328 | bytes 14000000 | tf_op jit(solution)/shard_map/forward/pallas_call | solution.py:196
  71.8 11.5 %collective-permute-start.18 = (bf16[5,96,1536]{2,1,0:T(8,128)(2,1)}, bf16[5,96,1536]{2,1,0:T(8,128)(2,1)S(1)}, u32[]{:S(2)}, u32[]{:S(2)}) collective-permute-start(bf16[5,96,1536]{2,1,0:T(8,128)(2,1)} %get-tuple-element.18), channel_id=1, source_target_pairs={{0,1},{1,0},{2,3},{3,2},{4,5},{5,4},{6,7},{7,6},{8,9},{9,8},{10,11... | collective-permute-start | bytes 4423688 | tf_op jit(solution)/shard_map/ppermute | solution.py:28
  83.3 5.1 %partial.1 = (bf16[1536,512]{1,0:T(8,128)(2,1)}, bf16[1536,512]{1,0:T(8,128)(2,1)}, bf16[1536,512]{1,0:T(8,128)(2,1)}, bf16[1536,512]{1,0:T(8,128)(2,1)}) custom-call(bf16[192,512]{1,0:T(8,128)(2,1)} %get-tuple-element.12.grad_ref, bf16[192,6144]{1,0:T(8,128)(2,1)} %order.1.up_ref.refs_10_), custom_call_target="tpu_custom_call" | custom-call | flops 1207959552 | bytes 9000000 | tf_op jit(solution)/shard_map/partial/pallas_call | solution.py:239
  92.2 3.4 %collective-permute-start.9 = (bf16[1536,512]{1,0:T(8,128)(2,1)}, bf16[1536,512]{1,0:T(8,128)(2,1)}, u32[]{:S(2)}, u32[]{:S(2)}) collective-permute-start(bf16[1536,512]{1,0:T(8,128)(2,1)} %get-tuple-element.14), channel_id=1, source_target_pairs={{0,128},{1,33},{32,160},{33,65},{64,192},{65,97},{96,224},{97,1},{... | collective-permute-start | bytes 4718600 | tf_op jit(solution)/shard_map/ppermute | solution.py:139
  98.6 10.3 %collective-permute-start.19 = (bf16[96,1536]{1,0:T(8,128)(2,1)S(1)}, bf16[96,1536]{1,0:T(8,128)(2,1)S(1)}, u32[]{:S(2)}, u32[]{:S(2)}) collective-permute-start(bf16[96,1536]{1,0:T(8,128)(2,1)S(1)} %get-tuple-element.21), channel_id=1, source_target_pairs={{0,2},{1,7},{2,4},{3,1},{4,6},{5,3},{6,0},{7,5},{8,10},{9,15},{10,... | collective-permute-start | bytes 884744 | tf_op jit(solution)/shard_map/ppermute | solution.py:146
  108.9 5.2 %collective-permute-start.21 = (bf16[96,1536]{1,0:T(8,128)(2,1)}, bf16[96,1536]{1,0:T(8,128)(2,1)S(1)}, u32[]{:S(2)}, u32[]{:S(2)}) collective-permute-start(bf16[96,1536]{1,0:T(8,128)(2,1)} %get-tuple-element.22), channel_id=1, source_target_pairs={{0,2},{1,7},{2,4},{3,1},{4,6},{5,3},{6,0},{7,5},{8,10},{9,15},{10,... | collective-permute-start | bytes 884744 | tf_op jit(solution)/shard_map/ppermute | solution.py:146
  114.1 3.3 %collective-permute-done.19 = bf16[96,1536]{1,0:T(8,128)(2,1)S(1)} collective-permute-done((bf16[96,1536]{1,0:T(8,128)(2,1)S(1)}, bf16[96,1536]{1,0:T(8,128)(2,1)S(1)}, u32[]{:S(2)}, u32[]{:S(2)}) %collective-permute-start.19) | collective-permute-done | bytes 294944 | tf_op jit(solution)/shard_map/ppermute | solution.py:146
  119.3 7.0 %collective-permute-start.20 = (bf16[96,1536]{1,0:T(8,128)(2,1)}, bf16[96,1536]{1,0:T(8,128)(2,1)}, u32[]{:S(2)}, u32[]{:S(2)}) collective-permute-start(bf16[96,1536]{1,0:T(8,128)(2,1)} %fusion.3), channel_id=1, source_target_pairs={{0,2},{1,7},{2,4},{3,1},{4,6},{5,3},{6,0},{7,5},{8,10},{9,15},{10,... | collective-permute-start | bytes 884744 | tf_op jit(solution)/shard_map/ppermute | solution.py:146
  126.4 15.8 %collective-permute-done.20 = bf16[96,1536]{1,0:T(8,128)(2,1)} collective-permute-done((bf16[96,1536]{1,0:T(8,128)(2,1)}, bf16[96,1536]{1,0:T(8,128)(2,1)}, u32[]{:S(2)}, u32[]{:S(2)}) %collective-permute-start.20) | collective-permute-done | bytes 294944 | tf_op jit(solution)/shard_map/ppermute | solution.py:146
  146.3 3.2 %add_convert_fusion = bf16[1536,512]{1,0:T(8,128)(2,1)S(1)} fusion(bf16[1536,512]{1,0:T(8,128)(2,1)} %collective-permute-done.11, bf16[1536,512]{1,0:T(8,128)(2,1)} %copy-done.6, bf16[1536,512]{1,0:T(8,128)(2,1)} %collective-permute-done.9, bf16[1536,512]{1,0:T(8,128)(2,1)S(1)} %copy-done.5), kind=kLoop, calls=%fused_computation | loop fusion | flops 6291456 | bytes 7864320 | tf_op jit(solution)/shard_map/convert_element_type | solution.py:249
  150.3 4.3 %collective-permute-start.12 = (bf16[384,512]{1,0:T(8,128)(2,1)}, bf16[384,512]{1,0:T(8,128)(2,1)}, u32[]{:S(2)}, u32[]{:S(2)}) collective-permute-start(bf16[384,512]{1,0:T(8,128)(2,1)} %get-tuple-element.23), channel_id=1, source_target_pairs={{0,32},{1,129},{32,64},{33,161},{64,96},{65,193},{96,0},{97,225},{... | collective-permute-start | bytes 1179656 | tf_op jit(solution)/shard_map/ppermute | solution.py:139
  154.7 9.0 %collective-permute-start.13 = (bf16[384,512]{1,0:T(8,128)(2,1)S(1)}, bf16[384,512]{1,0:T(8,128)(2,1)}, u32[]{:S(2)}, u32[]{:S(2)}) collective-permute-start(bf16[384,512]{1,0:T(8,128)(2,1)S(1)} %get-tuple-element.25), channel_id=1, source_target_pairs={{0,64},{1,257},{32,96},{33,289},{64,0},{65,321},{96,32},{97,353},{... | collective-permute-start | bytes 1179656 | tf_op jit(solution)/shard_map/ppermute | solution.py:139
  167.3 4.0 %collective-permute-start.23 = (bf16[96,1536]{1,0:T(8,128)(2,1)S(1)}, bf16[96,1536]{1,0:T(8,128)(2,1)S(1)}, u32[]{:S(2)}, u32[]{:S(2)}) collective-permute-start(bf16[96,1536]{1,0:T(8,128)(2,1)S(1)} %get-tuple-element.19), channel_id=1, source_target_pairs={{0,2},{1,7},{2,4},{3,1},{4,6},{5,3},{6,0},{7,5},{8,10},{9,15},{10,... | collective-permute-start | bytes 884744 | tf_op jit(solution)/shard_map/ppermute | solution.py:146
  171.3 5.3 %collective-permute-start.24 = (bf16[96,1536]{1,0:T(8,128)(2,1)S(1)}, bf16[96,1536]{1,0:T(8,128)(2,1)S(1)}, u32[]{:S(2)}, u32[]{:S(2)}) collective-permute-start(bf16[96,1536]{1,0:T(8,128)(2,1)S(1)} %get-tuple-element.20), channel_id=1, source_target_pairs={{0,2},{1,7},{2,4},{3,1},{4,6},{5,3},{6,0},{7,5},{8,10},{9,15},{10,... | collective-permute-start | bytes 884744 | tf_op jit(solution)/shard_map/ppermute | solution.py:146
  179.2 6.5 %collective-permute-start.25 = (bf16[96,1536]{1,0:T(8,128)(2,1)S(1)}, bf16[96,1536]{1,0:T(8,128)(2,1)S(1)}, u32[]{:S(2)}, u32[]{:S(2)}) collective-permute-start(bf16[96,1536]{1,0:T(8,128)(2,1)S(1)} %collective-permute-done.23), channel_id=1, source_target_pairs={{0,2},{1,7},{2,4},{3,1},{4,6},{5,3},{6,0},{7,5},{8,10},{9,15},{10,... | collective-permute-start | bytes 884744 | tf_op jit(solution)/shard_map/ppermute | solution.py:146
  186.4 3.8 %collective-permute-start.26 = (bf16[2,96,1536]{2,1,0:T(8,128)(2,1)S(1)}, bf16[2,96,1536]{2,1,0:T(8,128)(2,1)S(1)}, u32[]{:S(2)}, u32[]{:S(2)}) collective-permute-start(bf16[2,96,1536]{2,1,0:T(8,128)(2,1)S(1)} %pad_maximum_fusion.2.next_ref), channel_id=1, source_target_pairs={{0,1},{1,0},{2,3},{3,2},{4,5},{5,4},{6,7},{7,6},{8,9},{9,8},{10,11... | collective-permute-start | bytes 1769480 | tf_op jit(solution)/shard_map/ppermute | solution.py:28
  190.9 4.6 %collective-permute-start.15 = (bf16[96,512]{1,0:T(8,128)(2,1)}, bf16[96,512]{1,0:T(8,128)(2,1)S(1)}, u32[]{:S(2)}, u32[]{:S(2)}) collective-permute-start(bf16[96,512]{1,0:T(8,128)(2,1)} %get-tuple-element.26), channel_id=1, source_target_pairs={{0,8},{8,16},{16,24},{24,0},{1,9},{9,17},{17,25},{25,1},{2,10},{10... | collective-permute-start | bytes 294920 | tf_op jit(solution)/shard_map/ppermute | solution.py:28
  195.5 21.7 %collective-permute-start.16 = (bf16[96,512]{1,0:T(8,128)(2,1)S(1)}, bf16[96,512]{1,0:T(8,128)(2,1)S(1)}, u32[]{:S(2)}, u32[]{:S(2)}) collective-permute-start(bf16[96,512]{1,0:T(8,128)(2,1)S(1)} %get-tuple-element.28), channel_id=1, source_target_pairs={{0,16},{8,24},{16,0},{24,8},{1,17},{9,25},{17,1},{25,9},{2,18},{10... | collective-permute-start | bytes 294920 | tf_op jit(solution)/shard_map/ppermute | solution.py:28
  219.2 2.5 %collective-permute-start.27 = (bf16[96,1536]{1,0:T(8,128)(2,1)S(1)}, bf16[96,1536]{1,0:T(8,128)(2,1)S(1)}, u32[]{:S(2)}, u32[]{:S(2)}) collective-permute-start(bf16[96,1536]{1,0:T(8,128)(2,1)S(1)} %collective-permute-done.25.far_ref), channel_id=1, source_target_pairs={{0,1},{1,0},{2,3},{3,2},{4,5},{5,4},{6,7},{7,6},{8,9},{9,8},{10,11... | collective-permute-start | bytes 884744 | tf_op jit(solution)/shard_map/ppermute | solution.py:28
  228.0 3.2 %place.1 = bf16[192,6144]{1,0:T(8,128)(2,1)} custom-call(s32[4]{0:T(128)} %pad_add_fusion.pos_ref, bf16[2,96,1536]{2,1,0:T(8,128)(2,1)} %pad_maximum_fusion.1.mine_ref, bf16[2,96,1536]{2,1,0:T(8,128)(2,1)} %copy-done.4, bf16[96,1536]{1,0:T(8,128)(2,1)} %copy-done.9, bf16[2,96,1536]{2,1,0:T(8,128)(2,1)} %copy-done.8, bf16[96,1536]{1,0:T(8,128)(2,1)} %copy-done.10), custom_call_target="tpu_custom_call" | custom-call | bytes 4718592 | tf_op jit(solution)/shard_map/place/pallas_call | solution.py:230
  (68 shorter events, 36.4 us)
Async XLA Ops:
  15.6 11.5 %collective-permute-start.1 = (bf16[384,512]{1,0:T(8,128)(2,1)S(1)}, bf16[384,512]{1,0:T(8,128)(2,1)S(1)}, u32[]{:S(2)}, u32[]{:S(2)}) collective-permute-start(bf16[384,512]{1,0:T(8,128)(2,1)S(1)} %all_gather.3), channel_id=1, source_target_pairs={{0,64},{1,257},{32,96},{33,289},{64,0},{65,321},{96,32},{97,353},{... | collective-permute-start | bytes 1179656 | tf_op jit(solution)/shard_map/ppermute | solution.py:139
  20.5 10.0 %collective-permute-start.2 = (bf16[384,512]{1,0:T(8,128)(2,1)S(1)}, bf16[384,512]{1,0:T(8,128)(2,1)S(1)}, u32[]{:S(2)}, u32[]{:S(2)}) collective-permute-start(bf16[384,512]{1,0:T(8,128)(2,1)S(1)} %all_gather.3), channel_id=1, source_target_pairs={{0,32},{1,129},{32,64},{33,161},{64,96},{65,193},{96,0},{97,225},{... | collective-permute-start | bytes 1179656 | tf_op jit(solution)/shard_map/ppermute | solution.py:139
  22.9 10.6 %collective-permute-start = (bf16[384,512]{1,0:T(8,128)(2,1)S(1)}, bf16[384,512]{1,0:T(8,128)(2,1)S(1)}, u32[]{:S(2)}, u32[]{:S(2)}) collective-permute-start(bf16[384,512]{1,0:T(8,128)(2,1)S(1)} %all_gather.3), channel_id=1, source_target_pairs={{0,96},{1,385},{32,0},{33,417},{64,32},{65,449},{96,64},{97,481},{... | collective-permute-start | bytes 1179656 | tf_op jit(solution)/shard_map/ppermute | solution.py:139
  30.6 26.2 %copy-start.1 = (bf16[768,512]{1,0:T(8,128)(2,1)}, bf16[768,512]{1,0:T(8,128)(2,1)S(1)}, u32[]{:S(2)}) copy-start(bf16[768,512]{1,0:T(8,128)(2,1)S(1)} %constant_dynamic-update-slice_fusion.2.refs_1_) | copy-start | bytes 2359300
  30.6 15.6 %collective-permute-start.6 = (bf16[768,512]{1,0:T(8,128)(2,1)S(1)}, bf16[768,512]{1,0:T(8,128)(2,1)S(1)}, u32[]{:S(2)}, u32[]{:S(2)}) collective-permute-start(bf16[768,512]{1,0:T(8,128)(2,1)S(1)} %constant_dynamic-update-slice_fusion.2.refs_1_), channel_id=1, source_target_pairs={{0,128},{1,33},{32,160},{33,65},{64,192},{65,97},{96,224},{97,1},{... | collective-permute-start | bytes 2359304 | tf_op jit(solution)/shard_map/ppermute | solution.py:139
  33.5 23.3 %copy-start = (bf16[768,512]{1,0:T(8,128)(2,1)}, bf16[768,512]{1,0:T(8,128)(2,1)S(1)}, u32[]{:S(2)}) copy-start(bf16[768,512]{1,0:T(8,128)(2,1)S(1)} %constant_dynamic-update-slice_fusion.refs_0_) | copy-start | bytes 2359300
  33.5 14.7 %collective-permute-start.3 = (bf16[768,512]{1,0:T(8,128)(2,1)S(1)}, bf16[768,512]{1,0:T(8,128)(2,1)S(1)}, u32[]{:S(2)}, u32[]{:S(2)}) collective-permute-start(bf16[768,512]{1,0:T(8,128)(2,1)S(1)} %constant_dynamic-update-slice_fusion.refs_0_), channel_id=1, source_target_pairs={{0,384},{1,97},{32,416},{33,1},{64,448},{65,33},{96,480},{97,65},{... | collective-permute-start | bytes 2359304 | tf_op jit(solution)/shard_map/ppermute | solution.py:139
  37.2 19.6 %collective-permute-start.4 = (bf16[768,512]{1,0:T(8,128)(2,1)S(1)}, bf16[768,512]{1,0:T(8,128)(2,1)}, u32[]{:S(2)}, u32[]{:S(2)}) collective-permute-start(bf16[768,512]{1,0:T(8,128)(2,1)S(1)} %constant_dynamic-update-slice_fusion.2.refs_1_), channel_id=1, source_target_pairs={{0,384},{1,97},{32,416},{33,1},{64,448},{65,33},{96,480},{97,65},{... | collective-permute-start | bytes 2359304 | tf_op jit(solution)/shard_map/ppermute | solution.py:139
  40.1 16.7 %collective-permute-start.8 = (bf16[768,512]{1,0:T(8,128)(2,1)S(1)}, bf16[768,512]{1,0:T(8,128)(2,1)}, u32[]{:S(2)}, u32[]{:S(2)}) collective-permute-start(bf16[768,512]{1,0:T(8,128)(2,1)S(1)} %constant_dynamic-update-slice_fusion.refs_0_), channel_id=1, source_target_pairs={{0,128},{1,33},{32,160},{33,65},{64,192},{65,97},{96,224},{97,1},{... | collective-permute-start | bytes 2359304 | tf_op jit(solution)/shard_map/ppermute | solution.py:139
  46.2 17.0 %collective-permute-start.7 = (bf16[768,512]{1,0:T(8,128)(2,1)S(1)}, bf16[768,512]{1,0:T(8,128)(2,1)}, u32[]{:S(2)}, u32[]{:S(2)}) collective-permute-start(bf16[768,512]{1,0:T(8,128)(2,1)S(1)} %collective-permute-done.6.refs_5_.refs_7_), channel_id=1, source_target_pairs={{0,128},{1,33},{32,160},{33,65},{64,192},{65,97},{96,224},{97,1},{... | collective-permute-start | bytes 2359304 | tf_op jit(solution)/shard_map/ppermute | solution.py:139
  48.2 15.3 %collective-permute-start.5 = (bf16[768,512]{1,0:T(8,128)(2,1)S(1)}, bf16[768,512]{1,0:T(8,128)(2,1)}, u32[]{:S(2)}, u32[]{:S(2)}) collective-permute-start(bf16[768,512]{1,0:T(8,128)(2,1)S(1)} %collective-permute-done.3.refs_2_), channel_id=1, source_target_pairs={{0,384},{1,97},{32,416},{33,1},{64,448},{65,33},{96,480},{97,65},{... | collective-permute-start | bytes 2359304 | tf_op jit(solution)/shard_map/ppermute | solution.py:139
  71.8 23.8 %collective-permute-start.18 = (bf16[5,96,1536]{2,1,0:T(8,128)(2,1)}, bf16[5,96,1536]{2,1,0:T(8,128)(2,1)S(1)}, u32[]{:S(2)}, u32[]{:S(2)}) collective-permute-start(bf16[5,96,1536]{2,1,0:T(8,128)(2,1)} %get-tuple-element.18), channel_id=1, source_target_pairs={{0,1},{1,0},{2,3},{3,2},{4,5},{5,4},{6,7},{7,6},{8,9},{9,8},{10,11... | collective-permute-start | bytes 4423688 | tf_op jit(solution)/shard_map/ppermute | solution.py:28
  88.3 56.8 %collective-permute-start.10 = (bf16[1536,512]{1,0:T(8,128)(2,1)}, bf16[1536,512]{1,0:T(8,128)(2,1)S(1)}, u32[]{:S(2)}, u32[]{:S(2)}) collective-permute-start(bf16[1536,512]{1,0:T(8,128)(2,1)} %get-tuple-element.15), channel_id=1, source_target_pairs={{0,256},{1,65},{32,288},{33,97},{64,320},{65,1},{96,352},{97,33},{... | collective-permute-start | bytes 4718600 | tf_op jit(solution)/shard_map/ppermute | solution.py:139
  90.3 54.9 %collective-permute-start.11 = (bf16[1536,512]{1,0:T(8,128)(2,1)}, bf16[1536,512]{1,0:T(8,128)(2,1)}, u32[]{:S(2)}, u32[]{:S(2)}) collective-permute-start(bf16[1536,512]{1,0:T(8,128)(2,1)} %get-tuple-element.16), channel_id=1, source_target_pairs={{0,384},{1,97},{32,416},{33,1},{64,448},{65,33},{96,480},{97,65},{... | collective-permute-start | bytes 4718600 | tf_op jit(solution)/shard_map/ppermute | solution.py:139
  92.2 53.0 %collective-permute-start.9 = (bf16[1536,512]{1,0:T(8,128)(2,1)}, bf16[1536,512]{1,0:T(8,128)(2,1)}, u32[]{:S(2)}, u32[]{:S(2)}) collective-permute-start(bf16[1536,512]{1,0:T(8,128)(2,1)} %get-tuple-element.14), channel_id=1, source_target_pairs={{0,128},{1,33},{32,160},{33,65},{64,192},{65,97},{96,224},{97,1},{... | collective-permute-start | bytes 4718600 | tf_op jit(solution)/shard_map/ppermute | solution.py:139
  98.6 47.7 %copy-start.5 = (bf16[1536,512]{1,0:T(8,128)(2,1)S(1)}, bf16[1536,512]{1,0:T(8,128)(2,1)}, u32[]{:S(2)}) copy-start(bf16[1536,512]{1,0:T(8,128)(2,1)} %get-tuple-element.13) | copy-start | bytes 4718596
  98.6 18.8 %collective-permute-start.19 = (bf16[96,1536]{1,0:T(8,128)(2,1)S(1)}, bf16[96,1536]{1,0:T(8,128)(2,1)S(1)}, u32[]{:S(2)}, u32[]{:S(2)}) collective-permute-start(bf16[96,1536]{1,0:T(8,128)(2,1)S(1)} %get-tuple-element.21), channel_id=1, source_target_pairs={{0,2},{1,7},{2,4},{3,1},{4,6},{5,3},{6,0},{7,5},{8,10},{9,15},{10,... | collective-permute-start | bytes 884744 | tf_op jit(solution)/shard_map/ppermute | solution.py:146
  108.9 17.5 %collective-permute-start.21 = (bf16[96,1536]{1,0:T(8,128)(2,1)}, bf16[96,1536]{1,0:T(8,128)(2,1)S(1)}, u32[]{:S(2)}, u32[]{:S(2)}) collective-permute-start(bf16[96,1536]{1,0:T(8,128)(2,1)} %get-tuple-element.22), channel_id=1, source_target_pairs={{0,2},{1,7},{2,4},{3,1},{4,6},{5,3},{6,0},{7,5},{8,10},{9,15},{10,... | collective-permute-start | bytes 884744 | tf_op jit(solution)/shard_map/ppermute | solution.py:146
  119.3 22.9 %collective-permute-start.20 = (bf16[96,1536]{1,0:T(8,128)(2,1)}, bf16[96,1536]{1,0:T(8,128)(2,1)}, u32[]{:S(2)}, u32[]{:S(2)}) collective-permute-start(bf16[96,1536]{1,0:T(8,128)(2,1)} %fusion.3), channel_id=1, source_target_pairs={{0,2},{1,7},{2,4},{3,1},{4,6},{5,3},{6,0},{7,5},{8,10},{9,15},{10,... | collective-permute-start | bytes 884744 | tf_op jit(solution)/shard_map/ppermute | solution.py:146
  143.2 22.4 %collective-permute-start.22 = (bf16[2,96,1536]{2,1,0:T(8,128)(2,1)S(1)}, bf16[2,96,1536]{2,1,0:T(8,128)(2,1)S(1)}, u32[]{:S(2)}, u32[]{:S(2)}) collective-permute-start(bf16[2,96,1536]{2,1,0:T(8,128)(2,1)S(1)} %pad_maximum_fusion), channel_id=1, source_target_pairs={{0,1},{1,0},{2,3},{3,2},{4,5},{5,4},{6,7},{7,6},{8,9},{9,8},{10,11... | collective-permute-start | bytes 1769480 | tf_op jit(solution)/shard_map/ppermute | solution.py:28
  150.3 26.3 %collective-permute-start.12 = (bf16[384,512]{1,0:T(8,128)(2,1)}, bf16[384,512]{1,0:T(8,128)(2,1)}, u32[]{:S(2)}, u32[]{:S(2)}) collective-permute-start(bf16[384,512]{1,0:T(8,128)(2,1)} %get-tuple-element.23), channel_id=1, source_target_pairs={{0,32},{1,129},{32,64},{33,161},{64,96},{65,193},{96,0},{97,225},{... | collective-permute-start | bytes 1179656 | tf_op jit(solution)/shard_map/ppermute | solution.py:139
  154.7 22.0 %collective-permute-start.13 = (bf16[384,512]{1,0:T(8,128)(2,1)S(1)}, bf16[384,512]{1,0:T(8,128)(2,1)}, u32[]{:S(2)}, u32[]{:S(2)}) collective-permute-start(bf16[384,512]{1,0:T(8,128)(2,1)S(1)} %get-tuple-element.25), channel_id=1, source_target_pairs={{0,64},{1,257},{32,96},{33,289},{64,0},{65,321},{96,32},{97,353},{... | collective-permute-start | bytes 1179656 | tf_op jit(solution)/shard_map/ppermute | solution.py:139
  163.7 13.0 %collective-permute-start.14 = (bf16[384,512]{1,0:T(8,128)(2,1)S(1)}, bf16[384,512]{1,0:T(8,128)(2,1)}, u32[]{:S(2)}, u32[]{:S(2)}) collective-permute-start(bf16[384,512]{1,0:T(8,128)(2,1)S(1)} %get-tuple-element.24), channel_id=1, source_target_pairs={{0,96},{1,385},{32,0},{33,417},{64,32},{65,449},{96,64},{97,481},{... | collective-permute-start | bytes 1179656 | tf_op jit(solution)/shard_map/ppermute | solution.py:139
  167.3 11.8 %collective-permute-start.23 = (bf16[96,1536]{1,0:T(8,128)(2,1)S(1)}, bf16[96,1536]{1,0:T(8,128)(2,1)S(1)}, u32[]{:S(2)}, u32[]{:S(2)}) collective-permute-start(bf16[96,1536]{1,0:T(8,128)(2,1)S(1)} %get-tuple-element.19), channel_id=1, source_target_pairs={{0,2},{1,7},{2,4},{3,1},{4,6},{5,3},{6,0},{7,5},{8,10},{9,15},{10,... | collective-permute-start | bytes 884744 | tf_op jit(solution)/shard_map/ppermute | solution.py:146
  171.3 15.0 %collective-permute-start.24 = (bf16[96,1536]{1,0:T(8,128)(2,1)S(1)}, bf16[96,1536]{1,0:T(8,128)(2,1)S(1)}, u32[]{:S(2)}, u32[]{:S(2)}) collective-permute-start(bf16[96,1536]{1,0:T(8,128)(2,1)S(1)} %get-tuple-element.20), channel_id=1, source_target_pairs={{0,2},{1,7},{2,4},{3,1},{4,6},{5,3},{6,0},{7,5},{8,10},{9,15},{10,... | collective-permute-start | bytes 884744 | tf_op jit(solution)/shard_map/ppermute | solution.py:146
  179.2 40.0 %collective-permute-start.25 = (bf16[96,1536]{1,0:T(8,128)(2,1)S(1)}, bf16[96,1536]{1,0:T(8,128)(2,1)S(1)}, u32[]{:S(2)}, u32[]{:S(2)}) collective-permute-start(bf16[96,1536]{1,0:T(8,128)(2,1)S(1)} %collective-permute-done.23), channel_id=1, source_target_pairs={{0,2},{1,7},{2,4},{3,1},{4,6},{5,3},{6,0},{7,5},{8,10},{9,15},{10,... | collective-permute-start | bytes 884744 | tf_op jit(solution)/shard_map/ppermute | solution.py:146
  186.4 40.1 %copy-start.4 = (bf16[2,96,1536]{2,1,0:T(8,128)(2,1)}, bf16[2,96,1536]{2,1,0:T(8,128)(2,1)S(1)}, u32[]{:S(2)}) copy-start(bf16[2,96,1536]{2,1,0:T(8,128)(2,1)S(1)} %pad_maximum_fusion.2.next_ref) | copy-start | bytes 1769476
  186.4 40.0 %collective-permute-start.26 = (bf16[2,96,1536]{2,1,0:T(8,128)(2,1)S(1)}, bf16[2,96,1536]{2,1,0:T(8,128)(2,1)S(1)}, u32[]{:S(2)}, u32[]{:S(2)}) collective-permute-start(bf16[2,96,1536]{2,1,0:T(8,128)(2,1)S(1)} %pad_maximum_fusion.2.next_ref), channel_id=1, source_target_pairs={{0,1},{1,0},{2,3},{3,2},{4,5},{5,4},{6,7},{7,6},{8,9},{9,8},{10,11... | collective-permute-start | bytes 1769480 | tf_op jit(solution)/shard_map/ppermute | solution.py:28
  190.9 30.8 %collective-permute-start.15 = (bf16[96,512]{1,0:T(8,128)(2,1)}, bf16[96,512]{1,0:T(8,128)(2,1)S(1)}, u32[]{:S(2)}, u32[]{:S(2)}) collective-permute-start(bf16[96,512]{1,0:T(8,128)(2,1)} %get-tuple-element.26), channel_id=1, source_target_pairs={{0,8},{8,16},{16,24},{24,0},{1,9},{9,17},{17,25},{25,1},{2,10},{10... | collective-permute-start | bytes 294920 | tf_op jit(solution)/shard_map/ppermute | solution.py:28
  195.5 27.3 %collective-permute-start.16 = (bf16[96,512]{1,0:T(8,128)(2,1)S(1)}, bf16[96,512]{1,0:T(8,128)(2,1)S(1)}, u32[]{:S(2)}, u32[]{:S(2)}) collective-permute-start(bf16[96,512]{1,0:T(8,128)(2,1)S(1)} %get-tuple-element.28), channel_id=1, source_target_pairs={{0,16},{8,24},{16,0},{24,8},{1,17},{9,25},{17,1},{25,9},{2,18},{10... | collective-permute-start | bytes 294920 | tf_op jit(solution)/shard_map/ppermute | solution.py:28
  217.2 7.7 %collective-permute-start.17 = (bf16[96,512]{1,0:T(8,128)(2,1)S(1)}, bf16[96,512]{1,0:T(8,128)(2,1)S(1)}, u32[]{:S(2)}, u32[]{:S(2)}) collective-permute-start(bf16[96,512]{1,0:T(8,128)(2,1)S(1)} %get-tuple-element.27), channel_id=1, source_target_pairs={{0,24},{8,0},{16,8},{24,16},{1,25},{9,1},{17,9},{25,17},{2,26},{10... | collective-permute-start | bytes 294920 | tf_op jit(solution)/shard_map/ppermute | solution.py:28
  219.2 7.3 %collective-permute-start.27 = (bf16[96,1536]{1,0:T(8,128)(2,1)S(1)}, bf16[96,1536]{1,0:T(8,128)(2,1)S(1)}, u32[]{:S(2)}, u32[]{:S(2)}) collective-permute-start(bf16[96,1536]{1,0:T(8,128)(2,1)S(1)} %collective-permute-done.25.far_ref), channel_id=1, source_target_pairs={{0,1},{1,0},{2,3},{3,2},{4,5},{5,4},{6,7},{7,6},{8,9},{9,8},{10,11... | collective-permute-start | bytes 884744 | tf_op jit(solution)/shard_map/ppermute | solution.py:28
  (7 other events, 30.4 us)

commit v5 on v4

--- a/solution.py
+++ b/solution.py
@@ -89,9 +89,9 @@
             for at in range(2):
                 term_ref[at, quarter, :, where] = term[at * rows : (at + 1) * rows, part * width : (part + 1) * width]
     near, away = 1 + 2 * core, 3 - 2 * core
-    for at, (half, quarter) in enumerate(((0, 2), (1, near), (0, near), (0, 0), (1, 0))):
+    for at, (half, quarter) in enumerate(((0, 2), (1, near), (0, near), (0, 0))):
         keep_ref[at] = term_ref[half, quarter]
-    for at, (half, quarter) in enumerate(((1, 2), (0, away), (1, away), (1, 0), (0, 0))):
+    for at, (half, quarter) in enumerate(((1, 2), (0, away), (1, away), (1, 0))):
         send_ref[at] = term_ref[half, quarter]
 
 
@@ -103,23 +103,16 @@
         outs[d][...] = term.astype(BF16)
 
 
-def place_kernel(pos_ref, mine_ref, next_ref, far_ref, other_next_ref, other_far_ref, out_ref):
+def place_kernel(pos_ref, *refs):
     core, zh = pos_ref[2], pos_ref[3]
-    rows, depth = far_ref.shape
+    out_ref = refs[-1]
+    rows, depth = refs[0].shape
     lead = pl.ds(pl.multiple_of(core * rows, 16), rows)
     follow = pl.ds(pl.multiple_of((1 - core) * rows, 16), rows)
-
-    def at(d):
-        return pl.ds(pl.multiple_of(lax.rem(zh + d, RING) * depth, 128), depth)
-
-    out_ref[lead, at(0)] = mine_ref[0]
-    out_ref[follow, at(0)] = mine_ref[1]
-    out_ref[lead, at(3 - 2 * core)] = next_ref[0]
-    out_ref[follow, at(3 - 2 * core)] = next_ref[1]
-    out_ref[follow, at(1 + 2 * core)] = other_next_ref[0]
-    out_ref[lead, at(1 + 2 * core)] = other_next_ref[1]
-    out_ref[lead, at(2)] = far_ref[...]
-    out_ref[follow, at(2)] = other_far_ref[...]
+    behind, ahead = 3 - 2 * core, 1 + 2 * core
+    spots = ((lead, 0), (follow, 0), (lead, behind), (follow, behind), (follow, ahead), (lead, ahead), (lead, 2), (follow, 2))
+    for ref, (where, d) in zip(refs[:-1], spots):
+        out_ref[where, pl.ds(pl.multiple_of(lax.rem(zh + d, RING) * depth, 128), depth)] = ref[...]
 
 
 def vmem(count):
@@ -139,10 +132,13 @@
     return lax.ppermute(value, ("y", "x", "c"), [(flat(*s), flat(*target(*s))) for s in spots])
 
 
-def advance(value):
+def advance(value, cross=False):
     pairs = []
     for zh in range(RING):
-        pairs += [(zh * 2, (zh + 1) % RING * 2), (zh * 2 + 1, (zh - 1) % RING * 2 + 1)]
+        pairs += [
+            (zh * 2, (zh + 1) % RING * 2 + cross),
+            (zh * 2 + 1, (zh - 1) % RING * 2 + 1 - cross),
+        ]
     return lax.ppermute(value, ("zh", "c"), pairs)
 
 
@@ -177,7 +173,11 @@
         cost_estimate=pl.CostEstimate(flops=0, bytes_accessed=4 * hid * width, transcendentals=0),
     )(pos, up_rows)
 
-    block = lax.all_gather(normed.T, "zl", axis=0, tiled=True)
+    share = normed.T
+    shares = [share] + [shift(share, "zl", -d) for d in range(1, RING)]
+    block = jnp.zeros((RING * share.shape[0], tokens), BF16)
+    for d in range(RING):
+        block = lax.dynamic_update_slice_in_dim(block, shares[d], (zl + d) % RING * share.shape[0], axis=0)
     quarters = gather(block, False)
     upper, lower = jnp.concatenate(quarters[:2], axis=0), jnp.concatenate(quarters[2:], axis=0)
     upper1, lower3 = turn(upper, True, -1), turn(lower, True, 1)
@@ -198,7 +198,7 @@
         in_specs=[scalars] + vmem(2 * RING + 3),
         out_specs=vmem(4),
         out_shape=[jax.ShapeDtypeStruct((hid, tokens), BF16)] * 2
-        + [jax.ShapeDtypeStruct((5, hid // 2, width // RING), BF16)] * 2,
+        + [jax.ShapeDtypeStruct((4, hid // 2, width // RING), BF16)] * 2,
         scratch_shapes=[
             pltpu.VMEM((hid, tokens), BF16),
             pltpu.VMEM((2, RING, hid // 2, width // RING), BF16),
@@ -212,29 +212,24 @@
     arrived = shift(send, "c", 1)
     opposite, follow, lead = (add_up([keep[at], arrived[at]]) for at in range(3))
     passed = advance(opposite.astype(BF16))
-    follow_in = advance(follow.astype(BF16))
+    cross_in = advance(follow.astype(BF16), cross=True)
     lead_in = advance((lead + passed.astype(F32)).astype(BF16))
-    other_in = shift(jnp.stack([follow_in, lead_in]), "c", 1)
-
-    def finish(at, here, there):
-        left, right = jnp.where(core == 0, here, there), jnp.where(core == 0, there, here)
-        return (add_up([keep[at], arrived[at], left, right]) / (2 * RING)).astype(BF16)
-
-    mine_lead, mine_follow = finish(3, lead_in, other_in[0]), finish(4, follow_in, other_in[1])
-    next_lead = advance(mine_lead)
-    next_follow = advance(mine_follow)
+    mine = (add_up([keep[3], arrived[3], cross_in, lead_in]) / (2 * RING)).astype(BF16)
+    next_lead = advance(mine)
+    other_mine = shift(mine, "c", 1)
+    next_follow = advance(other_mine)
     far = advance(next_lead)
-    near = jnp.stack([next_lead, next_follow])
-    other_near = shift(near, "c", 1)
+    other_next_lead = shift(next_lead, "c", 1)
+    other_next_follow = shift(next_follow, "c", 1)
     other_far = shift(far, "c", 1)
     up_grad = pl.pallas_call(
         place_kernel,
-        in_specs=[scalars] + vmem(5),
+        in_specs=[scalars] + vmem(8),
         out_specs=vmem(1)[0],
         out_shape=jax.ShapeDtypeStruct((hid, width), BF16),
         name="place",
         cost_estimate=pl.CostEstimate(flops=0, bytes_accessed=4 * hid * width, transcendentals=0),
-    )(pos, jnp.stack([mine_lead, mine_follow]), near, far, other_near, other_far)
+    )(pos, mine, other_mine, next_lead, next_follow, other_next_lead, other_next_follow, far, other_far)
 
     parts = pl.pallas_call(
         input_grad_kernel,

time: 232 us -> 212 us (0.914)
  the two profiles are of different devices: /device:TPU:1 before, /device:TPU:69 now
where the time goes in v5:
time: 212 us; the launch traced here: 211 us
  starting transfers between devices  137 us (65%)
  waiting for transfers between devices  43.3 us (20%)
  Pallas kernels  24.6 us (12%)
  other arithmetic  2.82 us (1%)
  local copies, waits for them, and re-layouts  2.25 us (1%)
    ppermute x11, starting transfers between devices, shift(): lax.ppermute(value, axis, [(i, (i + by) % size) for i in range(size)])  56.3 us
    ppermute x15, starting transfers between devices, turn(): lax.ppermute(value, ('y', 'x', 'c'), [(flat(*s), flat(*target(*s))) for s...  44.3 us
    ppermute x6, starting transfers between devices, advance(): return lax.ppermute(value, ('zh', 'c'), pairs)  36.5 us
    ppermute x15, waiting for transfers between devices, turn(): lax.ppermute(value, ('y', 'x', 'c'), [(flat(*s), flat(*target(*s))) for s...  21.4 us
    ppermute x6, waiting for transfers between devices, advance(): return lax.ppermute(value, ('zh', 'c'), pairs)  17 us
    pallas_call x1, Pallas kernels, work(): pl.pallas_call(forward_kernel, in_specs=[scalars] + vmem(2 * RING + 3), o...  8.08 us
    pallas_call x1, Pallas kernels, work(): pl.pallas_call(input_grad_kernel, in_specs=vmem(2), out_specs=vmem(RING),...  5.16 us
    ppermute x11, waiting for transfers between devices, shift(): lax.ppermute(value, axis, [(i, (i + by) % size) for i in range(size)])  4.85 us
  transfers between devices with their start and end apart: 32, of which 14 were waited for; matrix products, arithmetic and copies ran while one was open for 2% of the time, Pallas kernels for 6%

profile of v5, /device:TPU:69, one launch (start us, length us, event | category | flops | bytes accessed | tf_op | source)
XLA Modules:
  0.0 211.3 jit_solution(5483287368430570957)
XLA Ops:
  2.6 4.7 %collective-permute-start = (bf16[96,512]{1,0:T(8,128)(2,1)}, bf16[96,512]{1,0:T(8,128)(2,1)S(1)}, u32[]{:S(2)}, u32[]{:S(2)}) collective-permute-start(bf16[96,512]{1,0:T(8,128)(2,1)} %bitcast.28), channel_id=1, source_target_pairs={{0,24},{8,0},{16,8},{24,16},{1,25},{9,1},{17,9},{25,17},{2,26},{10... | collective-permute-start | bytes 294920 | tf_op jit(solution)/shard_map/ppermute | solution.py:28
  10.2 3.5 %collective-permute-done.2 = bf16[96,512]{1,0:T(8,128)(2,1)S(1)} collective-permute-done((bf16[96,512]{1,0:T(8,128)(2,1)}, bf16[96,512]{1,0:T(8,128)(2,1)S(1)}, u32[]{:S(2)}, u32[]{:S(2)}) %collective-permute-start.2) | collective-permute-done | bytes 98336 | tf_op jit(solution)/shard_map/ppermute | solution.py:28
  13.8 4.6 %collective-permute-start.3 = (bf16[384,512]{1,0:T(8,128)(2,1)S(1)}, bf16[384,512]{1,0:T(8,128)(2,1)S(1)}, u32[]{:S(2)}, u32[]{:S(2)}) collective-permute-start(bf16[384,512]{1,0:T(8,128)(2,1)S(1)} %constant_dynamic-update-slice_fusion.2), channel_id=1, source_target_pairs={{0,96},{1,385},{32,0},{33,417},{64,32},{65,449},{96,64},{97,481},{... | collective-permute-start | bytes 1179656 | tf_op jit(solution)/shard_map/ppermute | solution.py:132
  23.3 4.0 %collective-permute-done.3 = bf16[384,512]{1,0:T(8,128)(2,1)S(1)} collective-permute-done((bf16[384,512]{1,0:T(8,128)(2,1)S(1)}, bf16[384,512]{1,0:T(8,128)(2,1)S(1)}, u32[]{:S(2)}, u32[]{:S(2)}) %collective-permute-start.3) | collective-permute-done | bytes 393248 | tf_op jit(solution)/shard_map/ppermute | solution.py:132
  29.6 3.0 %collective-permute-done.5 = bf16[384,512]{1,0:T(8,128)(2,1)S(1)} collective-permute-done((bf16[384,512]{1,0:T(8,128)(2,1)S(1)}, bf16[384,512]{1,0:T(8,128)(2,1)S(1)}, u32[]{:S(2)}, u32[]{:S(2)}) %collective-permute-start.5) | collective-permute-done | bytes 393248 | tf_op jit(solution)/shard_map/ppermute | solution.py:132
  32.7 2.8 %collective-permute-start.9 = (bf16[768,512]{1,0:T(8,128)(2,1)S(1)}, bf16[768,512]{1,0:T(8,128)(2,1)S(1)}, u32[]{:S(2)}, u32[]{:S(2)}) collective-permute-start(bf16[768,512]{1,0:T(8,128)(2,1)S(1)} %constant_dynamic-update-slice_fusion.refs_1_), channel_id=1, source_target_pairs={{0,128},{1,33},{32,160},{33,65},{64,192},{65,97},{96,224},{97,1},{... | collective-permute-start | bytes 2359304 | tf_op jit(solution)/shard_map/ppermute | solution.py:132
  37.9 2.9 %collective-permute-start.7 = (bf16[768,512]{1,0:T(8,128)(2,1)S(1)}, bf16[768,512]{1,0:T(8,128)(2,1)}, u32[]{:S(2)}, u32[]{:S(2)}) collective-permute-start(bf16[768,512]{1,0:T(8,128)(2,1)S(1)} %constant_dynamic-update-slice_fusion.refs_1_), channel_id=1, source_target_pairs={{0,384},{1,97},{32,416},{33,1},{64,448},{65,33},{96,480},{97,65},{... | collective-permute-start | bytes 2359304 | tf_op jit(solution)/shard_map/ppermute | solution.py:132
  45.8 2.8 %collective-permute-start.10 = (bf16[768,512]{1,0:T(8,128)(2,1)S(1)}, bf16[768,512]{1,0:T(8,128)(2,1)}, u32[]{:S(2)}, u32[]{:S(2)}) collective-permute-start(bf16[768,512]{1,0:T(8,128)(2,1)S(1)} %collective-permute-done.9.refs_5_.refs_7_), channel_id=1, source_target_pairs={{0,128},{1,33},{32,160},{33,65},{64,192},{65,97},{96,224},{97,1},{... | collective-permute-start | bytes 2359304 | tf_op jit(solution)/shard_map/ppermute | solution.py:132
  49.3 3.4 %order.1.up_ref.refs_10_ = bf16[192,6144]{1,0:T(8,128)(2,1)} custom-call(s32[4]{0:T(128)} %pad_add_fusion.pos_ref, bf16[192,6144]{1,0:T(8,128)(2,1)} %up_ref.1), custom_call_target="tpu_custom_call" | custom-call | bytes 4718592 | tf_op jit(solution)/shard_map/order/pallas_call | solution.py:167
  54.3 4.8 %early.1.refs_8_ = f32[192,512]{1,0:T(8,128)} custom-call(bf16[192,6144]{1,0:T(8,128)(2,1)} %order.1.up_ref.refs_10_, bf16[768,512]{1,0:T(8,128)(2,1)} %copy-done, bf16[768,512]{1,0:T(8,128)(2,1)} %copy-done.1, bf16[768,512]{1,0:T(8,128)(2,1)} %copy-done.2, bf16[768,512]{1,0:T(8,128)(2,1)} %collective-permute-done.7.refs_3_, ...), custom_call_target="tpu_custom_call" | custom-call | flops 905969664 | bytes 7000000 | tf_op jit(solution)/shard_map/early/pallas_call | solution.py:187
  59.5 3.2 %collective-permute-done.10.refs_5_ = bf16[768,512]{1,0:T(8,128)(2,1)} collective-permute-done((bf16[768,512]{1,0:T(8,128)(2,1)S(1)}, bf16[768,512]{1,0:T(8,128)(2,1)}, u32[]{:S(2)}, u32[]{:S(2)}) %collective-permute-start.10) | collective-permute-done | bytes 786464 | tf_op jit(solution)/shard_map/ppermute | solution.py:132
  62.7 8.1 %forward.1 = (bf16[192,512]{1,0:T(8,128)(2,1)}, bf16[192,512]{1,0:T(8,128)(2,1)}, bf16[4,96,1536]{2,1,0:T(8,128)(2,1)}, bf16[4,96,1536]{2,1,0:T(8,128)(2,1)}) custom-call(s32[4]{0:T(128)} %pad_add_fusion.pos_ref, bf16[768,512]{1,0:T(8,128)(2,1)} %copy-done, bf16[768,512]{1,0:T(8,128)(2,1)} %copy-done.1, bf16[768,512]{1,0:T(8,128)(2,1)} %copy-done.2, ...), custom_call_target="tpu_custom_call" | custom-call | flops 1811939328 | bytes 14000000 | tf_op jit(solution)/shard_map/forward/pallas_call | solution.py:196
  70.8 4.4 %collective-permute-start.21 = (bf16[4,96,1536]{2,1,0:T(8,128)(2,1)}, bf16[4,96,1536]{2,1,0:T(8,128)(2,1)S(1)}, u32[]{:S(2)}, u32[]{:S(2)}) collective-permute-start(bf16[4,96,1536]{2,1,0:T(8,128)(2,1)} %get-tuple-element.18), channel_id=1, source_target_pairs={{0,1},{1,0},{2,3},{3,2},{4,5},{5,4},{6,7},{7,6},{8,9},{9,8},{10,11... | collective-permute-start | bytes 3538952 | tf_op jit(solution)/shard_map/ppermute | solution.py:28
  75.2 5.2 %partial.1 = (bf16[1536,512]{1,0:T(8,128)(2,1)}, bf16[1536,512]{1,0:T(8,128)(2,1)}, bf16[1536,512]{1,0:T(8,128)(2,1)}, bf16[1536,512]{1,0:T(8,128)(2,1)}) custom-call(bf16[192,512]{1,0:T(8,128)(2,1)} %get-tuple-element.12.grad_ref, bf16[192,6144]{1,0:T(8,128)(2,1)} %order.1.up_ref.refs_10_), custom_call_target="tpu_custom_call" | custom-call | flops 1207959552 | bytes 9000000 | tf_op jit(solution)/shard_map/partial/pallas_call | solution.py:234
  80.3 5.3 %collective-permute-start.12 = (bf16[1536,512]{1,0:T(8,128)(2,1)}, bf16[1536,512]{1,0:T(8,128)(2,1)S(1)}, u32[]{:S(2)}, u32[]{:S(2)}) collective-permute-start(bf16[1536,512]{1,0:T(8,128)(2,1)} %get-tuple-element.14), channel_id=1, source_target_pairs={{0,128},{1,33},{32,160},{33,65},{64,192},{65,97},{96,224},{97,1},{... | collective-permute-start | bytes 4718600 | tf_op jit(solution)/shard_map/ppermute | solution.py:132
  87.6 3.2 %collective-permute-start.14 = (bf16[1536,512]{1,0:T(8,128)(2,1)}, bf16[1536,512]{1,0:T(8,128)(2,1)S(1)}, u32[]{:S(2)}, u32[]{:S(2)}) collective-permute-start(bf16[1536,512]{1,0:T(8,128)(2,1)} %get-tuple-element.16), channel_id=1, source_target_pairs={{0,384},{1,97},{32,416},{33,1},{64,448},{65,33},{96,480},{97,65},{... | collective-permute-start | bytes 4718600 | tf_op jit(solution)/shard_map/ppermute | solution.py:132
  90.9 10.2 %collective-permute-start.23 = (bf16[96,1536]{1,0:T(8,128)(2,1)S(1)}, bf16[96,1536]{1,0:T(8,128)(2,1)S(1)}, u32[]{:S(2)}, u32[]{:S(2)}) collective-permute-start(bf16[96,1536]{1,0:T(8,128)(2,1)S(1)} %get-tuple-element.20), channel_id=1, source_target_pairs={{0,2},{1,7},{2,4},{3,1},{4,6},{5,3},{6,0},{7,5},{8,10},{9,15},{10,... | collective-permute-start | bytes 884744 | tf_op jit(solution)/shard_map/ppermute | solution.py:142
  103.0 6.0 %collective-permute-done.23 = bf16[96,1536]{1,0:T(8,128)(2,1)S(1)} collective-permute-done((bf16[96,1536]{1,0:T(8,128)(2,1)S(1)}, bf16[96,1536]{1,0:T(8,128)(2,1)S(1)}, u32[]{:S(2)}, u32[]{:S(2)}) %collective-permute-start.23) | collective-permute-done | bytes 294944 | tf_op jit(solution)/shard_map/ppermute | solution.py:142
  109.1 7.1 %collective-permute-start.24 = (bf16[96,1536]{1,0:T(8,128)(2,1)S(1)}, bf16[96,1536]{1,0:T(8,128)(2,1)S(1)}, u32[]{:S(2)}, u32[]{:S(2)}) collective-permute-start(bf16[96,1536]{1,0:T(8,128)(2,1)S(1)} %fusion), channel_id=1, source_target_pairs={{0,2},{1,7},{2,4},{3,1},{4,6},{5,3},{6,0},{7,5},{8,10},{9,15},{10,... | collective-permute-start | bytes 884744 | tf_op jit(solution)/shard_map/ppermute | solution.py:142
  116.2 3.9 %collective-permute-done.13 = bf16[1536,512]{1,0:T(8,128)(2,1)S(1)} collective-permute-done((bf16[1536,512]{1,0:T(8,128)(2,1)}, bf16[1536,512]{1,0:T(8,128)(2,1)S(1)}, u32[]{:S(2)}, u32[]{:S(2)}) %collective-permute-start.13) | collective-permute-done | bytes 1572896 | tf_op jit(solution)/shard_map/ppermute | solution.py:132
  120.1 2.7 %collective-permute-done.14 = bf16[1536,512]{1,0:T(8,128)(2,1)S(1)} collective-permute-done((bf16[1536,512]{1,0:T(8,128)(2,1)}, bf16[1536,512]{1,0:T(8,128)(2,1)S(1)}, u32[]{:S(2)}, u32[]{:S(2)}) %collective-permute-start.14) | collective-permute-done | bytes 1572896 | tf_op jit(solution)/shard_map/ppermute | solution.py:132
  125.8 4.5 %collective-permute-start.17 = (bf16[384,512]{1,0:T(8,128)(2,1)S(1)}, bf16[384,512]{1,0:T(8,128)(2,1)S(1)}, u32[]{:S(2)}, u32[]{:S(2)}) collective-permute-start(bf16[384,512]{1,0:T(8,128)(2,1)S(1)} %get-tuple-element.22), channel_id=1, source_target_pairs={{0,96},{1,385},{32,0},{33,417},{64,32},{65,449},{96,64},{97,481},{... | collective-permute-start | bytes 1179656 | tf_op jit(solution)/shard_map/ppermute | solution.py:132
  132.7 4.7 %collective-permute-done.24 = bf16[96,1536]{1,0:T(8,128)(2,1)S(1)} collective-permute-done((bf16[96,1536]{1,0:T(8,128)(2,1)S(1)}, bf16[96,1536]{1,0:T(8,128)(2,1)S(1)}, u32[]{:S(2)}, u32[]{:S(2)}) %collective-permute-start.24) | collective-permute-done | bytes 294944 | tf_op jit(solution)/shard_map/ppermute | solution.py:142
  137.6 6.8 %collective-permute-start.26 = (bf16[96,1536]{1,0:T(8,128)(2,1)S(1)}, bf16[96,1536]{1,0:T(8,128)(2,1)S(1)}, u32[]{:S(2)}, u32[]{:S(2)}) collective-permute-start(bf16[96,1536]{1,0:T(8,128)(2,1)S(1)} %fusion.3.refs_0_), channel_id=1, source_target_pairs={{0,2},{1,7},{2,4},{3,1},{4,6},{5,3},{6,0},{7,5},{8,10},{9,15},{10,... | collective-permute-start | bytes 884744 | tf_op jit(solution)/shard_map/ppermute | solution.py:142
  144.4 3.3 %collective-permute-start.25 = (bf16[96,1536]{1,0:T(8,128)(2,1)S(1)}, bf16[96,1536]{1,0:T(8,128)(2,1)S(1)}, u32[]{:S(2)}, u32[]{:S(2)}) collective-permute-start(bf16[96,1536]{1,0:T(8,128)(2,1)S(1)} %fusion.3.refs_0_), channel_id=1, source_target_pairs={{0,1},{1,0},{2,3},{3,2},{4,5},{5,4},{6,7},{7,6},{8,9},{9,8},{10,11... | collective-permute-start | bytes 884744 | tf_op jit(solution)/shard_map/ppermute | solution.py:28
  147.8 6.3 %collective-permute-done.26.refs_2_ = bf16[96,1536]{1,0:T(8,128)(2,1)S(1)} collective-permute-done((bf16[96,1536]{1,0:T(8,128)(2,1)S(1)}, bf16[96,1536]{1,0:T(8,128)(2,1)S(1)}, u32[]{:S(2)}, u32[]{:S(2)}) %collective-permute-start.26) | collective-permute-done | bytes 294944 | tf_op jit(solution)/shard_map/ppermute | solution.py:142
  154.1 6.3 %collective-permute-start.30 = (bf16[96,1536]{1,0:T(8,128)(2,1)S(1)}, bf16[96,1536]{1,0:T(8,128)(2,1)S(1)}, u32[]{:S(2)}, u32[]{:S(2)}) collective-permute-start(bf16[96,1536]{1,0:T(8,128)(2,1)S(1)} %collective-permute-done.26.refs_2_), channel_id=1, source_target_pairs={{0,2},{1,7},{2,4},{3,1},{4,6},{5,3},{6,0},{7,5},{8,10},{9,15},{10,... | collective-permute-start | bytes 884744 | tf_op jit(solution)/shard_map/ppermute | solution.py:142
  160.4 4.2 %collective-permute-start.27 = (bf16[96,1536]{1,0:T(8,128)(2,1)S(1)}, bf16[96,1536]{1,0:T(8,128)(2,1)S(1)}, u32[]{:S(2)}, u32[]{:S(2)}) collective-permute-start(bf16[96,1536]{1,0:T(8,128)(2,1)S(1)} %collective-permute-done.25.refs_1_), channel_id=1, source_target_pairs={{0,2},{1,7},{2,4},{3,1},{4,6},{5,3},{6,0},{7,5},{8,10},{9,15},{10,... | collective-permute-start | bytes 884744 | tf_op jit(solution)/shard_map/ppermute | solution.py:142
  166.8 4.7 %collective-permute-start.20 = (bf16[96,512]{1,0:T(8,128)(2,1)S(1)}, bf16[96,512]{1,0:T(8,128)(2,1)S(1)}, u32[]{:S(2)}, u32[]{:S(2)}) collective-permute-start(bf16[96,512]{1,0:T(8,128)(2,1)S(1)} %get-tuple-element.25), channel_id=1, source_target_pairs={{0,24},{8,0},{16,8},{24,16},{1,25},{9,1},{17,9},{25,17},{2,26},{10... | collective-permute-start | bytes 294920 | tf_op jit(solution)/shard_map/ppermute | solution.py:28
  171.6 9.2 %collective-permute-start.19 = (bf16[96,512]{1,0:T(8,128)(2,1)S(1)}, bf16[96,512]{1,0:T(8,128)(2,1)S(1)}, u32[]{:S(2)}, u32[]{:S(2)}) collective-permute-start(bf16[96,512]{1,0:T(8,128)(2,1)S(1)} %get-tuple-element.26), channel_id=1, source_target_pairs={{0,16},{8,24},{16,0},{24,8},{1,17},{9,25},{17,1},{25,9},{2,18},{10... | collective-permute-start | bytes 294920 | tf_op jit(solution)/shard_map/ppermute | solution.py:28
  181.7 19.8 %collective-permute-start.28 = (bf16[96,1536]{1,0:T(8,128)(2,1)S(1)}, bf16[96,1536]{1,0:T(8,128)(2,1)S(1)}, u32[]{:S(2)}, u32[]{:S(2)}) collective-permute-start(bf16[96,1536]{1,0:T(8,128)(2,1)S(1)} %collective-permute-done.26.refs_2_), channel_id=1, source_target_pairs={{0,1},{1,0},{2,3},{3,2},{4,5},{5,4},{6,7},{7,6},{8,9},{9,8},{10,11... | collective-permute-start | bytes 884744 | tf_op jit(solution)/shard_map/ppermute | solution.py:28
  208.2 3.2 %place.1 = bf16[192,6144]{1,0:T(8,128)(2,1)} custom-call(s32[4]{0:T(128)} %pad_add_fusion.pos_ref, bf16[96,1536]{1,0:T(8,128)(2,1)} %copy-done.5, bf16[96,1536]{1,0:T(8,128)(2,1)} %copy-done.8, bf16[96,1536]{1,0:T(8,128)(2,1)} %copy-done.7, bf16[96,1536]{1,0:T(8,128)(2,1)} %copy-done.10, bf16[96,1536]{1,0:T(8,128)(2,1)} %copy-done.11, ...), custom_call_target="tpu_custom_call" | custom-call | bytes 4718592 | tf_op jit(solution)/shard_map/place/pallas_call | solution.py:225
  (82 shorter events, 41.2 us)
Async XLA Ops:
  0.6 9.6 %collective-permute-start.1 = (bf16[96,512]{1,0:T(8,128)(2,1)}, bf16[96,512]{1,0:T(8,128)(2,1)S(1)}, u32[]{:S(2)}, u32[]{:S(2)}) collective-permute-start(bf16[96,512]{1,0:T(8,128)(2,1)} %bitcast.27), channel_id=1, source_target_pairs={{0,16},{8,24},{16,0},{24,8},{1,17},{9,25},{17,1},{25,9},{2,18},{10... | collective-permute-start | bytes 294920 | tf_op jit(solution)/shard_map/ppermute | solution.py:28
  2.6 7.6 %collective-permute-start = (bf16[96,512]{1,0:T(8,128)(2,1)}, bf16[96,512]{1,0:T(8,128)(2,1)S(1)}, u32[]{:S(2)}, u32[]{:S(2)}) collective-permute-start(bf16[96,512]{1,0:T(8,128)(2,1)} %bitcast.28), channel_id=1, source_target_pairs={{0,24},{8,0},{16,8},{24,16},{1,25},{9,1},{17,9},{25,17},{2,26},{10... | collective-permute-start | bytes 294920 | tf_op jit(solution)/shard_map/ppermute | solution.py:28
  7.3 6.5 %collective-permute-start.2 = (bf16[96,512]{1,0:T(8,128)(2,1)}, bf16[96,512]{1,0:T(8,128)(2,1)S(1)}, u32[]{:S(2)}, u32[]{:S(2)}) collective-permute-start(bf16[96,512]{1,0:T(8,128)(2,1)} %bitcast.29), channel_id=1, source_target_pairs={{0,8},{8,16},{16,24},{24,0},{1,9},{9,17},{17,25},{25,1},{2,10},{10... | collective-permute-start | bytes 294920 | tf_op jit(solution)/shard_map/ppermute | solution.py:28
  13.8 13.6 %collective-permute-start.3 = (bf16[384,512]{1,0:T(8,128)(2,1)S(1)}, bf16[384,512]{1,0:T(8,128)(2,1)S(1)}, u32[]{:S(2)}, u32[]{:S(2)}) collective-permute-start(bf16[384,512]{1,0:T(8,128)(2,1)S(1)} %constant_dynamic-update-slice_fusion.2), channel_id=1, source_target_pairs={{0,96},{1,385},{32,0},{33,417},{64,32},{65,449},{96,64},{97,481},{... | collective-permute-start | bytes 1179656 | tf_op jit(solution)/shard_map/ppermute | solution.py:132
  18.4 11.2 %collective-permute-start.4 = (bf16[384,512]{1,0:T(8,128)(2,1)S(1)}, bf16[384,512]{1,0:T(8,128)(2,1)S(1)}, u32[]{:S(2)}, u32[]{:S(2)}) collective-permute-start(bf16[384,512]{1,0:T(8,128)(2,1)S(1)} %constant_dynamic-update-slice_fusion.2), channel_id=1, source_target_pairs={{0,64},{1,257},{32,96},{33,289},{64,0},{65,321},{96,32},{97,353},{... | collective-permute-start | bytes 1179656 | tf_op jit(solution)/shard_map/ppermute | solution.py:132
  20.7 12.0 %collective-permute-start.5 = (bf16[384,512]{1,0:T(8,128)(2,1)S(1)}, bf16[384,512]{1,0:T(8,128)(2,1)S(1)}, u32[]{:S(2)}, u32[]{:S(2)}) collective-permute-start(bf16[384,512]{1,0:T(8,128)(2,1)S(1)} %constant_dynamic-update-slice_fusion.2), channel_id=1, source_target_pairs={{0,32},{1,129},{32,64},{33,161},{64,96},{65,193},{96,0},{97,225},{... | collective-permute-start | bytes 1179656 | tf_op jit(solution)/shard_map/ppermute | solution.py:132
  27.4 13.4 %collective-permute-start.6 = (bf16[768,512]{1,0:T(8,128)(2,1)S(1)}, bf16[768,512]{1,0:T(8,128)(2,1)S(1)}, u32[]{:S(2)}, u32[]{:S(2)}) collective-permute-start(bf16[768,512]{1,0:T(8,128)(2,1)S(1)} %pad_maximum_fusion.refs_0_), channel_id=1, source_target_pairs={{0,384},{1,97},{32,416},{33,1},{64,448},{65,33},{96,480},{97,65},{... | collective-permute-start | bytes 2359304 | tf_op jit(solution)/shard_map/ppermute | solution.py:132
  32.7 13.1 %collective-permute-start.9 = (bf16[768,512]{1,0:T(8,128)(2,1)S(1)}, bf16[768,512]{1,0:T(8,128)(2,1)S(1)}, u32[]{:S(2)}, u32[]{:S(2)}) collective-permute-start(bf16[768,512]{1,0:T(8,128)(2,1)S(1)} %constant_dynamic-update-slice_fusion.refs_1_), channel_id=1, source_target_pairs={{0,128},{1,33},{32,160},{33,65},{64,192},{65,97},{96,224},{97,1},{... | collective-permute-start | bytes 2359304 | tf_op jit(solution)/shard_map/ppermute | solution.py:132
  35.5 18.7 %collective-permute-start.11 = (bf16[768,512]{1,0:T(8,128)(2,1)S(1)}, bf16[768,512]{1,0:T(8,128)(2,1)}, u32[]{:S(2)}, u32[]{:S(2)}) collective-permute-start(bf16[768,512]{1,0:T(8,128)(2,1)S(1)} %pad_maximum_fusion.refs_0_), channel_id=1, source_target_pairs={{0,128},{1,33},{32,160},{33,65},{64,192},{65,97},{96,224},{97,1},{... | collective-permute-start | bytes 2359304 | tf_op jit(solution)/shard_map/ppermute | solution.py:132
  37.9 16.3 %collective-permute-start.7 = (bf16[768,512]{1,0:T(8,128)(2,1)S(1)}, bf16[768,512]{1,0:T(8,128)(2,1)}, u32[]{:S(2)}, u32[]{:S(2)}) collective-permute-start(bf16[768,512]{1,0:T(8,128)(2,1)S(1)} %constant_dynamic-update-slice_fusion.refs_1_), channel_id=1, source_target_pairs={{0,384},{1,97},{32,416},{33,1},{64,448},{65,33},{96,480},{97,65},{... | collective-permute-start | bytes 2359304 | tf_op jit(solution)/shard_map/ppermute | solution.py:132
  40.9 18.7 %collective-permute-start.8 = (bf16[768,512]{1,0:T(8,128)(2,1)S(1)}, bf16[768,512]{1,0:T(8,128)(2,1)}, u32[]{:S(2)}, u32[]{:S(2)}) collective-permute-start(bf16[768,512]{1,0:T(8,128)(2,1)S(1)} %collective-permute-done.6.refs_2_), channel_id=1, source_target_pairs={{0,384},{1,97},{32,416},{33,1},{64,448},{65,33},{96,480},{97,65},{... | collective-permute-start | bytes 2359304 | tf_op jit(solution)/shard_map/ppermute | solution.py:132
  45.8 16.9 %collective-permute-start.10 = (bf16[768,512]{1,0:T(8,128)(2,1)S(1)}, bf16[768,512]{1,0:T(8,128)(2,1)}, u32[]{:S(2)}, u32[]{:S(2)}) collective-permute-start(bf16[768,512]{1,0:T(8,128)(2,1)S(1)} %collective-permute-done.9.refs_5_.refs_7_), channel_id=1, source_target_pairs={{0,128},{1,33},{32,160},{33,65},{64,192},{65,97},{96,224},{97,1},{... | collective-permute-start | bytes 2359304 | tf_op jit(solution)/shard_map/ppermute | solution.py:132
  70.8 20.0 %collective-permute-start.21 = (bf16[4,96,1536]{2,1,0:T(8,128)(2,1)}, bf16[4,96,1536]{2,1,0:T(8,128)(2,1)S(1)}, u32[]{:S(2)}, u32[]{:S(2)}) collective-permute-start(bf16[4,96,1536]{2,1,0:T(8,128)(2,1)} %get-tuple-element.18), channel_id=1, source_target_pairs={{0,1},{1,0},{2,3},{3,2},{4,5},{5,4},{6,7},{7,6},{8,9},{9,8},{10,11... | collective-permute-start | bytes 3538952 | tf_op jit(solution)/shard_map/ppermute | solution.py:28
  80.3 35.9 %collective-permute-start.12 = (bf16[1536,512]{1,0:T(8,128)(2,1)}, bf16[1536,512]{1,0:T(8,128)(2,1)S(1)}, u32[]{:S(2)}, u32[]{:S(2)}) collective-permute-start(bf16[1536,512]{1,0:T(8,128)(2,1)} %get-tuple-element.14), channel_id=1, source_target_pairs={{0,128},{1,33},{32,160},{33,65},{64,192},{65,97},{96,224},{97,1},{... | collective-permute-start | bytes 4718600 | tf_op jit(solution)/shard_map/ppermute | solution.py:132
  85.6 34.5 %collective-permute-start.13 = (bf16[1536,512]{1,0:T(8,128)(2,1)}, bf16[1536,512]{1,0:T(8,128)(2,1)S(1)}, u32[]{:S(2)}, u32[]{:S(2)}) collective-permute-start(bf16[1536,512]{1,0:T(8,128)(2,1)} %get-tuple-element.15), channel_id=1, source_target_pairs={{0,256},{1,65},{32,288},{33,97},{64,320},{65,1},{96,352},{97,33},{... | collective-permute-start | bytes 4718600 | tf_op jit(solution)/shard_map/ppermute | solution.py:132
  87.6 35.3 %collective-permute-start.14 = (bf16[1536,512]{1,0:T(8,128)(2,1)}, bf16[1536,512]{1,0:T(8,128)(2,1)S(1)}, u32[]{:S(2)}, u32[]{:S(2)}) collective-permute-start(bf16[1536,512]{1,0:T(8,128)(2,1)} %get-tuple-element.16), channel_id=1, source_target_pairs={{0,384},{1,97},{32,416},{33,1},{64,448},{65,33},{96,480},{97,65},{... | collective-permute-start | bytes 4718600 | tf_op jit(solution)/shard_map/ppermute | solution.py:132
  90.9 18.1 %collective-permute-start.23 = (bf16[96,1536]{1,0:T(8,128)(2,1)S(1)}, bf16[96,1536]{1,0:T(8,128)(2,1)S(1)}, u32[]{:S(2)}, u32[]{:S(2)}) collective-permute-start(bf16[96,1536]{1,0:T(8,128)(2,1)S(1)} %get-tuple-element.20), channel_id=1, source_target_pairs={{0,2},{1,7},{2,4},{3,1},{4,6},{5,3},{6,0},{7,5},{8,10},{9,15},{10,... | collective-permute-start | bytes 884744 | tf_op jit(solution)/shard_map/ppermute | solution.py:142
  101.1 31.6 %collective-permute-start.22 = (bf16[96,1536]{1,0:T(8,128)(2,1)S(1)}, bf16[96,1536]{1,0:T(8,128)(2,1)S(1)}, u32[]{:S(2)}, u32[]{:S(2)}) collective-permute-start(bf16[96,1536]{1,0:T(8,128)(2,1)S(1)} %get-tuple-element.19), channel_id=1, source_target_pairs={{0,3},{1,6},{2,5},{3,0},{4,7},{5,2},{6,1},{7,4},{8,11},{9,14},{10,... | collective-permute-start | bytes 884744 | tf_op jit(solution)/shard_map/ppermute | solution.py:142
  109.1 28.3 %collective-permute-start.24 = (bf16[96,1536]{1,0:T(8,128)(2,1)S(1)}, bf16[96,1536]{1,0:T(8,128)(2,1)S(1)}, u32[]{:S(2)}, u32[]{:S(2)}) collective-permute-start(bf16[96,1536]{1,0:T(8,128)(2,1)S(1)} %fusion), channel_id=1, source_target_pairs={{0,2},{1,7},{2,4},{3,1},{4,6},{5,3},{6,0},{7,5},{8,10},{9,15},{10,... | collective-permute-start | bytes 884744 | tf_op jit(solution)/shard_map/ppermute | solution.py:142
  123.8 40.9 %collective-permute-start.15 = (bf16[384,512]{1,0:T(8,128)(2,1)S(1)}, bf16[384,512]{1,0:T(8,128)(2,1)S(1)}, u32[]{:S(2)}, u32[]{:S(2)}) collective-permute-start(bf16[384,512]{1,0:T(8,128)(2,1)S(1)} %get-tuple-element.21), channel_id=1, source_target_pairs={{0,32},{1,129},{32,64},{33,161},{64,96},{65,193},{96,0},{97,225},{... | collective-permute-start | bytes 1179656 | tf_op jit(solution)/shard_map/ppermute | solution.py:132
  125.8 38.9 %collective-permute-start.17 = (bf16[384,512]{1,0:T(8,128)(2,1)S(1)}, bf16[384,512]{1,0:T(8,128)(2,1)S(1)}, u32[]{:S(2)}, u32[]{:S(2)}) collective-permute-start(bf16[384,512]{1,0:T(8,128)(2,1)S(1)} %get-tuple-element.22), channel_id=1, source_target_pairs={{0,96},{1,385},{32,0},{33,417},{64,32},{65,449},{96,64},{97,481},{... | collective-permute-start | bytes 1179656 | tf_op jit(solution)/shard_map/ppermute | solution.py:132
  130.3 34.4 %collective-permute-start.16 = (bf16[384,512]{1,0:T(8,128)(2,1)S(1)}, bf16[384,512]{1,0:T(8,128)(2,1)S(1)}, u32[]{:S(2)}, u32[]{:S(2)}) collective-permute-start(bf16[384,512]{1,0:T(8,128)(2,1)S(1)} %get-tuple-element.23), channel_id=1, source_target_pairs={{0,64},{1,257},{32,96},{33,289},{64,0},{65,321},{96,32},{97,353},{... | collective-permute-start | bytes 1179656 | tf_op jit(solution)/shard_map/ppermute | solution.py:132
  137.6 16.5 %collective-permute-start.26 = (bf16[96,1536]{1,0:T(8,128)(2,1)S(1)}, bf16[96,1536]{1,0:T(8,128)(2,1)S(1)}, u32[]{:S(2)}, u32[]{:S(2)}) collective-permute-start(bf16[96,1536]{1,0:T(8,128)(2,1)S(1)} %fusion.3.refs_0_), channel_id=1, source_target_pairs={{0,2},{1,7},{2,4},{3,1},{4,6},{5,3},{6,0},{7,5},{8,10},{9,15},{10,... | collective-permute-start | bytes 884744 | tf_op jit(solution)/shard_map/ppermute | solution.py:142
  144.4 16.0 %collective-permute-start.25 = (bf16[96,1536]{1,0:T(8,128)(2,1)S(1)}, bf16[96,1536]{1,0:T(8,128)(2,1)S(1)}, u32[]{:S(2)}, u32[]{:S(2)}) collective-permute-start(bf16[96,1536]{1,0:T(8,128)(2,1)S(1)} %fusion.3.refs_0_), channel_id=1, source_target_pairs={{0,1},{1,0},{2,3},{3,2},{4,5},{5,4},{6,7},{7,6},{8,9},{9,8},{10,11... | collective-permute-start | bytes 884744 | tf_op jit(solution)/shard_map/ppermute | solution.py:28
  154.1 47.4 %collective-permute-start.30 = (bf16[96,1536]{1,0:T(8,128)(2,1)S(1)}, bf16[96,1536]{1,0:T(8,128)(2,1)S(1)}, u32[]{:S(2)}, u32[]{:S(2)}) collective-permute-start(bf16[96,1536]{1,0:T(8,128)(2,1)S(1)} %collective-permute-done.26.refs_2_), channel_id=1, source_target_pairs={{0,2},{1,7},{2,4},{3,1},{4,6},{5,3},{6,0},{7,5},{8,10},{9,15},{10,... | collective-permute-start | bytes 884744 | tf_op jit(solution)/shard_map/ppermute | solution.py:142
  160.4 43.1 %collective-permute-start.27 = (bf16[96,1536]{1,0:T(8,128)(2,1)S(1)}, bf16[96,1536]{1,0:T(8,128)(2,1)S(1)}, u32[]{:S(2)}, u32[]{:S(2)}) collective-permute-start(bf16[96,1536]{1,0:T(8,128)(2,1)S(1)} %collective-permute-done.25.refs_1_), channel_id=1, source_target_pairs={{0,2},{1,7},{2,4},{3,1},{4,6},{5,3},{6,0},{7,5},{8,10},{9,15},{10,... | collective-permute-start | bytes 884744 | tf_op jit(solution)/shard_map/ppermute | solution.py:142
  164.9 16.7 %collective-permute-start.18 = (bf16[96,512]{1,0:T(8,128)(2,1)S(1)}, bf16[96,512]{1,0:T(8,128)(2,1)S(1)}, u32[]{:S(2)}, u32[]{:S(2)}) collective-permute-start(bf16[96,512]{1,0:T(8,128)(2,1)S(1)} %get-tuple-element.24), channel_id=1, source_target_pairs={{0,8},{8,16},{16,24},{24,0},{1,9},{9,17},{17,25},{25,1},{2,10},{10... | collective-permute-start | bytes 294920 | tf_op jit(solution)/shard_map/ppermute | solution.py:28
  166.8 39.1 %collective-permute-start.20 = (bf16[96,512]{1,0:T(8,128)(2,1)S(1)}, bf16[96,512]{1,0:T(8,128)(2,1)S(1)}, u32[]{:S(2)}, u32[]{:S(2)}) collective-permute-start(bf16[96,512]{1,0:T(8,128)(2,1)S(1)} %get-tuple-element.25), channel_id=1, source_target_pairs={{0,24},{8,0},{16,8},{24,16},{1,25},{9,1},{17,9},{25,17},{2,26},{10... | collective-permute-start | bytes 294920 | tf_op jit(solution)/shard_map/ppermute | solution.py:28
  171.6 34.3 %collective-permute-start.19 = (bf16[96,512]{1,0:T(8,128)(2,1)S(1)}, bf16[96,512]{1,0:T(8,128)(2,1)S(1)}, u32[]{:S(2)}, u32[]{:S(2)}) collective-permute-start(bf16[96,512]{1,0:T(8,128)(2,1)S(1)} %get-tuple-element.26), channel_id=1, source_target_pairs={{0,16},{8,24},{16,0},{24,8},{1,17},{9,25},{17,1},{25,9},{2,18},{10... | collective-permute-start | bytes 294920 | tf_op jit(solution)/shard_map/ppermute | solution.py:28
  181.7 25.0 %collective-permute-start.28 = (bf16[96,1536]{1,0:T(8,128)(2,1)S(1)}, bf16[96,1536]{1,0:T(8,128)(2,1)S(1)}, u32[]{:S(2)}, u32[]{:S(2)}) collective-permute-start(bf16[96,1536]{1,0:T(8,128)(2,1)S(1)} %collective-permute-done.26.refs_2_), channel_id=1, source_target_pairs={{0,1},{1,0},{2,3},{3,2},{4,5},{5,4},{6,7},{7,6},{8,9},{9,8},{10,11... | collective-permute-start | bytes 884744 | tf_op jit(solution)/shard_map/ppermute | solution.py:28
  201.5 5.1 %collective-permute-start.31 = (bf16[96,1536]{1,0:T(8,128)(2,1)S(1)}, bf16[96,1536]{1,0:T(8,128)(2,1)S(1)}, u32[]{:S(2)}, u32[]{:S(2)}) collective-permute-start(bf16[96,1536]{1,0:T(8,128)(2,1)S(1)} %collective-permute-done.30.refs_6_), channel_id=1, source_target_pairs={{0,1},{1,0},{2,3},{3,2},{4,5},{5,4},{6,7},{7,6},{8,9},{9,8},{10,11... | collective-permute-start | bytes 884744 | tf_op jit(solution)/shard_map/ppermute | solution.py:28
  203.5 3.6 %collective-permute-start.29 = (bf16[96,1536]{1,0:T(8,128)(2,1)S(1)}, bf16[96,1536]{1,0:T(8,128)(2,1)S(1)}, u32[]{:S(2)}, u32[]{:S(2)}) collective-permute-start(bf16[96,1536]{1,0:T(8,128)(2,1)S(1)} %collective-permute-done.27.refs_3_), channel_id=1, source_target_pairs={{0,1},{1,0},{2,3},{3,2},{4,5},{5,4},{6,7},{7,6},{8,9},{9,8},{10,11... | collective-permute-start | bytes 884744 | tf_op jit(solution)/shard_map/ppermute | solution.py:28
  (14 other events, 302.6 us)

commit v6 on v5

--- a/solution.py
+++ b/solution.py
@@ -105,14 +105,26 @@
 
 def place_kernel(pos_ref, *refs):
     core, zh = pos_ref[2], pos_ref[3]
-    out_ref = refs[-1]
-    rows, depth = refs[0].shape
-    lead = pl.ds(pl.multiple_of(core * rows, 16), rows)
-    follow = pl.ds(pl.multiple_of((1 - core) * rows, 16), rows)
+    pieces, (out_ref, whole_ref, sems) = refs[:8], refs[8:]
+    rows, depth = pieces[0].shape
     behind, ahead = 3 - 2 * core, 1 + 2 * core
-    spots = ((lead, 0), (follow, 0), (lead, behind), (follow, behind), (follow, ahead), (lead, ahead), (lead, 2), (follow, 2))
-    for ref, (where, d) in zip(refs[:-1], spots):
-        out_ref[where, pl.ds(pl.multiple_of(lax.rem(zh + d, RING) * depth, 128), depth)] = ref[...]
+    halves = []
+    for half, places in ((core, ((0, 0), (2, behind), (5, ahead), (6, 2))), (1 - core, ((1, 0), (3, behind), (4, ahead), (7, 2)))):
+        where = pl.ds(pl.multiple_of(half * rows, 16), rows)
+        copies = []
+        for at, d in places:
+            columns = pl.ds(pl.multiple_of(lax.rem(zh + d, RING) * depth, 128), depth)
+            copies.append(pltpu.make_async_copy(pieces[at], whole_ref.at[where, columns], sems.at[at]))
+            copies[-1].start()
+        halves.append((where, copies))
+    outs = []
+    for at, (where, copies) in enumerate(halves):
+        for copy in copies:
+            copy.wait()
+        outs.append(pltpu.make_async_copy(whole_ref.at[where, :], out_ref.at[where, :], sems.at[8 + at]))
+        outs[-1].start()
+    for copy in outs:
+        copy.wait()
 
 
 def vmem(count):
@@ -224,9 +236,11 @@
     other_far = shift(far, "c", 1)
     up_grad = pl.pallas_call(
         place_kernel,
-        in_specs=[scalars] + vmem(8),
-        out_specs=vmem(1)[0],
+        in_specs=[scalars] + [pl.BlockSpec(memory_space=pl.ANY)] * 8,
+        out_specs=pl.BlockSpec(memory_space=pl.ANY),
         out_shape=jax.ShapeDtypeStruct((hid, width), BF16),
+        scratch_shapes=[pltpu.VMEM((hid, width), BF16), pltpu.SemaphoreType.DMA((10,))],
+        compiler_params=pltpu.CompilerParams(vmem_limit_bytes=8 << 20),
         name="place",
         cost_estimate=pl.CostEstimate(flops=0, bytes_accessed=4 * hid * width, transcendentals=0),
     )(pos, mine, other_mine, next_lead, next_follow, other_next_lead, other_next_follow, far, other_far)
@@ -243,10 +257,17 @@
     )(hidden_grad, ordered)
     stage = scatter_sum(parts, True).astype(BF16)
     depth = stage.shape[0] // RING
-    stage = scatter_sum([stage[d * depth : (d + 1) * depth] for d in range(RING)], False).astype(BF16)
-    depth = stage.shape[0] // RING
-    shares = [lax.dynamic_slice_in_dim(stage, ((zl + d) % RING) * depth, depth, axis=0) for d in range(RING)]
-    input_grad = add_up(shares[:1] + [shift(shares[d], "zl", d) for d in range(1, RING)]).astype(BF16)
+    blocks = [stage[d * depth : (d + 1) * depth] for d in range(RING)]
+    arrived = [turn(blocks[2], False, 2), turn(blocks[1], False, 1)]
+    arrived += [turn(blocks[3], False, 3)]
+    stage = add_up([blocks[0]] + arrived).astype(BF16)
+    for bit in (2, 1):
+        depth = stage.shape[0] // 2
+        side = zl // bit % 2
+        other = lax.dynamic_slice_in_dim(stage, (1 - side) * depth, depth, axis=0)
+        arrived = lax.ppermute(other, "zl", [(i, i ^ bit) for i in range(RING)])
+        stage = add_up([lax.dynamic_slice_in_dim(stage, side * depth, depth, axis=0), arrived]).astype(BF16)
+    input_grad = stage
     return (hidden.T, input_grad.T, up_grad)
 
 

time: 212 us -> 213 us (level)
  the two profiles are of different devices: /device:TPU:69 before, /device:TPU:7 now
where the time goes in v6:
time: 213 us; the launch traced here: 212 us
  starting transfers between devices  126 us (59%)
  waiting for transfers between devices  51.9 us (24%)
  Pallas kernels  23.6 us (11%)
  other arithmetic  8.82 us (4%)
    ppermute x15, starting transfers between devices, turn(): lax.ppermute(value, ('y', 'x', 'c'), [(flat(*s), flat(*target(*s))) for s...  52.4 us
    ppermute x6, starting transfers between devices, advance(): return lax.ppermute(value, ('zh', 'c'), pairs)  36 us
    ppermute x8, starting transfers between devices, shift(): lax.ppermute(value, axis, [(i, (i + by) % size) for i in range(size)])  30.3 us
    ppermute x2, waiting for transfers between devices, work(): arrived = lax.ppermute(other, 'zl', [(i, i ^ bit) for i in range(RING)])  26.9 us
    ppermute x15, waiting for transfers between devices, turn(): lax.ppermute(value, ('y', 'x', 'c'), [(flat(*s), flat(*target(*s))) for s...  12.2 us
    ppermute x6, waiting for transfers between devices, advance(): return lax.ppermute(value, ('zh', 'c'), pairs)  8.16 us
    pallas_call x1, Pallas kernels, work(): pl.pallas_call(forward_kernel, in_specs=[scalars] + vmem(2 * RING + 3), o...  8 us
    ppermute x2, starting transfers between devices, work(): arrived = lax.ppermute(other, 'zl', [(i, i ^ bit) for i in range(RING)])  6.86 us
  transfers between devices with their start and end apart: 31, of which 11 were waited for; matrix products, arithmetic and copies ran while one was open for 5% of the time, Pallas kernels for 6%

profile of v6, /device:TPU:7, one launch (start us, length us, event | category | flops | bytes accessed | tf_op | source)
XLA Modules:
  0.0 212.3 jit_solution(6005211440429876030)
XLA Ops:
  0.6 6.3 %collective-permute-start = (bf16[96,512]{1,0:T(8,128)(2,1)}, bf16[96,512]{1,0:T(8,128)(2,1)S(1)}, u32[]{:S(2)}, u32[]{:S(2)}) collective-permute-start(bf16[96,512]{1,0:T(8,128)(2,1)} %bitcast.27), channel_id=1, source_target_pairs={{0,24},{8,0},{16,8},{24,16},{1,25},{9,1},{17,9},{25,17},{2,26},{10... | collective-permute-start | bytes 294920 | tf_op jit(solution)/shard_map/ppermute | solution.py:28
  13.4 2.8 %collective-permute-done.2 = bf16[96,512]{1,0:T(8,128)(2,1)S(1)} collective-permute-done((bf16[96,512]{1,0:T(8,128)(2,1)}, bf16[96,512]{1,0:T(8,128)(2,1)S(1)}, u32[]{:S(2)}, u32[]{:S(2)}) %collective-permute-start.2) | collective-permute-done | bytes 98336 | tf_op jit(solution)/shard_map/ppermute | solution.py:28
  16.2 4.8 %collective-permute-start.4 = (bf16[384,512]{1,0:T(8,128)(2,1)S(1)}, bf16[384,512]{1,0:T(8,128)(2,1)S(1)}, u32[]{:S(2)}, u32[]{:S(2)}) collective-permute-start(bf16[384,512]{1,0:T(8,128)(2,1)S(1)} %constant_dynamic-update-slice_fusion.2), channel_id=1, source_target_pairs={{0,64},{1,257},{32,96},{33,289},{64,0},{65,321},{96,32},{97,353},{... | collective-permute-start | bytes 1179656 | tf_op jit(solution)/shard_map/ppermute | solution.py:144
  23.4 4.2 %collective-permute-start.3 = (bf16[384,512]{1,0:T(8,128)(2,1)S(1)}, bf16[384,512]{1,0:T(8,128)(2,1)S(1)}, u32[]{:S(2)}, u32[]{:S(2)}) collective-permute-start(bf16[384,512]{1,0:T(8,128)(2,1)S(1)} %constant_dynamic-update-slice_fusion.2), channel_id=1, source_target_pairs={{0,96},{1,385},{32,0},{33,417},{64,32},{65,449},{96,64},{97,481},{... | collective-permute-start | bytes 1179656 | tf_op jit(solution)/shard_map/ppermute | solution.py:144
  27.6 3.2 %collective-permute-done.5 = bf16[384,512]{1,0:T(8,128)(2,1)S(1)} collective-permute-done((bf16[384,512]{1,0:T(8,128)(2,1)S(1)}, bf16[384,512]{1,0:T(8,128)(2,1)S(1)}, u32[]{:S(2)}, u32[]{:S(2)}) %collective-permute-start.5) | collective-permute-done | bytes 393248 | tf_op jit(solution)/shard_map/ppermute | solution.py:144
  30.8 2.5 %collective-permute-start.9 = (bf16[768,512]{1,0:T(8,128)(2,1)S(1)}, bf16[768,512]{1,0:T(8,128)(2,1)S(1)}, u32[]{:S(2)}, u32[]{:S(2)}) collective-permute-start(bf16[768,512]{1,0:T(8,128)(2,1)S(1)} %constant_dynamic-update-slice_fusion.refs_1_), channel_id=1, source_target_pairs={{0,128},{1,33},{32,160},{33,65},{64,192},{65,97},{96,224},{97,1},{... | collective-permute-start | bytes 2359304 | tf_op jit(solution)/shard_map/ppermute | solution.py:144
  33.4 2.8 %collective-permute-start.6 = (bf16[768,512]{1,0:T(8,128)(2,1)S(1)}, bf16[768,512]{1,0:T(8,128)(2,1)S(1)}, u32[]{:S(2)}, u32[]{:S(2)}) collective-permute-start(bf16[768,512]{1,0:T(8,128)(2,1)S(1)} %pad_maximum_fusion.refs_0_), channel_id=1, source_target_pairs={{0,384},{1,97},{32,416},{33,1},{64,448},{65,33},{96,480},{97,65},{... | collective-permute-start | bytes 2359304 | tf_op jit(solution)/shard_map/ppermute | solution.py:144
  36.2 2.5 %collective-permute-start.7 = (bf16[768,512]{1,0:T(8,128)(2,1)S(1)}, bf16[768,512]{1,0:T(8,128)(2,1)}, u32[]{:S(2)}, u32[]{:S(2)}) collective-permute-start(bf16[768,512]{1,0:T(8,128)(2,1)S(1)} %constant_dynamic-update-slice_fusion.refs_1_), channel_id=1, source_target_pairs={{0,384},{1,97},{32,416},{33,1},{64,448},{65,33},{96,480},{97,65},{... | collective-permute-start | bytes 2359304 | tf_op jit(solution)/shard_map/ppermute | solution.py:144
  38.7 4.0 %collective-permute-start.11 = (bf16[768,512]{1,0:T(8,128)(2,1)S(1)}, bf16[768,512]{1,0:T(8,128)(2,1)}, u32[]{:S(2)}, u32[]{:S(2)}) collective-permute-start(bf16[768,512]{1,0:T(8,128)(2,1)S(1)} %pad_maximum_fusion.refs_0_), channel_id=1, source_target_pairs={{0,128},{1,33},{32,160},{33,65},{64,192},{65,97},{96,224},{97,1},{... | collective-permute-start | bytes 2359304 | tf_op jit(solution)/shard_map/ppermute | solution.py:144
  43.8 3.7 %collective-permute-start.10 = (bf16[768,512]{1,0:T(8,128)(2,1)S(1)}, bf16[768,512]{1,0:T(8,128)(2,1)}, u32[]{:S(2)}, u32[]{:S(2)}) collective-permute-start(bf16[768,512]{1,0:T(8,128)(2,1)S(1)} %collective-permute-done.9.refs_5_.refs_7_), channel_id=1, source_target_pairs={{0,128},{1,33},{32,160},{33,65},{64,192},{65,97},{96,224},{97,1},{... | collective-permute-start | bytes 2359304 | tf_op jit(solution)/shard_map/ppermute | solution.py:144
  50.0 3.3 %order.1.up_ref.refs_10_ = bf16[192,6144]{1,0:T(8,128)(2,1)} custom-call(s32[4]{0:T(128)} %pad_add_fusion.pos_ref, bf16[192,6144]{1,0:T(8,128)(2,1)} %up_ref.1), custom_call_target="tpu_custom_call" | custom-call | bytes 4718592 | tf_op jit(solution)/shard_map/order/pallas_call | solution.py:179
  53.4 2.7 %collective-permute-done.7.refs_3_ = bf16[768,512]{1,0:T(8,128)(2,1)} collective-permute-done((bf16[768,512]{1,0:T(8,128)(2,1)S(1)}, bf16[768,512]{1,0:T(8,128)(2,1)}, u32[]{:S(2)}, u32[]{:S(2)}) %collective-permute-start.7) | collective-permute-done | bytes 786464 | tf_op jit(solution)/shard_map/ppermute | solution.py:144
  56.1 4.9 %early.1.refs_8_ = f32[192,512]{1,0:T(8,128)} custom-call(bf16[192,6144]{1,0:T(8,128)(2,1)} %order.1.up_ref.refs_10_, bf16[768,512]{1,0:T(8,128)(2,1)} %copy-done.1, bf16[768,512]{1,0:T(8,128)(2,1)} %copy-done.2, bf16[768,512]{1,0:T(8,128)(2,1)} %copy-done.4, bf16[768,512]{1,0:T(8,128)(2,1)} %collective-permute-done.7.refs_3_, ...), custom_call_target="tpu_custom_call" | custom-call | flops 905969664 | bytes 7000000 | tf_op jit(solution)/shard_map/early/pallas_call | solution.py:199
  61.0 3.6 %collective-permute-done.8.refs_4_ = bf16[768,512]{1,0:T(8,128)(2,1)} collective-permute-done((bf16[768,512]{1,0:T(8,128)(2,1)S(1)}, bf16[768,512]{1,0:T(8,128)(2,1)}, u32[]{:S(2)}, u32[]{:S(2)}) %collective-permute-start.8) | collective-permute-done | bytes 786464 | tf_op jit(solution)/shard_map/ppermute | solution.py:144
  64.6 8.0 %forward.1 = (bf16[192,512]{1,0:T(8,128)(2,1)}, bf16[192,512]{1,0:T(8,128)(2,1)}, bf16[4,96,1536]{2,1,0:T(8,128)(2,1)}, bf16[4,96,1536]{2,1,0:T(8,128)(2,1)}) custom-call(s32[4]{0:T(128)} %pad_add_fusion.pos_ref, bf16[768,512]{1,0:T(8,128)(2,1)} %copy-done.1, bf16[768,512]{1,0:T(8,128)(2,1)} %copy-done.2, bf16[768,512]{1,0:T(8,128)(2,1)} %copy-done.4, ...), custom_call_target="tpu_custom_call" | custom-call | flops 1811939328 | bytes 14000000 | tf_op jit(solution)/shard_map/forward/pallas_call | solution.py:208
  72.6 5.2 %collective-permute-start.20 = (bf16[4,96,1536]{2,1,0:T(8,128)(2,1)}, bf16[4,96,1536]{2,1,0:T(8,128)(2,1)}, u32[]{:S(2)}, u32[]{:S(2)}) collective-permute-start(bf16[4,96,1536]{2,1,0:T(8,128)(2,1)} %get-tuple-element.18), channel_id=1, source_target_pairs={{0,1},{1,0},{2,3},{3,2},{4,5},{5,4},{6,7},{7,6},{8,9},{9,8},{10,11... | collective-permute-start | bytes 3538952 | tf_op jit(solution)/shard_map/ppermute | solution.py:28
  77.8 5.0 %partial.1 = (bf16[1536,512]{1,0:T(8,128)(2,1)}, bf16[1536,512]{1,0:T(8,128)(2,1)}, bf16[1536,512]{1,0:T(8,128)(2,1)}, bf16[1536,512]{1,0:T(8,128)(2,1)}) custom-call(bf16[192,512]{1,0:T(8,128)(2,1)} %get-tuple-element.12.grad_ref, bf16[192,6144]{1,0:T(8,128)(2,1)} %order.1.up_ref.refs_10_), custom_call_target="tpu_custom_call" | custom-call | flops 1207959552 | bytes 9000000 | tf_op jit(solution)/shard_map/partial/pallas_call | solution.py:248
  82.8 3.0 %collective-permute-start.12 = (bf16[1536,512]{1,0:T(8,128)(2,1)}, bf16[1536,512]{1,0:T(8,128)(2,1)S(1)}, u32[]{:S(2)}, u32[]{:S(2)}) collective-permute-start(bf16[1536,512]{1,0:T(8,128)(2,1)} %get-tuple-element.14), channel_id=1, source_target_pairs={{0,128},{1,33},{32,160},{33,65},{64,192},{65,97},{96,224},{97,1},{... | collective-permute-start | bytes 4718600 | tf_op jit(solution)/shard_map/ppermute | solution.py:144
  85.8 4.0 %collective-permute-start.13 = (bf16[1536,512]{1,0:T(8,128)(2,1)}, bf16[1536,512]{1,0:T(8,128)(2,1)}, u32[]{:S(2)}, u32[]{:S(2)}) collective-permute-start(bf16[1536,512]{1,0:T(8,128)(2,1)} %get-tuple-element.15), channel_id=1, source_target_pairs={{0,256},{1,65},{32,288},{33,97},{64,320},{65,1},{96,352},{97,33},{... | collective-permute-start | bytes 4718600 | tf_op jit(solution)/shard_map/ppermute | solution.py:144
  93.9 10.0 %collective-permute-start.22 = (bf16[96,1536]{1,0:T(8,128)(2,1)}, bf16[96,1536]{1,0:T(8,128)(2,1)}, u32[]{:S(2)}, u32[]{:S(2)}) collective-permute-start(bf16[96,1536]{1,0:T(8,128)(2,1)} %get-tuple-element.20), channel_id=1, source_target_pairs={{0,2},{1,7},{2,4},{3,1},{4,6},{5,3},{6,0},{7,5},{8,10},{9,15},{10,... | collective-permute-start | bytes 884744 | tf_op jit(solution)/shard_map/ppermute | solution.py:154
  103.9 4.5 %collective-permute-start.21 = (bf16[96,1536]{1,0:T(8,128)(2,1)S(1)}, bf16[96,1536]{1,0:T(8,128)(2,1)S(1)}, u32[]{:S(2)}, u32[]{:S(2)}) collective-permute-start(bf16[96,1536]{1,0:T(8,128)(2,1)S(1)} %get-tuple-element.19), channel_id=1, source_target_pairs={{0,3},{1,6},{2,5},{3,0},{4,7},{5,2},{6,1},{7,4},{8,11},{9,14},{10,... | collective-permute-start | bytes 884744 | tf_op jit(solution)/shard_map/ppermute | solution.py:154
  108.3 7.3 %collective-permute-done.22 = bf16[96,1536]{1,0:T(8,128)(2,1)} collective-permute-done((bf16[96,1536]{1,0:T(8,128)(2,1)}, bf16[96,1536]{1,0:T(8,128)(2,1)}, u32[]{:S(2)}, u32[]{:S(2)}) %collective-permute-start.22) | collective-permute-done | bytes 294944 | tf_op jit(solution)/shard_map/ppermute | solution.py:154
  116.9 7.2 %collective-permute-start.23 = (bf16[96,1536]{1,0:T(8,128)(2,1)S(1)}, bf16[96,1536]{1,0:T(8,128)(2,1)S(1)}, u32[]{:S(2)}, u32[]{:S(2)}) collective-permute-start(bf16[96,1536]{1,0:T(8,128)(2,1)S(1)} %fusion), channel_id=1, source_target_pairs={{0,2},{1,7},{2,4},{3,1},{4,6},{5,3},{6,0},{7,5},{8,10},{9,15},{10,... | collective-permute-start | bytes 884744 | tf_op jit(solution)/shard_map/ppermute | solution.py:154
  125.7 2.7 %add_convert_fusion = bf16[1536,512]{1,0:T(8,128)(2,1)S(1)} fusion(bf16[1536,512]{1,0:T(8,128)(2,1)} %collective-permute-done.14, bf16[1536,512]{1,0:T(8,128)(2,1)} %collective-permute-done.13, bf16[1536,512]{1,0:T(8,128)(2,1)S(1)} %collective-permute-done.12, bf16[1536,512]{1,0:T(8,128)(2,1)S(1)} %copy-done.5), kind=kLoop, calls=%fused_computation | loop fusion | flops 6291456 | bytes 7864320 | tf_op jit(solution)/shard_map/convert_element_type | solution.py:258
  128.5 7.0 %collective-permute-start.15 = (bf16[384,512]{1,0:T(8,128)(2,1)S(1)}, bf16[384,512]{1,0:T(8,128)(2,1)S(1)}, u32[]{:S(2)}, u32[]{:S(2)}) collective-permute-start(bf16[384,512]{1,0:T(8,128)(2,1)S(1)} %get-tuple-element.21), channel_id=1, source_target_pairs={{0,64},{1,257},{32,96},{33,289},{64,0},{65,321},{96,32},{97,353},{... | collective-permute-start | bytes 1179656 | tf_op jit(solution)/shard_map/ppermute | solution.py:144
  135.5 5.9 %collective-permute-start.16 = (bf16[384,512]{1,0:T(8,128)(2,1)S(1)}, bf16[384,512]{1,0:T(8,128)(2,1)S(1)}, u32[]{:S(2)}, u32[]{:S(2)}) collective-permute-start(bf16[384,512]{1,0:T(8,128)(2,1)S(1)} %get-tuple-element.23), channel_id=1, source_target_pairs={{0,32},{1,129},{32,64},{33,161},{64,96},{65,193},{96,0},{97,225},{... | collective-permute-start | bytes 1179656 | tf_op jit(solution)/shard_map/ppermute | solution.py:144
  146.5 6.7 %collective-permute-start.25 = (bf16[96,1536]{1,0:T(8,128)(2,1)S(1)}, bf16[96,1536]{1,0:T(8,128)(2,1)S(1)}, u32[]{:S(2)}, u32[]{:S(2)}) collective-permute-start(bf16[96,1536]{1,0:T(8,128)(2,1)S(1)} %fusion.3.refs_0_), channel_id=1, source_target_pairs={{0,2},{1,7},{2,4},{3,1},{4,6},{5,3},{6,0},{7,5},{8,10},{9,15},{10,... | collective-permute-start | bytes 884744 | tf_op jit(solution)/shard_map/ppermute | solution.py:154
  153.4 4.9 %collective-permute-start.18 = (bf16[192,512]{1,0:T(8,128)(2,1)S(1)}, bf16[192,512]{1,0:T(8,128)(2,1)S(1)}, u32[]{:S(2)}, u32[]{:S(2)}) collective-permute-start(bf16[192,512]{1,0:T(8,128)(2,1)S(1)} %constant_dynamic-slice_fusion.1), channel_id=1, source_target_pairs={{0,16},{8,24},{16,0},{24,8},{1,17},{9,25},{17,1},{25,9},{2,18},{10... | collective-permute-start | bytes 589832 | tf_op jit(solution)/shard_map/ppermute | solution.py:268
  158.4 3.8 %collective-permute-start.26 = (bf16[96,1536]{1,0:T(8,128)(2,1)S(1)}, bf16[96,1536]{1,0:T(8,128)(2,1)S(1)}, u32[]{:S(2)}, u32[]{:S(2)}) collective-permute-start(bf16[96,1536]{1,0:T(8,128)(2,1)S(1)} %collective-permute-done.24.refs_1_), channel_id=1, source_target_pairs={{0,2},{1,7},{2,4},{3,1},{4,6},{5,3},{6,0},{7,5},{8,10},{9,15},{10,... | collective-permute-start | bytes 884744 | tf_op jit(solution)/shard_map/ppermute | solution.py:154
  163.1 3.8 %collective-permute-start.29 = (bf16[96,1536]{1,0:T(8,128)(2,1)S(1)}, bf16[96,1536]{1,0:T(8,128)(2,1)S(1)}, u32[]{:S(2)}, u32[]{:S(2)}) collective-permute-start(bf16[96,1536]{1,0:T(8,128)(2,1)S(1)} %collective-permute-done.25.refs_2_), channel_id=1, source_target_pairs={{0,2},{1,7},{2,4},{3,1},{4,6},{5,3},{6,0},{7,5},{8,10},{9,15},{10,... | collective-permute-start | bytes 884744 | tf_op jit(solution)/shard_map/ppermute | solution.py:154
  167.0 26.9 %collective-permute-done.18 = bf16[192,512]{1,0:T(8,128)(2,1)S(1)} collective-permute-done((bf16[192,512]{1,0:T(8,128)(2,1)S(1)}, bf16[192,512]{1,0:T(8,128)(2,1)S(1)}, u32[]{:S(2)}, u32[]{:S(2)}) %collective-permute-start.18) | collective-permute-done | bytes 196640 | tf_op jit(solution)/shard_map/ppermute | solution.py:268
  195.8 8.5 %collective-permute-start.27 = (bf16[96,1536]{1,0:T(8,128)(2,1)S(1)}, bf16[96,1536]{1,0:T(8,128)(2,1)S(1)}, u32[]{:S(2)}, u32[]{:S(2)}) collective-permute-start(bf16[96,1536]{1,0:T(8,128)(2,1)S(1)} %collective-permute-done.25.refs_2_), channel_id=1, source_target_pairs={{0,1},{1,0},{2,3},{3,2},{4,5},{5,4},{6,7},{7,6},{8,9},{9,8},{10,11... | collective-permute-start | bytes 884744 | tf_op jit(solution)/shard_map/ppermute | solution.py:28
  (66 shorter events, 35.4 us)
Async XLA Ops:
  0.6 11.4 %collective-permute-start = (bf16[96,512]{1,0:T(8,128)(2,1)}, bf16[96,512]{1,0:T(8,128)(2,1)S(1)}, u32[]{:S(2)}, u32[]{:S(2)}) collective-permute-start(bf16[96,512]{1,0:T(8,128)(2,1)} %bitcast.27), channel_id=1, source_target_pairs={{0,24},{8,0},{16,8},{24,16},{1,25},{9,1},{17,9},{25,17},{2,26},{10... | collective-permute-start | bytes 294920 | tf_op jit(solution)/shard_map/ppermute | solution.py:28
  6.9 6.5 %collective-permute-start.1 = (bf16[96,512]{1,0:T(8,128)(2,1)}, bf16[96,512]{1,0:T(8,128)(2,1)S(1)}, u32[]{:S(2)}, u32[]{:S(2)}) collective-permute-start(bf16[96,512]{1,0:T(8,128)(2,1)} %bitcast.28), channel_id=1, source_target_pairs={{0,16},{8,24},{16,0},{24,8},{1,17},{9,25},{17,1},{25,9},{2,18},{10... | collective-permute-start | bytes 294920 | tf_op jit(solution)/shard_map/ppermute | solution.py:28
  8.8 7.4 %collective-permute-start.2 = (bf16[96,512]{1,0:T(8,128)(2,1)}, bf16[96,512]{1,0:T(8,128)(2,1)S(1)}, u32[]{:S(2)}, u32[]{:S(2)}) collective-permute-start(bf16[96,512]{1,0:T(8,128)(2,1)} %bitcast.29), channel_id=1, source_target_pairs={{0,8},{8,16},{16,24},{24,0},{1,9},{9,17},{17,25},{25,1},{2,10},{10... | collective-permute-start | bytes 294920 | tf_op jit(solution)/shard_map/ppermute | solution.py:28
  16.2 11.3 %collective-permute-start.4 = (bf16[384,512]{1,0:T(8,128)(2,1)S(1)}, bf16[384,512]{1,0:T(8,128)(2,1)S(1)}, u32[]{:S(2)}, u32[]{:S(2)}) collective-permute-start(bf16[384,512]{1,0:T(8,128)(2,1)S(1)} %constant_dynamic-update-slice_fusion.2), channel_id=1, source_target_pairs={{0,64},{1,257},{32,96},{33,289},{64,0},{65,321},{96,32},{97,353},{... | collective-permute-start | bytes 1179656 | tf_op jit(solution)/shard_map/ppermute | solution.py:144
  21.0 9.7 %collective-permute-start.5 = (bf16[384,512]{1,0:T(8,128)(2,1)S(1)}, bf16[384,512]{1,0:T(8,128)(2,1)S(1)}, u32[]{:S(2)}, u32[]{:S(2)}) collective-permute-start(bf16[384,512]{1,0:T(8,128)(2,1)S(1)} %constant_dynamic-update-slice_fusion.2), channel_id=1, source_target_pairs={{0,32},{1,129},{32,64},{33,161},{64,96},{65,193},{96,0},{97,225},{... | collective-permute-start | bytes 1179656 | tf_op jit(solution)/shard_map/ppermute | solution.py:144
  23.4 9.9 %collective-permute-start.3 = (bf16[384,512]{1,0:T(8,128)(2,1)S(1)}, bf16[384,512]{1,0:T(8,128)(2,1)S(1)}, u32[]{:S(2)}, u32[]{:S(2)}) collective-permute-start(bf16[384,512]{1,0:T(8,128)(2,1)S(1)} %constant_dynamic-update-slice_fusion.2), channel_id=1, source_target_pairs={{0,96},{1,385},{32,0},{33,417},{64,32},{65,449},{96,64},{97,481},{... | collective-permute-start | bytes 1179656 | tf_op jit(solution)/shard_map/ppermute | solution.py:144
  30.8 13.0 %collective-permute-start.9 = (bf16[768,512]{1,0:T(8,128)(2,1)S(1)}, bf16[768,512]{1,0:T(8,128)(2,1)S(1)}, u32[]{:S(2)}, u32[]{:S(2)}) collective-permute-start(bf16[768,512]{1,0:T(8,128)(2,1)S(1)} %constant_dynamic-update-slice_fusion.refs_1_), channel_id=1, source_target_pairs={{0,128},{1,33},{32,160},{33,65},{64,192},{65,97},{96,224},{97,1},{... | collective-permute-start | bytes 2359304 | tf_op jit(solution)/shard_map/ppermute | solution.py:144
  33.4 14.2 %collective-permute-start.6 = (bf16[768,512]{1,0:T(8,128)(2,1)S(1)}, bf16[768,512]{1,0:T(8,128)(2,1)S(1)}, u32[]{:S(2)}, u32[]{:S(2)}) collective-permute-start(bf16[768,512]{1,0:T(8,128)(2,1)S(1)} %pad_maximum_fusion.refs_0_), channel_id=1, source_target_pairs={{0,384},{1,97},{32,416},{33,1},{64,448},{65,33},{96,480},{97,65},{... | collective-permute-start | bytes 2359304 | tf_op jit(solution)/shard_map/ppermute | solution.py:144
  36.2 19.9 %collective-permute-start.7 = (bf16[768,512]{1,0:T(8,128)(2,1)S(1)}, bf16[768,512]{1,0:T(8,128)(2,1)}, u32[]{:S(2)}, u32[]{:S(2)}) collective-permute-start(bf16[768,512]{1,0:T(8,128)(2,1)S(1)} %constant_dynamic-update-slice_fusion.refs_1_), channel_id=1, source_target_pairs={{0,384},{1,97},{32,416},{33,1},{64,448},{65,33},{96,480},{97,65},{... | collective-permute-start | bytes 2359304 | tf_op jit(solution)/shard_map/ppermute | solution.py:144
  38.7 17.5 %collective-permute-start.11 = (bf16[768,512]{1,0:T(8,128)(2,1)S(1)}, bf16[768,512]{1,0:T(8,128)(2,1)}, u32[]{:S(2)}, u32[]{:S(2)}) collective-permute-start(bf16[768,512]{1,0:T(8,128)(2,1)S(1)} %pad_maximum_fusion.refs_0_), channel_id=1, source_target_pairs={{0,128},{1,33},{32,160},{33,65},{64,192},{65,97},{96,224},{97,1},{... | collective-permute-start | bytes 2359304 | tf_op jit(solution)/shard_map/ppermute | solution.py:144
  43.8 17.2 %collective-permute-start.10 = (bf16[768,512]{1,0:T(8,128)(2,1)S(1)}, bf16[768,512]{1,0:T(8,128)(2,1)}, u32[]{:S(2)}, u32[]{:S(2)}) collective-permute-start(bf16[768,512]{1,0:T(8,128)(2,1)S(1)} %collective-permute-done.9.refs_5_.refs_7_), channel_id=1, source_target_pairs={{0,128},{1,33},{32,160},{33,65},{64,192},{65,97},{96,224},{97,1},{... | collective-permute-start | bytes 2359304 | tf_op jit(solution)/shard_map/ppermute | solution.py:144
  47.5 17.0 %collective-permute-start.8 = (bf16[768,512]{1,0:T(8,128)(2,1)S(1)}, bf16[768,512]{1,0:T(8,128)(2,1)}, u32[]{:S(2)}, u32[]{:S(2)}) collective-permute-start(bf16[768,512]{1,0:T(8,128)(2,1)S(1)} %collective-permute-done.6.refs_2_), channel_id=1, source_target_pairs={{0,384},{1,97},{32,416},{33,1},{64,448},{65,33},{96,480},{97,65},{... | collective-permute-start | bytes 2359304 | tf_op jit(solution)/shard_map/ppermute | solution.py:144
  72.6 19.2 %collective-permute-start.20 = (bf16[4,96,1536]{2,1,0:T(8,128)(2,1)}, bf16[4,96,1536]{2,1,0:T(8,128)(2,1)}, u32[]{:S(2)}, u32[]{:S(2)}) collective-permute-start(bf16[4,96,1536]{2,1,0:T(8,128)(2,1)} %get-tuple-element.18), channel_id=1, source_target_pairs={{0,1},{1,0},{2,3},{3,2},{4,5},{5,4},{6,7},{7,6},{8,9},{9,8},{10,11... | collective-permute-start | bytes 3538952 | tf_op jit(solution)/shard_map/ppermute | solution.py:28
  82.8 41.3 %collective-permute-start.12 = (bf16[1536,512]{1,0:T(8,128)(2,1)}, bf16[1536,512]{1,0:T(8,128)(2,1)S(1)}, u32[]{:S(2)}, u32[]{:S(2)}) collective-permute-start(bf16[1536,512]{1,0:T(8,128)(2,1)} %get-tuple-element.14), channel_id=1, source_target_pairs={{0,128},{1,33},{32,160},{33,65},{64,192},{65,97},{96,224},{97,1},{... | collective-permute-start | bytes 4718600 | tf_op jit(solution)/shard_map/ppermute | solution.py:144
  85.8 38.3 %collective-permute-start.13 = (bf16[1536,512]{1,0:T(8,128)(2,1)}, bf16[1536,512]{1,0:T(8,128)(2,1)}, u32[]{:S(2)}, u32[]{:S(2)}) collective-permute-start(bf16[1536,512]{1,0:T(8,128)(2,1)} %get-tuple-element.15), channel_id=1, source_target_pairs={{0,256},{1,65},{32,288},{33,97},{64,320},{65,1},{96,352},{97,33},{... | collective-permute-start | bytes 4718600 | tf_op jit(solution)/shard_map/ppermute | solution.py:144
  89.8 35.9 %collective-permute-start.14 = (bf16[1536,512]{1,0:T(8,128)(2,1)}, bf16[1536,512]{1,0:T(8,128)(2,1)}, u32[]{:S(2)}, u32[]{:S(2)}) collective-permute-start(bf16[1536,512]{1,0:T(8,128)(2,1)} %get-tuple-element.16), channel_id=1, source_target_pairs={{0,384},{1,97},{32,416},{33,1},{64,448},{65,33},{96,480},{97,65},{... | collective-permute-start | bytes 4718600 | tf_op jit(solution)/shard_map/ppermute | solution.py:144
  93.9 21.8 %collective-permute-start.22 = (bf16[96,1536]{1,0:T(8,128)(2,1)}, bf16[96,1536]{1,0:T(8,128)(2,1)}, u32[]{:S(2)}, u32[]{:S(2)}) collective-permute-start(bf16[96,1536]{1,0:T(8,128)(2,1)} %get-tuple-element.20), channel_id=1, source_target_pairs={{0,2},{1,7},{2,4},{3,1},{4,6},{5,3},{6,0},{7,5},{8,10},{9,15},{10,... | collective-permute-start | bytes 884744 | tf_op jit(solution)/shard_map/ppermute | solution.py:154
  103.9 39.4 %collective-permute-start.21 = (bf16[96,1536]{1,0:T(8,128)(2,1)S(1)}, bf16[96,1536]{1,0:T(8,128)(2,1)S(1)}, u32[]{:S(2)}, u32[]{:S(2)}) collective-permute-start(bf16[96,1536]{1,0:T(8,128)(2,1)S(1)} %get-tuple-element.19), channel_id=1, source_target_pairs={{0,3},{1,6},{2,5},{3,0},{4,7},{5,2},{6,1},{7,4},{8,11},{9,14},{10,... | collective-permute-start | bytes 884744 | tf_op jit(solution)/shard_map/ppermute | solution.py:154
  116.9 26.4 %collective-permute-start.23 = (bf16[96,1536]{1,0:T(8,128)(2,1)S(1)}, bf16[96,1536]{1,0:T(8,128)(2,1)S(1)}, u32[]{:S(2)}, u32[]{:S(2)}) collective-permute-start(bf16[96,1536]{1,0:T(8,128)(2,1)S(1)} %fusion), channel_id=1, source_target_pairs={{0,2},{1,7},{2,4},{3,1},{4,6},{5,3},{6,0},{7,5},{8,10},{9,15},{10,... | collective-permute-start | bytes 884744 | tf_op jit(solution)/shard_map/ppermute | solution.py:154
  128.5 24.7 %collective-permute-start.15 = (bf16[384,512]{1,0:T(8,128)(2,1)S(1)}, bf16[384,512]{1,0:T(8,128)(2,1)S(1)}, u32[]{:S(2)}, u32[]{:S(2)}) collective-permute-start(bf16[384,512]{1,0:T(8,128)(2,1)S(1)} %get-tuple-element.21), channel_id=1, source_target_pairs={{0,64},{1,257},{32,96},{33,289},{64,0},{65,321},{96,32},{97,353},{... | collective-permute-start | bytes 1179656 | tf_op jit(solution)/shard_map/ppermute | solution.py:144
  135.5 17.7 %collective-permute-start.16 = (bf16[384,512]{1,0:T(8,128)(2,1)S(1)}, bf16[384,512]{1,0:T(8,128)(2,1)S(1)}, u32[]{:S(2)}, u32[]{:S(2)}) collective-permute-start(bf16[384,512]{1,0:T(8,128)(2,1)S(1)} %get-tuple-element.23), channel_id=1, source_target_pairs={{0,32},{1,129},{32,64},{33,161},{64,96},{65,193},{96,0},{97,225},{... | collective-permute-start | bytes 1179656 | tf_op jit(solution)/shard_map/ppermute | solution.py:144
  141.4 11.8 %collective-permute-start.17 = (bf16[384,512]{1,0:T(8,128)(2,1)S(1)}, bf16[384,512]{1,0:T(8,128)(2,1)S(1)}, u32[]{:S(2)}, u32[]{:S(2)}) collective-permute-start(bf16[384,512]{1,0:T(8,128)(2,1)S(1)} %get-tuple-element.22), channel_id=1, source_target_pairs={{0,96},{1,385},{32,0},{33,417},{64,32},{65,449},{96,64},{97,481},{... | collective-permute-start | bytes 1179656 | tf_op jit(solution)/shard_map/ppermute | solution.py:144
  144.6 65.4 %copy-start = (s32[4]{0:T(128)S(1)}, s32[4]{0:T(128)}, u32[]{:S(2)}) copy-start(s32[4]{0:T(128)} %pad_add_fusion.pos_ref) | copy-start | bytes 52
  144.6 13.8 %collective-permute-start.24 = (bf16[96,1536]{1,0:T(8,128)(2,1)S(1)}, bf16[96,1536]{1,0:T(8,128)(2,1)S(1)}, u32[]{:S(2)}, u32[]{:S(2)}) collective-permute-start(bf16[96,1536]{1,0:T(8,128)(2,1)S(1)} %fusion.3.refs_0_), channel_id=1, source_target_pairs={{0,1},{1,0},{2,3},{3,2},{4,5},{5,4},{6,7},{7,6},{8,9},{9,8},{10,11... | collective-permute-start | bytes 884744 | tf_op jit(solution)/shard_map/ppermute | solution.py:28
  146.5 16.6 %collective-permute-start.25 = (bf16[96,1536]{1,0:T(8,128)(2,1)S(1)}, bf16[96,1536]{1,0:T(8,128)(2,1)S(1)}, u32[]{:S(2)}, u32[]{:S(2)}) collective-permute-start(bf16[96,1536]{1,0:T(8,128)(2,1)S(1)} %fusion.3.refs_0_), channel_id=1, source_target_pairs={{0,2},{1,7},{2,4},{3,1},{4,6},{5,3},{6,0},{7,5},{8,10},{9,15},{10,... | collective-permute-start | bytes 884744 | tf_op jit(solution)/shard_map/ppermute | solution.py:154
  153.4 40.4 %collective-permute-start.18 = (bf16[192,512]{1,0:T(8,128)(2,1)S(1)}, bf16[192,512]{1,0:T(8,128)(2,1)S(1)}, u32[]{:S(2)}, u32[]{:S(2)}) collective-permute-start(bf16[192,512]{1,0:T(8,128)(2,1)S(1)} %constant_dynamic-slice_fusion.1), channel_id=1, source_target_pairs={{0,16},{8,24},{16,0},{24,8},{1,17},{9,25},{17,1},{25,9},{2,18},{10... | collective-permute-start | bytes 589832 | tf_op jit(solution)/shard_map/ppermute | solution.py:268
  158.4 46.0 %collective-permute-start.26 = (bf16[96,1536]{1,0:T(8,128)(2,1)S(1)}, bf16[96,1536]{1,0:T(8,128)(2,1)S(1)}, u32[]{:S(2)}, u32[]{:S(2)}) collective-permute-start(bf16[96,1536]{1,0:T(8,128)(2,1)S(1)} %collective-permute-done.24.refs_1_), channel_id=1, source_target_pairs={{0,2},{1,7},{2,4},{3,1},{4,6},{5,3},{6,0},{7,5},{8,10},{9,15},{10,... | collective-permute-start | bytes 884744 | tf_op jit(solution)/shard_map/ppermute | solution.py:154
  163.1 43.2 %collective-permute-start.29 = (bf16[96,1536]{1,0:T(8,128)(2,1)S(1)}, bf16[96,1536]{1,0:T(8,128)(2,1)S(1)}, u32[]{:S(2)}, u32[]{:S(2)}) collective-permute-start(bf16[96,1536]{1,0:T(8,128)(2,1)S(1)} %collective-permute-done.25.refs_2_), channel_id=1, source_target_pairs={{0,2},{1,7},{2,4},{3,1},{4,6},{5,3},{6,0},{7,5},{8,10},{9,15},{10,... | collective-permute-start | bytes 884744 | tf_op jit(solution)/shard_map/ppermute | solution.py:154
  193.9 14.8 %collective-permute-start.19 = (bf16[96,512]{1,0:T(8,128)(2,1)S(1)}, bf16[96,512]{1,0:T(8,128)(2,1)S(1)}, u32[]{:S(2)}, u32[]{:S(2)}) collective-permute-start(bf16[96,512]{1,0:T(8,128)(2,1)S(1)} %constant_dynamic-slice_fusion), channel_id=1, source_target_pairs={{0,8},{8,0},{16,24},{24,16},{1,9},{9,1},{17,25},{25,17},{2,10},{10... | collective-permute-start | bytes 294920 | tf_op jit(solution)/shard_map/ppermute | solution.py:268
  195.8 13.6 %collective-permute-start.27 = (bf16[96,1536]{1,0:T(8,128)(2,1)S(1)}, bf16[96,1536]{1,0:T(8,128)(2,1)S(1)}, u32[]{:S(2)}, u32[]{:S(2)}) collective-permute-start(bf16[96,1536]{1,0:T(8,128)(2,1)S(1)} %collective-permute-done.25.refs_2_), channel_id=1, source_target_pairs={{0,1},{1,0},{2,3},{3,2},{4,5},{5,4},{6,7},{7,6},{8,9},{9,8},{10,11... | collective-permute-start | bytes 884744 | tf_op jit(solution)/shard_map/ppermute | solution.py:28
  204.4 5.0 %collective-permute-start.28 = (bf16[96,1536]{1,0:T(8,128)(2,1)S(1)}, bf16[96,1536]{1,0:T(8,128)(2,1)S(1)}, u32[]{:S(2)}, u32[]{:S(2)}) collective-permute-start(bf16[96,1536]{1,0:T(8,128)(2,1)S(1)} %collective-permute-done.26.refs_3_), channel_id=1, source_target_pairs={{0,1},{1,0},{2,3},{3,2},{4,5},{5,4},{6,7},{7,6},{8,9},{9,8},{10,11... | collective-permute-start | bytes 884744 | tf_op jit(solution)/shard_map/ppermute | solution.py:28
  206.3 3.6 %collective-permute-start.30 = (bf16[96,1536]{1,0:T(8,128)(2,1)S(1)}, bf16[96,1536]{1,0:T(8,128)(2,1)S(1)}, u32[]{:S(2)}, u32[]{:S(2)}) collective-permute-start(bf16[96,1536]{1,0:T(8,128)(2,1)S(1)} %collective-permute-done.29.refs_6_), channel_id=1, source_target_pairs={{0,1},{1,0},{2,3},{3,2},{4,5},{5,4},{6,7},{7,6},{8,9},{9,8},{10,11... | collective-permute-start | bytes 884744 | tf_op jit(solution)/shard_map/ppermute | solution.py:28
  (5 other events, 100.8 us)

commit v7 on v6

--- a/solution.py
+++ b/solution.py
@@ -261,13 +261,9 @@
     arrived = [turn(blocks[2], False, 2), turn(blocks[1], False, 1)]
     arrived += [turn(blocks[3], False, 3)]
     stage = add_up([blocks[0]] + arrived).astype(BF16)
-    for bit in (2, 1):
-        depth = stage.shape[0] // 2
-        side = zl // bit % 2
-        other = lax.dynamic_slice_in_dim(stage, (1 - side) * depth, depth, axis=0)
-        arrived = lax.ppermute(other, "zl", [(i, i ^ bit) for i in range(RING)])
-        stage = add_up([lax.dynamic_slice_in_dim(stage, side * depth, depth, axis=0), arrived]).astype(BF16)
-    input_grad = stage
+    depth = stage.shape[0] // RING
+    shares = [lax.dynamic_slice_in_dim(stage, ((zl + d) % RING) * depth, depth, axis=0) for d in range(RING)]
+    input_grad = add_up(shares[:1] + [shift(shares[d], "zl", d) for d in range(1, RING)]).astype(BF16)
     return (hidden.T, input_grad.T, up_grad)
 
 

time: 213 us -> 211 us (level)
  the two profiles are of different devices: /device:TPU:7 before, /device:TPU:93 now
where the time goes in v7:
time: 211 us; the launch traced here: 210 us
  starting transfers between devices  143 us (68%)
  waiting for transfers between devices  38.2 us (18%)
  Pallas kernels  23.7 us (11%)
  other arithmetic  2.77 us (1%)
    ppermute x11, starting transfers between devices, shift(): lax.ppermute(value, axis, [(i, (i + by) % size) for i in range(size)])  57.3 us
    ppermute x15, starting transfers between devices, turn(): lax.ppermute(value, ('y', 'x', 'c'), [(flat(*s), flat(*target(*s))) for s...  45.1 us
    ppermute x6, starting transfers between devices, advance(): return lax.ppermute(value, ('zh', 'c'), pairs)  40.4 us
    ppermute x6, waiting for transfers between devices, advance(): return lax.ppermute(value, ('zh', 'c'), pairs)  16.6 us
    ppermute x15, waiting for transfers between devices, turn(): lax.ppermute(value, ('y', 'x', 'c'), [(flat(*s), flat(*target(*s))) for s...  14.9 us
    pallas_call x1, Pallas kernels, work(): pl.pallas_call(forward_kernel, in_specs=[scalars] + vmem(2 * RING + 3), o...  8.06 us
    ppermute x11, waiting for transfers between devices, shift(): lax.ppermute(value, axis, [(i, (i + by) % size) for i in range(size)])  6.66 us
    pallas_call x1, Pallas kernels, work(): pl.pallas_call(input_grad_kernel, in_specs=vmem(2), out_specs=vmem(RING),...  5.14 us
  transfers between devices with their start and end apart: 32, of which 13 were waited for; matrix products, arithmetic and copies ran while one was open for 2% of the time, Pallas kernels for 6%

profile of v7, /device:TPU:93, one launch (start us, length us, event | category | flops | bytes accessed | tf_op | source)
XLA Modules:
  0.0 209.7 jit_solution(12616935264921434092)
XLA Ops:
  2.6 4.7 %collective-permute-start = (bf16[96,512]{1,0:T(8,128)(2,1)}, bf16[96,512]{1,0:T(8,128)(2,1)S(1)}, u32[]{:S(2)}, u32[]{:S(2)}) collective-permute-start(bf16[96,512]{1,0:T(8,128)(2,1)} %bitcast.28), channel_id=1, source_target_pairs={{0,24},{8,0},{16,8},{24,16},{1,25},{9,1},{17,9},{25,17},{2,26},{10... | collective-permute-start | bytes 294920 | tf_op jit(solution)/shard_map/ppermute | solution.py:28
  10.2 3.5 %collective-permute-done.2 = bf16[96,512]{1,0:T(8,128)(2,1)S(1)} collective-permute-done((bf16[96,512]{1,0:T(8,128)(2,1)}, bf16[96,512]{1,0:T(8,128)(2,1)S(1)}, u32[]{:S(2)}, u32[]{:S(2)}) %collective-permute-start.2) | collective-permute-done | bytes 98336 | tf_op jit(solution)/shard_map/ppermute | solution.py:28
  16.2 2.6 %collective-permute-start.4 = (bf16[384,512]{1,0:T(8,128)(2,1)S(1)}, bf16[384,512]{1,0:T(8,128)(2,1)S(1)}, u32[]{:S(2)}, u32[]{:S(2)}) collective-permute-start(bf16[384,512]{1,0:T(8,128)(2,1)S(1)} %constant_dynamic-update-slice_fusion.2), channel_id=1, source_target_pairs={{0,64},{1,257},{32,96},{33,289},{64,0},{65,321},{96,32},{97,353},{... | collective-permute-start | bytes 1179656 | tf_op jit(solution)/shard_map/ppermute | solution.py:144
  18.7 3.8 %collective-permute-start.5 = (bf16[384,512]{1,0:T(8,128)(2,1)S(1)}, bf16[384,512]{1,0:T(8,128)(2,1)S(1)}, u32[]{:S(2)}, u32[]{:S(2)}) collective-permute-start(bf16[384,512]{1,0:T(8,128)(2,1)S(1)} %constant_dynamic-update-slice_fusion.2), channel_id=1, source_target_pairs={{0,32},{1,129},{32,64},{33,161},{64,96},{65,193},{96,0},{97,225},{... | collective-permute-start | bytes 1179656 | tf_op jit(solution)/shard_map/ppermute | solution.py:144
  22.5 5.3 %collective-permute-done.3 = bf16[384,512]{1,0:T(8,128)(2,1)S(1)} collective-permute-done((bf16[384,512]{1,0:T(8,128)(2,1)S(1)}, bf16[384,512]{1,0:T(8,128)(2,1)S(1)}, u32[]{:S(2)}, u32[]{:S(2)}) %collective-permute-start.3) | collective-permute-done | bytes 393248 | tf_op jit(solution)/shard_map/ppermute | solution.py:144
  30.6 2.8 %collective-permute-start.9 = (bf16[768,512]{1,0:T(8,128)(2,1)S(1)}, bf16[768,512]{1,0:T(8,128)(2,1)S(1)}, u32[]{:S(2)}, u32[]{:S(2)}) collective-permute-start(bf16[768,512]{1,0:T(8,128)(2,1)S(1)} %constant_dynamic-update-slice_fusion.refs_1_), channel_id=1, source_target_pairs={{0,128},{1,33},{32,160},{33,65},{64,192},{65,97},{96,224},{97,1},{... | collective-permute-start | bytes 2359304 | tf_op jit(solution)/shard_map/ppermute | solution.py:144
  33.4 4.1 %collective-permute-start.11 = (bf16[768,512]{1,0:T(8,128)(2,1)S(1)}, bf16[768,512]{1,0:T(8,128)(2,1)}, u32[]{:S(2)}, u32[]{:S(2)}) collective-permute-start(bf16[768,512]{1,0:T(8,128)(2,1)S(1)} %pad_maximum_fusion.refs_0_), channel_id=1, source_target_pairs={{0,128},{1,33},{32,160},{33,65},{64,192},{65,97},{96,224},{97,1},{... | collective-permute-start | bytes 2359304 | tf_op jit(solution)/shard_map/ppermute | solution.py:144
  43.6 3.5 %collective-permute-start.10 = (bf16[768,512]{1,0:T(8,128)(2,1)S(1)}, bf16[768,512]{1,0:T(8,128)(2,1)}, u32[]{:S(2)}, u32[]{:S(2)}) collective-permute-start(bf16[768,512]{1,0:T(8,128)(2,1)S(1)} %collective-permute-done.9.refs_5_.refs_7_), channel_id=1, source_target_pairs={{0,128},{1,33},{32,160},{33,65},{64,192},{65,97},{96,224},{97,1},{... | collective-permute-start | bytes 2359304 | tf_op jit(solution)/shard_map/ppermute | solution.py:144
  47.7 3.3 %order.1.up_ref.refs_10_ = bf16[192,6144]{1,0:T(8,128)(2,1)} custom-call(s32[4]{0:T(128)} %pad_add_fusion.pos_ref, bf16[192,6144]{1,0:T(8,128)(2,1)} %up_ref.1), custom_call_target="tpu_custom_call" | custom-call | bytes 4718592 | tf_op jit(solution)/shard_map/order/pallas_call | solution.py:179
  52.2 4.9 %early.1.refs_8_ = f32[192,512]{1,0:T(8,128)} custom-call(bf16[192,6144]{1,0:T(8,128)(2,1)} %order.1.up_ref.refs_10_, bf16[768,512]{1,0:T(8,128)(2,1)} %copy-done.1, bf16[768,512]{1,0:T(8,128)(2,1)} %copy-done.2, bf16[768,512]{1,0:T(8,128)(2,1)} %copy-done.3, bf16[768,512]{1,0:T(8,128)(2,1)} %collective-permute-done.7.refs_3_, ...), custom_call_target="tpu_custom_call" | custom-call | flops 905969664 | bytes 7000000 | tf_op jit(solution)/shard_map/early/pallas_call | solution.py:199
  60.6 8.1 %forward.1 = (bf16[192,512]{1,0:T(8,128)(2,1)}, bf16[192,512]{1,0:T(8,128)(2,1)}, bf16[4,96,1536]{2,1,0:T(8,128)(2,1)}, bf16[4,96,1536]{2,1,0:T(8,128)(2,1)}) custom-call(s32[4]{0:T(128)} %pad_add_fusion.pos_ref, bf16[768,512]{1,0:T(8,128)(2,1)} %copy-done.1, bf16[768,512]{1,0:T(8,128)(2,1)} %copy-done.2, bf16[768,512]{1,0:T(8,128)(2,1)} %copy-done.3, ...), custom_call_target="tpu_custom_call" | custom-call | flops 1811939328 | bytes 14000000 | tf_op jit(solution)/shard_map/forward/pallas_call | solution.py:208
  68.6 5.3 %collective-permute-start.21 = (bf16[4,96,1536]{2,1,0:T(8,128)(2,1)}, bf16[4,96,1536]{2,1,0:T(8,128)(2,1)S(1)}, u32[]{:S(2)}, u32[]{:S(2)}) collective-permute-start(bf16[4,96,1536]{2,1,0:T(8,128)(2,1)} %get-tuple-element.18), channel_id=1, source_target_pairs={{0,1},{1,0},{2,3},{3,2},{4,5},{5,4},{6,7},{7,6},{8,9},{9,8},{10,11... | collective-permute-start | bytes 3538952 | tf_op jit(solution)/shard_map/ppermute | solution.py:28
  74.0 5.1 %partial.1 = (bf16[1536,512]{1,0:T(8,128)(2,1)}, bf16[1536,512]{1,0:T(8,128)(2,1)}, bf16[1536,512]{1,0:T(8,128)(2,1)}, bf16[1536,512]{1,0:T(8,128)(2,1)}) custom-call(bf16[192,512]{1,0:T(8,128)(2,1)} %get-tuple-element.12.grad_ref, bf16[192,6144]{1,0:T(8,128)(2,1)} %order.1.up_ref.refs_10_), custom_call_target="tpu_custom_call" | custom-call | flops 1207959552 | bytes 9000000 | tf_op jit(solution)/shard_map/partial/pallas_call | solution.py:248
  79.1 3.4 %collective-permute-start.12 = (bf16[1536,512]{1,0:T(8,128)(2,1)}, bf16[1536,512]{1,0:T(8,128)(2,1)S(1)}, u32[]{:S(2)}, u32[]{:S(2)}) collective-permute-start(bf16[1536,512]{1,0:T(8,128)(2,1)} %get-tuple-element.14), channel_id=1, source_target_pairs={{0,128},{1,33},{32,160},{33,65},{64,192},{65,97},{96,224},{97,1},{... | collective-permute-start | bytes 4718600 | tf_op jit(solution)/shard_map/ppermute | solution.py:144
  82.5 3.0 %collective-permute-start.13 = (bf16[1536,512]{1,0:T(8,128)(2,1)}, bf16[1536,512]{1,0:T(8,128)(2,1)S(1)}, u32[]{:S(2)}, u32[]{:S(2)}) collective-permute-start(bf16[1536,512]{1,0:T(8,128)(2,1)} %get-tuple-element.15), channel_id=1, source_target_pairs={{0,256},{1,65},{32,288},{33,97},{64,320},{65,1},{96,352},{97,33},{... | collective-permute-start | bytes 4718600 | tf_op jit(solution)/shard_map/ppermute | solution.py:144
  85.5 4.0 %collective-permute-start.14 = (bf16[1536,512]{1,0:T(8,128)(2,1)}, bf16[1536,512]{1,0:T(8,128)(2,1)S(1)}, u32[]{:S(2)}, u32[]{:S(2)}) collective-permute-start(bf16[1536,512]{1,0:T(8,128)(2,1)} %get-tuple-element.16), channel_id=1, source_target_pairs={{0,384},{1,97},{32,416},{33,1},{64,448},{65,33},{96,480},{97,65},{... | collective-permute-start | bytes 4718600 | tf_op jit(solution)/shard_map/ppermute | solution.py:144
  89.7 10.2 %collective-permute-start.23 = (bf16[96,1536]{1,0:T(8,128)(2,1)S(1)}, bf16[96,1536]{1,0:T(8,128)(2,1)S(1)}, u32[]{:S(2)}, u32[]{:S(2)}) collective-permute-start(bf16[96,1536]{1,0:T(8,128)(2,1)S(1)} %get-tuple-element.20), channel_id=1, source_target_pairs={{0,2},{1,7},{2,4},{3,1},{4,6},{5,3},{6,0},{7,5},{8,10},{9,15},{10,... | collective-permute-start | bytes 884744 | tf_op jit(solution)/shard_map/ppermute | solution.py:154
  101.8 10.1 %collective-permute-done.23 = bf16[96,1536]{1,0:T(8,128)(2,1)S(1)} collective-permute-done((bf16[96,1536]{1,0:T(8,128)(2,1)S(1)}, bf16[96,1536]{1,0:T(8,128)(2,1)S(1)}, u32[]{:S(2)}, u32[]{:S(2)}) %collective-permute-start.23) | collective-permute-done | bytes 294944 | tf_op jit(solution)/shard_map/ppermute | solution.py:154
  111.9 7.2 %collective-permute-start.24 = (bf16[96,1536]{1,0:T(8,128)(2,1)S(1)}, bf16[96,1536]{1,0:T(8,128)(2,1)S(1)}, u32[]{:S(2)}, u32[]{:S(2)}) collective-permute-start(bf16[96,1536]{1,0:T(8,128)(2,1)S(1)} %fusion), channel_id=1, source_target_pairs={{0,2},{1,7},{2,4},{3,1},{4,6},{5,3},{6,0},{7,5},{8,10},{9,15},{10,... | collective-permute-start | bytes 884744 | tf_op jit(solution)/shard_map/ppermute | solution.py:154
  119.2 2.4 %collective-permute-done.14 = bf16[1536,512]{1,0:T(8,128)(2,1)S(1)} collective-permute-done((bf16[1536,512]{1,0:T(8,128)(2,1)}, bf16[1536,512]{1,0:T(8,128)(2,1)S(1)}, u32[]{:S(2)}, u32[]{:S(2)}) %collective-permute-start.14) | collective-permute-done | bytes 1572896 | tf_op jit(solution)/shard_map/ppermute | solution.py:144
  122.5 2.9 %collective-permute-start.15 = (bf16[384,512]{1,0:T(8,128)(2,1)S(1)}, bf16[384,512]{1,0:T(8,128)(2,1)S(1)}, u32[]{:S(2)}, u32[]{:S(2)}) collective-permute-start(bf16[384,512]{1,0:T(8,128)(2,1)S(1)} %get-tuple-element.21), channel_id=1, source_target_pairs={{0,64},{1,257},{32,96},{33,289},{64,0},{65,321},{96,32},{97,353},{... | collective-permute-start | bytes 1179656 | tf_op jit(solution)/shard_map/ppermute | solution.py:144
  125.4 2.7 %collective-permute-start.17 = (bf16[384,512]{1,0:T(8,128)(2,1)S(1)}, bf16[384,512]{1,0:T(8,128)(2,1)S(1)}, u32[]{:S(2)}, u32[]{:S(2)}) collective-permute-start(bf16[384,512]{1,0:T(8,128)(2,1)S(1)} %get-tuple-element.22), channel_id=1, source_target_pairs={{0,96},{1,385},{32,0},{33,417},{64,32},{65,449},{96,64},{97,481},{... | collective-permute-start | bytes 1179656 | tf_op jit(solution)/shard_map/ppermute | solution.py:144
  128.1 3.8 %collective-permute-start.16 = (bf16[384,512]{1,0:T(8,128)(2,1)S(1)}, bf16[384,512]{1,0:T(8,128)(2,1)S(1)}, u32[]{:S(2)}, u32[]{:S(2)}) collective-permute-start(bf16[384,512]{1,0:T(8,128)(2,1)S(1)} %get-tuple-element.23), channel_id=1, source_target_pairs={{0,32},{1,129},{32,64},{33,161},{64,96},{65,193},{96,0},{97,225},{... | collective-permute-start | bytes 1179656 | tf_op jit(solution)/shard_map/ppermute | solution.py:144
  132.1 10.2 %collective-permute-start.26 = (bf16[96,1536]{1,0:T(8,128)(2,1)S(1)}, bf16[96,1536]{1,0:T(8,128)(2,1)S(1)}, u32[]{:S(2)}, u32[]{:S(2)}) collective-permute-start(bf16[96,1536]{1,0:T(8,128)(2,1)S(1)} %fusion.3.refs_0_), channel_id=1, source_target_pairs={{0,2},{1,7},{2,4},{3,1},{4,6},{5,3},{6,0},{7,5},{8,10},{9,15},{10,... | collective-permute-start | bytes 884744 | tf_op jit(solution)/shard_map/ppermute | solution.py:154
  142.3 4.1 %collective-permute-start.25 = (bf16[96,1536]{1,0:T(8,128)(2,1)S(1)}, bf16[96,1536]{1,0:T(8,128)(2,1)S(1)}, u32[]{:S(2)}, u32[]{:S(2)}) collective-permute-start(bf16[96,1536]{1,0:T(8,128)(2,1)S(1)} %fusion.3.refs_0_), channel_id=1, source_target_pairs={{0,1},{1,0},{2,3},{3,2},{4,5},{5,4},{6,7},{7,6},{8,9},{9,8},{10,11... | collective-permute-start | bytes 884744 | tf_op jit(solution)/shard_map/ppermute | solution.py:28
  146.4 6.6 %collective-permute-done.26.refs_2_ = bf16[96,1536]{1,0:T(8,128)(2,1)S(1)} collective-permute-done((bf16[96,1536]{1,0:T(8,128)(2,1)S(1)}, bf16[96,1536]{1,0:T(8,128)(2,1)S(1)}, u32[]{:S(2)}, u32[]{:S(2)}) %collective-permute-start.26) | collective-permute-done | bytes 294944 | tf_op jit(solution)/shard_map/ppermute | solution.py:154
  152.9 5.5 %collective-permute-start.30 = (bf16[96,1536]{1,0:T(8,128)(2,1)S(1)}, bf16[96,1536]{1,0:T(8,128)(2,1)S(1)}, u32[]{:S(2)}, u32[]{:S(2)}) collective-permute-start(bf16[96,1536]{1,0:T(8,128)(2,1)S(1)} %collective-permute-done.26.refs_2_), channel_id=1, source_target_pairs={{0,2},{1,7},{2,4},{3,1},{4,6},{5,3},{6,0},{7,5},{8,10},{9,15},{10,... | collective-permute-start | bytes 884744 | tf_op jit(solution)/shard_map/ppermute | solution.py:154
  158.4 5.5 %collective-permute-start.27 = (bf16[96,1536]{1,0:T(8,128)(2,1)S(1)}, bf16[96,1536]{1,0:T(8,128)(2,1)S(1)}, u32[]{:S(2)}, u32[]{:S(2)}) collective-permute-start(bf16[96,1536]{1,0:T(8,128)(2,1)S(1)} %collective-permute-done.25.refs_1_), channel_id=1, source_target_pairs={{0,2},{1,7},{2,4},{3,1},{4,6},{5,3},{6,0},{7,5},{8,10},{9,15},{10,... | collective-permute-start | bytes 884744 | tf_op jit(solution)/shard_map/ppermute | solution.py:154
  166.1 4.8 %collective-permute-start.20 = (bf16[96,512]{1,0:T(8,128)(2,1)S(1)}, bf16[96,512]{1,0:T(8,128)(2,1)S(1)}, u32[]{:S(2)}, u32[]{:S(2)}) collective-permute-start(bf16[96,512]{1,0:T(8,128)(2,1)S(1)} %get-tuple-element.25), channel_id=1, source_target_pairs={{0,24},{8,0},{16,8},{24,16},{1,25},{9,1},{17,9},{25,17},{2,26},{10... | collective-permute-start | bytes 294920 | tf_op jit(solution)/shard_map/ppermute | solution.py:28
  170.9 9.2 %collective-permute-start.19 = (bf16[96,512]{1,0:T(8,128)(2,1)S(1)}, bf16[96,512]{1,0:T(8,128)(2,1)S(1)}, u32[]{:S(2)}, u32[]{:S(2)}) collective-permute-start(bf16[96,512]{1,0:T(8,128)(2,1)S(1)} %get-tuple-element.26), channel_id=1, source_target_pairs={{0,16},{8,24},{16,0},{24,8},{1,17},{9,25},{17,1},{25,9},{2,18},{10... | collective-permute-start | bytes 294920 | tf_op jit(solution)/shard_map/ppermute | solution.py:28
  180.1 2.7 %collective-permute-done.18 = bf16[96,512]{1,0:T(8,128)(2,1)S(1)} collective-permute-done((bf16[96,512]{1,0:T(8,128)(2,1)S(1)}, bf16[96,512]{1,0:T(8,128)(2,1)S(1)}, u32[]{:S(2)}, u32[]{:S(2)}) %collective-permute-start.18) | collective-permute-done | bytes 98336 | tf_op jit(solution)/shard_map/ppermute | solution.py:28
  182.8 19.1 %collective-permute-start.28 = (bf16[96,1536]{1,0:T(8,128)(2,1)S(1)}, bf16[96,1536]{1,0:T(8,128)(2,1)S(1)}, u32[]{:S(2)}, u32[]{:S(2)}) collective-permute-start(bf16[96,1536]{1,0:T(8,128)(2,1)S(1)} %collective-permute-done.26.refs_2_), channel_id=1, source_target_pairs={{0,1},{1,0},{2,3},{3,2},{4,5},{5,4},{6,7},{7,6},{8,9},{9,8},{10,11... | collective-permute-start | bytes 884744 | tf_op jit(solution)/shard_map/ppermute | solution.py:28
  (68 shorter events, 34.5 us)
Async XLA Ops:
  0.6 9.6 %collective-permute-start.1 = (bf16[96,512]{1,0:T(8,128)(2,1)}, bf16[96,512]{1,0:T(8,128)(2,1)S(1)}, u32[]{:S(2)}, u32[]{:S(2)}) collective-permute-start(bf16[96,512]{1,0:T(8,128)(2,1)} %bitcast.27), channel_id=1, source_target_pairs={{0,16},{8,24},{16,0},{24,8},{1,17},{9,25},{17,1},{25,9},{2,18},{10... | collective-permute-start | bytes 294920 | tf_op jit(solution)/shard_map/ppermute | solution.py:28
  2.6 7.6 %collective-permute-start = (bf16[96,512]{1,0:T(8,128)(2,1)}, bf16[96,512]{1,0:T(8,128)(2,1)S(1)}, u32[]{:S(2)}, u32[]{:S(2)}) collective-permute-start(bf16[96,512]{1,0:T(8,128)(2,1)} %bitcast.28), channel_id=1, source_target_pairs={{0,24},{8,0},{16,8},{24,16},{1,25},{9,1},{17,9},{25,17},{2,26},{10... | collective-permute-start | bytes 294920 | tf_op jit(solution)/shard_map/ppermute | solution.py:28
  7.3 6.5 %collective-permute-start.2 = (bf16[96,512]{1,0:T(8,128)(2,1)}, bf16[96,512]{1,0:T(8,128)(2,1)S(1)}, u32[]{:S(2)}, u32[]{:S(2)}) collective-permute-start(bf16[96,512]{1,0:T(8,128)(2,1)} %bitcast.29), channel_id=1, source_target_pairs={{0,8},{8,16},{16,24},{24,0},{1,9},{9,17},{17,25},{25,1},{2,10},{10... | collective-permute-start | bytes 294920 | tf_op jit(solution)/shard_map/ppermute | solution.py:28
  13.8 14.1 %collective-permute-start.3 = (bf16[384,512]{1,0:T(8,128)(2,1)S(1)}, bf16[384,512]{1,0:T(8,128)(2,1)S(1)}, u32[]{:S(2)}, u32[]{:S(2)}) collective-permute-start(bf16[384,512]{1,0:T(8,128)(2,1)S(1)} %constant_dynamic-update-slice_fusion.2), channel_id=1, source_target_pairs={{0,96},{1,385},{32,0},{33,417},{64,32},{65,449},{96,64},{97,481},{... | collective-permute-start | bytes 1179656 | tf_op jit(solution)/shard_map/ppermute | solution.py:144
  16.2 13.9 %collective-permute-start.4 = (bf16[384,512]{1,0:T(8,128)(2,1)S(1)}, bf16[384,512]{1,0:T(8,128)(2,1)S(1)}, u32[]{:S(2)}, u32[]{:S(2)}) collective-permute-start(bf16[384,512]{1,0:T(8,128)(2,1)S(1)} %constant_dynamic-update-slice_fusion.2), channel_id=1, source_target_pairs={{0,64},{1,257},{32,96},{33,289},{64,0},{65,321},{96,32},{97,353},{... | collective-permute-start | bytes 1179656 | tf_op jit(solution)/shard_map/ppermute | solution.py:144
  18.7 11.8 %collective-permute-start.5 = (bf16[384,512]{1,0:T(8,128)(2,1)S(1)}, bf16[384,512]{1,0:T(8,128)(2,1)S(1)}, u32[]{:S(2)}, u32[]{:S(2)}) collective-permute-start(bf16[384,512]{1,0:T(8,128)(2,1)S(1)} %constant_dynamic-update-slice_fusion.2), channel_id=1, source_target_pairs={{0,32},{1,129},{32,64},{33,161},{64,96},{65,193},{96,0},{97,225},{... | collective-permute-start | bytes 1179656 | tf_op jit(solution)/shard_map/ppermute | solution.py:144
  27.9 13.0 %collective-permute-start.6 = (bf16[768,512]{1,0:T(8,128)(2,1)S(1)}, bf16[768,512]{1,0:T(8,128)(2,1)S(1)}, u32[]{:S(2)}, u32[]{:S(2)}) collective-permute-start(bf16[768,512]{1,0:T(8,128)(2,1)S(1)} %pad_maximum_fusion.refs_0_), channel_id=1, source_target_pairs={{0,384},{1,97},{32,416},{33,1},{64,448},{65,33},{96,480},{97,65},{... | collective-permute-start | bytes 2359304 | tf_op jit(solution)/shard_map/ppermute | solution.py:144
  30.6 13.0 %collective-permute-start.9 = (bf16[768,512]{1,0:T(8,128)(2,1)S(1)}, bf16[768,512]{1,0:T(8,128)(2,1)S(1)}, u32[]{:S(2)}, u32[]{:S(2)}) collective-permute-start(bf16[768,512]{1,0:T(8,128)(2,1)S(1)} %constant_dynamic-update-slice_fusion.refs_1_), channel_id=1, source_target_pairs={{0,128},{1,33},{32,160},{33,65},{64,192},{65,97},{96,224},{97,1},{... | collective-permute-start | bytes 2359304 | tf_op jit(solution)/shard_map/ppermute | solution.py:144
  33.4 18.7 %collective-permute-start.11 = (bf16[768,512]{1,0:T(8,128)(2,1)S(1)}, bf16[768,512]{1,0:T(8,128)(2,1)}, u32[]{:S(2)}, u32[]{:S(2)}) collective-permute-start(bf16[768,512]{1,0:T(8,128)(2,1)S(1)} %pad_maximum_fusion.refs_0_), channel_id=1, source_target_pairs={{0,128},{1,33},{32,160},{33,65},{64,192},{65,97},{96,224},{97,1},{... | collective-permute-start | bytes 2359304 | tf_op jit(solution)/shard_map/ppermute | solution.py:144
  37.5 14.6 %collective-permute-start.7 = (bf16[768,512]{1,0:T(8,128)(2,1)S(1)}, bf16[768,512]{1,0:T(8,128)(2,1)}, u32[]{:S(2)}, u32[]{:S(2)}) collective-permute-start(bf16[768,512]{1,0:T(8,128)(2,1)S(1)} %constant_dynamic-update-slice_fusion.refs_1_), channel_id=1, source_target_pairs={{0,384},{1,97},{32,416},{33,1},{64,448},{65,33},{96,480},{97,65},{... | collective-permute-start | bytes 2359304 | tf_op jit(solution)/shard_map/ppermute | solution.py:144
  41.0 18.1 %collective-permute-start.8 = (bf16[768,512]{1,0:T(8,128)(2,1)S(1)}, bf16[768,512]{1,0:T(8,128)(2,1)}, u32[]{:S(2)}, u32[]{:S(2)}) collective-permute-start(bf16[768,512]{1,0:T(8,128)(2,1)S(1)} %collective-permute-done.6.refs_2_), channel_id=1, source_target_pairs={{0,384},{1,97},{32,416},{33,1},{64,448},{65,33},{96,480},{97,65},{... | collective-permute-start | bytes 2359304 | tf_op jit(solution)/shard_map/ppermute | solution.py:144
  43.6 17.0 %collective-permute-start.10 = (bf16[768,512]{1,0:T(8,128)(2,1)S(1)}, bf16[768,512]{1,0:T(8,128)(2,1)}, u32[]{:S(2)}, u32[]{:S(2)}) collective-permute-start(bf16[768,512]{1,0:T(8,128)(2,1)S(1)} %collective-permute-done.9.refs_5_.refs_7_), channel_id=1, source_target_pairs={{0,128},{1,33},{32,160},{33,65},{64,192},{65,97},{96,224},{97,1},{... | collective-permute-start | bytes 2359304 | tf_op jit(solution)/shard_map/ppermute | solution.py:144
  68.6 20.9 %collective-permute-start.21 = (bf16[4,96,1536]{2,1,0:T(8,128)(2,1)}, bf16[4,96,1536]{2,1,0:T(8,128)(2,1)S(1)}, u32[]{:S(2)}, u32[]{:S(2)}) collective-permute-start(bf16[4,96,1536]{2,1,0:T(8,128)(2,1)} %get-tuple-element.18), channel_id=1, source_target_pairs={{0,1},{1,0},{2,3},{3,2},{4,5},{5,4},{6,7},{7,6},{8,9},{9,8},{10,11... | collective-permute-start | bytes 3538952 | tf_op jit(solution)/shard_map/ppermute | solution.py:28
  79.1 40.0 %collective-permute-start.12 = (bf16[1536,512]{1,0:T(8,128)(2,1)}, bf16[1536,512]{1,0:T(8,128)(2,1)S(1)}, u32[]{:S(2)}, u32[]{:S(2)}) collective-permute-start(bf16[1536,512]{1,0:T(8,128)(2,1)} %get-tuple-element.14), channel_id=1, source_target_pairs={{0,128},{1,33},{32,160},{33,65},{64,192},{65,97},{96,224},{97,1},{... | collective-permute-start | bytes 4718600 | tf_op jit(solution)/shard_map/ppermute | solution.py:144
  82.5 36.6 %collective-permute-start.13 = (bf16[1536,512]{1,0:T(8,128)(2,1)}, bf16[1536,512]{1,0:T(8,128)(2,1)S(1)}, u32[]{:S(2)}, u32[]{:S(2)}) collective-permute-start(bf16[1536,512]{1,0:T(8,128)(2,1)} %get-tuple-element.15), channel_id=1, source_target_pairs={{0,256},{1,65},{32,288},{33,97},{64,320},{65,1},{96,352},{97,33},{... | collective-permute-start | bytes 4718600 | tf_op jit(solution)/shard_map/ppermute | solution.py:144
  85.5 36.1 %collective-permute-start.14 = (bf16[1536,512]{1,0:T(8,128)(2,1)}, bf16[1536,512]{1,0:T(8,128)(2,1)S(1)}, u32[]{:S(2)}, u32[]{:S(2)}) collective-permute-start(bf16[1536,512]{1,0:T(8,128)(2,1)} %get-tuple-element.16), channel_id=1, source_target_pairs={{0,384},{1,97},{32,416},{33,1},{64,448},{65,33},{96,480},{97,65},{... | collective-permute-start | bytes 4718600 | tf_op jit(solution)/shard_map/ppermute | solution.py:144
  89.7 22.2 %collective-permute-start.23 = (bf16[96,1536]{1,0:T(8,128)(2,1)S(1)}, bf16[96,1536]{1,0:T(8,128)(2,1)S(1)}, u32[]{:S(2)}, u32[]{:S(2)}) collective-permute-start(bf16[96,1536]{1,0:T(8,128)(2,1)S(1)} %get-tuple-element.20), channel_id=1, source_target_pairs={{0,2},{1,7},{2,4},{3,1},{4,6},{5,3},{6,0},{7,5},{8,10},{9,15},{10,... | collective-permute-start | bytes 884744 | tf_op jit(solution)/shard_map/ppermute | solution.py:154
  99.8 32.1 %collective-permute-start.22 = (bf16[96,1536]{1,0:T(8,128)(2,1)S(1)}, bf16[96,1536]{1,0:T(8,128)(2,1)S(1)}, u32[]{:S(2)}, u32[]{:S(2)}) collective-permute-start(bf16[96,1536]{1,0:T(8,128)(2,1)S(1)} %get-tuple-element.19), channel_id=1, source_target_pairs={{0,3},{1,6},{2,5},{3,0},{4,7},{5,2},{6,1},{7,4},{8,11},{9,14},{10,... | collective-permute-start | bytes 884744 | tf_op jit(solution)/shard_map/ppermute | solution.py:154
  111.9 20.0 %collective-permute-start.24 = (bf16[96,1536]{1,0:T(8,128)(2,1)S(1)}, bf16[96,1536]{1,0:T(8,128)(2,1)S(1)}, u32[]{:S(2)}, u32[]{:S(2)}) collective-permute-start(bf16[96,1536]{1,0:T(8,128)(2,1)S(1)} %fusion), channel_id=1, source_target_pairs={{0,2},{1,7},{2,4},{3,1},{4,6},{5,3},{6,0},{7,5},{8,10},{9,15},{10,... | collective-permute-start | bytes 884744 | tf_op jit(solution)/shard_map/ppermute | solution.py:154
  122.5 41.3 %collective-permute-start.15 = (bf16[384,512]{1,0:T(8,128)(2,1)S(1)}, bf16[384,512]{1,0:T(8,128)(2,1)S(1)}, u32[]{:S(2)}, u32[]{:S(2)}) collective-permute-start(bf16[384,512]{1,0:T(8,128)(2,1)S(1)} %get-tuple-element.21), channel_id=1, source_target_pairs={{0,64},{1,257},{32,96},{33,289},{64,0},{65,321},{96,32},{97,353},{... | collective-permute-start | bytes 1179656 | tf_op jit(solution)/shard_map/ppermute | solution.py:144
  125.4 38.5 %collective-permute-start.17 = (bf16[384,512]{1,0:T(8,128)(2,1)S(1)}, bf16[384,512]{1,0:T(8,128)(2,1)S(1)}, u32[]{:S(2)}, u32[]{:S(2)}) collective-permute-start(bf16[384,512]{1,0:T(8,128)(2,1)S(1)} %get-tuple-element.22), channel_id=1, source_target_pairs={{0,96},{1,385},{32,0},{33,417},{64,32},{65,449},{96,64},{97,481},{... | collective-permute-start | bytes 1179656 | tf_op jit(solution)/shard_map/ppermute | solution.py:144
  128.1 35.8 %collective-permute-start.16 = (bf16[384,512]{1,0:T(8,128)(2,1)S(1)}, bf16[384,512]{1,0:T(8,128)(2,1)S(1)}, u32[]{:S(2)}, u32[]{:S(2)}) collective-permute-start(bf16[384,512]{1,0:T(8,128)(2,1)S(1)} %get-tuple-element.23), channel_id=1, source_target_pairs={{0,32},{1,129},{32,64},{33,161},{64,96},{65,193},{96,0},{97,225},{... | collective-permute-start | bytes 1179656 | tf_op jit(solution)/shard_map/ppermute | solution.py:144
  132.1 20.8 %collective-permute-start.26 = (bf16[96,1536]{1,0:T(8,128)(2,1)S(1)}, bf16[96,1536]{1,0:T(8,128)(2,1)S(1)}, u32[]{:S(2)}, u32[]{:S(2)}) collective-permute-start(bf16[96,1536]{1,0:T(8,128)(2,1)S(1)} %fusion.3.refs_0_), channel_id=1, source_target_pairs={{0,2},{1,7},{2,4},{3,1},{4,6},{5,3},{6,0},{7,5},{8,10},{9,15},{10,... | collective-permute-start | bytes 884744 | tf_op jit(solution)/shard_map/ppermute | solution.py:154
  142.3 16.1 %collective-permute-start.25 = (bf16[96,1536]{1,0:T(8,128)(2,1)S(1)}, bf16[96,1536]{1,0:T(8,128)(2,1)S(1)}, u32[]{:S(2)}, u32[]{:S(2)}) collective-permute-start(bf16[96,1536]{1,0:T(8,128)(2,1)S(1)} %fusion.3.refs_0_), channel_id=1, source_target_pairs={{0,1},{1,0},{2,3},{3,2},{4,5},{5,4},{6,7},{7,6},{8,9},{9,8},{10,11... | collective-permute-start | bytes 884744 | tf_op jit(solution)/shard_map/ppermute | solution.py:28
  152.9 48.9 %collective-permute-start.30 = (bf16[96,1536]{1,0:T(8,128)(2,1)S(1)}, bf16[96,1536]{1,0:T(8,128)(2,1)S(1)}, u32[]{:S(2)}, u32[]{:S(2)}) collective-permute-start(bf16[96,1536]{1,0:T(8,128)(2,1)S(1)} %collective-permute-done.26.refs_2_), channel_id=1, source_target_pairs={{0,2},{1,7},{2,4},{3,1},{4,6},{5,3},{6,0},{7,5},{8,10},{9,15},{10,... | collective-permute-start | bytes 884744 | tf_op jit(solution)/shard_map/ppermute | solution.py:154
  158.4 45.4 %collective-permute-start.27 = (bf16[96,1536]{1,0:T(8,128)(2,1)S(1)}, bf16[96,1536]{1,0:T(8,128)(2,1)S(1)}, u32[]{:S(2)}, u32[]{:S(2)}) collective-permute-start(bf16[96,1536]{1,0:T(8,128)(2,1)S(1)} %collective-permute-done.25.refs_1_), channel_id=1, source_target_pairs={{0,2},{1,7},{2,4},{3,1},{4,6},{5,3},{6,0},{7,5},{8,10},{9,15},{10,... | collective-permute-start | bytes 884744 | tf_op jit(solution)/shard_map/ppermute | solution.py:154
  164.1 18.7 %collective-permute-start.18 = (bf16[96,512]{1,0:T(8,128)(2,1)S(1)}, bf16[96,512]{1,0:T(8,128)(2,1)S(1)}, u32[]{:S(2)}, u32[]{:S(2)}) collective-permute-start(bf16[96,512]{1,0:T(8,128)(2,1)S(1)} %get-tuple-element.24), channel_id=1, source_target_pairs={{0,8},{8,16},{16,24},{24,0},{1,9},{9,17},{17,25},{25,1},{2,10},{10... | collective-permute-start | bytes 294920 | tf_op jit(solution)/shard_map/ppermute | solution.py:28
  166.1 40.2 %collective-permute-start.20 = (bf16[96,512]{1,0:T(8,128)(2,1)S(1)}, bf16[96,512]{1,0:T(8,128)(2,1)S(1)}, u32[]{:S(2)}, u32[]{:S(2)}) collective-permute-start(bf16[96,512]{1,0:T(8,128)(2,1)S(1)} %get-tuple-element.25), channel_id=1, source_target_pairs={{0,24},{8,0},{16,8},{24,16},{1,25},{9,1},{17,9},{25,17},{2,26},{10... | collective-permute-start | bytes 294920 | tf_op jit(solution)/shard_map/ppermute | solution.py:28
  170.9 35.3 %collective-permute-start.19 = (bf16[96,512]{1,0:T(8,128)(2,1)S(1)}, bf16[96,512]{1,0:T(8,128)(2,1)S(1)}, u32[]{:S(2)}, u32[]{:S(2)}) collective-permute-start(bf16[96,512]{1,0:T(8,128)(2,1)S(1)} %get-tuple-element.26), channel_id=1, source_target_pairs={{0,16},{8,24},{16,0},{24,8},{1,17},{9,25},{17,1},{25,9},{2,18},{10... | collective-permute-start | bytes 294920 | tf_op jit(solution)/shard_map/ppermute | solution.py:28
  182.8 24.2 %collective-permute-start.28 = (bf16[96,1536]{1,0:T(8,128)(2,1)S(1)}, bf16[96,1536]{1,0:T(8,128)(2,1)S(1)}, u32[]{:S(2)}, u32[]{:S(2)}) collective-permute-start(bf16[96,1536]{1,0:T(8,128)(2,1)S(1)} %collective-permute-done.26.refs_2_), channel_id=1, source_target_pairs={{0,1},{1,0},{2,3},{3,2},{4,5},{5,4},{6,7},{7,6},{8,9},{9,8},{10,11... | collective-permute-start | bytes 884744 | tf_op jit(solution)/shard_map/ppermute | solution.py:28
  201.9 5.1 %collective-permute-start.31 = (bf16[96,1536]{1,0:T(8,128)(2,1)S(1)}, bf16[96,1536]{1,0:T(8,128)(2,1)S(1)}, u32[]{:S(2)}, u32[]{:S(2)}) collective-permute-start(bf16[96,1536]{1,0:T(8,128)(2,1)S(1)} %collective-permute-done.30.refs_6_), channel_id=1, source_target_pairs={{0,1},{1,0},{2,3},{3,2},{4,5},{5,4},{6,7},{7,6},{8,9},{9,8},{10,11... | collective-permute-start | bytes 884744 | tf_op jit(solution)/shard_map/ppermute | solution.py:28
  203.8 3.6 %collective-permute-start.29 = (bf16[96,1536]{1,0:T(8,128)(2,1)S(1)}, bf16[96,1536]{1,0:T(8,128)(2,1)S(1)}, u32[]{:S(2)}, u32[]{:S(2)}) collective-permute-start(bf16[96,1536]{1,0:T(8,128)(2,1)S(1)} %collective-permute-done.27.refs_3_), channel_id=1, source_target_pairs={{0,1},{1,0},{2,3},{3,2},{4,5},{5,4},{6,7},{7,6},{8,9},{9,8},{10,11... | collective-permute-start | bytes 884744 | tf_op jit(solution)/shard_map/ppermute | solution.py:28
  (7 other events, 194.3 us)

commit v8 on v7

--- a/solution.py
+++ b/solution.py
@@ -98,7 +98,7 @@
 def input_grad_kernel(grad_ref, up_ref, *outs):
     grads = grad_ref[...]
     depth = outs[0].shape[0]
-    for d in range(RING):
+    for d in range(2 * RING):
         term = dot(up_ref[:, pl.ds(d * depth, depth)], grads, ((0,), (0,)))
         outs[d][...] = term.astype(BF16)
 
@@ -163,10 +163,6 @@
     for value in values[1:]:
         total = total + value.astype(F32)
     return total
-
-
-def scatter_sum(values, late):
-    return add_up([values[0]] + [turn(values[d], late, d) for d in range(1, RING)])
 
 
 def work(normed, hidden_cot, up_rows):
@@ -248,14 +244,25 @@
     parts = pl.pallas_call(
         input_grad_kernel,
         in_specs=vmem(2),
-        out_specs=vmem(RING),
-        out_shape=[jax.ShapeDtypeStruct((width // RING, tokens), BF16)] * RING,
+        out_specs=vmem(2 * RING),
+        out_shape=[jax.ShapeDtypeStruct((width // RING // 2, tokens), BF16)] * (2 * RING),
         name="partial",
         cost_estimate=pl.CostEstimate(
             flops=2 * hid * tokens * width, bytes_accessed=9_000_000, transcendentals=0
         ),
     )(hidden_grad, ordered)
-    stage = scatter_sum(parts, True).astype(BF16)
+    upper, lower = parts[0::2], parts[1::2]
+    upper_in, lower_in = turn(upper[2], True, 1), turn(lower[2], True, -1)
+    lower_left, upper_right = turn(lower[1], True, 1), turn(upper[3], True, -1)
+    upper_left = turn(add_up([upper[1], upper_in]).astype(BF16), True, 1)
+    lower_right = turn(add_up([lower[3], lower_in]).astype(BF16), True, -1)
+    stage = jnp.concatenate(
+        [
+            add_up([upper[0], upper_left, upper_right]).astype(BF16),
+            add_up([lower[0], lower_left, lower_right]).astype(BF16),
+        ],
+        axis=0,
+    )
     depth = stage.shape[0] // RING
     blocks = [stage[d * depth : (d + 1) * depth] for d in range(RING)]
     arrived = [turn(blocks[2], False, 2), turn(blocks[1], False, 1)]

time: 211 us -> 222 us (1.052)
  the two profiles are of different devices: /device:TPU:93 before, /device:TPU:37 now
where the time goes in v8:
time: 222 us; the launch traced here: 221 us
  starting transfers between devices  141 us (64%)
  waiting for transfers between devices  49.7 us (22%)
  Pallas kernels  23.4 us (11%)
  other arithmetic  4.33 us (2%)
    ppermute x18, starting transfers between devices, turn(): lax.ppermute(value, ('y', 'x', 'c'), [(flat(*s), flat(*target(*s))) for s...  51.7 us
    ppermute x11, starting transfers between devices, shift(): lax.ppermute(value, axis, [(i, (i + by) % size) for i in range(size)])  45.4 us
    ppermute x6, starting transfers between devices, advance(): return lax.ppermute(value, ('zh', 'c'), pairs)  44.2 us
    ppermute x6, waiting for transfers between devices, advance(): return lax.ppermute(value, ('zh', 'c'), pairs)  27.4 us
    ppermute x18, waiting for transfers between devices, turn(): lax.ppermute(value, ('y', 'x', 'c'), [(flat(*s), flat(*target(*s))) for s...  20.3 us
    pallas_call x1, Pallas kernels, work(): pl.pallas_call(forward_kernel, in_specs=[scalars] + vmem(2 * RING + 3), o...  7.99 us
    pallas_call x1, Pallas kernels, work(): pl.pallas_call(input_grad_kernel, in_specs=vmem(2), out_specs=vmem(2 * RI...  4.87 us
    pallas_call x1, Pallas kernels, work(): pl.pallas_call(early_kernel, in_specs=vmem(7), out_specs=vmem(1)[0], out_...  4.86 us
  transfers between devices with their start and end apart: 35, of which 13 were waited for; matrix products, arithmetic and copies ran while one was open for 2% of the time, Pallas kernels for 6%

profile of v8, /device:TPU:37, one launch (start us, length us, event | category | flops | bytes accessed | tf_op | source)
XLA Modules:
  0.0 221.2 jit_solution(3061387261112237860)
XLA Ops:
  0.6 4.9 %collective-permute-start.1 = (bf16[96,512]{1,0:T(8,128)(2,1)}, bf16[96,512]{1,0:T(8,128)(2,1)S(1)}, u32[]{:S(2)}, u32[]{:S(2)}) collective-permute-start(bf16[96,512]{1,0:T(8,128)(2,1)} %bitcast.27), channel_id=1, source_target_pairs={{0,16},{8,24},{16,0},{24,8},{1,17},{9,25},{17,1},{25,9},{2,18},{10... | collective-permute-start | bytes 294920 | tf_op jit(solution)/shard_map/ppermute | solution.py:28
  7.5 3.4 %collective-permute-start.2 = (bf16[96,512]{1,0:T(8,128)(2,1)}, bf16[96,512]{1,0:T(8,128)(2,1)S(1)}, u32[]{:S(2)}, u32[]{:S(2)}) collective-permute-start(bf16[96,512]{1,0:T(8,128)(2,1)} %bitcast.29), channel_id=1, source_target_pairs={{0,8},{8,16},{16,24},{24,0},{1,9},{9,17},{17,25},{25,1},{2,10},{10... | collective-permute-start | bytes 294920 | tf_op jit(solution)/shard_map/ppermute | solution.py:28
  13.3 4.6 %collective-permute-start.3 = (bf16[384,512]{1,0:T(8,128)(2,1)S(1)}, bf16[384,512]{1,0:T(8,128)(2,1)S(1)}, u32[]{:S(2)}, u32[]{:S(2)}) collective-permute-start(bf16[384,512]{1,0:T(8,128)(2,1)S(1)} %constant_dynamic-update-slice_fusion.2), channel_id=1, source_target_pairs={{0,96},{1,385},{32,0},{33,417},{64,32},{65,449},{96,64},{97,481},{... | collective-permute-start | bytes 1179656 | tf_op jit(solution)/shard_map/ppermute | solution.py:144
  20.2 2.6 %collective-permute-start.5 = (bf16[384,512]{1,0:T(8,128)(2,1)S(1)}, bf16[384,512]{1,0:T(8,128)(2,1)S(1)}, u32[]{:S(2)}, u32[]{:S(2)}) collective-permute-start(bf16[384,512]{1,0:T(8,128)(2,1)S(1)} %constant_dynamic-update-slice_fusion.2), channel_id=1, source_target_pairs={{0,32},{1,129},{32,64},{33,161},{64,96},{65,193},{96,0},{97,225},{... | collective-permute-start | bytes 1179656 | tf_op jit(solution)/shard_map/ppermute | solution.py:144
  22.8 4.0 %collective-permute-done.3 = bf16[384,512]{1,0:T(8,128)(2,1)S(1)} collective-permute-done((bf16[384,512]{1,0:T(8,128)(2,1)S(1)}, bf16[384,512]{1,0:T(8,128)(2,1)S(1)}, u32[]{:S(2)}, u32[]{:S(2)}) %collective-permute-start.3) | collective-permute-done | bytes 393248 | tf_op jit(solution)/shard_map/ppermute | solution.py:144
  29.1 3.0 %collective-permute-done.5 = bf16[384,512]{1,0:T(8,128)(2,1)S(1)} collective-permute-done((bf16[384,512]{1,0:T(8,128)(2,1)S(1)}, bf16[384,512]{1,0:T(8,128)(2,1)S(1)}, u32[]{:S(2)}, u32[]{:S(2)}) %collective-permute-start.5) | collective-permute-done | bytes 393248 | tf_op jit(solution)/shard_map/ppermute | solution.py:144
  32.2 2.8 %collective-permute-start.9 = (bf16[768,512]{1,0:T(8,128)(2,1)S(1)}, bf16[768,512]{1,0:T(8,128)(2,1)S(1)}, u32[]{:S(2)}, u32[]{:S(2)}) collective-permute-start(bf16[768,512]{1,0:T(8,128)(2,1)S(1)} %constant_dynamic-update-slice_fusion.refs_1_), channel_id=1, source_target_pairs={{0,128},{1,33},{32,160},{33,65},{64,192},{65,97},{96,224},{97,1},{... | collective-permute-start | bytes 2359304 | tf_op jit(solution)/shard_map/ppermute | solution.py:144
  37.5 2.9 %collective-permute-start.7 = (bf16[768,512]{1,0:T(8,128)(2,1)S(1)}, bf16[768,512]{1,0:T(8,128)(2,1)}, u32[]{:S(2)}, u32[]{:S(2)}) collective-permute-start(bf16[768,512]{1,0:T(8,128)(2,1)S(1)} %constant_dynamic-update-slice_fusion.refs_1_), channel_id=1, source_target_pairs={{0,384},{1,97},{32,416},{33,1},{64,448},{65,33},{96,480},{97,65},{... | collective-permute-start | bytes 2359304 | tf_op jit(solution)/shard_map/ppermute | solution.py:144
  40.4 2.5 %collective-permute-start.8 = (bf16[768,512]{1,0:T(8,128)(2,1)S(1)}, bf16[768,512]{1,0:T(8,128)(2,1)}, u32[]{:S(2)}, u32[]{:S(2)}) collective-permute-start(bf16[768,512]{1,0:T(8,128)(2,1)S(1)} %collective-permute-done.6.refs_2_), channel_id=1, source_target_pairs={{0,384},{1,97},{32,416},{33,1},{64,448},{65,33},{96,480},{97,65},{... | collective-permute-start | bytes 2359304 | tf_op jit(solution)/shard_map/ppermute | solution.py:144
  42.8 2.5 %collective-permute-done.9.refs_5_.refs_7_ = bf16[768,512]{1,0:T(8,128)(2,1)S(1)} collective-permute-done((bf16[768,512]{1,0:T(8,128)(2,1)S(1)}, bf16[768,512]{1,0:T(8,128)(2,1)S(1)}, u32[]{:S(2)}, u32[]{:S(2)}) %collective-permute-start.9) | collective-permute-done | bytes 786464 | tf_op jit(solution)/shard_map/ppermute | solution.py:144
  45.4 2.7 %collective-permute-start.10 = (bf16[768,512]{1,0:T(8,128)(2,1)S(1)}, bf16[768,512]{1,0:T(8,128)(2,1)}, u32[]{:S(2)}, u32[]{:S(2)}) collective-permute-start(bf16[768,512]{1,0:T(8,128)(2,1)S(1)} %collective-permute-done.9.refs_5_.refs_7_), channel_id=1, source_target_pairs={{0,128},{1,33},{32,160},{33,65},{64,192},{65,97},{96,224},{97,1},{... | collective-permute-start | bytes 2359304 | tf_op jit(solution)/shard_map/ppermute | solution.py:144
  48.7 3.4 %order.1.up_ref.refs_10_ = bf16[192,6144]{1,0:T(8,128)(2,1)} custom-call(s32[4]{0:T(128)} %pad_add_fusion.pos_ref, bf16[192,6144]{1,0:T(8,128)(2,1)} %up_ref.1), custom_call_target="tpu_custom_call" | custom-call | bytes 4718592 | tf_op jit(solution)/shard_map/order/pallas_call | solution.py:175
  53.8 4.9 %early.1.refs_8_ = f32[192,512]{1,0:T(8,128)} custom-call(bf16[192,6144]{1,0:T(8,128)(2,1)} %order.1.up_ref.refs_10_, bf16[768,512]{1,0:T(8,128)(2,1)} %copy-done.1, bf16[768,512]{1,0:T(8,128)(2,1)} %copy-done.2, bf16[768,512]{1,0:T(8,128)(2,1)} %copy-done.3, bf16[768,512]{1,0:T(8,128)(2,1)} %collective-permute-done.7.refs_3_, ...), custom_call_target="tpu_custom_call" | custom-call | flops 905969664 | bytes 7000000 | tf_op jit(solution)/shard_map/early/pallas_call | solution.py:195
  59.0 3.2 %collective-permute-done.10.refs_5_ = bf16[768,512]{1,0:T(8,128)(2,1)} collective-permute-done((bf16[768,512]{1,0:T(8,128)(2,1)S(1)}, bf16[768,512]{1,0:T(8,128)(2,1)}, u32[]{:S(2)}, u32[]{:S(2)}) %collective-permute-start.10) | collective-permute-done | bytes 786464 | tf_op jit(solution)/shard_map/ppermute | solution.py:144
  62.2 8.0 %forward.1 = (bf16[192,512]{1,0:T(8,128)(2,1)}, bf16[192,512]{1,0:T(8,128)(2,1)}, bf16[4,96,1536]{2,1,0:T(8,128)(2,1)}, bf16[4,96,1536]{2,1,0:T(8,128)(2,1)}) custom-call(s32[4]{0:T(128)} %pad_add_fusion.pos_ref, bf16[768,512]{1,0:T(8,128)(2,1)} %copy-done.1, bf16[768,512]{1,0:T(8,128)(2,1)} %copy-done.2, bf16[768,512]{1,0:T(8,128)(2,1)} %copy-done.3, ...), custom_call_target="tpu_custom_call" | custom-call | flops 1811939328 | bytes 14000000 | tf_op jit(solution)/shard_map/forward/pallas_call | solution.py:204
  70.2 4.9 %collective-permute-start.24 = (bf16[4,96,1536]{2,1,0:T(8,128)(2,1)}, bf16[4,96,1536]{2,1,0:T(8,128)(2,1)S(1)}, u32[]{:S(2)}, u32[]{:S(2)}) collective-permute-start(bf16[4,96,1536]{2,1,0:T(8,128)(2,1)} %get-tuple-element.26), channel_id=1, source_target_pairs={{0,1},{1,0},{2,3},{3,2},{4,5},{5,4},{6,7},{7,6},{8,9},{9,8},{10,11... | collective-permute-start | bytes 3538952 | tf_op jit(solution)/shard_map/ppermute | solution.py:28
  75.1 4.9 %partial.1 = (bf16[768,512]{1,0:T(8,128)(2,1)}, bf16[768,512]{1,0:T(8,128)(2,1)}, bf16[768,512]{1,0:T(8,128)(2,1)}, bf16[768,512]{1,0:T(8,128)(2,1)}, bf16[768,5...) custom-call(bf16[192,512]{1,0:T(8,128)(2,1)} %get-tuple-element.16.grad_ref, ...), custom_call_target="tpu_custom_call" | custom-call | flops 1207959552 | bytes 9000000 | tf_op jit(solution)/shard_map/partial/pallas_call | solution.py:244
  80.0 5.3 %collective-permute-start.12 = (bf16[768,512]{1,0:T(8,128)(2,1)}, bf16[768,512]{1,0:T(8,128)(2,1)S(1)}, u32[]{:S(2)}, u32[]{:S(2)}) collective-permute-start(bf16[768,512]{1,0:T(8,128)(2,1)} %get-tuple-element.19), channel_id=1, source_target_pairs={{0,128},{1,33},{32,160},{33,65},{64,192},{65,97},{96,224},{97,1},{... | collective-permute-start | bytes 2359304 | tf_op jit(solution)/shard_map/ppermute | solution.py:144
  89.1 5.4 %collective-permute-done.12 = bf16[768,512]{1,0:T(8,128)(2,1)S(1)} collective-permute-done((bf16[768,512]{1,0:T(8,128)(2,1)}, bf16[768,512]{1,0:T(8,128)(2,1)S(1)}, u32[]{:S(2)}, u32[]{:S(2)}) %collective-permute-start.12) | collective-permute-done | bytes 786464 | tf_op jit(solution)/shard_map/ppermute | solution.py:144
  95.9 4.0 %collective-permute-start.13 = (bf16[768,512]{1,0:T(8,128)(2,1)S(1)}, bf16[768,512]{1,0:T(8,128)(2,1)S(1)}, u32[]{:S(2)}, u32[]{:S(2)}) collective-permute-start(bf16[768,512]{1,0:T(8,128)(2,1)S(1)} %add_convert_fusion.3), channel_id=1, source_target_pairs={{0,128},{1,33},{32,160},{33,65},{64,192},{65,97},{96,224},{97,1},{... | collective-permute-start | bytes 2359304 | tf_op jit(solution)/shard_map/ppermute | solution.py:144
  100.1 10.7 %collective-permute-start.26 = (bf16[96,1536]{1,0:T(8,128)(2,1)S(1)}, bf16[96,1536]{1,0:T(8,128)(2,1)S(1)}, u32[]{:S(2)}, u32[]{:S(2)}) collective-permute-start(bf16[96,1536]{1,0:T(8,128)(2,1)S(1)} %get-tuple-element.28), channel_id=1, source_target_pairs={{0,2},{1,7},{2,4},{3,1},{4,6},{5,3},{6,0},{7,5},{8,10},{9,15},{10,... | collective-permute-start | bytes 884744 | tf_op jit(solution)/shard_map/ppermute | solution.py:154
  110.9 3.2 %collective-permute-start.15 = (bf16[768,512]{1,0:T(8,128)(2,1)S(1)}, bf16[768,512]{1,0:T(8,128)(2,1)S(1)}, u32[]{:S(2)}, u32[]{:S(2)}) collective-permute-start(bf16[768,512]{1,0:T(8,128)(2,1)S(1)} %copy-done.9), channel_id=1, source_target_pairs={{0,128},{1,33},{32,160},{33,65},{64,192},{65,97},{96,224},{97,1},{... | collective-permute-start | bytes 2359304 | tf_op jit(solution)/shard_map/ppermute | solution.py:144
  116.4 7.6 %collective-permute-done.26 = bf16[96,1536]{1,0:T(8,128)(2,1)S(1)} collective-permute-done((bf16[96,1536]{1,0:T(8,128)(2,1)S(1)}, bf16[96,1536]{1,0:T(8,128)(2,1)S(1)}, u32[]{:S(2)}, u32[]{:S(2)}) %collective-permute-start.26) | collective-permute-done | bytes 294944 | tf_op jit(solution)/shard_map/ppermute | solution.py:154
  126.0 7.8 %collective-permute-start.27 = (bf16[96,1536]{1,0:T(8,128)(2,1)S(1)}, bf16[96,1536]{1,0:T(8,128)(2,1)S(1)}, u32[]{:S(2)}, u32[]{:S(2)}) collective-permute-start(bf16[96,1536]{1,0:T(8,128)(2,1)S(1)} %fusion), channel_id=1, source_target_pairs={{0,2},{1,7},{2,4},{3,1},{4,6},{5,3},{6,0},{7,5},{8,10},{9,15},{10,... | collective-permute-start | bytes 884744 | tf_op jit(solution)/shard_map/ppermute | solution.py:154
  136.6 2.8 %collective-permute-start.18 = (bf16[384,512]{1,0:T(8,128)(2,1)S(1)}, bf16[384,512]{1,0:T(8,128)(2,1)S(1)}, u32[]{:S(2)}, u32[]{:S(2)}) collective-permute-start(bf16[384,512]{1,0:T(8,128)(2,1)S(1)} %get-tuple-element.29), channel_id=1, source_target_pairs={{0,64},{1,257},{32,96},{33,289},{64,0},{65,321},{96,32},{97,353},{... | collective-permute-start | bytes 1179656 | tf_op jit(solution)/shard_map/ppermute | solution.py:144
  139.4 3.7 %collective-permute-start.20 = (bf16[384,512]{1,0:T(8,128)(2,1)S(1)}, bf16[384,512]{1,0:T(8,128)(2,1)S(1)}, u32[]{:S(2)}, u32[]{:S(2)}) collective-permute-start(bf16[384,512]{1,0:T(8,128)(2,1)S(1)} %get-tuple-element.30), channel_id=1, source_target_pairs={{0,96},{1,385},{32,0},{33,417},{64,32},{65,449},{96,64},{97,481},{... | collective-permute-start | bytes 1179656 | tf_op jit(solution)/shard_map/ppermute | solution.py:144
  143.1 11.3 %collective-permute-done.25 = bf16[96,1536]{1,0:T(8,128)(2,1)S(1)} collective-permute-done((bf16[96,1536]{1,0:T(8,128)(2,1)S(1)}, bf16[96,1536]{1,0:T(8,128)(2,1)S(1)}, u32[]{:S(2)}, u32[]{:S(2)}) %collective-permute-start.25) | collective-permute-done | bytes 294944 | tf_op jit(solution)/shard_map/ppermute | solution.py:154
  154.5 7.3 %collective-permute-start.29 = (bf16[96,1536]{1,0:T(8,128)(2,1)S(1)}, bf16[96,1536]{1,0:T(8,128)(2,1)S(1)}, u32[]{:S(2)}, u32[]{:S(2)}) collective-permute-start(bf16[96,1536]{1,0:T(8,128)(2,1)S(1)} %fusion.3.refs_0_), channel_id=1, source_target_pairs={{0,2},{1,7},{2,4},{3,1},{4,6},{5,3},{6,0},{7,5},{8,10},{9,15},{10,... | collective-permute-start | bytes 884744 | tf_op jit(solution)/shard_map/ppermute | solution.py:154
  163.8 8.6 %collective-permute-done.29.refs_2_ = bf16[96,1536]{1,0:T(8,128)(2,1)S(1)} collective-permute-done((bf16[96,1536]{1,0:T(8,128)(2,1)S(1)}, bf16[96,1536]{1,0:T(8,128)(2,1)S(1)}, u32[]{:S(2)}, u32[]{:S(2)}) %collective-permute-start.29) | collective-permute-done | bytes 294944 | tf_op jit(solution)/shard_map/ppermute | solution.py:154
  172.4 14.6 %collective-permute-start.33 = (bf16[96,1536]{1,0:T(8,128)(2,1)S(1)}, bf16[96,1536]{1,0:T(8,128)(2,1)S(1)}, u32[]{:S(2)}, u32[]{:S(2)}) collective-permute-start(bf16[96,1536]{1,0:T(8,128)(2,1)S(1)} %collective-permute-done.29.refs_2_), channel_id=1, source_target_pairs={{0,2},{1,7},{2,4},{3,1},{4,6},{5,3},{6,0},{7,5},{8,10},{9,15},{10,... | collective-permute-start | bytes 884744 | tf_op jit(solution)/shard_map/ppermute | solution.py:154
  191.1 3.4 %collective-permute-start.23 = (bf16[96,512]{1,0:T(8,128)(2,1)S(1)}, bf16[96,512]{1,0:T(8,128)(2,1)S(1)}, u32[]{:S(2)}, u32[]{:S(2)}) collective-permute-start(bf16[96,512]{1,0:T(8,128)(2,1)S(1)} %get-tuple-element.32), channel_id=1, source_target_pairs={{0,24},{8,0},{16,8},{24,16},{1,25},{9,1},{17,9},{25,17},{2,26},{10... | collective-permute-start | bytes 294920 | tf_op jit(solution)/shard_map/ppermute | solution.py:28
  196.4 16.9 %collective-permute-start.31 = (bf16[96,1536]{1,0:T(8,128)(2,1)S(1)}, bf16[96,1536]{1,0:T(8,128)(2,1)S(1)}, u32[]{:S(2)}, u32[]{:S(2)}) collective-permute-start(bf16[96,1536]{1,0:T(8,128)(2,1)S(1)} %collective-permute-done.29.refs_2_), channel_id=1, source_target_pairs={{0,1},{1,0},{2,3},{3,2},{4,5},{5,4},{6,7},{7,6},{8,9},{9,8},{10,11... | collective-permute-start | bytes 884744 | tf_op jit(solution)/shard_map/ppermute | solution.py:28
  (84 shorter events, 42.4 us)
Async XLA Ops:
  0.6 11.3 %collective-permute-start.1 = (bf16[96,512]{1,0:T(8,128)(2,1)}, bf16[96,512]{1,0:T(8,128)(2,1)S(1)}, u32[]{:S(2)}, u32[]{:S(2)}) collective-permute-start(bf16[96,512]{1,0:T(8,128)(2,1)} %bitcast.27), channel_id=1, source_target_pairs={{0,16},{8,24},{16,0},{24,8},{1,17},{9,25},{17,1},{25,9},{2,18},{10... | collective-permute-start | bytes 294920 | tf_op jit(solution)/shard_map/ppermute | solution.py:28
  5.5 6.3 %collective-permute-start = (bf16[96,512]{1,0:T(8,128)(2,1)}, bf16[96,512]{1,0:T(8,128)(2,1)S(1)}, u32[]{:S(2)}, u32[]{:S(2)}) collective-permute-start(bf16[96,512]{1,0:T(8,128)(2,1)} %bitcast.28), channel_id=1, source_target_pairs={{0,24},{8,0},{16,8},{24,16},{1,25},{9,1},{17,9},{25,17},{2,26},{10... | collective-permute-start | bytes 294920 | tf_op jit(solution)/shard_map/ppermute | solution.py:28
  13.3 13.6 %collective-permute-start.3 = (bf16[384,512]{1,0:T(8,128)(2,1)S(1)}, bf16[384,512]{1,0:T(8,128)(2,1)S(1)}, u32[]{:S(2)}, u32[]{:S(2)}) collective-permute-start(bf16[384,512]{1,0:T(8,128)(2,1)S(1)} %constant_dynamic-update-slice_fusion.2), channel_id=1, source_target_pairs={{0,96},{1,385},{32,0},{33,417},{64,32},{65,449},{96,64},{97,481},{... | collective-permute-start | bytes 1179656 | tf_op jit(solution)/shard_map/ppermute | solution.py:144
  17.9 11.2 %collective-permute-start.4 = (bf16[384,512]{1,0:T(8,128)(2,1)S(1)}, bf16[384,512]{1,0:T(8,128)(2,1)S(1)}, u32[]{:S(2)}, u32[]{:S(2)}) collective-permute-start(bf16[384,512]{1,0:T(8,128)(2,1)S(1)} %constant_dynamic-update-slice_fusion.2), channel_id=1, source_target_pairs={{0,64},{1,257},{32,96},{33,289},{64,0},{65,321},{96,32},{97,353},{... | collective-permute-start | bytes 1179656 | tf_op jit(solution)/shard_map/ppermute | solution.py:144
  20.2 12.0 %collective-permute-start.5 = (bf16[384,512]{1,0:T(8,128)(2,1)S(1)}, bf16[384,512]{1,0:T(8,128)(2,1)S(1)}, u32[]{:S(2)}, u32[]{:S(2)}) collective-permute-start(bf16[384,512]{1,0:T(8,128)(2,1)S(1)} %constant_dynamic-update-slice_fusion.2), channel_id=1, source_target_pairs={{0,32},{1,129},{32,64},{33,161},{64,96},{65,193},{96,0},{97,225},{... | collective-permute-start | bytes 1179656 | tf_op jit(solution)/shard_map/ppermute | solution.py:144
  26.9 13.4 %collective-permute-start.6 = (bf16[768,512]{1,0:T(8,128)(2,1)S(1)}, bf16[768,512]{1,0:T(8,128)(2,1)S(1)}, u32[]{:S(2)}, u32[]{:S(2)}) collective-permute-start(bf16[768,512]{1,0:T(8,128)(2,1)S(1)} %pad_maximum_fusion.refs_0_), channel_id=1, source_target_pairs={{0,384},{1,97},{32,416},{33,1},{64,448},{65,33},{96,480},{97,65},{... | collective-permute-start | bytes 2359304 | tf_op jit(solution)/shard_map/ppermute | solution.py:144
  32.2 13.1 %collective-permute-start.9 = (bf16[768,512]{1,0:T(8,128)(2,1)S(1)}, bf16[768,512]{1,0:T(8,128)(2,1)S(1)}, u32[]{:S(2)}, u32[]{:S(2)}) collective-permute-start(bf16[768,512]{1,0:T(8,128)(2,1)S(1)} %constant_dynamic-update-slice_fusion.refs_1_), channel_id=1, source_target_pairs={{0,128},{1,33},{32,160},{33,65},{64,192},{65,97},{96,224},{97,1},{... | collective-permute-start | bytes 2359304 | tf_op jit(solution)/shard_map/ppermute | solution.py:144
  35.1 18.7 %collective-permute-start.11 = (bf16[768,512]{1,0:T(8,128)(2,1)S(1)}, bf16[768,512]{1,0:T(8,128)(2,1)}, u32[]{:S(2)}, u32[]{:S(2)}) collective-permute-start(bf16[768,512]{1,0:T(8,128)(2,1)S(1)} %pad_maximum_fusion.refs_0_), channel_id=1, source_target_pairs={{0,128},{1,33},{32,160},{33,65},{64,192},{65,97},{96,224},{97,1},{... | collective-permute-start | bytes 2359304 | tf_op jit(solution)/shard_map/ppermute | solution.py:144
  37.5 16.3 %collective-permute-start.7 = (bf16[768,512]{1,0:T(8,128)(2,1)S(1)}, bf16[768,512]{1,0:T(8,128)(2,1)}, u32[]{:S(2)}, u32[]{:S(2)}) collective-permute-start(bf16[768,512]{1,0:T(8,128)(2,1)S(1)} %constant_dynamic-update-slice_fusion.refs_1_), channel_id=1, source_target_pairs={{0,384},{1,97},{32,416},{33,1},{64,448},{65,33},{96,480},{97,65},{... | collective-permute-start | bytes 2359304 | tf_op jit(solution)/shard_map/ppermute | solution.py:144
  40.4 18.7 %collective-permute-start.8 = (bf16[768,512]{1,0:T(8,128)(2,1)S(1)}, bf16[768,512]{1,0:T(8,128)(2,1)}, u32[]{:S(2)}, u32[]{:S(2)}) collective-permute-start(bf16[768,512]{1,0:T(8,128)(2,1)S(1)} %collective-permute-done.6.refs_2_), channel_id=1, source_target_pairs={{0,384},{1,97},{32,416},{33,1},{64,448},{65,33},{96,480},{97,65},{... | collective-permute-start | bytes 2359304 | tf_op jit(solution)/shard_map/ppermute | solution.py:144
  45.4 16.9 %collective-permute-start.10 = (bf16[768,512]{1,0:T(8,128)(2,1)S(1)}, bf16[768,512]{1,0:T(8,128)(2,1)}, u32[]{:S(2)}, u32[]{:S(2)}) collective-permute-start(bf16[768,512]{1,0:T(8,128)(2,1)S(1)} %collective-permute-done.9.refs_5_.refs_7_), channel_id=1, source_target_pairs={{0,128},{1,33},{32,160},{33,65},{64,192},{65,97},{96,224},{97,1},{... | collective-permute-start | bytes 2359304 | tf_op jit(solution)/shard_map/ppermute | solution.py:144
  70.2 29.8 %collective-permute-start.24 = (bf16[4,96,1536]{2,1,0:T(8,128)(2,1)}, bf16[4,96,1536]{2,1,0:T(8,128)(2,1)S(1)}, u32[]{:S(2)}, u32[]{:S(2)}) collective-permute-start(bf16[4,96,1536]{2,1,0:T(8,128)(2,1)} %get-tuple-element.26), channel_id=1, source_target_pairs={{0,1},{1,0},{2,3},{3,2},{4,5},{5,4},{6,7},{7,6},{8,9},{9,8},{10,11... | collective-permute-start | bytes 3538952 | tf_op jit(solution)/shard_map/ppermute | solution.py:28
  80.0 14.5 %collective-permute-start.12 = (bf16[768,512]{1,0:T(8,128)(2,1)}, bf16[768,512]{1,0:T(8,128)(2,1)S(1)}, u32[]{:S(2)}, u32[]{:S(2)}) collective-permute-start(bf16[768,512]{1,0:T(8,128)(2,1)} %get-tuple-element.19), channel_id=1, source_target_pairs={{0,128},{1,33},{32,160},{33,65},{64,192},{65,97},{96,224},{97,1},{... | collective-permute-start | bytes 2359304 | tf_op jit(solution)/shard_map/ppermute | solution.py:144
  85.2 28.9 %collective-permute-start.16 = (bf16[768,512]{1,0:T(8,128)(2,1)}, bf16[768,512]{1,0:T(8,128)(2,1)S(1)}, u32[]{:S(2)}, u32[]{:S(2)}) collective-permute-start(bf16[768,512]{1,0:T(8,128)(2,1)} %get-tuple-element.24), channel_id=1, source_target_pairs={{0,384},{1,97},{32,416},{33,1},{64,448},{65,33},{96,480},{97,65},{... | collective-permute-start | bytes 2359304 | tf_op jit(solution)/shard_map/ppermute | solution.py:144
  87.2 38.9 %collective-permute-start.14 = (bf16[768,512]{1,0:T(8,128)(2,1)}, bf16[768,512]{1,0:T(8,128)(2,1)S(1)}, u32[]{:S(2)}, u32[]{:S(2)}) collective-permute-start(bf16[768,512]{1,0:T(8,128)(2,1)} %get-tuple-element.20), channel_id=1, source_target_pairs={{0,384},{1,97},{32,416},{33,1},{64,448},{65,33},{96,480},{97,65},{... | collective-permute-start | bytes 2359304 | tf_op jit(solution)/shard_map/ppermute | solution.py:144
  95.9 37.9 %collective-permute-start.13 = (bf16[768,512]{1,0:T(8,128)(2,1)S(1)}, bf16[768,512]{1,0:T(8,128)(2,1)S(1)}, u32[]{:S(2)}, u32[]{:S(2)}) collective-permute-start(bf16[768,512]{1,0:T(8,128)(2,1)S(1)} %add_convert_fusion.3), channel_id=1, source_target_pairs={{0,128},{1,33},{32,160},{33,65},{64,192},{65,97},{96,224},{97,1},{... | collective-permute-start | bytes 2359304 | tf_op jit(solution)/shard_map/ppermute | solution.py:144
  100.1 23.9 %collective-permute-start.26 = (bf16[96,1536]{1,0:T(8,128)(2,1)S(1)}, bf16[96,1536]{1,0:T(8,128)(2,1)S(1)}, u32[]{:S(2)}, u32[]{:S(2)}) collective-permute-start(bf16[96,1536]{1,0:T(8,128)(2,1)S(1)} %get-tuple-element.28), channel_id=1, source_target_pairs={{0,2},{1,7},{2,4},{3,1},{4,6},{5,3},{6,0},{7,5},{8,10},{9,15},{10,... | collective-permute-start | bytes 884744 | tf_op jit(solution)/shard_map/ppermute | solution.py:154
  110.9 25.3 %collective-permute-start.15 = (bf16[768,512]{1,0:T(8,128)(2,1)S(1)}, bf16[768,512]{1,0:T(8,128)(2,1)S(1)}, u32[]{:S(2)}, u32[]{:S(2)}) collective-permute-start(bf16[768,512]{1,0:T(8,128)(2,1)S(1)} %copy-done.9), channel_id=1, source_target_pairs={{0,128},{1,33},{32,160},{33,65},{64,192},{65,97},{96,224},{97,1},{... | collective-permute-start | bytes 2359304 | tf_op jit(solution)/shard_map/ppermute | solution.py:144
  114.4 21.8 %collective-permute-start.17 = (bf16[768,512]{1,0:T(8,128)(2,1)S(1)}, bf16[768,512]{1,0:T(8,128)(2,1)S(1)}, u32[]{:S(2)}, u32[]{:S(2)}) collective-permute-start(bf16[768,512]{1,0:T(8,128)(2,1)S(1)} %add_convert_fusion.1), channel_id=1, source_target_pairs={{0,384},{1,97},{32,416},{33,1},{64,448},{65,33},{96,480},{97,65},{... | collective-permute-start | bytes 2359304 | tf_op jit(solution)/shard_map/ppermute | solution.py:144
  124.0 30.4 %collective-permute-start.25 = (bf16[96,1536]{1,0:T(8,128)(2,1)S(1)}, bf16[96,1536]{1,0:T(8,128)(2,1)S(1)}, u32[]{:S(2)}, u32[]{:S(2)}) collective-permute-start(bf16[96,1536]{1,0:T(8,128)(2,1)S(1)} %get-tuple-element.27), channel_id=1, source_target_pairs={{0,3},{1,6},{2,5},{3,0},{4,7},{5,2},{6,1},{7,4},{8,11},{9,14},{10,... | collective-permute-start | bytes 884744 | tf_op jit(solution)/shard_map/ppermute | solution.py:154
  126.0 28.3 %collective-permute-start.27 = (bf16[96,1536]{1,0:T(8,128)(2,1)S(1)}, bf16[96,1536]{1,0:T(8,128)(2,1)S(1)}, u32[]{:S(2)}, u32[]{:S(2)}) collective-permute-start(bf16[96,1536]{1,0:T(8,128)(2,1)S(1)} %fusion), channel_id=1, source_target_pairs={{0,2},{1,7},{2,4},{3,1},{4,6},{5,3},{6,0},{7,5},{8,10},{9,15},{10,... | collective-permute-start | bytes 884744 | tf_op jit(solution)/shard_map/ppermute | solution.py:154
  134.2 54.7 %collective-permute-start.19 = (bf16[384,512]{1,0:T(8,128)(2,1)S(1)}, bf16[384,512]{1,0:T(8,128)(2,1)S(1)}, u32[]{:S(2)}, u32[]{:S(2)}) collective-permute-start(bf16[384,512]{1,0:T(8,128)(2,1)S(1)} %slice.50), channel_id=1, source_target_pairs={{0,32},{1,129},{32,64},{33,161},{64,96},{65,193},{96,0},{97,225},{... | collective-permute-start | bytes 1179656 | tf_op jit(solution)/shard_map/ppermute | solution.py:144
  136.6 52.3 %collective-permute-start.18 = (bf16[384,512]{1,0:T(8,128)(2,1)S(1)}, bf16[384,512]{1,0:T(8,128)(2,1)S(1)}, u32[]{:S(2)}, u32[]{:S(2)}) collective-permute-start(bf16[384,512]{1,0:T(8,128)(2,1)S(1)} %get-tuple-element.29), channel_id=1, source_target_pairs={{0,64},{1,257},{32,96},{33,289},{64,0},{65,321},{96,32},{97,353},{... | collective-permute-start | bytes 1179656 | tf_op jit(solution)/shard_map/ppermute | solution.py:144
  139.4 49.5 %collective-permute-start.20 = (bf16[384,512]{1,0:T(8,128)(2,1)S(1)}, bf16[384,512]{1,0:T(8,128)(2,1)S(1)}, u32[]{:S(2)}, u32[]{:S(2)}) collective-permute-start(bf16[384,512]{1,0:T(8,128)(2,1)S(1)} %get-tuple-element.30), channel_id=1, source_target_pairs={{0,96},{1,385},{32,0},{33,417},{64,32},{65,449},{96,64},{97,481},{... | collective-permute-start | bytes 1179656 | tf_op jit(solution)/shard_map/ppermute | solution.py:144
  154.5 17.9 %collective-permute-start.29 = (bf16[96,1536]{1,0:T(8,128)(2,1)S(1)}, bf16[96,1536]{1,0:T(8,128)(2,1)S(1)}, u32[]{:S(2)}, u32[]{:S(2)}) collective-permute-start(bf16[96,1536]{1,0:T(8,128)(2,1)S(1)} %fusion.3.refs_0_), channel_id=1, source_target_pairs={{0,2},{1,7},{2,4},{3,1},{4,6},{5,3},{6,0},{7,5},{8,10},{9,15},{10,... | collective-permute-start | bytes 884744 | tf_op jit(solution)/shard_map/ppermute | solution.py:154
  161.8 25.1 %collective-permute-start.28 = (bf16[96,1536]{1,0:T(8,128)(2,1)S(1)}, bf16[96,1536]{1,0:T(8,128)(2,1)S(1)}, u32[]{:S(2)}, u32[]{:S(2)}) collective-permute-start(bf16[96,1536]{1,0:T(8,128)(2,1)S(1)} %fusion.3.refs_0_), channel_id=1, source_target_pairs={{0,1},{1,0},{2,3},{3,2},{4,5},{5,4},{6,7},{7,6},{8,9},{9,8},{10,11... | collective-permute-start | bytes 884744 | tf_op jit(solution)/shard_map/ppermute | solution.py:28
  172.4 40.9 %collective-permute-start.33 = (bf16[96,1536]{1,0:T(8,128)(2,1)S(1)}, bf16[96,1536]{1,0:T(8,128)(2,1)S(1)}, u32[]{:S(2)}, u32[]{:S(2)}) collective-permute-start(bf16[96,1536]{1,0:T(8,128)(2,1)S(1)} %collective-permute-done.29.refs_2_), channel_id=1, source_target_pairs={{0,2},{1,7},{2,4},{3,1},{4,6},{5,3},{6,0},{7,5},{8,10},{9,15},{10,... | collective-permute-start | bytes 884744 | tf_op jit(solution)/shard_map/ppermute | solution.py:154
  187.0 28.3 %collective-permute-start.30 = (bf16[96,1536]{1,0:T(8,128)(2,1)S(1)}, bf16[96,1536]{1,0:T(8,128)(2,1)S(1)}, u32[]{:S(2)}, u32[]{:S(2)}) collective-permute-start(bf16[96,1536]{1,0:T(8,128)(2,1)S(1)} %collective-permute-done.28.refs_1_), channel_id=1, source_target_pairs={{0,2},{1,7},{2,4},{3,1},{4,6},{5,3},{6,0},{7,5},{8,10},{9,15},{10,... | collective-permute-start | bytes 884744 | tf_op jit(solution)/shard_map/ppermute | solution.py:154
  189.2 7.2 %collective-permute-start.21 = (bf16[96,512]{1,0:T(8,128)(2,1)S(1)}, bf16[96,512]{1,0:T(8,128)(2,1)S(1)}, u32[]{:S(2)}, u32[]{:S(2)}) collective-permute-start(bf16[96,512]{1,0:T(8,128)(2,1)S(1)} %get-tuple-element.31), channel_id=1, source_target_pairs={{0,8},{8,16},{16,24},{24,0},{1,9},{9,17},{17,25},{25,1},{2,10},{10... | collective-permute-start | bytes 294920 | tf_op jit(solution)/shard_map/ppermute | solution.py:28
  191.1 26.6 %collective-permute-start.23 = (bf16[96,512]{1,0:T(8,128)(2,1)S(1)}, bf16[96,512]{1,0:T(8,128)(2,1)S(1)}, u32[]{:S(2)}, u32[]{:S(2)}) collective-permute-start(bf16[96,512]{1,0:T(8,128)(2,1)S(1)} %get-tuple-element.32), channel_id=1, source_target_pairs={{0,24},{8,0},{16,8},{24,16},{1,25},{9,1},{17,9},{25,17},{2,26},{10... | collective-permute-start | bytes 294920 | tf_op jit(solution)/shard_map/ppermute | solution.py:28
  194.5 23.2 %collective-permute-start.22 = (bf16[96,512]{1,0:T(8,128)(2,1)S(1)}, bf16[96,512]{1,0:T(8,128)(2,1)S(1)}, u32[]{:S(2)}, u32[]{:S(2)}) collective-permute-start(bf16[96,512]{1,0:T(8,128)(2,1)S(1)} %get-tuple-element.33), channel_id=1, source_target_pairs={{0,16},{8,24},{16,0},{24,8},{1,17},{9,25},{17,1},{25,9},{2,18},{10... | collective-permute-start | bytes 294920 | tf_op jit(solution)/shard_map/ppermute | solution.py:28
  196.4 22.0 %collective-permute-start.31 = (bf16[96,1536]{1,0:T(8,128)(2,1)S(1)}, bf16[96,1536]{1,0:T(8,128)(2,1)S(1)}, u32[]{:S(2)}, u32[]{:S(2)}) collective-permute-start(bf16[96,1536]{1,0:T(8,128)(2,1)S(1)} %collective-permute-done.29.refs_2_), channel_id=1, source_target_pairs={{0,1},{1,0},{2,3},{3,2},{4,5},{5,4},{6,7},{7,6},{8,9},{9,8},{10,11... | collective-permute-start | bytes 884744 | tf_op jit(solution)/shard_map/ppermute | solution.py:28
  (13 other events, 220.2 us)

commit v9 on v8

--- a/solution.py
+++ b/solution.py
@@ -109,7 +109,7 @@
     rows, depth = pieces[0].shape
     behind, ahead = 3 - 2 * core, 1 + 2 * core
     halves = []
-    for half, places in ((core, ((0, 0), (2, behind), (5, ahead), (6, 2))), (1 - core, ((1, 0), (3, behind), (4, ahead), (7, 2)))):
+    for half, places in ((core, ((0, 0), (2, behind), (3, ahead), (6, 2))), (1 - core, ((1, 0), (4, ahead), (5, behind), (7, 2)))):
         where = pl.ds(pl.multiple_of(half * rows, 16), rows)
         copies = []
         for at, d in places:
@@ -144,13 +144,13 @@
     return lax.ppermute(value, ("y", "x", "c"), [(flat(*s), flat(*target(*s))) for s in spots])
 
 
-def advance(value, cross=False):
+def advance(value, cross=False, back=False):
     pairs = []
     for zh in range(RING):
-        pairs += [
-            (zh * 2, (zh + 1) % RING * 2 + cross),
-            (zh * 2 + 1, (zh - 1) % RING * 2 + 1 - cross),
-        ]
+        up, down = (zh + 1) % RING * 2, (zh - 1) % RING * 2
+        if back:
+            up, down = down, up
+        pairs += [(zh * 2, up + cross), (zh * 2 + 1, down + 1 - cross)]
     return lax.ppermute(value, ("zh", "c"), pairs)
 
 
@@ -223,13 +223,12 @@
     cross_in = advance(follow.astype(BF16), cross=True)
     lead_in = advance((lead + passed.astype(F32)).astype(BF16))
     mine = (add_up([keep[3], arrived[3], cross_in, lead_in]) / (2 * RING)).astype(BF16)
-    next_lead = advance(mine)
-    other_mine = shift(mine, "c", 1)
-    next_follow = advance(other_mine)
-    far = advance(next_lead)
-    other_next_lead = shift(next_lead, "c", 1)
-    other_next_follow = shift(next_follow, "c", 1)
-    other_far = shift(far, "c", 1)
+    behind = advance(mine)
+    ahead = advance(mine, back=True)
+    far = advance(behind)
+    swapped = []
+    for value in (mine, behind, ahead, far):
+        swapped.append(shift(value, "c", 1))
     up_grad = pl.pallas_call(
         place_kernel,
         in_specs=[scalars] + [pl.BlockSpec(memory_space=pl.ANY)] * 8,
@@ -239,7 +238,7 @@
         compiler_params=pltpu.CompilerParams(vmem_limit_bytes=8 << 20),
         name="place",
         cost_estimate=pl.CostEstimate(flops=0, bytes_accessed=4 * hid * width, transcendentals=0),
-    )(pos, mine, other_mine, next_lead, next_follow, other_next_lead, other_next_follow, far, other_far)
+    )(pos, mine, swapped[0], behind, ahead, swapped[1], swapped[2], far, swapped[3])
 
     parts = pl.pallas_call(
         input_grad_kernel,
@@ -265,8 +264,7 @@
     )
     depth = stage.shape[0] // RING
     blocks = [stage[d * depth : (d + 1) * depth] for d in range(RING)]
-    arrived = [turn(blocks[2], False, 2), turn(blocks[1], False, 1)]
-    arrived += [turn(blocks[3], False, 3)]
+    arrived = [turn(blocks[d], False, d) for d in range(1, RING)]
     stage = add_up([blocks[0]] + arrived).astype(BF16)
     depth = stage.shape[0] // RING
     shares = [lax.dynamic_slice_in_dim(stage, ((zl + d) % RING) * depth, depth, axis=0) for d in range(RING)]

time: 222 us -> 227 us (1.023)
  starting transfers between devices: 141 us -> 145 us
    ppermute x11, starting transfers between devices: 45.4 us -> 52.6 us  [shift(): lax.ppermute(value, axis, [(i, (i + by) % size) for i in range(size)])]
    ppermute x6, starting transfers between devices: 44.2 us -> 40.2 us  [advance(): return lax.ppermute(value, ('zh', 'c'), pairs)]
where the time goes in v9:
time: 227 us; the launch traced here: 226 us
  starting transfers between devices  145 us (64%)
  waiting for transfers between devices  51.3 us (23%)
  Pallas kernels  23.4 us (10%)
  other arithmetic  4.33 us (2%)
    ppermute x11, starting transfers between devices, shift(): lax.ppermute(value, axis, [(i, (i + by) % size) for i in range(size)])  52.6 us
    ppermute x18, starting transfers between devices, turn(): lax.ppermute(value, ('y', 'x', 'c'), [(flat(*s), flat(*target(*s))) for s...  51.7 us
    ppermute x6, starting transfers between devices, advance(): return lax.ppermute(value, ('zh', 'c'), pairs)  40.2 us
    ppermute x6, waiting for transfers between devices, advance(): return lax.ppermute(value, ('zh', 'c'), pairs)  28.7 us
    ppermute x18, waiting for transfers between devices, turn(): lax.ppermute(value, ('y', 'x', 'c'), [(flat(*s), flat(*target(*s))) for s...  20.3 us
    pallas_call x1, Pallas kernels, work(): pl.pallas_call(forward_kernel, in_specs=[scalars] + vmem(2 * RING + 3), o...  7.99 us
    pallas_call x1, Pallas kernels, work(): pl.pallas_call(input_grad_kernel, in_specs=vmem(2), out_specs=vmem(2 * RI...  4.87 us
    pallas_call x1, Pallas kernels, work(): pl.pallas_call(early_kernel, in_specs=vmem(7), out_specs=vmem(1)[0], out_...  4.86 us
  transfers between devices with their start and end apart: 35, of which 13 were waited for; matrix products, arithmetic and copies ran while one was open for 2% of the time, Pallas kernels for 6%

profile of v9, /device:TPU:37, one launch (start us, length us, event | category | flops | bytes accessed | tf_op | source)
XLA Modules:
  0.0 226.0 jit_solution(2771867131114871770)
XLA Ops:
  0.6 4.9 %collective-permute-start.1 = (bf16[96,512]{1,0:T(8,128)(2,1)}, bf16[96,512]{1,0:T(8,128)(2,1)S(1)}, u32[]{:S(2)}, u32[]{:S(2)}) collective-permute-start(bf16[96,512]{1,0:T(8,128)(2,1)} %bitcast.27), channel_id=1, source_target_pairs={{0,16},{8,24},{16,0},{24,8},{1,17},{9,25},{17,1},{25,9},{2,18},{10... | collective-permute-start | bytes 294920 | tf_op jit(solution)/shard_map/ppermute | solution.py:28
  7.5 3.4 %collective-permute-start.2 = (bf16[96,512]{1,0:T(8,128)(2,1)}, bf16[96,512]{1,0:T(8,128)(2,1)S(1)}, u32[]{:S(2)}, u32[]{:S(2)}) collective-permute-start(bf16[96,512]{1,0:T(8,128)(2,1)} %bitcast.29), channel_id=1, source_target_pairs={{0,8},{8,16},{16,24},{24,0},{1,9},{9,17},{17,25},{25,1},{2,10},{10... | collective-permute-start | bytes 294920 | tf_op jit(solution)/shard_map/ppermute | solution.py:28
  13.3 4.6 %collective-permute-start.3 = (bf16[384,512]{1,0:T(8,128)(2,1)S(1)}, bf16[384,512]{1,0:T(8,128)(2,1)S(1)}, u32[]{:S(2)}, u32[]{:S(2)}) collective-permute-start(bf16[384,512]{1,0:T(8,128)(2,1)S(1)} %constant_dynamic-update-slice_fusion.2), channel_id=1, source_target_pairs={{0,96},{1,385},{32,0},{33,417},{64,32},{65,449},{96,64},{97,481},{... | collective-permute-start | bytes 1179656 | tf_op jit(solution)/shard_map/ppermute | solution.py:144
  20.2 2.6 %collective-permute-start.5 = (bf16[384,512]{1,0:T(8,128)(2,1)S(1)}, bf16[384,512]{1,0:T(8,128)(2,1)S(1)}, u32[]{:S(2)}, u32[]{:S(2)}) collective-permute-start(bf16[384,512]{1,0:T(8,128)(2,1)S(1)} %constant_dynamic-update-slice_fusion.2), channel_id=1, source_target_pairs={{0,32},{1,129},{32,64},{33,161},{64,96},{65,193},{96,0},{97,225},{... | collective-permute-start | bytes 1179656 | tf_op jit(solution)/shard_map/ppermute | solution.py:144
  22.8 4.0 %collective-permute-done.3 = bf16[384,512]{1,0:T(8,128)(2,1)S(1)} collective-permute-done((bf16[384,512]{1,0:T(8,128)(2,1)S(1)}, bf16[384,512]{1,0:T(8,128)(2,1)S(1)}, u32[]{:S(2)}, u32[]{:S(2)}) %collective-permute-start.3) | collective-permute-done | bytes 393248 | tf_op jit(solution)/shard_map/ppermute | solution.py:144
  29.1 3.0 %collective-permute-done.5 = bf16[384,512]{1,0:T(8,128)(2,1)S(1)} collective-permute-done((bf16[384,512]{1,0:T(8,128)(2,1)S(1)}, bf16[384,512]{1,0:T(8,128)(2,1)S(1)}, u32[]{:S(2)}, u32[]{:S(2)}) %collective-permute-start.5) | collective-permute-done | bytes 393248 | tf_op jit(solution)/shard_map/ppermute | solution.py:144
  32.2 2.8 %collective-permute-start.9 = (bf16[768,512]{1,0:T(8,128)(2,1)S(1)}, bf16[768,512]{1,0:T(8,128)(2,1)S(1)}, u32[]{:S(2)}, u32[]{:S(2)}) collective-permute-start(bf16[768,512]{1,0:T(8,128)(2,1)S(1)} %constant_dynamic-update-slice_fusion.refs_1_), channel_id=1, source_target_pairs={{0,128},{1,33},{32,160},{33,65},{64,192},{65,97},{96,224},{97,1},{... | collective-permute-start | bytes 2359304 | tf_op jit(solution)/shard_map/ppermute | solution.py:144
  37.5 2.9 %collective-permute-start.7 = (bf16[768,512]{1,0:T(8,128)(2,1)S(1)}, bf16[768,512]{1,0:T(8,128)(2,1)}, u32[]{:S(2)}, u32[]{:S(2)}) collective-permute-start(bf16[768,512]{1,0:T(8,128)(2,1)S(1)} %constant_dynamic-update-slice_fusion.refs_1_), channel_id=1, source_target_pairs={{0,384},{1,97},{32,416},{33,1},{64,448},{65,33},{96,480},{97,65},{... | collective-permute-start | bytes 2359304 | tf_op jit(solution)/shard_map/ppermute | solution.py:144
  42.8 2.5 %collective-permute-done.9.refs_5_.refs_7_ = bf16[768,512]{1,0:T(8,128)(2,1)S(1)} collective-permute-done((bf16[768,512]{1,0:T(8,128)(2,1)S(1)}, bf16[768,512]{1,0:T(8,128)(2,1)S(1)}, u32[]{:S(2)}, u32[]{:S(2)}) %collective-permute-start.9) | collective-permute-done | bytes 786464 | tf_op jit(solution)/shard_map/ppermute | solution.py:144
  45.4 2.7 %collective-permute-start.10 = (bf16[768,512]{1,0:T(8,128)(2,1)S(1)}, bf16[768,512]{1,0:T(8,128)(2,1)}, u32[]{:S(2)}, u32[]{:S(2)}) collective-permute-start(bf16[768,512]{1,0:T(8,128)(2,1)S(1)} %collective-permute-done.9.refs_5_.refs_7_), channel_id=1, source_target_pairs={{0,128},{1,33},{32,160},{33,65},{64,192},{65,97},{96,224},{97,1},{... | collective-permute-start | bytes 2359304 | tf_op jit(solution)/shard_map/ppermute | solution.py:144
  48.7 3.4 %order.1.up_ref.refs_10_ = bf16[192,6144]{1,0:T(8,128)(2,1)} custom-call(s32[4]{0:T(128)} %pad_add_fusion.pos_ref, bf16[192,6144]{1,0:T(8,128)(2,1)} %up_ref.1), custom_call_target="tpu_custom_call" | custom-call | bytes 4718592 | tf_op jit(solution)/shard_map/order/pallas_call | solution.py:175
  53.8 4.9 %early.1.refs_8_ = f32[192,512]{1,0:T(8,128)} custom-call(bf16[192,6144]{1,0:T(8,128)(2,1)} %order.1.up_ref.refs_10_, bf16[768,512]{1,0:T(8,128)(2,1)} %copy-done.1, bf16[768,512]{1,0:T(8,128)(2,1)} %copy-done.2, bf16[768,512]{1,0:T(8,128)(2,1)} %copy-done.3, bf16[768,512]{1,0:T(8,128)(2,1)} %collective-permute-done.7.refs_3_, ...), custom_call_target="tpu_custom_call" | custom-call | flops 905969664 | bytes 7000000 | tf_op jit(solution)/shard_map/early/pallas_call | solution.py:195
  59.0 3.2 %collective-permute-done.10.refs_5_ = bf16[768,512]{1,0:T(8,128)(2,1)} collective-permute-done((bf16[768,512]{1,0:T(8,128)(2,1)S(1)}, bf16[768,512]{1,0:T(8,128)(2,1)}, u32[]{:S(2)}, u32[]{:S(2)}) %collective-permute-start.10) | collective-permute-done | bytes 786464 | tf_op jit(solution)/shard_map/ppermute | solution.py:144
  62.2 8.0 %forward.1 = (bf16[192,512]{1,0:T(8,128)(2,1)}, bf16[192,512]{1,0:T(8,128)(2,1)}, bf16[4,96,1536]{2,1,0:T(8,128)(2,1)}, bf16[4,96,1536]{2,1,0:T(8,128)(2,1)}) custom-call(s32[4]{0:T(128)} %pad_add_fusion.pos_ref, bf16[768,512]{1,0:T(8,128)(2,1)} %copy-done.1, bf16[768,512]{1,0:T(8,128)(2,1)} %copy-done.2, bf16[768,512]{1,0:T(8,128)(2,1)} %copy-done.3, ...), custom_call_target="tpu_custom_call" | custom-call | flops 1811939328 | bytes 14000000 | tf_op jit(solution)/shard_map/forward/pallas_call | solution.py:204
  70.2 4.9 %collective-permute-start.24 = (bf16[4,96,1536]{2,1,0:T(8,128)(2,1)}, bf16[4,96,1536]{2,1,0:T(8,128)(2,1)S(1)}, u32[]{:S(2)}, u32[]{:S(2)}) collective-permute-start(bf16[4,96,1536]{2,1,0:T(8,128)(2,1)} %get-tuple-element.26), channel_id=1, source_target_pairs={{0,1},{1,0},{2,3},{3,2},{4,5},{5,4},{6,7},{7,6},{8,9},{9,8},{10,11... | collective-permute-start | bytes 3538952 | tf_op jit(solution)/shard_map/ppermute | solution.py:28
  75.1 4.9 %partial.1 = (bf16[768,512]{1,0:T(8,128)(2,1)}, bf16[768,512]{1,0:T(8,128)(2,1)}, bf16[768,512]{1,0:T(8,128)(2,1)}, bf16[768,512]{1,0:T(8,128)(2,1)}, bf16[768,5...) custom-call(bf16[192,512]{1,0:T(8,128)(2,1)} %get-tuple-element.16.grad_ref, ...), custom_call_target="tpu_custom_call" | custom-call | flops 1207959552 | bytes 9000000 | tf_op jit(solution)/shard_map/partial/pallas_call | solution.py:243
  80.0 5.3 %collective-permute-start.12 = (bf16[768,512]{1,0:T(8,128)(2,1)}, bf16[768,512]{1,0:T(8,128)(2,1)S(1)}, u32[]{:S(2)}, u32[]{:S(2)}) collective-permute-start(bf16[768,512]{1,0:T(8,128)(2,1)} %get-tuple-element.19), channel_id=1, source_target_pairs={{0,128},{1,33},{32,160},{33,65},{64,192},{65,97},{96,224},{97,1},{... | collective-permute-start | bytes 2359304 | tf_op jit(solution)/shard_map/ppermute | solution.py:144
  89.1 5.4 %collective-permute-done.12 = bf16[768,512]{1,0:T(8,128)(2,1)S(1)} collective-permute-done((bf16[768,512]{1,0:T(8,128)(2,1)}, bf16[768,512]{1,0:T(8,128)(2,1)S(1)}, u32[]{:S(2)}, u32[]{:S(2)}) %collective-permute-start.12) | collective-permute-done | bytes 786464 | tf_op jit(solution)/shard_map/ppermute | solution.py:144
  95.9 4.0 %collective-permute-start.13 = (bf16[768,512]{1,0:T(8,128)(2,1)S(1)}, bf16[768,512]{1,0:T(8,128)(2,1)S(1)}, u32[]{:S(2)}, u32[]{:S(2)}) collective-permute-start(bf16[768,512]{1,0:T(8,128)(2,1)S(1)} %add_convert_fusion.3), channel_id=1, source_target_pairs={{0,128},{1,33},{32,160},{33,65},{64,192},{65,97},{96,224},{97,1},{... | collective-permute-start | bytes 2359304 | tf_op jit(solution)/shard_map/ppermute | solution.py:144
  100.1 10.7 %collective-permute-start.26 = (bf16[96,1536]{1,0:T(8,128)(2,1)S(1)}, bf16[96,1536]{1,0:T(8,128)(2,1)S(1)}, u32[]{:S(2)}, u32[]{:S(2)}) collective-permute-start(bf16[96,1536]{1,0:T(8,128)(2,1)S(1)} %get-tuple-element.28), channel_id=1, source_target_pairs={{0,2},{1,7},{2,4},{3,1},{4,6},{5,3},{6,0},{7,5},{8,10},{9,15},{10,... | collective-permute-start | bytes 884744 | tf_op jit(solution)/shard_map/ppermute | solution.py:154
  110.9 3.2 %collective-permute-start.16 = (bf16[768,512]{1,0:T(8,128)(2,1)S(1)}, bf16[768,512]{1,0:T(8,128)(2,1)S(1)}, u32[]{:S(2)}, u32[]{:S(2)}) collective-permute-start(bf16[768,512]{1,0:T(8,128)(2,1)S(1)} %copy-done.9), channel_id=1, source_target_pairs={{0,128},{1,33},{32,160},{33,65},{64,192},{65,97},{96,224},{97,1},{... | collective-permute-start | bytes 2359304 | tf_op jit(solution)/shard_map/ppermute | solution.py:144
  116.4 7.6 %collective-permute-done.26 = bf16[96,1536]{1,0:T(8,128)(2,1)S(1)} collective-permute-done((bf16[96,1536]{1,0:T(8,128)(2,1)S(1)}, bf16[96,1536]{1,0:T(8,128)(2,1)S(1)}, u32[]{:S(2)}, u32[]{:S(2)}) %collective-permute-start.26) | collective-permute-done | bytes 294944 | tf_op jit(solution)/shard_map/ppermute | solution.py:154
  126.0 7.8 %collective-permute-start.27 = (bf16[96,1536]{1,0:T(8,128)(2,1)S(1)}, bf16[96,1536]{1,0:T(8,128)(2,1)S(1)}, u32[]{:S(2)}, u32[]{:S(2)}) collective-permute-start(bf16[96,1536]{1,0:T(8,128)(2,1)S(1)} %fusion), channel_id=1, source_target_pairs={{0,2},{1,7},{2,4},{3,1},{4,6},{5,3},{6,0},{7,5},{8,10},{9,15},{10,... | collective-permute-start | bytes 884744 | tf_op jit(solution)/shard_map/ppermute | solution.py:154
  136.6 2.8 %collective-permute-start.19 = (bf16[384,512]{1,0:T(8,128)(2,1)S(1)}, bf16[384,512]{1,0:T(8,128)(2,1)S(1)}, u32[]{:S(2)}, u32[]{:S(2)}) collective-permute-start(bf16[384,512]{1,0:T(8,128)(2,1)S(1)} %get-tuple-element.29), channel_id=1, source_target_pairs={{0,64},{1,257},{32,96},{33,289},{64,0},{65,321},{96,32},{97,353},{... | collective-permute-start | bytes 1179656 | tf_op jit(solution)/shard_map/ppermute | solution.py:144
  139.4 3.7 %collective-permute-start.20 = (bf16[384,512]{1,0:T(8,128)(2,1)S(1)}, bf16[384,512]{1,0:T(8,128)(2,1)S(1)}, u32[]{:S(2)}, u32[]{:S(2)}) collective-permute-start(bf16[384,512]{1,0:T(8,128)(2,1)S(1)} %get-tuple-element.30), channel_id=1, source_target_pairs={{0,96},{1,385},{32,0},{33,417},{64,32},{65,449},{96,64},{97,481},{... | collective-permute-start | bytes 1179656 | tf_op jit(solution)/shard_map/ppermute | solution.py:144
  143.1 11.3 %collective-permute-done.25 = bf16[96,1536]{1,0:T(8,128)(2,1)S(1)} collective-permute-done((bf16[96,1536]{1,0:T(8,128)(2,1)S(1)}, bf16[96,1536]{1,0:T(8,128)(2,1)S(1)}, u32[]{:S(2)}, u32[]{:S(2)}) %collective-permute-start.25) | collective-permute-done | bytes 294944 | tf_op jit(solution)/shard_map/ppermute | solution.py:154
  154.5 8.3 %collective-permute-start.29 = (bf16[96,1536]{1,0:T(8,128)(2,1)S(1)}, bf16[96,1536]{1,0:T(8,128)(2,1)S(1)}, u32[]{:S(2)}, u32[]{:S(2)}) collective-permute-start(bf16[96,1536]{1,0:T(8,128)(2,1)S(1)} %fusion.3.refs_0_), channel_id=1, source_target_pairs={{0,2},{1,7},{2,4},{3,1},{4,6},{5,3},{6,0},{7,5},{8,10},{9,15},{10,... | collective-permute-start | bytes 884744 | tf_op jit(solution)/shard_map/ppermute | solution.py:154
  164.8 9.9 %collective-permute-done.29.refs_2_ = bf16[96,1536]{1,0:T(8,128)(2,1)S(1)} collective-permute-done((bf16[96,1536]{1,0:T(8,128)(2,1)S(1)}, bf16[96,1536]{1,0:T(8,128)(2,1)S(1)}, u32[]{:S(2)}, u32[]{:S(2)}) %collective-permute-start.29) | collective-permute-done | bytes 294944 | tf_op jit(solution)/shard_map/ppermute | solution.py:154
  174.7 9.5 %collective-permute-start.33 = (bf16[96,1536]{1,0:T(8,128)(2,1)S(1)}, bf16[96,1536]{1,0:T(8,128)(2,1)S(1)}, u32[]{:S(2)}, u32[]{:S(2)}) collective-permute-start(bf16[96,1536]{1,0:T(8,128)(2,1)S(1)} %collective-permute-done.29.refs_2_), channel_id=1, source_target_pairs={{0,2},{1,7},{2,4},{3,1},{4,6},{5,3},{6,0},{7,5},{8,10},{9,15},{10,... | collective-permute-start | bytes 884744 | tf_op jit(solution)/shard_map/ppermute | solution.py:154
  184.5 12.4 %collective-permute-start.21 = (bf16[96,512]{1,0:T(8,128)(2,1)S(1)}, bf16[96,512]{1,0:T(8,128)(2,1)S(1)}, u32[]{:S(2)}, u32[]{:S(2)}) collective-permute-start(bf16[96,512]{1,0:T(8,128)(2,1)S(1)} %get-tuple-element.31), channel_id=1, source_target_pairs={{0,8},{8,16},{16,24},{24,0},{1,9},{9,17},{17,25},{25,1},{2,10},{10... | collective-permute-start | bytes 294920 | tf_op jit(solution)/shard_map/ppermute | solution.py:28
  198.9 3.1 %collective-permute-start.22 = (bf16[96,512]{1,0:T(8,128)(2,1)S(1)}, bf16[96,512]{1,0:T(8,128)(2,1)S(1)}, u32[]{:S(2)}, u32[]{:S(2)}) collective-permute-start(bf16[96,512]{1,0:T(8,128)(2,1)S(1)} %get-tuple-element.33), channel_id=1, source_target_pairs={{0,16},{8,24},{16,0},{24,8},{1,17},{9,25},{17,1},{25,9},{2,18},{10... | collective-permute-start | bytes 294920 | tf_op jit(solution)/shard_map/ppermute | solution.py:28
  202.0 13.9 %collective-permute-start.28 = (bf16[96,1536]{1,0:T(8,128)(2,1)S(1)}, bf16[96,1536]{1,0:T(8,128)(2,1)S(1)}, u32[]{:S(2)}, u32[]{:S(2)}) collective-permute-start(bf16[96,1536]{1,0:T(8,128)(2,1)S(1)} %fusion.3.refs_0_), channel_id=1, source_target_pairs={{0,1},{1,0},{2,3},{3,2},{4,5},{5,4},{6,7},{7,6},{8,9},{9,8},{10,11... | collective-permute-start | bytes 884744 | tf_op jit(solution)/shard_map/ppermute | solution.py:28
  (84 shorter events, 43.3 us)
Async XLA Ops:
  0.6 11.3 %collective-permute-start.1 = (bf16[96,512]{1,0:T(8,128)(2,1)}, bf16[96,512]{1,0:T(8,128)(2,1)S(1)}, u32[]{:S(2)}, u32[]{:S(2)}) collective-permute-start(bf16[96,512]{1,0:T(8,128)(2,1)} %bitcast.27), channel_id=1, source_target_pairs={{0,16},{8,24},{16,0},{24,8},{1,17},{9,25},{17,1},{25,9},{2,18},{10... | collective-permute-start | bytes 294920 | tf_op jit(solution)/shard_map/ppermute | solution.py:28
  5.5 6.3 %collective-permute-start = (bf16[96,512]{1,0:T(8,128)(2,1)}, bf16[96,512]{1,0:T(8,128)(2,1)S(1)}, u32[]{:S(2)}, u32[]{:S(2)}) collective-permute-start(bf16[96,512]{1,0:T(8,128)(2,1)} %bitcast.28), channel_id=1, source_target_pairs={{0,24},{8,0},{16,8},{24,16},{1,25},{9,1},{17,9},{25,17},{2,26},{10... | collective-permute-start | bytes 294920 | tf_op jit(solution)/shard_map/ppermute | solution.py:28
  13.3 13.6 %collective-permute-start.3 = (bf16[384,512]{1,0:T(8,128)(2,1)S(1)}, bf16[384,512]{1,0:T(8,128)(2,1)S(1)}, u32[]{:S(2)}, u32[]{:S(2)}) collective-permute-start(bf16[384,512]{1,0:T(8,128)(2,1)S(1)} %constant_dynamic-update-slice_fusion.2), channel_id=1, source_target_pairs={{0,96},{1,385},{32,0},{33,417},{64,32},{65,449},{96,64},{97,481},{... | collective-permute-start | bytes 1179656 | tf_op jit(solution)/shard_map/ppermute | solution.py:144
  17.9 11.2 %collective-permute-start.4 = (bf16[384,512]{1,0:T(8,128)(2,1)S(1)}, bf16[384,512]{1,0:T(8,128)(2,1)S(1)}, u32[]{:S(2)}, u32[]{:S(2)}) collective-permute-start(bf16[384,512]{1,0:T(8,128)(2,1)S(1)} %constant_dynamic-update-slice_fusion.2), channel_id=1, source_target_pairs={{0,64},{1,257},{32,96},{33,289},{64,0},{65,321},{96,32},{97,353},{... | collective-permute-start | bytes 1179656 | tf_op jit(solution)/shard_map/ppermute | solution.py:144
  20.2 12.0 %collective-permute-start.5 = (bf16[384,512]{1,0:T(8,128)(2,1)S(1)}, bf16[384,512]{1,0:T(8,128)(2,1)S(1)}, u32[]{:S(2)}, u32[]{:S(2)}) collective-permute-start(bf16[384,512]{1,0:T(8,128)(2,1)S(1)} %constant_dynamic-update-slice_fusion.2), channel_id=1, source_target_pairs={{0,32},{1,129},{32,64},{33,161},{64,96},{65,193},{96,0},{97,225},{... | collective-permute-start | bytes 1179656 | tf_op jit(solution)/shard_map/ppermute | solution.py:144
  26.9 13.4 %collective-permute-start.6 = (bf16[768,512]{1,0:T(8,128)(2,1)S(1)}, bf16[768,512]{1,0:T(8,128)(2,1)S(1)}, u32[]{:S(2)}, u32[]{:S(2)}) collective-permute-start(bf16[768,512]{1,0:T(8,128)(2,1)S(1)} %pad_maximum_fusion.refs_0_), channel_id=1, source_target_pairs={{0,384},{1,97},{32,416},{33,1},{64,448},{65,33},{96,480},{97,65},{... | collective-permute-start | bytes 2359304 | tf_op jit(solution)/shard_map/ppermute | solution.py:144
  32.2 13.1 %collective-permute-start.9 = (bf16[768,512]{1,0:T(8,128)(2,1)S(1)}, bf16[768,512]{1,0:T(8,128)(2,1)S(1)}, u32[]{:S(2)}, u32[]{:S(2)}) collective-permute-start(bf16[768,512]{1,0:T(8,128)(2,1)S(1)} %constant_dynamic-update-slice_fusion.refs_1_), channel_id=1, source_target_pairs={{0,128},{1,33},{32,160},{33,65},{64,192},{65,97},{96,224},{97,1},{... | collective-permute-start | bytes 2359304 | tf_op jit(solution)/shard_map/ppermute | solution.py:144
  35.1 18.7 %collective-permute-start.11 = (bf16[768,512]{1,0:T(8,128)(2,1)S(1)}, bf16[768,512]{1,0:T(8,128)(2,1)}, u32[]{:S(2)}, u32[]{:S(2)}) collective-permute-start(bf16[768,512]{1,0:T(8,128)(2,1)S(1)} %pad_maximum_fusion.refs_0_), channel_id=1, source_target_pairs={{0,128},{1,33},{32,160},{33,65},{64,192},{65,97},{96,224},{97,1},{... | collective-permute-start | bytes 2359304 | tf_op jit(solution)/shard_map/ppermute | solution.py:144
  37.5 16.3 %collective-permute-start.7 = (bf16[768,512]{1,0:T(8,128)(2,1)S(1)}, bf16[768,512]{1,0:T(8,128)(2,1)}, u32[]{:S(2)}, u32[]{:S(2)}) collective-permute-start(bf16[768,512]{1,0:T(8,128)(2,1)S(1)} %constant_dynamic-update-slice_fusion.refs_1_), channel_id=1, source_target_pairs={{0,384},{1,97},{32,416},{33,1},{64,448},{65,33},{96,480},{97,65},{... | collective-permute-start | bytes 2359304 | tf_op jit(solution)/shard_map/ppermute | solution.py:144
  40.4 18.7 %collective-permute-start.8 = (bf16[768,512]{1,0:T(8,128)(2,1)S(1)}, bf16[768,512]{1,0:T(8,128)(2,1)}, u32[]{:S(2)}, u32[]{:S(2)}) collective-permute-start(bf16[768,512]{1,0:T(8,128)(2,1)S(1)} %collective-permute-done.6.refs_2_), channel_id=1, source_target_pairs={{0,384},{1,97},{32,416},{33,1},{64,448},{65,33},{96,480},{97,65},{... | collective-permute-start | bytes 2359304 | tf_op jit(solution)/shard_map/ppermute | solution.py:144
  45.4 16.9 %collective-permute-start.10 = (bf16[768,512]{1,0:T(8,128)(2,1)S(1)}, bf16[768,512]{1,0:T(8,128)(2,1)}, u32[]{:S(2)}, u32[]{:S(2)}) collective-permute-start(bf16[768,512]{1,0:T(8,128)(2,1)S(1)} %collective-permute-done.9.refs_5_.refs_7_), channel_id=1, source_target_pairs={{0,128},{1,33},{32,160},{33,65},{64,192},{65,97},{96,224},{97,1},{... | collective-permute-start | bytes 2359304 | tf_op jit(solution)/shard_map/ppermute | solution.py:144
  70.2 29.8 %collective-permute-start.24 = (bf16[4,96,1536]{2,1,0:T(8,128)(2,1)}, bf16[4,96,1536]{2,1,0:T(8,128)(2,1)S(1)}, u32[]{:S(2)}, u32[]{:S(2)}) collective-permute-start(bf16[4,96,1536]{2,1,0:T(8,128)(2,1)} %get-tuple-element.26), channel_id=1, source_target_pairs={{0,1},{1,0},{2,3},{3,2},{4,5},{5,4},{6,7},{7,6},{8,9},{9,8},{10,11... | collective-permute-start | bytes 3538952 | tf_op jit(solution)/shard_map/ppermute | solution.py:28
  80.0 14.5 %collective-permute-start.12 = (bf16[768,512]{1,0:T(8,128)(2,1)}, bf16[768,512]{1,0:T(8,128)(2,1)S(1)}, u32[]{:S(2)}, u32[]{:S(2)}) collective-permute-start(bf16[768,512]{1,0:T(8,128)(2,1)} %get-tuple-element.19), channel_id=1, source_target_pairs={{0,128},{1,33},{32,160},{33,65},{64,192},{65,97},{96,224},{97,1},{... | collective-permute-start | bytes 2359304 | tf_op jit(solution)/shard_map/ppermute | solution.py:144
  85.2 28.9 %collective-permute-start.17 = (bf16[768,512]{1,0:T(8,128)(2,1)}, bf16[768,512]{1,0:T(8,128)(2,1)S(1)}, u32[]{:S(2)}, u32[]{:S(2)}) collective-permute-start(bf16[768,512]{1,0:T(8,128)(2,1)} %get-tuple-element.24), channel_id=1, source_target_pairs={{0,384},{1,97},{32,416},{33,1},{64,448},{65,33},{96,480},{97,65},{... | collective-permute-start | bytes 2359304 | tf_op jit(solution)/shard_map/ppermute | solution.py:144
  87.2 38.9 %collective-permute-start.14 = (bf16[768,512]{1,0:T(8,128)(2,1)}, bf16[768,512]{1,0:T(8,128)(2,1)S(1)}, u32[]{:S(2)}, u32[]{:S(2)}) collective-permute-start(bf16[768,512]{1,0:T(8,128)(2,1)} %get-tuple-element.20), channel_id=1, source_target_pairs={{0,384},{1,97},{32,416},{33,1},{64,448},{65,33},{96,480},{97,65},{... | collective-permute-start | bytes 2359304 | tf_op jit(solution)/shard_map/ppermute | solution.py:144
  95.9 37.9 %collective-permute-start.13 = (bf16[768,512]{1,0:T(8,128)(2,1)S(1)}, bf16[768,512]{1,0:T(8,128)(2,1)S(1)}, u32[]{:S(2)}, u32[]{:S(2)}) collective-permute-start(bf16[768,512]{1,0:T(8,128)(2,1)S(1)} %add_convert_fusion.3), channel_id=1, source_target_pairs={{0,128},{1,33},{32,160},{33,65},{64,192},{65,97},{96,224},{97,1},{... | collective-permute-start | bytes 2359304 | tf_op jit(solution)/shard_map/ppermute | solution.py:144
  100.1 23.9 %collective-permute-start.26 = (bf16[96,1536]{1,0:T(8,128)(2,1)S(1)}, bf16[96,1536]{1,0:T(8,128)(2,1)S(1)}, u32[]{:S(2)}, u32[]{:S(2)}) collective-permute-start(bf16[96,1536]{1,0:T(8,128)(2,1)S(1)} %get-tuple-element.28), channel_id=1, source_target_pairs={{0,2},{1,7},{2,4},{3,1},{4,6},{5,3},{6,0},{7,5},{8,10},{9,15},{10,... | collective-permute-start | bytes 884744 | tf_op jit(solution)/shard_map/ppermute | solution.py:154
  110.9 25.3 %collective-permute-start.16 = (bf16[768,512]{1,0:T(8,128)(2,1)S(1)}, bf16[768,512]{1,0:T(8,128)(2,1)S(1)}, u32[]{:S(2)}, u32[]{:S(2)}) collective-permute-start(bf16[768,512]{1,0:T(8,128)(2,1)S(1)} %copy-done.9), channel_id=1, source_target_pairs={{0,128},{1,33},{32,160},{33,65},{64,192},{65,97},{96,224},{97,1},{... | collective-permute-start | bytes 2359304 | tf_op jit(solution)/shard_map/ppermute | solution.py:144
  114.4 21.8 %collective-permute-start.18 = (bf16[768,512]{1,0:T(8,128)(2,1)S(1)}, bf16[768,512]{1,0:T(8,128)(2,1)S(1)}, u32[]{:S(2)}, u32[]{:S(2)}) collective-permute-start(bf16[768,512]{1,0:T(8,128)(2,1)S(1)} %add_convert_fusion.1), channel_id=1, source_target_pairs={{0,384},{1,97},{32,416},{33,1},{64,448},{65,33},{96,480},{97,65},{... | collective-permute-start | bytes 2359304 | tf_op jit(solution)/shard_map/ppermute | solution.py:144
  124.0 30.4 %collective-permute-start.25 = (bf16[96,1536]{1,0:T(8,128)(2,1)S(1)}, bf16[96,1536]{1,0:T(8,128)(2,1)S(1)}, u32[]{:S(2)}, u32[]{:S(2)}) collective-permute-start(bf16[96,1536]{1,0:T(8,128)(2,1)S(1)} %get-tuple-element.27), channel_id=1, source_target_pairs={{0,3},{1,6},{2,5},{3,0},{4,7},{5,2},{6,1},{7,4},{8,11},{9,14},{10,... | collective-permute-start | bytes 884744 | tf_op jit(solution)/shard_map/ppermute | solution.py:154
  126.0 28.3 %collective-permute-start.27 = (bf16[96,1536]{1,0:T(8,128)(2,1)S(1)}, bf16[96,1536]{1,0:T(8,128)(2,1)S(1)}, u32[]{:S(2)}, u32[]{:S(2)}) collective-permute-start(bf16[96,1536]{1,0:T(8,128)(2,1)S(1)} %fusion), channel_id=1, source_target_pairs={{0,2},{1,7},{2,4},{3,1},{4,6},{5,3},{6,0},{7,5},{8,10},{9,15},{10,... | collective-permute-start | bytes 884744 | tf_op jit(solution)/shard_map/ppermute | solution.py:154
  134.2 50.0 %collective-permute-start.15 = (bf16[384,512]{1,0:T(8,128)(2,1)S(1)}, bf16[384,512]{1,0:T(8,128)(2,1)S(1)}, u32[]{:S(2)}, u32[]{:S(2)}) collective-permute-start(bf16[384,512]{1,0:T(8,128)(2,1)S(1)} %slice.49), channel_id=1, source_target_pairs={{0,32},{1,129},{32,64},{33,161},{64,96},{65,193},{96,0},{97,225},{... | collective-permute-start | bytes 1179656 | tf_op jit(solution)/shard_map/ppermute | solution.py:144
  136.6 47.7 %collective-permute-start.19 = (bf16[384,512]{1,0:T(8,128)(2,1)S(1)}, bf16[384,512]{1,0:T(8,128)(2,1)S(1)}, u32[]{:S(2)}, u32[]{:S(2)}) collective-permute-start(bf16[384,512]{1,0:T(8,128)(2,1)S(1)} %get-tuple-element.29), channel_id=1, source_target_pairs={{0,64},{1,257},{32,96},{33,289},{64,0},{65,321},{96,32},{97,353},{... | collective-permute-start | bytes 1179656 | tf_op jit(solution)/shard_map/ppermute | solution.py:144
  139.4 44.9 %collective-permute-start.20 = (bf16[384,512]{1,0:T(8,128)(2,1)S(1)}, bf16[384,512]{1,0:T(8,128)(2,1)S(1)}, u32[]{:S(2)}, u32[]{:S(2)}) collective-permute-start(bf16[384,512]{1,0:T(8,128)(2,1)S(1)} %get-tuple-element.30), channel_id=1, source_target_pairs={{0,96},{1,385},{32,0},{33,417},{64,32},{65,449},{96,64},{97,481},{... | collective-permute-start | bytes 1179656 | tf_op jit(solution)/shard_map/ppermute | solution.py:144
  154.5 20.2 %collective-permute-start.29 = (bf16[96,1536]{1,0:T(8,128)(2,1)S(1)}, bf16[96,1536]{1,0:T(8,128)(2,1)S(1)}, u32[]{:S(2)}, u32[]{:S(2)}) collective-permute-start(bf16[96,1536]{1,0:T(8,128)(2,1)S(1)} %fusion.3.refs_0_), channel_id=1, source_target_pairs={{0,2},{1,7},{2,4},{3,1},{4,6},{5,3},{6,0},{7,5},{8,10},{9,15},{10,... | collective-permute-start | bytes 884744 | tf_op jit(solution)/shard_map/ppermute | solution.py:154
  162.9 39.1 %collective-permute-start.30 = (bf16[96,1536]{1,0:T(8,128)(2,1)S(1)}, bf16[96,1536]{1,0:T(8,128)(2,1)S(1)}, u32[]{:S(2)}, u32[]{:S(2)}) collective-permute-start(bf16[96,1536]{1,0:T(8,128)(2,1)S(1)} %fusion.3.refs_0_), channel_id=1, source_target_pairs={{0,6},{1,3},{2,0},{3,5},{4,2},{5,7},{6,4},{7,1},{8,14},{9,11},{10,... | collective-permute-start | bytes 884744 | tf_op jit(solution)/shard_map/ppermute | solution.py:154
  174.7 45.5 %collective-permute-start.33 = (bf16[96,1536]{1,0:T(8,128)(2,1)S(1)}, bf16[96,1536]{1,0:T(8,128)(2,1)S(1)}, u32[]{:S(2)}, u32[]{:S(2)}) collective-permute-start(bf16[96,1536]{1,0:T(8,128)(2,1)S(1)} %collective-permute-done.29.refs_2_), channel_id=1, source_target_pairs={{0,2},{1,7},{2,4},{3,1},{4,6},{5,3},{6,0},{7,5},{8,10},{9,15},{10,... | collective-permute-start | bytes 884744 | tf_op jit(solution)/shard_map/ppermute | solution.py:154
  184.5 31.4 %collective-permute-start.21 = (bf16[96,512]{1,0:T(8,128)(2,1)S(1)}, bf16[96,512]{1,0:T(8,128)(2,1)S(1)}, u32[]{:S(2)}, u32[]{:S(2)}) collective-permute-start(bf16[96,512]{1,0:T(8,128)(2,1)S(1)} %get-tuple-element.31), channel_id=1, source_target_pairs={{0,8},{8,16},{16,24},{24,0},{1,9},{9,17},{17,25},{25,1},{2,10},{10... | collective-permute-start | bytes 294920 | tf_op jit(solution)/shard_map/ppermute | solution.py:28
  196.9 20.9 %collective-permute-start.23 = (bf16[96,512]{1,0:T(8,128)(2,1)S(1)}, bf16[96,512]{1,0:T(8,128)(2,1)S(1)}, u32[]{:S(2)}, u32[]{:S(2)}) collective-permute-start(bf16[96,512]{1,0:T(8,128)(2,1)S(1)} %get-tuple-element.32), channel_id=1, source_target_pairs={{0,24},{8,0},{16,8},{24,16},{1,25},{9,1},{17,9},{25,17},{2,26},{10... | collective-permute-start | bytes 294920 | tf_op jit(solution)/shard_map/ppermute | solution.py:28
  198.9 23.3 %collective-permute-start.22 = (bf16[96,512]{1,0:T(8,128)(2,1)S(1)}, bf16[96,512]{1,0:T(8,128)(2,1)S(1)}, u32[]{:S(2)}, u32[]{:S(2)}) collective-permute-start(bf16[96,512]{1,0:T(8,128)(2,1)S(1)} %get-tuple-element.33), channel_id=1, source_target_pairs={{0,16},{8,24},{16,0},{24,8},{1,17},{9,25},{17,1},{25,9},{2,18},{10... | collective-permute-start | bytes 294920 | tf_op jit(solution)/shard_map/ppermute | solution.py:28
  202.0 20.9 %collective-permute-start.28 = (bf16[96,1536]{1,0:T(8,128)(2,1)S(1)}, bf16[96,1536]{1,0:T(8,128)(2,1)S(1)}, u32[]{:S(2)}, u32[]{:S(2)}) collective-permute-start(bf16[96,1536]{1,0:T(8,128)(2,1)S(1)} %fusion.3.refs_0_), channel_id=1, source_target_pairs={{0,1},{1,0},{2,3},{3,2},{4,5},{5,4},{6,7},{7,6},{8,9},{9,8},{10,11... | collective-permute-start | bytes 884744 | tf_op jit(solution)/shard_map/ppermute | solution.py:28
  215.9 7.0 %collective-permute-start.31 = (bf16[96,1536]{1,0:T(8,128)(2,1)S(1)}, bf16[96,1536]{1,0:T(8,128)(2,1)S(1)}, u32[]{:S(2)}, u32[]{:S(2)}) collective-permute-start(bf16[96,1536]{1,0:T(8,128)(2,1)S(1)} %collective-permute-done.29.refs_2_), channel_id=1, source_target_pairs={{0,1},{1,0},{2,3},{3,2},{4,5},{5,4},{6,7},{7,6},{8,9},{9,8},{10,11... | collective-permute-start | bytes 884744 | tf_op jit(solution)/shard_map/ppermute | solution.py:28
  (13 other events, 224.9 us)

commit v10 on v9

--- a/solution.py
+++ b/solution.py
@@ -264,11 +264,14 @@
     )
     depth = stage.shape[0] // RING
     blocks = [stage[d * depth : (d + 1) * depth] for d in range(RING)]
-    arrived = [turn(blocks[d], False, d) for d in range(1, RING)]
+    arrived = [turn(blocks[2], False, 2), turn(blocks[1], False, 1)]
+    arrived += [turn(blocks[3], False, 3)]
     stage = add_up([blocks[0]] + arrived).astype(BF16)
     depth = stage.shape[0] // RING
     shares = [lax.dynamic_slice_in_dim(stage, ((zl + d) % RING) * depth, depth, axis=0) for d in range(RING)]
-    input_grad = add_up(shares[:1] + [shift(shares[d], "zl", d) for d in range(1, RING)]).astype(BF16)
+    arrived = [shift(shares[d], "zl", d) for d in range(1, RING)]
+    up_grad, *arrived = lax.optimization_barrier([up_grad, *arrived])
+    input_grad = add_up(shares[:1] + arrived).astype(BF16)
     return (hidden.T, input_grad.T, up_grad)
 
 

time: 227 us -> 227 us (level)
  the two profiles are of different devices: /device:TPU:37 before, /device:TPU:6 now
where the time goes in v10:
time: 227 us; the launch traced here: 225 us
  starting transfers between devices  132 us (58%)
  waiting for transfers between devices  63.5 us (28%)
  Pallas kernels  23.4 us (10%)
  other arithmetic  4.33 us (2%)
    ppermute x18, starting transfers between devices, turn(): lax.ppermute(value, ('y', 'x', 'c'), [(flat(*s), flat(*target(*s))) for s...  60.7 us
    ppermute x11, starting transfers between devices, shift(): lax.ppermute(value, axis, [(i, (i + by) % size) for i in range(size)])  40.7 us
    ppermute x6, waiting for transfers between devices, advance(): return lax.ppermute(value, ('zh', 'c'), pairs)  40.4 us
    ppermute x6, starting transfers between devices, advance(): return lax.ppermute(value, ('zh', 'c'), pairs)  30.4 us
    ppermute x18, waiting for transfers between devices, turn(): lax.ppermute(value, ('y', 'x', 'c'), [(flat(*s), flat(*target(*s))) for s...  14.2 us
    ppermute x11, waiting for transfers between devices, shift(): lax.ppermute(value, axis, [(i, (i + by) % size) for i in range(size)])  8.95 us
    pallas_call x1, Pallas kernels, work(): pl.pallas_call(forward_kernel, in_specs=[scalars] + vmem(2 * RING + 3), o...  8 us
    pallas_call x1, Pallas kernels, work(): pl.pallas_call(input_grad_kernel, in_specs=vmem(2), out_specs=vmem(2 * RI...  4.86 us
  transfers between devices with their start and end apart: 35, of which 16 were waited for; matrix products, arithmetic and copies ran while one was open for 2% of the time, Pallas kernels for 7%

profile of v10, /device:TPU:6, one launch (start us, length us, event | category | flops | bytes accessed | tf_op | source)
XLA Modules:
  0.0 225.4 jit_solution(14763947712834768729)
XLA Ops:
  0.6 5.2 %collective-permute-start.1 = (bf16[96,512]{1,0:T(8,128)(2,1)}, bf16[96,512]{1,0:T(8,128)(2,1)S(1)}, u32[]{:S(2)}, u32[]{:S(2)}) collective-permute-start(bf16[96,512]{1,0:T(8,128)(2,1)} %bitcast.27), channel_id=1, source_target_pairs={{0,16},{8,24},{16,0},{24,8},{1,17},{9,25},{17,1},{25,9},{2,18},{10... | collective-permute-start | bytes 294920 | tf_op jit(solution)/shard_map/ppermute | solution.py:28
  5.8 3.3 %collective-permute-start = (bf16[96,512]{1,0:T(8,128)(2,1)}, bf16[96,512]{1,0:T(8,128)(2,1)S(1)}, u32[]{:S(2)}, u32[]{:S(2)}) collective-permute-start(bf16[96,512]{1,0:T(8,128)(2,1)} %bitcast.28), channel_id=1, source_target_pairs={{0,24},{8,0},{16,8},{24,16},{1,25},{9,1},{17,9},{25,17},{2,26},{10... | collective-permute-start | bytes 294920 | tf_op jit(solution)/shard_map/ppermute | solution.py:28
  13.0 4.6 %collective-permute-done.2 = bf16[96,512]{1,0:T(8,128)(2,1)S(1)} collective-permute-done((bf16[96,512]{1,0:T(8,128)(2,1)}, bf16[96,512]{1,0:T(8,128)(2,1)S(1)}, u32[]{:S(2)}, u32[]{:S(2)}) %collective-permute-start.2) | collective-permute-done | bytes 98336 | tf_op jit(solution)/shard_map/ppermute | solution.py:28
  17.6 2.7 %collective-permute-start.3 = (bf16[384,512]{1,0:T(8,128)(2,1)S(1)}, bf16[384,512]{1,0:T(8,128)(2,1)S(1)}, u32[]{:S(2)}, u32[]{:S(2)}) collective-permute-start(bf16[384,512]{1,0:T(8,128)(2,1)S(1)} %constant_dynamic-update-slice_fusion.2), channel_id=1, source_target_pairs={{0,96},{1,385},{32,0},{33,417},{64,32},{65,449},{96,64},{97,481},{... | collective-permute-start | bytes 1179656 | tf_op jit(solution)/shard_map/ppermute | solution.py:144
  20.4 4.3 %collective-permute-start.4 = (bf16[384,512]{1,0:T(8,128)(2,1)S(1)}, bf16[384,512]{1,0:T(8,128)(2,1)S(1)}, u32[]{:S(2)}, u32[]{:S(2)}) collective-permute-start(bf16[384,512]{1,0:T(8,128)(2,1)S(1)} %constant_dynamic-update-slice_fusion.2), channel_id=1, source_target_pairs={{0,64},{1,257},{32,96},{33,289},{64,0},{65,321},{96,32},{97,353},{... | collective-permute-start | bytes 1179656 | tf_op jit(solution)/shard_map/ppermute | solution.py:144
  24.7 2.7 %collective-permute-start.5 = (bf16[384,512]{1,0:T(8,128)(2,1)S(1)}, bf16[384,512]{1,0:T(8,128)(2,1)S(1)}, u32[]{:S(2)}, u32[]{:S(2)}) collective-permute-start(bf16[384,512]{1,0:T(8,128)(2,1)S(1)} %constant_dynamic-update-slice_fusion.2), channel_id=1, source_target_pairs={{0,32},{1,129},{32,64},{33,161},{64,96},{65,193},{96,0},{97,225},{... | collective-permute-start | bytes 1179656 | tf_op jit(solution)/shard_map/ppermute | solution.py:144
  28.6 9.1 %collective-permute-start.6 = (bf16[768,512]{1,0:T(8,128)(2,1)S(1)}, bf16[768,512]{1,0:T(8,128)(2,1)S(1)}, u32[]{:S(2)}, u32[]{:S(2)}) collective-permute-start(bf16[768,512]{1,0:T(8,128)(2,1)S(1)} %pad_maximum_fusion.refs_0_), channel_id=1, source_target_pairs={{0,384},{1,97},{32,416},{33,1},{64,448},{65,33},{96,480},{97,65},{... | collective-permute-start | bytes 2359304 | tf_op jit(solution)/shard_map/ppermute | solution.py:144
  39.8 3.0 %collective-permute-start.11 = (bf16[768,512]{1,0:T(8,128)(2,1)S(1)}, bf16[768,512]{1,0:T(8,128)(2,1)}, u32[]{:S(2)}, u32[]{:S(2)}) collective-permute-start(bf16[768,512]{1,0:T(8,128)(2,1)S(1)} %pad_maximum_fusion.refs_0_), channel_id=1, source_target_pairs={{0,128},{1,33},{32,160},{33,65},{64,192},{65,97},{96,224},{97,1},{... | collective-permute-start | bytes 2359304 | tf_op jit(solution)/shard_map/ppermute | solution.py:144
  42.7 4.1 %collective-permute-start.7 = (bf16[768,512]{1,0:T(8,128)(2,1)S(1)}, bf16[768,512]{1,0:T(8,128)(2,1)}, u32[]{:S(2)}, u32[]{:S(2)}) collective-permute-start(bf16[768,512]{1,0:T(8,128)(2,1)S(1)} %constant_dynamic-update-slice_fusion.refs_1_), channel_id=1, source_target_pairs={{0,384},{1,97},{32,416},{33,1},{64,448},{65,33},{96,480},{97,65},{... | collective-permute-start | bytes 2359304 | tf_op jit(solution)/shard_map/ppermute | solution.py:144
  47.2 5.6 %collective-permute-start.8 = (bf16[768,512]{1,0:T(8,128)(2,1)S(1)}, bf16[768,512]{1,0:T(8,128)(2,1)}, u32[]{:S(2)}, u32[]{:S(2)}) collective-permute-start(bf16[768,512]{1,0:T(8,128)(2,1)S(1)} %collective-permute-done.6.refs_2_), channel_id=1, source_target_pairs={{0,384},{1,97},{32,416},{33,1},{64,448},{65,33},{96,480},{97,65},{... | collective-permute-start | bytes 2359304 | tf_op jit(solution)/shard_map/ppermute | solution.py:144
  55.4 3.3 %order.1.up_ref.refs_10_ = bf16[192,6144]{1,0:T(8,128)(2,1)} custom-call(s32[4]{0:T(128)} %pad_add_fusion.pos_ref, bf16[192,6144]{1,0:T(8,128)(2,1)} %up_ref.1), custom_call_target="tpu_custom_call" | custom-call | bytes 4718592 | tf_op jit(solution)/shard_map/order/pallas_call | solution.py:175
  61.5 4.9 %early.1.refs_8_ = f32[192,512]{1,0:T(8,128)} custom-call(bf16[192,6144]{1,0:T(8,128)(2,1)} %order.1.up_ref.refs_10_, bf16[768,512]{1,0:T(8,128)(2,1)} %copy-done.1, bf16[768,512]{1,0:T(8,128)(2,1)} %copy-done.2, bf16[768,512]{1,0:T(8,128)(2,1)} %copy-done.3, bf16[768,512]{1,0:T(8,128)(2,1)} %collective-permute-done.7.refs_3_, ...), custom_call_target="tpu_custom_call" | custom-call | flops 905969664 | bytes 7000000 | tf_op jit(solution)/shard_map/early/pallas_call | solution.py:195
  66.3 3.6 %collective-permute-done.10.refs_5_ = bf16[768,512]{1,0:T(8,128)(2,1)} collective-permute-done((bf16[768,512]{1,0:T(8,128)(2,1)S(1)}, bf16[768,512]{1,0:T(8,128)(2,1)}, u32[]{:S(2)}, u32[]{:S(2)}) %collective-permute-start.10) | collective-permute-done | bytes 786464 | tf_op jit(solution)/shard_map/ppermute | solution.py:144
  69.9 8.0 %forward.1 = (bf16[192,512]{1,0:T(8,128)(2,1)}, bf16[192,512]{1,0:T(8,128)(2,1)}, bf16[4,96,1536]{2,1,0:T(8,128)(2,1)}, bf16[4,96,1536]{2,1,0:T(8,128)(2,1)}) custom-call(s32[4]{0:T(128)} %pad_add_fusion.pos_ref, bf16[768,512]{1,0:T(8,128)(2,1)} %copy-done.1, bf16[768,512]{1,0:T(8,128)(2,1)} %copy-done.2, bf16[768,512]{1,0:T(8,128)(2,1)} %copy-done.3, ...), custom_call_target="tpu_custom_call" | custom-call | flops 1811939328 | bytes 14000000 | tf_op jit(solution)/shard_map/forward/pallas_call | solution.py:204
  79.8 4.9 %partial.1 = (bf16[768,512]{1,0:T(8,128)(2,1)}, bf16[768,512]{1,0:T(8,128)(2,1)}, bf16[768,512]{1,0:T(8,128)(2,1)}, bf16[768,512]{1,0:T(8,128)(2,1)}, bf16[768,5...) custom-call(bf16[192,512]{1,0:T(8,128)(2,1)} %get-tuple-element.20.grad_ref, ...), custom_call_target="tpu_custom_call" | custom-call | flops 1207959552 | bytes 9000000 | tf_op jit(solution)/shard_map/partial/pallas_call | solution.py:243
  86.7 5.1 %collective-permute-start.16 = (bf16[768,512]{1,0:T(8,128)(2,1)}, bf16[768,512]{1,0:T(8,128)(2,1)S(1)}, u32[]{:S(2)}, u32[]{:S(2)}) collective-permute-start(bf16[768,512]{1,0:T(8,128)(2,1)} %get-tuple-element.28), channel_id=1, source_target_pairs={{0,384},{1,97},{32,416},{33,1},{64,448},{65,33},{96,480},{97,65},{... | collective-permute-start | bytes 2359304 | tf_op jit(solution)/shard_map/ppermute | solution.py:144
  93.8 6.3 %collective-permute-done.12 = bf16[768,512]{1,0:T(8,128)(2,1)S(1)} collective-permute-done((bf16[768,512]{1,0:T(8,128)(2,1)}, bf16[768,512]{1,0:T(8,128)(2,1)S(1)}, u32[]{:S(2)}, u32[]{:S(2)}) %collective-permute-start.12) | collective-permute-done | bytes 786464 | tf_op jit(solution)/shard_map/ppermute | solution.py:144
  103.7 9.1 %collective-permute-start.23 = (bf16[96,1536]{1,0:T(8,128)(2,1)S(1)}, bf16[96,1536]{1,0:T(8,128)(2,1)S(1)}, u32[]{:S(2)}, u32[]{:S(2)}) collective-permute-start(bf16[96,1536]{1,0:T(8,128)(2,1)S(1)} %get-tuple-element.36), channel_id=1, source_target_pairs={{0,2},{1,7},{2,4},{3,1},{4,6},{5,3},{6,0},{7,5},{8,10},{9,15},{10,... | collective-permute-start | bytes 884744 | tf_op jit(solution)/shard_map/ppermute | solution.py:154
  115.0 5.1 %collective-permute-start.17 = (bf16[768,512]{1,0:T(8,128)(2,1)S(1)}, bf16[768,512]{1,0:T(8,128)(2,1)S(1)}, u32[]{:S(2)}, u32[]{:S(2)}) collective-permute-start(bf16[768,512]{1,0:T(8,128)(2,1)S(1)} %add_convert_fusion.1), channel_id=1, source_target_pairs={{0,384},{1,97},{32,416},{33,1},{64,448},{65,33},{96,480},{97,65},{... | collective-permute-start | bytes 2359304 | tf_op jit(solution)/shard_map/ppermute | solution.py:144
  120.1 7.7 %collective-permute-done.23 = bf16[96,1536]{1,0:T(8,128)(2,1)S(1)} collective-permute-done((bf16[96,1536]{1,0:T(8,128)(2,1)S(1)}, bf16[96,1536]{1,0:T(8,128)(2,1)S(1)}, u32[]{:S(2)}, u32[]{:S(2)}) %collective-permute-start.23) | collective-permute-done | bytes 294944 | tf_op jit(solution)/shard_map/ppermute | solution.py:154
  127.8 3.7 %collective-permute-start.22 = (bf16[96,1536]{1,0:T(8,128)(2,1)S(1)}, bf16[96,1536]{1,0:T(8,128)(2,1)S(1)}, u32[]{:S(2)}, u32[]{:S(2)}) collective-permute-start(bf16[96,1536]{1,0:T(8,128)(2,1)S(1)} %get-tuple-element.35), channel_id=1, source_target_pairs={{0,3},{1,6},{2,5},{3,0},{4,7},{5,2},{6,1},{7,4},{8,11},{9,14},{10,... | collective-permute-start | bytes 884744 | tf_op jit(solution)/shard_map/ppermute | solution.py:154
  131.7 5.9 %collective-permute-start.24 = (bf16[96,1536]{1,0:T(8,128)(2,1)S(1)}, bf16[96,1536]{1,0:T(8,128)(2,1)S(1)}, u32[]{:S(2)}, u32[]{:S(2)}) collective-permute-start(bf16[96,1536]{1,0:T(8,128)(2,1)S(1)} %fusion), channel_id=1, source_target_pairs={{0,2},{1,7},{2,4},{3,1},{4,6},{5,3},{6,0},{7,5},{8,10},{9,15},{10,... | collective-permute-start | bytes 884744 | tf_op jit(solution)/shard_map/ppermute | solution.py:154
  140.6 9.4 %collective-permute-done.22 = bf16[96,1536]{1,0:T(8,128)(2,1)S(1)} collective-permute-done((bf16[96,1536]{1,0:T(8,128)(2,1)S(1)}, bf16[96,1536]{1,0:T(8,128)(2,1)S(1)}, u32[]{:S(2)}, u32[]{:S(2)}) %collective-permute-start.22) | collective-permute-done | bytes 294944 | tf_op jit(solution)/shard_map/ppermute | solution.py:154
  150.0 5.1 %collective-permute-done.24 = bf16[96,1536]{1,0:T(8,128)(2,1)S(1)} collective-permute-done((bf16[96,1536]{1,0:T(8,128)(2,1)S(1)}, bf16[96,1536]{1,0:T(8,128)(2,1)S(1)}, u32[]{:S(2)}, u32[]{:S(2)}) %collective-permute-start.24) | collective-permute-done | bytes 294944 | tf_op jit(solution)/shard_map/ppermute | solution.py:154
  155.3 4.3 %collective-permute-start.26 = (bf16[96,1536]{1,0:T(8,128)(2,1)S(1)}, bf16[96,1536]{1,0:T(8,128)(2,1)S(1)}, u32[]{:S(2)}, u32[]{:S(2)}) collective-permute-start(bf16[96,1536]{1,0:T(8,128)(2,1)S(1)} %fusion.3.refs_0_), channel_id=1, source_target_pairs={{0,2},{1,7},{2,4},{3,1},{4,6},{5,3},{6,0},{7,5},{8,10},{9,15},{10,... | collective-permute-start | bytes 884744 | tf_op jit(solution)/shard_map/ppermute | solution.py:154
  161.6 3.1 %collective-permute-start.20 = (bf16[384,512]{1,0:T(8,128)(2,1)S(1)}, bf16[384,512]{1,0:T(8,128)(2,1)S(1)}, u32[]{:S(2)}, u32[]{:S(2)}) collective-permute-start(bf16[384,512]{1,0:T(8,128)(2,1)S(1)} %get-tuple-element.38), channel_id=1, source_target_pairs={{0,96},{1,385},{32,0},{33,417},{64,32},{65,449},{96,64},{97,481},{... | collective-permute-start | bytes 1179656 | tf_op jit(solution)/shard_map/ppermute | solution.py:144
  164.7 5.5 %collective-permute-start.27 = (bf16[96,1536]{1,0:T(8,128)(2,1)S(1)}, bf16[96,1536]{1,0:T(8,128)(2,1)S(1)}, u32[]{:S(2)}, u32[]{:S(2)}) collective-permute-start(bf16[96,1536]{1,0:T(8,128)(2,1)S(1)} %fusion.3.refs_0_), channel_id=1, source_target_pairs={{0,6},{1,3},{2,0},{3,5},{4,2},{5,7},{6,4},{7,1},{8,14},{9,11},{10,... | collective-permute-start | bytes 884744 | tf_op jit(solution)/shard_map/ppermute | solution.py:154
  170.2 8.6 %collective-permute-done.26.refs_2_ = bf16[96,1536]{1,0:T(8,128)(2,1)S(1)} collective-permute-done((bf16[96,1536]{1,0:T(8,128)(2,1)S(1)}, bf16[96,1536]{1,0:T(8,128)(2,1)S(1)}, u32[]{:S(2)}, u32[]{:S(2)}) %collective-permute-start.26) | collective-permute-done | bytes 294944 | tf_op jit(solution)/shard_map/ppermute | solution.py:154
  185.1 5.5 %collective-permute-done.27.refs_3_ = bf16[96,1536]{1,0:T(8,128)(2,1)S(1)} collective-permute-done((bf16[96,1536]{1,0:T(8,128)(2,1)S(1)}, bf16[96,1536]{1,0:T(8,128)(2,1)S(1)}, u32[]{:S(2)}, u32[]{:S(2)}) %collective-permute-start.27) | collective-permute-done | bytes 294944 | tf_op jit(solution)/shard_map/ppermute | solution.py:154
  192.5 4.0 %collective-permute-done.30.refs_6_ = bf16[96,1536]{1,0:T(8,128)(2,1)S(1)} collective-permute-done((bf16[96,1536]{1,0:T(8,128)(2,1)S(1)}, bf16[96,1536]{1,0:T(8,128)(2,1)S(1)}, u32[]{:S(2)}, u32[]{:S(2)}) %collective-permute-start.30) | collective-permute-done | bytes 294944 | tf_op jit(solution)/shard_map/ppermute | solution.py:154
  198.7 14.1 %collective-permute-start.34 = (bf16[96,512]{1,0:T(8,128)(2,1)S(1)}, bf16[96,512]{1,0:T(8,128)(2,1)S(1)}, u32[]{:S(2)}, u32[]{:S(2)}) collective-permute-start(bf16[96,512]{1,0:T(8,128)(2,1)S(1)} %get-tuple-element.39), channel_id=1, source_target_pairs={{0,24},{8,0},{16,8},{24,16},{1,25},{9,1},{17,9},{25,17},{2,26},{10... | collective-permute-start | bytes 294920 | tf_op jit(solution)/shard_map/ppermute | solution.py:28
  212.9 3.5 %collective-permute-start.33 = (bf16[96,512]{1,0:T(8,128)(2,1)S(1)}, bf16[96,512]{1,0:T(8,128)(2,1)S(1)}, u32[]{:S(2)}, u32[]{:S(2)}) collective-permute-start(bf16[96,512]{1,0:T(8,128)(2,1)S(1)} %get-tuple-element.40), channel_id=1, source_target_pairs={{0,16},{8,24},{16,0},{24,8},{1,17},{9,25},{17,1},{25,9},{2,18},{10... | collective-permute-start | bytes 294920 | tf_op jit(solution)/shard_map/ppermute | solution.py:28
  (84 shorter events, 48.7 us)
Async XLA Ops:
  0.6 12.3 %collective-permute-start.1 = (bf16[96,512]{1,0:T(8,128)(2,1)}, bf16[96,512]{1,0:T(8,128)(2,1)S(1)}, u32[]{:S(2)}, u32[]{:S(2)}) collective-permute-start(bf16[96,512]{1,0:T(8,128)(2,1)} %bitcast.27), channel_id=1, source_target_pairs={{0,16},{8,24},{16,0},{24,8},{1,17},{9,25},{17,1},{25,9},{2,18},{10... | collective-permute-start | bytes 294920 | tf_op jit(solution)/shard_map/ppermute | solution.py:28
  17.6 10.9 %collective-permute-start.3 = (bf16[384,512]{1,0:T(8,128)(2,1)S(1)}, bf16[384,512]{1,0:T(8,128)(2,1)S(1)}, u32[]{:S(2)}, u32[]{:S(2)}) collective-permute-start(bf16[384,512]{1,0:T(8,128)(2,1)S(1)} %constant_dynamic-update-slice_fusion.2), channel_id=1, source_target_pairs={{0,96},{1,385},{32,0},{33,417},{64,32},{65,449},{96,64},{97,481},{... | collective-permute-start | bytes 1179656 | tf_op jit(solution)/shard_map/ppermute | solution.py:144
  20.4 17.3 %collective-permute-start.4 = (bf16[384,512]{1,0:T(8,128)(2,1)S(1)}, bf16[384,512]{1,0:T(8,128)(2,1)S(1)}, u32[]{:S(2)}, u32[]{:S(2)}) collective-permute-start(bf16[384,512]{1,0:T(8,128)(2,1)S(1)} %constant_dynamic-update-slice_fusion.2), channel_id=1, source_target_pairs={{0,64},{1,257},{32,96},{33,289},{64,0},{65,321},{96,32},{97,353},{... | collective-permute-start | bytes 1179656 | tf_op jit(solution)/shard_map/ppermute | solution.py:144
  24.7 13.1 %collective-permute-start.5 = (bf16[384,512]{1,0:T(8,128)(2,1)S(1)}, bf16[384,512]{1,0:T(8,128)(2,1)S(1)}, u32[]{:S(2)}, u32[]{:S(2)}) collective-permute-start(bf16[384,512]{1,0:T(8,128)(2,1)S(1)} %constant_dynamic-update-slice_fusion.2), channel_id=1, source_target_pairs={{0,32},{1,129},{32,64},{33,161},{64,96},{65,193},{96,0},{97,225},{... | collective-permute-start | bytes 1179656 | tf_op jit(solution)/shard_map/ppermute | solution.py:144
  28.6 18.6 %collective-permute-start.6 = (bf16[768,512]{1,0:T(8,128)(2,1)S(1)}, bf16[768,512]{1,0:T(8,128)(2,1)S(1)}, u32[]{:S(2)}, u32[]{:S(2)}) collective-permute-start(bf16[768,512]{1,0:T(8,128)(2,1)S(1)} %pad_maximum_fusion.refs_0_), channel_id=1, source_target_pairs={{0,384},{1,97},{32,416},{33,1},{64,448},{65,33},{96,480},{97,65},{... | collective-permute-start | bytes 2359304 | tf_op jit(solution)/shard_map/ppermute | solution.py:144
  37.8 15.1 %collective-permute-start.9 = (bf16[768,512]{1,0:T(8,128)(2,1)S(1)}, bf16[768,512]{1,0:T(8,128)(2,1)S(1)}, u32[]{:S(2)}, u32[]{:S(2)}) collective-permute-start(bf16[768,512]{1,0:T(8,128)(2,1)S(1)} %constant_dynamic-update-slice_fusion.refs_1_), channel_id=1, source_target_pairs={{0,128},{1,33},{32,160},{33,65},{64,192},{65,97},{96,224},{97,1},{... | collective-permute-start | bytes 2359304 | tf_op jit(solution)/shard_map/ppermute | solution.py:144
  39.8 21.7 %collective-permute-start.11 = (bf16[768,512]{1,0:T(8,128)(2,1)S(1)}, bf16[768,512]{1,0:T(8,128)(2,1)}, u32[]{:S(2)}, u32[]{:S(2)}) collective-permute-start(bf16[768,512]{1,0:T(8,128)(2,1)S(1)} %pad_maximum_fusion.refs_0_), channel_id=1, source_target_pairs={{0,128},{1,33},{32,160},{33,65},{64,192},{65,97},{96,224},{97,1},{... | collective-permute-start | bytes 2359304 | tf_op jit(solution)/shard_map/ppermute | solution.py:144
  42.7 18.7 %collective-permute-start.7 = (bf16[768,512]{1,0:T(8,128)(2,1)S(1)}, bf16[768,512]{1,0:T(8,128)(2,1)}, u32[]{:S(2)}, u32[]{:S(2)}) collective-permute-start(bf16[768,512]{1,0:T(8,128)(2,1)S(1)} %constant_dynamic-update-slice_fusion.refs_1_), channel_id=1, source_target_pairs={{0,384},{1,97},{32,416},{33,1},{64,448},{65,33},{96,480},{97,65},{... | collective-permute-start | bytes 2359304 | tf_op jit(solution)/shard_map/ppermute | solution.py:144
  47.2 19.1 %collective-permute-start.8 = (bf16[768,512]{1,0:T(8,128)(2,1)S(1)}, bf16[768,512]{1,0:T(8,128)(2,1)}, u32[]{:S(2)}, u32[]{:S(2)}) collective-permute-start(bf16[768,512]{1,0:T(8,128)(2,1)S(1)} %collective-permute-done.6.refs_2_), channel_id=1, source_target_pairs={{0,384},{1,97},{32,416},{33,1},{64,448},{65,33},{96,480},{97,65},{... | collective-permute-start | bytes 2359304 | tf_op jit(solution)/shard_map/ppermute | solution.py:144
  52.9 17.0 %collective-permute-start.10 = (bf16[768,512]{1,0:T(8,128)(2,1)S(1)}, bf16[768,512]{1,0:T(8,128)(2,1)}, u32[]{:S(2)}, u32[]{:S(2)}) collective-permute-start(bf16[768,512]{1,0:T(8,128)(2,1)S(1)} %collective-permute-done.9.refs_5_.refs_7_), channel_id=1, source_target_pairs={{0,128},{1,33},{32,160},{33,65},{64,192},{65,97},{96,224},{97,1},{... | collective-permute-start | bytes 2359304 | tf_op jit(solution)/shard_map/ppermute | solution.py:144
  77.9 25.6 %collective-permute-start.21 = (bf16[4,96,1536]{2,1,0:T(8,128)(2,1)}, bf16[4,96,1536]{2,1,0:T(8,128)(2,1)S(1)}, u32[]{:S(2)}, u32[]{:S(2)}) collective-permute-start(bf16[4,96,1536]{2,1,0:T(8,128)(2,1)} %get-tuple-element.30), channel_id=1, source_target_pairs={{0,1},{1,0},{2,3},{3,2},{4,5},{5,4},{6,7},{7,6},{8,9},{9,8},{10,11... | collective-permute-start | bytes 3538952 | tf_op jit(solution)/shard_map/ppermute | solution.py:28
  84.7 15.4 %collective-permute-start.12 = (bf16[768,512]{1,0:T(8,128)(2,1)}, bf16[768,512]{1,0:T(8,128)(2,1)S(1)}, u32[]{:S(2)}, u32[]{:S(2)}) collective-permute-start(bf16[768,512]{1,0:T(8,128)(2,1)} %get-tuple-element.23), channel_id=1, source_target_pairs={{0,128},{1,33},{32,160},{33,65},{64,192},{65,97},{96,224},{97,1},{... | collective-permute-start | bytes 2359304 | tf_op jit(solution)/shard_map/ppermute | solution.py:144
  86.7 28.0 %collective-permute-start.16 = (bf16[768,512]{1,0:T(8,128)(2,1)}, bf16[768,512]{1,0:T(8,128)(2,1)S(1)}, u32[]{:S(2)}, u32[]{:S(2)}) collective-permute-start(bf16[768,512]{1,0:T(8,128)(2,1)} %get-tuple-element.28), channel_id=1, source_target_pairs={{0,384},{1,97},{32,416},{33,1},{64,448},{65,33},{96,480},{97,65},{... | collective-permute-start | bytes 2359304 | tf_op jit(solution)/shard_map/ppermute | solution.py:144
  91.9 39.8 %collective-permute-start.14 = (bf16[768,512]{1,0:T(8,128)(2,1)}, bf16[768,512]{1,0:T(8,128)(2,1)S(1)}, u32[]{:S(2)}, u32[]{:S(2)}) collective-permute-start(bf16[768,512]{1,0:T(8,128)(2,1)} %get-tuple-element.24), channel_id=1, source_target_pairs={{0,384},{1,97},{32,416},{33,1},{64,448},{65,33},{96,480},{97,65},{... | collective-permute-start | bytes 2359304 | tf_op jit(solution)/shard_map/ppermute | solution.py:144
  101.6 36.0 %collective-permute-start.13 = (bf16[768,512]{1,0:T(8,128)(2,1)S(1)}, bf16[768,512]{1,0:T(8,128)(2,1)S(1)}, u32[]{:S(2)}, u32[]{:S(2)}) collective-permute-start(bf16[768,512]{1,0:T(8,128)(2,1)S(1)} %add_convert_fusion.3), channel_id=1, source_target_pairs={{0,128},{1,33},{32,160},{33,65},{64,192},{65,97},{96,224},{97,1},{... | collective-permute-start | bytes 2359304 | tf_op jit(solution)/shard_map/ppermute | solution.py:144
  103.7 24.2 %collective-permute-start.23 = (bf16[96,1536]{1,0:T(8,128)(2,1)S(1)}, bf16[96,1536]{1,0:T(8,128)(2,1)S(1)}, u32[]{:S(2)}, u32[]{:S(2)}) collective-permute-start(bf16[96,1536]{1,0:T(8,128)(2,1)S(1)} %get-tuple-element.36), channel_id=1, source_target_pairs={{0,2},{1,7},{2,4},{3,1},{4,6},{5,3},{6,0},{7,5},{8,10},{9,15},{10,... | collective-permute-start | bytes 884744 | tf_op jit(solution)/shard_map/ppermute | solution.py:154
  112.8 27.4 %collective-permute-start.15 = (bf16[768,512]{1,0:T(8,128)(2,1)S(1)}, bf16[768,512]{1,0:T(8,128)(2,1)S(1)}, u32[]{:S(2)}, u32[]{:S(2)}) collective-permute-start(bf16[768,512]{1,0:T(8,128)(2,1)S(1)} %copy-done.9), channel_id=1, source_target_pairs={{0,128},{1,33},{32,160},{33,65},{64,192},{65,97},{96,224},{97,1},{... | collective-permute-start | bytes 2359304 | tf_op jit(solution)/shard_map/ppermute | solution.py:144
  115.0 25.3 %collective-permute-start.17 = (bf16[768,512]{1,0:T(8,128)(2,1)S(1)}, bf16[768,512]{1,0:T(8,128)(2,1)S(1)}, u32[]{:S(2)}, u32[]{:S(2)}) collective-permute-start(bf16[768,512]{1,0:T(8,128)(2,1)S(1)} %add_convert_fusion.1), channel_id=1, source_target_pairs={{0,384},{1,97},{32,416},{33,1},{64,448},{65,33},{96,480},{97,65},{... | collective-permute-start | bytes 2359304 | tf_op jit(solution)/shard_map/ppermute | solution.py:144
  127.8 22.2 %collective-permute-start.22 = (bf16[96,1536]{1,0:T(8,128)(2,1)S(1)}, bf16[96,1536]{1,0:T(8,128)(2,1)S(1)}, u32[]{:S(2)}, u32[]{:S(2)}) collective-permute-start(bf16[96,1536]{1,0:T(8,128)(2,1)S(1)} %get-tuple-element.35), channel_id=1, source_target_pairs={{0,3},{1,6},{2,5},{3,0},{4,7},{5,2},{6,1},{7,4},{8,11},{9,14},{10,... | collective-permute-start | bytes 884744 | tf_op jit(solution)/shard_map/ppermute | solution.py:154
  131.7 23.5 %collective-permute-start.24 = (bf16[96,1536]{1,0:T(8,128)(2,1)S(1)}, bf16[96,1536]{1,0:T(8,128)(2,1)S(1)}, u32[]{:S(2)}, u32[]{:S(2)}) collective-permute-start(bf16[96,1536]{1,0:T(8,128)(2,1)S(1)} %fusion), channel_id=1, source_target_pairs={{0,2},{1,7},{2,4},{3,1},{4,6},{5,3},{6,0},{7,5},{8,10},{9,15},{10,... | collective-permute-start | bytes 884744 | tf_op jit(solution)/shard_map/ppermute | solution.py:154
  138.0 42.7 %collective-permute-start.19 = (bf16[384,512]{1,0:T(8,128)(2,1)S(1)}, bf16[384,512]{1,0:T(8,128)(2,1)S(1)}, u32[]{:S(2)}, u32[]{:S(2)}) collective-permute-start(bf16[384,512]{1,0:T(8,128)(2,1)S(1)} %slice.50), channel_id=1, source_target_pairs={{0,32},{1,129},{32,64},{33,161},{64,96},{65,193},{96,0},{97,225},{... | collective-permute-start | bytes 1179656 | tf_op jit(solution)/shard_map/ppermute | solution.py:144
  155.3 23.4 %collective-permute-start.26 = (bf16[96,1536]{1,0:T(8,128)(2,1)S(1)}, bf16[96,1536]{1,0:T(8,128)(2,1)S(1)}, u32[]{:S(2)}, u32[]{:S(2)}) collective-permute-start(bf16[96,1536]{1,0:T(8,128)(2,1)S(1)} %fusion.3.refs_0_), channel_id=1, source_target_pairs={{0,2},{1,7},{2,4},{3,1},{4,6},{5,3},{6,0},{7,5},{8,10},{9,15},{10,... | collective-permute-start | bytes 884744 | tf_op jit(solution)/shard_map/ppermute | solution.py:154
  159.7 23.0 %collective-permute-start.18 = (bf16[384,512]{1,0:T(8,128)(2,1)S(1)}, bf16[384,512]{1,0:T(8,128)(2,1)S(1)}, u32[]{:S(2)}, u32[]{:S(2)}) collective-permute-start(bf16[384,512]{1,0:T(8,128)(2,1)S(1)} %get-tuple-element.37), channel_id=1, source_target_pairs={{0,64},{1,257},{32,96},{33,289},{64,0},{65,321},{96,32},{97,353},{... | collective-permute-start | bytes 1179656 | tf_op jit(solution)/shard_map/ppermute | solution.py:144
  161.6 36.8 %collective-permute-start.20 = (bf16[384,512]{1,0:T(8,128)(2,1)S(1)}, bf16[384,512]{1,0:T(8,128)(2,1)S(1)}, u32[]{:S(2)}, u32[]{:S(2)}) collective-permute-start(bf16[384,512]{1,0:T(8,128)(2,1)S(1)} %get-tuple-element.38), channel_id=1, source_target_pairs={{0,96},{1,385},{32,0},{33,417},{64,32},{65,449},{96,64},{97,481},{... | collective-permute-start | bytes 1179656 | tf_op jit(solution)/shard_map/ppermute | solution.py:144
  164.7 25.8 %collective-permute-start.27 = (bf16[96,1536]{1,0:T(8,128)(2,1)S(1)}, bf16[96,1536]{1,0:T(8,128)(2,1)S(1)}, u32[]{:S(2)}, u32[]{:S(2)}) collective-permute-start(bf16[96,1536]{1,0:T(8,128)(2,1)S(1)} %fusion.3.refs_0_), channel_id=1, source_target_pairs={{0,6},{1,3},{2,0},{3,5},{4,2},{5,7},{6,4},{7,1},{8,14},{9,11},{10,... | collective-permute-start | bytes 884744 | tf_op jit(solution)/shard_map/ppermute | solution.py:154
  178.8 17.7 %collective-permute-start.30 = (bf16[96,1536]{1,0:T(8,128)(2,1)S(1)}, bf16[96,1536]{1,0:T(8,128)(2,1)S(1)}, u32[]{:S(2)}, u32[]{:S(2)}) collective-permute-start(bf16[96,1536]{1,0:T(8,128)(2,1)S(1)} %collective-permute-done.26.refs_2_), channel_id=1, source_target_pairs={{0,2},{1,7},{2,4},{3,1},{4,6},{5,3},{6,0},{7,5},{8,10},{9,15},{10,... | collective-permute-start | bytes 884744 | tf_op jit(solution)/shard_map/ppermute | solution.py:154
  180.7 32.1 %collective-permute-start.25 = (bf16[96,1536]{1,0:T(8,128)(2,1)S(1)}, bf16[96,1536]{1,0:T(8,128)(2,1)S(1)}, u32[]{:S(2)}, u32[]{:S(2)}) collective-permute-start(bf16[96,1536]{1,0:T(8,128)(2,1)S(1)} %fusion.3.refs_0_), channel_id=1, source_target_pairs={{0,1},{1,0},{2,3},{3,2},{4,5},{5,4},{6,7},{7,6},{8,9},{9,8},{10,11... | collective-permute-start | bytes 884744 | tf_op jit(solution)/shard_map/ppermute | solution.py:28
  182.6 35.7 %collective-permute-start.28 = (bf16[96,1536]{1,0:T(8,128)(2,1)S(1)}, bf16[96,1536]{1,0:T(8,128)(2,1)S(1)}, u32[]{:S(2)}, u32[]{:S(2)}) collective-permute-start(bf16[96,1536]{1,0:T(8,128)(2,1)S(1)} %collective-permute-done.26.refs_2_), channel_id=1, source_target_pairs={{0,1},{1,0},{2,3},{3,2},{4,5},{5,4},{6,7},{7,6},{8,9},{9,8},{10,11... | collective-permute-start | bytes 884744 | tf_op jit(solution)/shard_map/ppermute | solution.py:28
  190.6 25.8 %collective-permute-start.29 = (bf16[96,1536]{1,0:T(8,128)(2,1)S(1)}, bf16[96,1536]{1,0:T(8,128)(2,1)S(1)}, u32[]{:S(2)}, u32[]{:S(2)}) collective-permute-start(bf16[96,1536]{1,0:T(8,128)(2,1)S(1)} %collective-permute-done.27.refs_3_), channel_id=1, source_target_pairs={{0,1},{1,0},{2,3},{3,2},{4,5},{5,4},{6,7},{7,6},{8,9},{9,8},{10,11... | collective-permute-start | bytes 884744 | tf_op jit(solution)/shard_map/ppermute | solution.py:28
  196.5 21.8 %collective-permute-start.31 = (bf16[96,1536]{1,0:T(8,128)(2,1)S(1)}, bf16[96,1536]{1,0:T(8,128)(2,1)S(1)}, u32[]{:S(2)}, u32[]{:S(2)}) collective-permute-start(bf16[96,1536]{1,0:T(8,128)(2,1)S(1)} %collective-permute-done.30.refs_6_), channel_id=1, source_target_pairs={{0,1},{1,0},{2,3},{3,2},{4,5},{5,4},{6,7},{7,6},{8,9},{9,8},{10,11... | collective-permute-start | bytes 884744 | tf_op jit(solution)/shard_map/ppermute | solution.py:28
  198.7 22.0 %collective-permute-start.34 = (bf16[96,512]{1,0:T(8,128)(2,1)S(1)}, bf16[96,512]{1,0:T(8,128)(2,1)S(1)}, u32[]{:S(2)}, u32[]{:S(2)}) collective-permute-start(bf16[96,512]{1,0:T(8,128)(2,1)S(1)} %get-tuple-element.39), channel_id=1, source_target_pairs={{0,24},{8,0},{16,8},{24,16},{1,25},{9,1},{17,9},{25,17},{2,26},{10... | collective-permute-start | bytes 294920 | tf_op jit(solution)/shard_map/ppermute | solution.py:28
  212.9 9.2 %collective-permute-start.33 = (bf16[96,512]{1,0:T(8,128)(2,1)S(1)}, bf16[96,512]{1,0:T(8,128)(2,1)S(1)}, u32[]{:S(2)}, u32[]{:S(2)}) collective-permute-start(bf16[96,512]{1,0:T(8,128)(2,1)S(1)} %get-tuple-element.40), channel_id=1, source_target_pairs={{0,16},{8,24},{16,0},{24,8},{1,17},{9,25},{17,1},{25,9},{2,18},{10... | collective-permute-start | bytes 294920 | tf_op jit(solution)/shard_map/ppermute | solution.py:28
  (13 other events, 222.8 us)

commit v11 on v10

--- a/solution.py
+++ b/solution.py
@@ -105,23 +105,24 @@
 
 def place_kernel(pos_ref, *refs):
     core, zh = pos_ref[2], pos_ref[3]
-    pieces, (out_ref, whole_ref, sems) = refs[:8], refs[8:]
-    rows, depth = pieces[0].shape
+    own, (packed_ref, other_far_ref, out_ref, whole_ref, sems) = refs[:4], refs[4:]
+    rows, depth = own[0].shape
+    others = [packed_ref.at[:, pl.ds(at * depth, depth)] for at in range(3)] + [other_far_ref]
     behind, ahead = 3 - 2 * core, 1 + 2 * core
     halves = []
-    for half, places in ((core, ((0, 0), (2, behind), (3, ahead), (6, 2))), (1 - core, ((1, 0), (4, ahead), (5, behind), (7, 2)))):
+    for half, pieces, places in ((core, own, (0, behind, ahead, 2)), (1 - core, others, (0, ahead, behind, 2))):
         where = pl.ds(pl.multiple_of(half * rows, 16), rows)
         copies = []
-        for at, d in places:
+        for at, d in enumerate(places):
             columns = pl.ds(pl.multiple_of(lax.rem(zh + d, RING) * depth, 128), depth)
-            copies.append(pltpu.make_async_copy(pieces[at], whole_ref.at[where, columns], sems.at[at]))
+            copies.append(pltpu.make_async_copy(pieces[at], whole_ref.at[where, columns], sems.at[len(halves), at]))
             copies[-1].start()
         halves.append((where, copies))
     outs = []
     for at, (where, copies) in enumerate(halves):
         for copy in copies:
             copy.wait()
-        outs.append(pltpu.make_async_copy(whole_ref.at[where, :], out_ref.at[where, :], sems.at[8 + at]))
+        outs.append(pltpu.make_async_copy(whole_ref.at[where, :], out_ref.at[where, :], sems.at[at, RING]))
         outs[-1].start()
     for copy in outs:
         copy.wait()
@@ -226,19 +227,19 @@
     behind = advance(mine)
     ahead = advance(mine, back=True)
     far = advance(behind)
-    swapped = []
-    for value in (mine, behind, ahead, far):
-        swapped.append(shift(value, "c", 1))
+    packed = jnp.concatenate([mine, behind, ahead], axis=1)
+    other_packed = shift(packed, "c", 1)
+    other_far = shift(far, "c", 1)
     up_grad = pl.pallas_call(
         place_kernel,
-        in_specs=[scalars] + [pl.BlockSpec(memory_space=pl.ANY)] * 8,
+        in_specs=[scalars] + [pl.BlockSpec(memory_space=pl.ANY)] * 6,
         out_specs=pl.BlockSpec(memory_space=pl.ANY),
         out_shape=jax.ShapeDtypeStruct((hid, width), BF16),
-        scratch_shapes=[pltpu.VMEM((hid, width), BF16), pltpu.SemaphoreType.DMA((10,))],
+        scratch_shapes=[pltpu.VMEM((hid, width), BF16), pltpu.SemaphoreType.DMA((2, RING + 1))],
         compiler_params=pltpu.CompilerParams(vmem_limit_bytes=8 << 20),
         name="place",
         cost_estimate=pl.CostEstimate(flops=0, bytes_accessed=4 * hid * width, transcendentals=0),
-    )(pos, mine, swapped[0], behind, ahead, swapped[1], swapped[2], far, swapped[3])
+    )(pos, mine, behind, ahead, far, other_packed, other_far)
 
     parts = pl.pallas_call(
         input_grad_kernel,

time: 227 us -> 236 us (1.040)
  the two profiles are of different devices: /device:TPU:6 before, /device:TPU:16 now
where the time goes in v11:
time: 236 us; the launch traced here: 235 us
  starting transfers between devices  130 us (55%)
  waiting for transfers between devices  74.9 us (32%)
  Pallas kernels  23.4 us (10%)
  other arithmetic  4.43 us (2%)
    ppermute x18, starting transfers between devices, turn(): lax.ppermute(value, ('y', 'x', 'c'), [(flat(*s), flat(*target(*s))) for s...  54.8 us
    ppermute x6, waiting for transfers between devices, advance(): return lax.ppermute(value, ('zh', 'c'), pairs)  46.6 us
    ppermute x9, starting transfers between devices, shift(): lax.ppermute(value, axis, [(i, (i + by) % size) for i in range(size)])  41.8 us
    ppermute x6, starting transfers between devices, advance(): return lax.ppermute(value, ('zh', 'c'), pairs)  33.5 us
    ppermute x18, waiting for transfers between devices, turn(): lax.ppermute(value, ('y', 'x', 'c'), [(flat(*s), flat(*target(*s))) for s...  19.3 us
    ppermute x9, waiting for transfers between devices, shift(): lax.ppermute(value, axis, [(i, (i + by) % size) for i in range(size)])  8.97 us
    pallas_call x1, Pallas kernels, work(): pl.pallas_call(forward_kernel, in_specs=[scalars] + vmem(2 * RING + 3), o...  8 us
    pallas_call x1, Pallas kernels, work(): pl.pallas_call(input_grad_kernel, in_specs=vmem(2), out_specs=vmem(2 * RI...  4.88 us
  transfers between devices with their start and end apart: 33, of which 17 were waited for; matrix products, arithmetic and copies ran while one was open for 2% of the time, Pallas kernels for 7%

profile of v11, /device:TPU:16, one launch (start us, length us, event | category | flops | bytes accessed | tf_op | source)
XLA Modules:
  0.0 235.2 jit_solution(17446871192568033523)
XLA Ops:
  0.6 5.2 %collective-permute-start.1 = (bf16[96,512]{1,0:T(8,128)(2,1)}, bf16[96,512]{1,0:T(8,128)(2,1)S(1)}, u32[]{:S(2)}, u32[]{:S(2)}) collective-permute-start(bf16[96,512]{1,0:T(8,128)(2,1)} %bitcast.27), channel_id=1, source_target_pairs={{0,16},{8,24},{16,0},{24,8},{1,17},{9,25},{17,1},{25,9},{2,18},{10... | collective-permute-start | bytes 294920 | tf_op jit(solution)/shard_map/ppermute | solution.py:28
  5.8 3.3 %collective-permute-start = (bf16[96,512]{1,0:T(8,128)(2,1)}, bf16[96,512]{1,0:T(8,128)(2,1)S(1)}, u32[]{:S(2)}, u32[]{:S(2)}) collective-permute-start(bf16[96,512]{1,0:T(8,128)(2,1)} %bitcast.28), channel_id=1, source_target_pairs={{0,24},{8,0},{16,8},{24,16},{1,25},{9,1},{17,9},{25,17},{2,26},{10... | collective-permute-start | bytes 294920 | tf_op jit(solution)/shard_map/ppermute | solution.py:28
  13.0 4.6 %collective-permute-done.2 = bf16[96,512]{1,0:T(8,128)(2,1)S(1)} collective-permute-done((bf16[96,512]{1,0:T(8,128)(2,1)}, bf16[96,512]{1,0:T(8,128)(2,1)S(1)}, u32[]{:S(2)}, u32[]{:S(2)}) %collective-permute-start.2) | collective-permute-done | bytes 98336 | tf_op jit(solution)/shard_map/ppermute | solution.py:28
  17.6 4.7 %collective-permute-start.3 = (bf16[384,512]{1,0:T(8,128)(2,1)S(1)}, bf16[384,512]{1,0:T(8,128)(2,1)S(1)}, u32[]{:S(2)}, u32[]{:S(2)}) collective-permute-start(bf16[384,512]{1,0:T(8,128)(2,1)S(1)} %constant_dynamic-update-slice_fusion.2), channel_id=1, source_target_pairs={{0,96},{1,385},{32,0},{33,417},{64,32},{65,449},{96,64},{97,481},{... | collective-permute-start | bytes 1179656 | tf_op jit(solution)/shard_map/ppermute | solution.py:145
  27.8 3.3 %collective-permute-done.3 = bf16[384,512]{1,0:T(8,128)(2,1)S(1)} collective-permute-done((bf16[384,512]{1,0:T(8,128)(2,1)S(1)}, bf16[384,512]{1,0:T(8,128)(2,1)S(1)}, u32[]{:S(2)}, u32[]{:S(2)}) %collective-permute-start.3) | collective-permute-done | bytes 393248 | tf_op jit(solution)/shard_map/ppermute | solution.py:145
  31.2 3.4 %collective-permute-start.6 = (bf16[768,512]{1,0:T(8,128)(2,1)S(1)}, bf16[768,512]{1,0:T(8,128)(2,1)S(1)}, u32[]{:S(2)}, u32[]{:S(2)}) collective-permute-start(bf16[768,512]{1,0:T(8,128)(2,1)S(1)} %pad_maximum_fusion.1.refs_0_), channel_id=1, source_target_pairs={{0,384},{1,97},{32,416},{33,1},{64,448},{65,33},{96,480},{97,65},{... | collective-permute-start | bytes 2359304 | tf_op jit(solution)/shard_map/ppermute | solution.py:145
  37.7 3.2 %collective-permute-start.9 = (bf16[768,512]{1,0:T(8,128)(2,1)S(1)}, bf16[768,512]{1,0:T(8,128)(2,1)S(1)}, u32[]{:S(2)}, u32[]{:S(2)}) collective-permute-start(bf16[768,512]{1,0:T(8,128)(2,1)S(1)} %constant_dynamic-update-slice_fusion.refs_1_), channel_id=1, source_target_pairs={{0,128},{1,33},{32,160},{33,65},{64,192},{65,97},{96,224},{97,1},{... | collective-permute-start | bytes 2359304 | tf_op jit(solution)/shard_map/ppermute | solution.py:145
  43.1 3.7 %collective-permute-start.7 = (bf16[768,512]{1,0:T(8,128)(2,1)S(1)}, bf16[768,512]{1,0:T(8,128)(2,1)}, u32[]{:S(2)}, u32[]{:S(2)}) collective-permute-start(bf16[768,512]{1,0:T(8,128)(2,1)S(1)} %constant_dynamic-update-slice_fusion.refs_1_), channel_id=1, source_target_pairs={{0,384},{1,97},{32,416},{33,1},{64,448},{65,33},{96,480},{97,65},{... | collective-permute-start | bytes 2359304 | tf_op jit(solution)/shard_map/ppermute | solution.py:145
  51.6 3.2 %collective-permute-start.10 = (bf16[768,512]{1,0:T(8,128)(2,1)S(1)}, bf16[768,512]{1,0:T(8,128)(2,1)}, u32[]{:S(2)}, u32[]{:S(2)}) collective-permute-start(bf16[768,512]{1,0:T(8,128)(2,1)S(1)} %collective-permute-done.9.refs_5_.refs_7_), channel_id=1, source_target_pairs={{0,128},{1,33},{32,160},{33,65},{64,192},{65,97},{96,224},{97,1},{... | collective-permute-start | bytes 2359304 | tf_op jit(solution)/shard_map/ppermute | solution.py:145
  55.5 3.3 %order.1.up_ref.refs_10_ = bf16[192,6144]{1,0:T(8,128)(2,1)} custom-call(s32[4]{0:T(128)} %pad_add_fusion.pos_ref, bf16[192,6144]{1,0:T(8,128)(2,1)} %up_ref.1), custom_call_target="tpu_custom_call" | custom-call | bytes 4718592 | tf_op jit(solution)/shard_map/order/pallas_call | solution.py:176
  60.2 4.9 %early.1.refs_8_ = f32[192,512]{1,0:T(8,128)} custom-call(bf16[192,6144]{1,0:T(8,128)(2,1)} %order.1.up_ref.refs_10_, bf16[768,512]{1,0:T(8,128)(2,1)} %copy-done.1, bf16[768,512]{1,0:T(8,128)(2,1)} %copy-done.2, bf16[768,512]{1,0:T(8,128)(2,1)} %copy-done.3, bf16[768,512]{1,0:T(8,128)(2,1)} %collective-permute-done.7.refs_3_, ...), custom_call_target="tpu_custom_call" | custom-call | flops 905969664 | bytes 7000000 | tf_op jit(solution)/shard_map/early/pallas_call | solution.py:196
  68.6 8.0 %forward.1 = (bf16[192,512]{1,0:T(8,128)(2,1)}, bf16[192,512]{1,0:T(8,128)(2,1)}, bf16[4,96,1536]{2,1,0:T(8,128)(2,1)}, bf16[4,96,1536]{2,1,0:T(8,128)(2,1)}) custom-call(s32[4]{0:T(128)} %pad_add_fusion.pos_ref, bf16[768,512]{1,0:T(8,128)(2,1)} %copy-done.1, bf16[768,512]{1,0:T(8,128)(2,1)} %copy-done.2, bf16[768,512]{1,0:T(8,128)(2,1)} %copy-done.3, ...), custom_call_target="tpu_custom_call" | custom-call | flops 1811939328 | bytes 14000000 | tf_op jit(solution)/shard_map/forward/pallas_call | solution.py:205
  78.5 4.9 %partial.1 = (bf16[768,512]{1,0:T(8,128)(2,1)}, bf16[768,512]{1,0:T(8,128)(2,1)}, bf16[768,512]{1,0:T(8,128)(2,1)}, bf16[768,512]{1,0:T(8,128)(2,1)}, bf16[768,5...) custom-call(bf16[192,512]{1,0:T(8,128)(2,1)} %get-tuple-element.20.grad_ref, ...), custom_call_target="tpu_custom_call" | custom-call | flops 1207959552 | bytes 9000000 | tf_op jit(solution)/shard_map/partial/pallas_call | solution.py:244
  83.4 3.3 %collective-permute-start.12 = (bf16[768,512]{1,0:T(8,128)(2,1)}, bf16[768,512]{1,0:T(8,128)(2,1)S(1)}, u32[]{:S(2)}, u32[]{:S(2)}) collective-permute-start(bf16[768,512]{1,0:T(8,128)(2,1)} %get-tuple-element.23), channel_id=1, source_target_pairs={{0,128},{1,33},{32,160},{33,65},{64,192},{65,97},{96,224},{97,1},{... | collective-permute-start | bytes 2359304 | tf_op jit(solution)/shard_map/ppermute | solution.py:145
  91.7 5.9 %collective-permute-done.12 = bf16[768,512]{1,0:T(8,128)(2,1)S(1)} collective-permute-done((bf16[768,512]{1,0:T(8,128)(2,1)}, bf16[768,512]{1,0:T(8,128)(2,1)S(1)}, u32[]{:S(2)}, u32[]{:S(2)}) %collective-permute-start.12) | collective-permute-done | bytes 786464 | tf_op jit(solution)/shard_map/ppermute | solution.py:145
  99.1 3.2 %collective-permute-start.13 = (bf16[768,512]{1,0:T(8,128)(2,1)S(1)}, bf16[768,512]{1,0:T(8,128)(2,1)S(1)}, u32[]{:S(2)}, u32[]{:S(2)}) collective-permute-start(bf16[768,512]{1,0:T(8,128)(2,1)S(1)} %add_convert_fusion.3), channel_id=1, source_target_pairs={{0,128},{1,33},{32,160},{33,65},{64,192},{65,97},{96,224},{97,1},{... | collective-permute-start | bytes 2359304 | tf_op jit(solution)/shard_map/ppermute | solution.py:145
  102.4 9.1 %collective-permute-start.23 = (bf16[96,1536]{1,0:T(8,128)(2,1)S(1)}, bf16[96,1536]{1,0:T(8,128)(2,1)S(1)}, u32[]{:S(2)}, u32[]{:S(2)}) collective-permute-start(bf16[96,1536]{1,0:T(8,128)(2,1)S(1)} %get-tuple-element.36), channel_id=1, source_target_pairs={{0,2},{1,7},{2,4},{3,1},{4,6},{5,3},{6,0},{7,5},{8,10},{9,15},{10,... | collective-permute-start | bytes 884744 | tf_op jit(solution)/shard_map/ppermute | solution.py:155
  111.5 4.6 %collective-permute-start.15 = (bf16[768,512]{1,0:T(8,128)(2,1)S(1)}, bf16[768,512]{1,0:T(8,128)(2,1)S(1)}, u32[]{:S(2)}, u32[]{:S(2)}) collective-permute-start(bf16[768,512]{1,0:T(8,128)(2,1)S(1)} %copy-done.9), channel_id=1, source_target_pairs={{0,128},{1,33},{32,160},{33,65},{64,192},{65,97},{96,224},{97,1},{... | collective-permute-start | bytes 2359304 | tf_op jit(solution)/shard_map/ppermute | solution.py:145
  118.3 8.3 %collective-permute-done.23 = bf16[96,1536]{1,0:T(8,128)(2,1)S(1)} collective-permute-done((bf16[96,1536]{1,0:T(8,128)(2,1)S(1)}, bf16[96,1536]{1,0:T(8,128)(2,1)S(1)}, u32[]{:S(2)}, u32[]{:S(2)}) %collective-permute-start.23) | collective-permute-done | bytes 294944 | tf_op jit(solution)/shard_map/ppermute | solution.py:155
  126.6 3.3 %collective-permute-start.22 = (bf16[96,1536]{1,0:T(8,128)(2,1)S(1)}, bf16[96,1536]{1,0:T(8,128)(2,1)S(1)}, u32[]{:S(2)}, u32[]{:S(2)}) collective-permute-start(bf16[96,1536]{1,0:T(8,128)(2,1)S(1)} %get-tuple-element.35), channel_id=1, source_target_pairs={{0,3},{1,6},{2,5},{3,0},{4,7},{5,2},{6,1},{7,4},{8,11},{9,14},{10,... | collective-permute-start | bytes 884744 | tf_op jit(solution)/shard_map/ppermute | solution.py:155
  130.0 5.9 %collective-permute-start.24 = (bf16[96,1536]{1,0:T(8,128)(2,1)S(1)}, bf16[96,1536]{1,0:T(8,128)(2,1)S(1)}, u32[]{:S(2)}, u32[]{:S(2)}) collective-permute-start(bf16[96,1536]{1,0:T(8,128)(2,1)S(1)} %fusion), channel_id=1, source_target_pairs={{0,2},{1,7},{2,4},{3,1},{4,6},{5,3},{6,0},{7,5},{8,10},{9,15},{10,... | collective-permute-start | bytes 884744 | tf_op jit(solution)/shard_map/ppermute | solution.py:155
  138.4 9.8 %collective-permute-done.22 = bf16[96,1536]{1,0:T(8,128)(2,1)S(1)} collective-permute-done((bf16[96,1536]{1,0:T(8,128)(2,1)S(1)}, bf16[96,1536]{1,0:T(8,128)(2,1)S(1)}, u32[]{:S(2)}, u32[]{:S(2)}) %collective-permute-start.22) | collective-permute-done | bytes 294944 | tf_op jit(solution)/shard_map/ppermute | solution.py:155
  148.2 5.1 %collective-permute-done.24 = bf16[96,1536]{1,0:T(8,128)(2,1)S(1)} collective-permute-done((bf16[96,1536]{1,0:T(8,128)(2,1)S(1)}, bf16[96,1536]{1,0:T(8,128)(2,1)S(1)}, u32[]{:S(2)}, u32[]{:S(2)}) %collective-permute-start.24) | collective-permute-done | bytes 294944 | tf_op jit(solution)/shard_map/ppermute | solution.py:155
  153.5 6.5 %collective-permute-start.26 = (bf16[96,1536]{1,0:T(8,128)(2,1)S(1)}, bf16[96,1536]{1,0:T(8,128)(2,1)S(1)}, u32[]{:S(2)}, u32[]{:S(2)}) collective-permute-start(bf16[96,1536]{1,0:T(8,128)(2,1)S(1)} %fusion.3.refs_0_), channel_id=1, source_target_pairs={{0,6},{1,3},{2,0},{3,5},{4,2},{5,7},{6,4},{7,1},{8,14},{9,11},{10,... | collective-permute-start | bytes 884744 | tf_op jit(solution)/shard_map/ppermute | solution.py:155
  160.0 3.3 %collective-permute-start.25 = (bf16[96,1536]{1,0:T(8,128)(2,1)S(1)}, bf16[96,1536]{1,0:T(8,128)(2,1)S(1)}, u32[]{:S(2)}, u32[]{:S(2)}) collective-permute-start(bf16[96,1536]{1,0:T(8,128)(2,1)S(1)} %fusion.3.refs_0_), channel_id=1, source_target_pairs={{0,2},{1,7},{2,4},{3,1},{4,6},{5,3},{6,0},{7,5},{8,10},{9,15},{10,... | collective-permute-start | bytes 884744 | tf_op jit(solution)/shard_map/ppermute | solution.py:155
  163.7 3.2 %collective-permute-start.18 = (bf16[384,512]{1,0:T(8,128)(2,1)S(1)}, bf16[384,512]{1,0:T(8,128)(2,1)S(1)}, u32[]{:S(2)}, u32[]{:S(2)}) collective-permute-start(bf16[384,512]{1,0:T(8,128)(2,1)S(1)} %get-tuple-element.37), channel_id=1, source_target_pairs={{0,64},{1,257},{32,96},{33,289},{64,0},{65,321},{96,32},{97,353},{... | collective-permute-start | bytes 1179656 | tf_op jit(solution)/shard_map/ppermute | solution.py:145
  166.9 3.2 %collective-permute-start.20 = (bf16[384,512]{1,0:T(8,128)(2,1)S(1)}, bf16[384,512]{1,0:T(8,128)(2,1)S(1)}, u32[]{:S(2)}, u32[]{:S(2)}) collective-permute-start(bf16[384,512]{1,0:T(8,128)(2,1)S(1)} %get-tuple-element.38), channel_id=1, source_target_pairs={{0,96},{1,385},{32,0},{33,417},{64,32},{65,449},{96,64},{97,481},{... | collective-permute-start | bytes 1179656 | tf_op jit(solution)/shard_map/ppermute | solution.py:145
  172.0 7.8 %collective-permute-done.25.refs_1_ = bf16[96,1536]{1,0:T(8,128)(2,1)S(1)} collective-permute-done((bf16[96,1536]{1,0:T(8,128)(2,1)S(1)}, bf16[96,1536]{1,0:T(8,128)(2,1)S(1)}, u32[]{:S(2)}, u32[]{:S(2)}) %collective-permute-start.25) | collective-permute-done | bytes 294944 | tf_op jit(solution)/shard_map/ppermute | solution.py:155
  181.9 5.4 %collective-permute-start.27 = (bf16[96,1536]{1,0:T(8,128)(2,1)S(1)}, bf16[96,1536]{1,0:T(8,128)(2,1)S(1)}, u32[]{:S(2)}, u32[]{:S(2)}) collective-permute-start(bf16[96,1536]{1,0:T(8,128)(2,1)S(1)} %collective-permute-done.25.refs_1_), channel_id=1, source_target_pairs={{0,2},{1,7},{2,4},{3,1},{4,6},{5,3},{6,0},{7,5},{8,10},{9,15},{10,... | collective-permute-start | bytes 884744 | tf_op jit(solution)/shard_map/ppermute | solution.py:155
  187.3 13.6 %collective-permute-done.27.refs_3_ = bf16[96,1536]{1,0:T(8,128)(2,1)S(1)} collective-permute-done((bf16[96,1536]{1,0:T(8,128)(2,1)S(1)}, bf16[96,1536]{1,0:T(8,128)(2,1)S(1)}, u32[]{:S(2)}, u32[]{:S(2)}) %collective-permute-start.27) | collective-permute-done | bytes 294944 | tf_op jit(solution)/shard_map/ppermute | solution.py:155
  203.0 5.0 %collective-permute-start.32 = (bf16[96,512]{1,0:T(8,128)(2,1)S(1)}, bf16[96,512]{1,0:T(8,128)(2,1)S(1)}, u32[]{:S(2)}, u32[]{:S(2)}) collective-permute-start(bf16[96,512]{1,0:T(8,128)(2,1)S(1)} %get-tuple-element.39), channel_id=1, source_target_pairs={{0,24},{8,0},{16,8},{24,16},{1,25},{9,1},{17,9},{25,17},{2,26},{10... | collective-permute-start | bytes 294920 | tf_op jit(solution)/shard_map/ppermute | solution.py:28
  208.0 18.2 %collective-permute-start.31 = (bf16[96,512]{1,0:T(8,128)(2,1)S(1)}, bf16[96,512]{1,0:T(8,128)(2,1)S(1)}, u32[]{:S(2)}, u32[]{:S(2)}) collective-permute-start(bf16[96,512]{1,0:T(8,128)(2,1)S(1)} %get-tuple-element.40), channel_id=1, source_target_pairs={{0,16},{8,24},{16,0},{24,8},{1,17},{9,25},{17,1},{25,9},{2,18},{10... | collective-permute-start | bytes 294920 | tf_op jit(solution)/shard_map/ppermute | solution.py:28
  (81 shorter events, 53.9 us)
Async XLA Ops:
  0.6 12.3 %collective-permute-start.1 = (bf16[96,512]{1,0:T(8,128)(2,1)}, bf16[96,512]{1,0:T(8,128)(2,1)S(1)}, u32[]{:S(2)}, u32[]{:S(2)}) collective-permute-start(bf16[96,512]{1,0:T(8,128)(2,1)} %bitcast.27), channel_id=1, source_target_pairs={{0,16},{8,24},{16,0},{24,8},{1,17},{9,25},{17,1},{25,9},{2,18},{10... | collective-permute-start | bytes 294920 | tf_op jit(solution)/shard_map/ppermute | solution.py:28
  9.1 8.5 %collective-permute-start.2 = (bf16[96,512]{1,0:T(8,128)(2,1)}, bf16[96,512]{1,0:T(8,128)(2,1)S(1)}, u32[]{:S(2)}, u32[]{:S(2)}) collective-permute-start(bf16[96,512]{1,0:T(8,128)(2,1)} %bitcast.29), channel_id=1, source_target_pairs={{0,8},{8,16},{16,24},{24,0},{1,9},{9,17},{17,25},{25,1},{2,10},{10... | collective-permute-start | bytes 294920 | tf_op jit(solution)/shard_map/ppermute | solution.py:28
  17.6 13.5 %collective-permute-start.3 = (bf16[384,512]{1,0:T(8,128)(2,1)S(1)}, bf16[384,512]{1,0:T(8,128)(2,1)S(1)}, u32[]{:S(2)}, u32[]{:S(2)}) collective-permute-start(bf16[384,512]{1,0:T(8,128)(2,1)S(1)} %constant_dynamic-update-slice_fusion.2), channel_id=1, source_target_pairs={{0,96},{1,385},{32,0},{33,417},{64,32},{65,449},{96,64},{97,481},{... | collective-permute-start | bytes 1179656 | tf_op jit(solution)/shard_map/ppermute | solution.py:145
  22.3 12.3 %collective-permute-start.4 = (bf16[384,512]{1,0:T(8,128)(2,1)S(1)}, bf16[384,512]{1,0:T(8,128)(2,1)S(1)}, u32[]{:S(2)}, u32[]{:S(2)}) collective-permute-start(bf16[384,512]{1,0:T(8,128)(2,1)S(1)} %constant_dynamic-update-slice_fusion.2), channel_id=1, source_target_pairs={{0,64},{1,257},{32,96},{33,289},{64,0},{65,321},{96,32},{97,353},{... | collective-permute-start | bytes 1179656 | tf_op jit(solution)/shard_map/ppermute | solution.py:145
  25.0 12.7 %collective-permute-start.5 = (bf16[384,512]{1,0:T(8,128)(2,1)S(1)}, bf16[384,512]{1,0:T(8,128)(2,1)S(1)}, u32[]{:S(2)}, u32[]{:S(2)}) collective-permute-start(bf16[384,512]{1,0:T(8,128)(2,1)S(1)} %constant_dynamic-update-slice_fusion.2), channel_id=1, source_target_pairs={{0,32},{1,129},{32,64},{33,161},{64,96},{65,193},{96,0},{97,225},{... | collective-permute-start | bytes 1179656 | tf_op jit(solution)/shard_map/ppermute | solution.py:145
  31.2 15.6 %collective-permute-start.6 = (bf16[768,512]{1,0:T(8,128)(2,1)S(1)}, bf16[768,512]{1,0:T(8,128)(2,1)S(1)}, u32[]{:S(2)}, u32[]{:S(2)}) collective-permute-start(bf16[768,512]{1,0:T(8,128)(2,1)S(1)} %pad_maximum_fusion.1.refs_0_), channel_id=1, source_target_pairs={{0,384},{1,97},{32,416},{33,1},{64,448},{65,33},{96,480},{97,65},{... | collective-permute-start | bytes 2359304 | tf_op jit(solution)/shard_map/ppermute | solution.py:145
  37.7 13.9 %collective-permute-start.9 = (bf16[768,512]{1,0:T(8,128)(2,1)S(1)}, bf16[768,512]{1,0:T(8,128)(2,1)S(1)}, u32[]{:S(2)}, u32[]{:S(2)}) collective-permute-start(bf16[768,512]{1,0:T(8,128)(2,1)S(1)} %constant_dynamic-update-slice_fusion.refs_1_), channel_id=1, source_target_pairs={{0,128},{1,33},{32,160},{33,65},{64,192},{65,97},{96,224},{97,1},{... | collective-permute-start | bytes 2359304 | tf_op jit(solution)/shard_map/ppermute | solution.py:145
  40.9 19.2 %collective-permute-start.11 = (bf16[768,512]{1,0:T(8,128)(2,1)S(1)}, bf16[768,512]{1,0:T(8,128)(2,1)}, u32[]{:S(2)}, u32[]{:S(2)}) collective-permute-start(bf16[768,512]{1,0:T(8,128)(2,1)S(1)} %pad_maximum_fusion.1.refs_0_), channel_id=1, source_target_pairs={{0,128},{1,33},{32,160},{33,65},{64,192},{65,97},{96,224},{97,1},{... | collective-permute-start | bytes 2359304 | tf_op jit(solution)/shard_map/ppermute | solution.py:145
  43.1 17.1 %collective-permute-start.7 = (bf16[768,512]{1,0:T(8,128)(2,1)S(1)}, bf16[768,512]{1,0:T(8,128)(2,1)}, u32[]{:S(2)}, u32[]{:S(2)}) collective-permute-start(bf16[768,512]{1,0:T(8,128)(2,1)S(1)} %constant_dynamic-update-slice_fusion.refs_1_), channel_id=1, source_target_pairs={{0,384},{1,97},{32,416},{33,1},{64,448},{65,33},{96,480},{97,65},{... | collective-permute-start | bytes 2359304 | tf_op jit(solution)/shard_map/ppermute | solution.py:145
  46.8 18.7 %collective-permute-start.8 = (bf16[768,512]{1,0:T(8,128)(2,1)S(1)}, bf16[768,512]{1,0:T(8,128)(2,1)}, u32[]{:S(2)}, u32[]{:S(2)}) collective-permute-start(bf16[768,512]{1,0:T(8,128)(2,1)S(1)} %collective-permute-done.6.refs_2_), channel_id=1, source_target_pairs={{0,384},{1,97},{32,416},{33,1},{64,448},{65,33},{96,480},{97,65},{... | collective-permute-start | bytes 2359304 | tf_op jit(solution)/shard_map/ppermute | solution.py:145
  51.6 17.0 %collective-permute-start.10 = (bf16[768,512]{1,0:T(8,128)(2,1)S(1)}, bf16[768,512]{1,0:T(8,128)(2,1)}, u32[]{:S(2)}, u32[]{:S(2)}) collective-permute-start(bf16[768,512]{1,0:T(8,128)(2,1)S(1)} %collective-permute-done.9.refs_5_.refs_7_), channel_id=1, source_target_pairs={{0,128},{1,33},{32,160},{33,65},{64,192},{65,97},{96,224},{97,1},{... | collective-permute-start | bytes 2359304 | tf_op jit(solution)/shard_map/ppermute | solution.py:145
  76.6 25.7 %collective-permute-start.21 = (bf16[4,96,1536]{2,1,0:T(8,128)(2,1)}, bf16[4,96,1536]{2,1,0:T(8,128)(2,1)S(1)}, u32[]{:S(2)}, u32[]{:S(2)}) collective-permute-start(bf16[4,96,1536]{2,1,0:T(8,128)(2,1)} %get-tuple-element.30), channel_id=1, source_target_pairs={{0,1},{1,0},{2,3},{3,2},{4,5},{5,4},{6,7},{7,6},{8,9},{9,8},{10,11... | collective-permute-start | bytes 3538952 | tf_op jit(solution)/shard_map/ppermute | solution.py:28
  83.4 14.2 %collective-permute-start.12 = (bf16[768,512]{1,0:T(8,128)(2,1)}, bf16[768,512]{1,0:T(8,128)(2,1)S(1)}, u32[]{:S(2)}, u32[]{:S(2)}) collective-permute-start(bf16[768,512]{1,0:T(8,128)(2,1)} %get-tuple-element.23), channel_id=1, source_target_pairs={{0,128},{1,33},{32,160},{33,65},{64,192},{65,97},{96,224},{97,1},{... | collective-permute-start | bytes 2359304 | tf_op jit(solution)/shard_map/ppermute | solution.py:145
  86.7 29.4 %collective-permute-start.16 = (bf16[768,512]{1,0:T(8,128)(2,1)}, bf16[768,512]{1,0:T(8,128)(2,1)S(1)}, u32[]{:S(2)}, u32[]{:S(2)}) collective-permute-start(bf16[768,512]{1,0:T(8,128)(2,1)} %get-tuple-element.28), channel_id=1, source_target_pairs={{0,384},{1,97},{32,416},{33,1},{64,448},{65,33},{96,480},{97,65},{... | collective-permute-start | bytes 2359304 | tf_op jit(solution)/shard_map/ppermute | solution.py:145
  89.4 40.6 %collective-permute-start.14 = (bf16[768,512]{1,0:T(8,128)(2,1)}, bf16[768,512]{1,0:T(8,128)(2,1)S(1)}, u32[]{:S(2)}, u32[]{:S(2)}) collective-permute-start(bf16[768,512]{1,0:T(8,128)(2,1)} %get-tuple-element.24), channel_id=1, source_target_pairs={{0,384},{1,97},{32,416},{33,1},{64,448},{65,33},{96,480},{97,65},{... | collective-permute-start | bytes 2359304 | tf_op jit(solution)/shard_map/ppermute | solution.py:145
  99.1 36.9 %collective-permute-start.13 = (bf16[768,512]{1,0:T(8,128)(2,1)S(1)}, bf16[768,512]{1,0:T(8,128)(2,1)S(1)}, u32[]{:S(2)}, u32[]{:S(2)}) collective-permute-start(bf16[768,512]{1,0:T(8,128)(2,1)S(1)} %add_convert_fusion.3), channel_id=1, source_target_pairs={{0,128},{1,33},{32,160},{33,65},{64,192},{65,97},{96,224},{97,1},{... | collective-permute-start | bytes 2359304 | tf_op jit(solution)/shard_map/ppermute | solution.py:145
  102.4 24.2 %collective-permute-start.23 = (bf16[96,1536]{1,0:T(8,128)(2,1)S(1)}, bf16[96,1536]{1,0:T(8,128)(2,1)S(1)}, u32[]{:S(2)}, u32[]{:S(2)}) collective-permute-start(bf16[96,1536]{1,0:T(8,128)(2,1)S(1)} %get-tuple-element.36), channel_id=1, source_target_pairs={{0,2},{1,7},{2,4},{3,1},{4,6},{5,3},{6,0},{7,5},{8,10},{9,15},{10,... | collective-permute-start | bytes 884744 | tf_op jit(solution)/shard_map/ppermute | solution.py:155
  111.5 51.8 %collective-permute-start.15 = (bf16[768,512]{1,0:T(8,128)(2,1)S(1)}, bf16[768,512]{1,0:T(8,128)(2,1)S(1)}, u32[]{:S(2)}, u32[]{:S(2)}) collective-permute-start(bf16[768,512]{1,0:T(8,128)(2,1)S(1)} %copy-done.9), channel_id=1, source_target_pairs={{0,128},{1,33},{32,160},{33,65},{64,192},{65,97},{96,224},{97,1},{... | collective-permute-start | bytes 2359304 | tf_op jit(solution)/shard_map/ppermute | solution.py:145
  116.4 47.0 %collective-permute-start.17 = (bf16[768,512]{1,0:T(8,128)(2,1)S(1)}, bf16[768,512]{1,0:T(8,128)(2,1)S(1)}, u32[]{:S(2)}, u32[]{:S(2)}) collective-permute-start(bf16[768,512]{1,0:T(8,128)(2,1)S(1)} %add_convert_fusion.1), channel_id=1, source_target_pairs={{0,384},{1,97},{32,416},{33,1},{64,448},{65,33},{96,480},{97,65},{... | collective-permute-start | bytes 2359304 | tf_op jit(solution)/shard_map/ppermute | solution.py:145
  126.6 21.6 %collective-permute-start.22 = (bf16[96,1536]{1,0:T(8,128)(2,1)S(1)}, bf16[96,1536]{1,0:T(8,128)(2,1)S(1)}, u32[]{:S(2)}, u32[]{:S(2)}) collective-permute-start(bf16[96,1536]{1,0:T(8,128)(2,1)S(1)} %get-tuple-element.35), channel_id=1, source_target_pairs={{0,3},{1,6},{2,5},{3,0},{4,7},{5,2},{6,1},{7,4},{8,11},{9,14},{10,... | collective-permute-start | bytes 884744 | tf_op jit(solution)/shard_map/ppermute | solution.py:155
  130.0 23.4 %collective-permute-start.24 = (bf16[96,1536]{1,0:T(8,128)(2,1)S(1)}, bf16[96,1536]{1,0:T(8,128)(2,1)S(1)}, u32[]{:S(2)}, u32[]{:S(2)}) collective-permute-start(bf16[96,1536]{1,0:T(8,128)(2,1)S(1)} %fusion), channel_id=1, source_target_pairs={{0,2},{1,7},{2,4},{3,1},{4,6},{5,3},{6,0},{7,5},{8,10},{9,15},{10,... | collective-permute-start | bytes 884744 | tf_op jit(solution)/shard_map/ppermute | solution.py:155
  136.3 66.4 %collective-permute-start.19 = (bf16[384,512]{1,0:T(8,128)(2,1)S(1)}, bf16[384,512]{1,0:T(8,128)(2,1)S(1)}, u32[]{:S(2)}, u32[]{:S(2)}) collective-permute-start(bf16[384,512]{1,0:T(8,128)(2,1)S(1)} %slice.50), channel_id=1, source_target_pairs={{0,32},{1,129},{32,64},{33,161},{64,96},{65,193},{96,0},{97,225},{... | collective-permute-start | bytes 1179656 | tf_op jit(solution)/shard_map/ppermute | solution.py:145
  153.5 18.5 %collective-permute-start.26 = (bf16[96,1536]{1,0:T(8,128)(2,1)S(1)}, bf16[96,1536]{1,0:T(8,128)(2,1)S(1)}, u32[]{:S(2)}, u32[]{:S(2)}) collective-permute-start(bf16[96,1536]{1,0:T(8,128)(2,1)S(1)} %fusion.3.refs_0_), channel_id=1, source_target_pairs={{0,6},{1,3},{2,0},{3,5},{4,2},{5,7},{6,4},{7,1},{8,14},{9,11},{10,... | collective-permute-start | bytes 884744 | tf_op jit(solution)/shard_map/ppermute | solution.py:155
  160.0 19.8 %collective-permute-start.25 = (bf16[96,1536]{1,0:T(8,128)(2,1)S(1)}, bf16[96,1536]{1,0:T(8,128)(2,1)S(1)}, u32[]{:S(2)}, u32[]{:S(2)}) collective-permute-start(bf16[96,1536]{1,0:T(8,128)(2,1)S(1)} %fusion.3.refs_0_), channel_id=1, source_target_pairs={{0,2},{1,7},{2,4},{3,1},{4,6},{5,3},{6,0},{7,5},{8,10},{9,15},{10,... | collective-permute-start | bytes 884744 | tf_op jit(solution)/shard_map/ppermute | solution.py:155
  163.7 39.0 %collective-permute-start.18 = (bf16[384,512]{1,0:T(8,128)(2,1)S(1)}, bf16[384,512]{1,0:T(8,128)(2,1)S(1)}, u32[]{:S(2)}, u32[]{:S(2)}) collective-permute-start(bf16[384,512]{1,0:T(8,128)(2,1)S(1)} %get-tuple-element.37), channel_id=1, source_target_pairs={{0,64},{1,257},{32,96},{33,289},{64,0},{65,321},{96,32},{97,353},{... | collective-permute-start | bytes 1179656 | tf_op jit(solution)/shard_map/ppermute | solution.py:145
  166.9 35.9 %collective-permute-start.20 = (bf16[384,512]{1,0:T(8,128)(2,1)S(1)}, bf16[384,512]{1,0:T(8,128)(2,1)S(1)}, u32[]{:S(2)}, u32[]{:S(2)}) collective-permute-start(bf16[384,512]{1,0:T(8,128)(2,1)S(1)} %get-tuple-element.38), channel_id=1, source_target_pairs={{0,96},{1,385},{32,0},{33,417},{64,32},{65,449},{96,64},{97,481},{... | collective-permute-start | bytes 1179656 | tf_op jit(solution)/shard_map/ppermute | solution.py:145
  179.9 48.2 %collective-permute-start.28 = (bf16[96,4608]{1,0:T(8,128)(2,1)S(1)}, bf16[96,4608]{1,0:T(8,128)(2,1)S(1)}, u32[]{:S(2)}, u32[]{:S(2)}) collective-permute-start(bf16[96,4608]{1,0:T(8,128)(2,1)S(1)} %pad_maximum_fusion), channel_id=1, source_target_pairs={{0,1},{1,0},{2,3},{3,2},{4,5},{5,4},{6,7},{7,6},{8,9},{9,8},{10,11... | collective-permute-start | bytes 2654216 | tf_op jit(solution)/shard_map/ppermute | solution.py:28
  181.9 19.0 %collective-permute-start.27 = (bf16[96,1536]{1,0:T(8,128)(2,1)S(1)}, bf16[96,1536]{1,0:T(8,128)(2,1)S(1)}, u32[]{:S(2)}, u32[]{:S(2)}) collective-permute-start(bf16[96,1536]{1,0:T(8,128)(2,1)S(1)} %collective-permute-done.25.refs_1_), channel_id=1, source_target_pairs={{0,2},{1,7},{2,4},{3,1},{4,6},{5,3},{6,0},{7,5},{8,10},{9,15},{10,... | collective-permute-start | bytes 884744 | tf_op jit(solution)/shard_map/ppermute | solution.py:155
  200.8 27.3 %collective-permute-start.29 = (bf16[96,1536]{1,0:T(8,128)(2,1)S(1)}, bf16[96,1536]{1,0:T(8,128)(2,1)S(1)}, u32[]{:S(2)}, u32[]{:S(2)}) collective-permute-start(bf16[96,1536]{1,0:T(8,128)(2,1)S(1)} %collective-permute-done.27.refs_3_), channel_id=1, source_target_pairs={{0,1},{1,0},{2,3},{3,2},{4,5},{5,4},{6,7},{7,6},{8,9},{9,8},{10,11... | collective-permute-start | bytes 884744 | tf_op jit(solution)/shard_map/ppermute | solution.py:28
  203.0 27.5 %collective-permute-start.32 = (bf16[96,512]{1,0:T(8,128)(2,1)S(1)}, bf16[96,512]{1,0:T(8,128)(2,1)S(1)}, u32[]{:S(2)}, u32[]{:S(2)}) collective-permute-start(bf16[96,512]{1,0:T(8,128)(2,1)S(1)} %get-tuple-element.39), channel_id=1, source_target_pairs={{0,24},{8,0},{16,8},{24,16},{1,25},{9,1},{17,9},{25,17},{2,26},{10... | collective-permute-start | bytes 294920 | tf_op jit(solution)/shard_map/ppermute | solution.py:28
  208.0 23.6 %collective-permute-start.31 = (bf16[96,512]{1,0:T(8,128)(2,1)S(1)}, bf16[96,512]{1,0:T(8,128)(2,1)S(1)}, u32[]{:S(2)}, u32[]{:S(2)}) collective-permute-start(bf16[96,512]{1,0:T(8,128)(2,1)S(1)} %get-tuple-element.40), channel_id=1, source_target_pairs={{0,16},{8,24},{16,0},{24,8},{1,17},{9,25},{17,1},{25,9},{2,18},{10... | collective-permute-start | bytes 294920 | tf_op jit(solution)/shard_map/ppermute | solution.py:28
  226.2 8.3 %collective-permute-start.30 = (bf16[96,512]{1,0:T(8,128)(2,1)S(1)}, bf16[96,512]{1,0:T(8,128)(2,1)S(1)}, u32[]{:S(2)}, u32[]{:S(2)}) collective-permute-start(bf16[96,512]{1,0:T(8,128)(2,1)S(1)} %get-tuple-element.41), channel_id=1, source_target_pairs={{0,8},{8,16},{16,24},{24,0},{1,9},{9,17},{17,25},{25,1},{2,10},{10... | collective-permute-start | bytes 294920 | tf_op jit(solution)/shard_map/ppermute | solution.py:28
  (11 other events, 221.4 us)
